TPU v7x, 32 devices: a whole 2x2x4 slice. The times are simulated.
32 devices in a mesh: dp: 2 (over core), seq: 16 (over z, y, x).
Axes of the slice: x: 2, y: 2, z: 4, core: 2. Of those that a mesh axis runs over, the one named last changes fastest.
Arguments:
- inputs: bfloat16 [2, 2048, 2048], P('dp', 'seq'), may hold values from -6 to 6
- positions: int32 [2, 2048], P('dp', 'seq'), may hold values from 0 to 4095
- select: int32 [2, 2048], P('dp', 'seq'), may hold values 0 or 1
- cotangent: bfloat16 [2, 2048, 2048], P('dp', 'seq'), may hold values from -6 to 6
- gain_attn: bfloat16 [2048], P('seq'), may hold values from 0.25 to 1.75
- w_query: bfloat16 [2048, 2048], P('seq'), may hold values from -0.1875 to 0.1875
- w_key: bfloat16 [2048, 256], P('seq'), may hold values from -0.1875 to 0.1875
- w_value: bfloat16 [2048, 256], P('seq'), may hold values from -0.125 to 0.125
- w_out: bfloat16 [2048, 2048], P('seq'), may hold values from -0.5 to 0.5
- gain_mlp: bfloat16 [2048], P('seq'), may hold values from 0.25 to 1.75
- w_gate: bfloat16 [2048, 5632], P('seq'), may hold values from -0.125 to 0.125
- w_up: bfloat16 [2048, 5632], P('seq'), may hold values from -0.125 to 0.125
- w_down: bfloat16 [5632, 2048], P('seq'), may hold values from -0.078125 to 0.078125
Outputs:
- outputs: bfloat16 [2, 2048, 2048], P('dp', 'seq')
- grad_inputs: float32 [2, 2048, 2048], P('dp', 'seq')
- grad_gain_attn: float32 [2048], P('seq')
- grad_w_query: float32 [2048, 2048], P('seq')
- grad_w_key: float32 [2048, 256], P('seq')
- grad_w_value: float32 [2048, 256], P('seq')
- grad_w_out: float32 [2048, 2048], P('seq')
- grad_gain_mlp: float32 [2048], P('seq')
- grad_w_gate: float32 [2048, 5632], P('seq')
- grad_w_up: float32 [2048, 5632], P('seq')
- grad_w_down: float32 [5632, 2048], P('seq')
All inputs are finite; a program needn't handle non-finite values. No bound on the sum of `select` on one device may be relied on, other than what follows from the above.
Results may differ from a plain program's by a relative error of at most 0.025.
Values may be sent and summed in bfloat16 or wider, within the bound.
No kernel may reach another device: no remote copies, remote signals or barrier semaphores. Data moves between devices by JAX's collectives and lax.ppermute only.
A program may use at most 384 MiB of HBM per device.

v0:
```python
import jax
import jax.numpy as jnp
from jax import lax
from jax.sharding import PartitionSpec as P

HEADS = 32
KV_HEADS = 4
HEAD_DIM = 64


epsilon = 1e-05
rope_base = 10000.0
masked_score = -1e30


def normalize(values, gain):
    inverse = lax.rsqrt(jnp.mean(values * values, axis=-1, keepdims=True) + epsilon)
    normed = values * inverse
    return (normed, inverse, (normed * gain.astype(jnp.float32)).astype(jnp.bfloat16))


def norm_back(grad_out, normed, inverse, gain):
    gain_grad = jnp.sum(grad_out * normed, axis=(0, 1))
    inner = grad_out * gain.astype(jnp.float32)
    grad_in = inverse * (inner - normed * jnp.mean(inner * normed, axis=-1, keepdims=True))
    return (grad_in, gain_grad)


def rope_tables(positions):
    half_dim = HEAD_DIM // 2
    frequency = rope_base ** (-(jnp.arange(half_dim).astype(jnp.float32) * 2.0 / HEAD_DIM))
    angles = positions.astype(jnp.float32)[..., None] * frequency
    angles = jnp.concatenate([angles, angles], axis=-1)
    return (jnp.cos(angles)[:, :, None], jnp.sin(angles)[:, :, None])


def rotate(values, cosine, sine):
    half_dim = values.shape[-1] // 2
    turned = jnp.concatenate([-values[..., half_dim:], values[..., :half_dim]], axis=-1)
    return values * cosine + turned * sine


def unrotate(grads, cosine, sine):
    half_dim = grads.shape[-1] // 2
    scaled = grads * sine
    back_part = jnp.concatenate([scaled[..., half_dim:], -scaled[..., :half_dim]], axis=-1)
    return grads * cosine + back_part


def attend(blocks):
    queries, keys, values = blocks
    seq_count, length, row_width = queries.shape
    head_count = row_width // HEAD_DIM
    query_four = queries.reshape(seq_count, length, head_count, HEAD_DIM)
    key_four = keys.reshape(seq_count, length, head_count, HEAD_DIM)
    value_four = values.reshape(seq_count, length, head_count, HEAD_DIM)
    span = min(512, length)
    key_rows = jnp.arange(length)
    score_scale = HEAD_DIM ** (-0.5)

    def one_block(index):
        start = index * span
        query_block = lax.dynamic_slice_in_dim(query_four, start, span, 1)
        scores = (
            jnp.einsum("nqhd,nkhd->nhqk", query_block, key_four, preferred_element_type=jnp.float32)
            * score_scale
        )
        allowed = key_rows[None, :] <= (start + jnp.arange(span))[:, None]
        scores = jnp.where(allowed, scores, masked_score)
        highest_score = jnp.max(scores, axis=-1, keepdims=True)
        weights = jnp.exp(scores - highest_score)
        total = jnp.sum(weights, axis=-1, keepdims=True)
        probs = (weights / total).astype(jnp.bfloat16)
        attended = jnp.einsum(
            "nhqk,nkhd->nqhd", probs, value_four, preferred_element_type=jnp.float32
        )
        log_total = (highest_score + jnp.log(total))[..., 0]
        return (attended.astype(jnp.bfloat16).reshape(seq_count, span, row_width), log_total)

    pieces, log_parts = lax.map(one_block, jnp.arange(length // span))
    attended_all = jnp.moveaxis(pieces, 0, 1).reshape(seq_count, length, row_width)
    log_totals = jnp.transpose(log_parts, (1, 2, 0, 3)).reshape(seq_count, head_count, length)
    return (queries, keys, values, attended_all, log_totals)


def attend_back(queries, keys, values, grad_out, log_totals):
    seq_count, length, row_width = queries.shape
    head_count = row_width // HEAD_DIM
    four_shape = (seq_count, length, head_count, HEAD_DIM)
    query_four = queries.reshape(four_shape)
    key_four = keys.reshape(four_shape)
    value_four = values.reshape(four_shape)
    grad_four = grad_out.reshape(four_shape)
    span = min(512, length)
    key_rows = jnp.arange(length)
    score_scale = HEAD_DIM ** (-0.5)

    def one_block(carry, index):
        key_grad, value_grad = carry
        start = index * span
        query_block = lax.dynamic_slice_in_dim(query_four, start, span, 1)
        grad_block = lax.dynamic_slice_in_dim(grad_four, start, span, 1)
        log_block = lax.dynamic_slice_in_dim(log_totals, start, span, 2)
        scores = (
            jnp.einsum("nqhd,nkhd->nhqk", query_block, key_four, preferred_element_type=jnp.float32)
            * score_scale
        )
        allowed = key_rows[None, :] <= (start + jnp.arange(span))[:, None]
        scores = jnp.where(allowed, scores, masked_score)
        probs = jnp.exp(scores - log_block[..., None])
        value_grad = value_grad + jnp.einsum(
            "nhqk,nqhd->nkhd",
            probs.astype(jnp.bfloat16),
            grad_block,
            preferred_element_type=jnp.float32,
        )
        prob_grad = jnp.einsum(
            "nqhd,nkhd->nhqk", grad_block, value_four, preferred_element_type=jnp.float32
        )
        inner = jnp.sum(probs * prob_grad, axis=-1, keepdims=True)
        score_grad = (probs * (prob_grad - inner)).astype(jnp.bfloat16)
        query_grad = (
            jnp.einsum("nhqk,nkhd->nqhd", score_grad, key_four, preferred_element_type=jnp.float32)
            * score_scale
        )
        key_grad = (
            key_grad
            + jnp.einsum(
                "nhqk,nqhd->nkhd", score_grad, query_block, preferred_element_type=jnp.float32
            )
            * score_scale
        )
        return (
            (key_grad, value_grad),
            query_grad.astype(jnp.bfloat16).reshape(seq_count, span, row_width),
        )

    empty = jnp.zeros(four_shape, jnp.float32)
    (key_grad, value_grad), pieces = lax.scan(one_block, (empty, empty), jnp.arange(length // span))
    query_grad = jnp.moveaxis(pieces, 0, 1).reshape(seq_count, length, row_width)
    key_low = key_grad.astype(jnp.bfloat16).reshape(seq_count, length, row_width)
    value_low = value_grad.astype(jnp.bfloat16).reshape(seq_count, length, row_width)
    return (query_grad, key_low, value_low)


def forward(inputs, positions, attn_full, mlp_full):
    gain_one, query_weight, key_weight, value_weight, out_weight = attn_full
    gain_two, gate_weight, up_weight, down_weight = mlp_full
    seq_count, row_count, model_width = inputs.shape
    x_in = inputs.astype(jnp.float32)
    normed_one, inverse_one, low_one = normalize(x_in, gain_one)
    cosine, sine = rope_tables(positions)
    query = jnp.einsum("srd,dk->srk", low_one, query_weight, preferred_element_type=jnp.float32)
    key = jnp.einsum("srd,dk->srk", low_one, key_weight, preferred_element_type=jnp.float32)
    value = jnp.einsum("srd,dk->srk", low_one, value_weight, preferred_element_type=jnp.float32)
    query = query.reshape(seq_count, row_count, HEADS, HEAD_DIM)
    key = key.reshape(seq_count, row_count, KV_HEADS, HEAD_DIM)
    value = value.reshape(seq_count, row_count, KV_HEADS, HEAD_DIM)
    query_low = (
        rotate(query, cosine, sine).astype(jnp.bfloat16).reshape(seq_count, row_count, model_width)
    )
    key_low = rotate(key, cosine, sine).astype(jnp.bfloat16)
    value_low = value.astype(jnp.bfloat16)
    repeat = HEADS // KV_HEADS
    key_all = jnp.repeat(key_low, repeat, axis=2).reshape(seq_count, row_count, model_width)
    value_all = jnp.repeat(value_low, repeat, axis=2).reshape(seq_count, row_count, model_width)
    q_heads, k_heads, v_heads, o_heads, log_totals = attend(
        (
            lax.all_to_all(query_low, "seq", split_axis=2, concat_axis=1, tiled=True),
            lax.all_to_all(key_all, "seq", split_axis=2, concat_axis=1, tiled=True),
            lax.all_to_all(value_all, "seq", split_axis=2, concat_axis=1, tiled=True),
        )
    )
    o_rows = lax.all_to_all(o_heads, "seq", split_axis=1, concat_axis=2, tiled=True)
    branch = jnp.einsum("srk,kd->srd", o_rows, out_weight, preferred_element_type=jnp.float32)
    x_mid = x_in + branch
    normed_two, inverse_two, low_two = normalize(x_mid, gain_two)
    gate = jnp.einsum("srd,df->srf", low_two, gate_weight, preferred_element_type=jnp.float32)
    up_part = jnp.einsum("srd,df->srf", low_two, up_weight, preferred_element_type=jnp.float32)
    hidden = (gate / (1.0 + jnp.exp(-gate)) * up_part).astype(jnp.bfloat16)
    mixed = jnp.einsum("srf,fd->srd", hidden, down_weight, preferred_element_type=jnp.float32)
    return (
        x_in,
        normed_one,
        inverse_one,
        low_one,
        cosine,
        sine,
        q_heads,
        k_heads,
        v_heads,
        log_totals,
        o_rows,
        x_mid,
        normed_two,
        inverse_two,
        low_two,
        gate,
        up_part,
        hidden,
        mixed,
    )


def body(
    inputs,
    positions,
    select,
    cotangent,
    gain_attn,
    w_query,
    w_key,
    w_value,
    w_out,
    gain_mlp,
    w_gate,
    w_up,
    w_down,
):
    attn_full = (
        lax.all_gather(gain_attn, "seq", axis=0, tiled=True),
        lax.all_gather(w_query, "seq", axis=0, tiled=True),
        lax.all_gather(w_key, "seq", axis=0, tiled=True),
        lax.all_gather(w_value, "seq", axis=0, tiled=True),
        lax.all_gather(w_out, "seq", axis=0, tiled=True),
    )
    mlp_full = (
        lax.all_gather(gain_mlp, "seq", axis=0, tiled=True),
        lax.all_gather(w_gate, "seq", axis=0, tiled=True),
        lax.all_gather(w_up, "seq", axis=0, tiled=True),
        lax.all_gather(w_down, "seq", axis=0, tiled=True),
    )
    saved = forward(inputs, positions, attn_full, mlp_full)
    outputs = (saved[11] + saved[18]).astype(jnp.bfloat16)
    (
        x_in,
        normed_one,
        inverse_one,
        low_one,
        cosine,
        sine,
        q_heads,
        k_heads,
        v_heads,
        log_totals,
        o_rows,
        x_mid,
        normed_two,
        inverse_two,
        low_two,
        gate,
        up_part,
        hidden,
        mixed,
    ) = saved
    gain_one, query_weight, key_weight, value_weight, out_weight = attn_full
    gain_two, gate_weight, up_weight, down_weight = mlp_full
    seq_count, row_count, model_width = inputs.shape
    grad_y = cotangent.astype(jnp.float32) * select.astype(jnp.float32)[..., None]
    grad_y_low = grad_y.astype(jnp.bfloat16)
    grad_down = jnp.einsum("srf,srd->fd", hidden, grad_y_low, preferred_element_type=jnp.float32)
    grad_hidden = jnp.einsum(
        "srd,fd->srf", grad_y_low, down_weight, preferred_element_type=jnp.float32
    )
    sigmoid_gate = 1.0 / (1.0 + jnp.exp(-gate))
    grad_gate = (grad_hidden * up_part * sigmoid_gate * (1.0 + gate * (1.0 - sigmoid_gate))).astype(
        jnp.bfloat16
    )
    grad_up = (grad_hidden * gate * sigmoid_gate).astype(jnp.bfloat16)
    grad_gate_weight = jnp.einsum(
        "srd,srf->df", low_two, grad_gate, preferred_element_type=jnp.float32
    )
    grad_up_weight = jnp.einsum("srd,srf->df", low_two, grad_up, preferred_element_type=jnp.float32)
    grad_low_two = jnp.einsum(
        "srf,df->srd", grad_gate, gate_weight, preferred_element_type=jnp.float32
    )
    grad_low_two = grad_low_two + jnp.einsum(
        "srf,df->srd", grad_up, up_weight, preferred_element_type=jnp.float32
    )
    grad_x_norm, grad_gain_two = norm_back(grad_low_two, normed_two, inverse_two, gain_two)
    grad_x_mid = grad_y + grad_x_norm
    mlp_sums = (
        lax.psum_scatter(
            grad_gain_two.astype(jnp.bfloat16), "seq", scatter_dimension=0, tiled=True
        ).astype(jnp.float32),
        lax.psum_scatter(
            grad_gate_weight.astype(jnp.bfloat16), "seq", scatter_dimension=0, tiled=True
        ).astype(jnp.float32),
        lax.psum_scatter(
            grad_up_weight.astype(jnp.bfloat16), "seq", scatter_dimension=0, tiled=True
        ).astype(jnp.float32),
        lax.psum_scatter(
            grad_down.astype(jnp.bfloat16), "seq", scatter_dimension=0, tiled=True
        ).astype(jnp.float32),
    )
    grad_branch = grad_x_mid.astype(jnp.bfloat16)
    grad_out_weight = jnp.einsum(
        "srk,srd->kd", o_rows, grad_branch, preferred_element_type=jnp.float32
    )
    grad_o_rows = jnp.einsum(
        "srd,kd->srk", grad_branch, out_weight, preferred_element_type=jnp.float32
    ).astype(jnp.bfloat16)
    grad_o_heads = lax.all_to_all(grad_o_rows, "seq", split_axis=2, concat_axis=1, tiled=True)
    query_grad, key_grad, value_grad = attend_back(
        q_heads, k_heads, v_heads, grad_o_heads, log_totals
    )
    query_rows, key_rows, value_rows = (
        lax.all_to_all(query_grad, "seq", split_axis=1, concat_axis=2, tiled=True),
        lax.all_to_all(key_grad, "seq", split_axis=1, concat_axis=2, tiled=True),
        lax.all_to_all(value_grad, "seq", split_axis=1, concat_axis=2, tiled=True),
    )
    repeat = HEADS // KV_HEADS
    query_four = query_rows.astype(jnp.float32).reshape(seq_count, row_count, HEADS, HEAD_DIM)
    key_four = jnp.sum(
        key_rows.astype(jnp.float32).reshape(seq_count, row_count, KV_HEADS, repeat, HEAD_DIM),
        axis=3,
    )
    value_four = jnp.sum(
        value_rows.astype(jnp.float32).reshape(seq_count, row_count, KV_HEADS, repeat, HEAD_DIM),
        axis=3,
    )
    query_pre = (
        unrotate(query_four, cosine, sine)
        .astype(jnp.bfloat16)
        .reshape(seq_count, row_count, model_width)
    )
    key_pre = (
        unrotate(key_four, cosine, sine)
        .astype(jnp.bfloat16)
        .reshape(seq_count, row_count, KV_HEADS * HEAD_DIM)
    )
    value_pre = value_four.astype(jnp.bfloat16).reshape(seq_count, row_count, KV_HEADS * HEAD_DIM)
    grad_query_weight = jnp.einsum(
        "srd,srk->dk", low_one, query_pre, preferred_element_type=jnp.float32
    )
    grad_key_weight = jnp.einsum(
        "srd,srk->dk", low_one, key_pre, preferred_element_type=jnp.float32
    )
    grad_value_weight = jnp.einsum(
        "srd,srk->dk", low_one, value_pre, preferred_element_type=jnp.float32
    )
    grad_low_one = jnp.einsum(
        "srk,dk->srd", query_pre, query_weight, preferred_element_type=jnp.float32
    )
    grad_low_one = grad_low_one + jnp.einsum(
        "srk,dk->srd", key_pre, key_weight, preferred_element_type=jnp.float32
    )
    grad_low_one = grad_low_one + jnp.einsum(
        "srk,dk->srd", value_pre, value_weight, preferred_element_type=jnp.float32
    )
    grad_x_first, grad_gain_one = norm_back(grad_low_one, normed_one, inverse_one, gain_one)
    grad_inputs = grad_x_mid + grad_x_first
    attn_sums = (
        lax.psum_scatter(
            grad_gain_one.astype(jnp.bfloat16), "seq", scatter_dimension=0, tiled=True
        ).astype(jnp.float32),
        lax.psum_scatter(
            grad_query_weight.astype(jnp.bfloat16), "seq", scatter_dimension=0, tiled=True
        ).astype(jnp.float32),
        lax.psum_scatter(
            grad_key_weight.astype(jnp.bfloat16), "seq", scatter_dimension=0, tiled=True
        ).astype(jnp.float32),
        lax.psum_scatter(
            grad_value_weight.astype(jnp.bfloat16), "seq", scatter_dimension=0, tiled=True
        ).astype(jnp.float32),
        lax.psum_scatter(
            grad_out_weight.astype(jnp.bfloat16), "seq", scatter_dimension=0, tiled=True
        ).astype(jnp.float32),
    )
    totals = (
        lax.psum(attn_sums[0].astype(jnp.bfloat16), "dp").astype(jnp.float32),
        lax.psum(attn_sums[1].astype(jnp.bfloat16), "dp").astype(jnp.float32),
        lax.psum(attn_sums[2].astype(jnp.bfloat16), "dp").astype(jnp.float32),
        lax.psum(attn_sums[3].astype(jnp.bfloat16), "dp").astype(jnp.float32),
        lax.psum(attn_sums[4].astype(jnp.bfloat16), "dp").astype(jnp.float32),
        lax.psum(mlp_sums[0].astype(jnp.bfloat16), "dp").astype(jnp.float32),
        lax.psum(mlp_sums[1].astype(jnp.bfloat16), "dp").astype(jnp.float32),
        lax.psum(mlp_sums[2].astype(jnp.bfloat16), "dp").astype(jnp.float32),
        lax.psum(mlp_sums[3].astype(jnp.bfloat16), "dp").astype(jnp.float32),
    )
    return (
        outputs,
        grad_inputs,
        totals[0],
        totals[1],
        totals[2],
        totals[3],
        totals[4],
        totals[5],
        totals[6],
        totals[7],
        totals[8],
    )


def solution(mesh):
    in_specs = (
        P("dp", "seq", None),
        P("dp", "seq"),
        P("dp", "seq"),
        P("dp", "seq", None),
        P("seq"),
        P("seq", None),
        P("seq", None),
        P("seq", None),
        P("seq", None),
        P("seq"),
        P("seq", None),
        P("seq", None),
        P("seq", None),
    )
    out_specs = (
        P("dp", "seq", None),
        P("dp", "seq", None),
        P("seq"),
        P("seq", None),
        P("seq", None),
        P("seq", None),
        P("seq", None),
        P("seq"),
        P("seq", None),
        P("seq", None),
        P("seq", None),
    )
    return jax.shard_map(body, mesh=mesh, in_specs=in_specs, out_specs=out_specs, check_vma=False)
```

profile of v0, /device:TPU:1, one launch (start us, length us, event | category | flops | bytes accessed | tf_op | source)
XLA Modules:
  0.0 3395.5 jit_solution(11471329758658169685)
XLA Ops:
  11.9 34.7 %all-gather = bf16[16,1,128]{2,1,0:T(2,128)(2,1)S(1)} all-gather(bf16[1,1,128]{2,1,0:T(2,128)(2,1)} %bitcast.387), channel_id=1, replica_groups=mesh['dp'=2,'seq'=16] {'seq'}, dimensions={0}, use_global_device_ids=true | all-gather | bytes 4352 | tf_op jit(solution)/shard_map/all_gather | solution.py:221
  48.7 17.2 all-gather.12.cloned.1.call-done
  96.6 28.4 all-gather.14.cloned.1.call-done
  152.1 91.5 %all-gather.10.cloned.1.call-done = bf16[2048,2048]{1,0:T(8,128)(2,1)} async-done(((bf16[128,2048]{1,0:T(8,128)(2,1)}), bf16[2048,2048]{1,0:T(8,128)(2,1)}) %all-gather.10.cloned.1.call-update) | async-done | bytes 8388624 | tf_op jit(solution)/shard_map/all_gather | solution.py:222
  290.3 43.2 %while.28 = (s32[]{:T(128)}, bf16[4,1,512,128]{3,2,0,1:T(8,128)(2,1)}, f32[4,1,2,512]{3,2,1,0:T(2,128)S(1)}, s32[4]{0:T(128)S(1)}, bf16[1,2048,2,64]{1,3,2,0:T(8...) while((s32[]{:T(128)}, ...), condition=%wide.region_4.5_spmd.clone, body=%wide.region_1.4_spmd.clone.sunk | while | flops 563150336 | bytes 31232192 | solution.py:80
  347.8 13.0 all-to-all-start.3
  360.8 34.8 %all-gather.1 = bf16[16,1,128]{2,1,0:T(2,128)(2,1)S(1)} all-gather(bf16[1,1,128]{2,1,0:T(2,128)(2,1)S(1)} %bitcast.388), channel_id=1, replica_groups=mesh['dp'=2,'seq'=16] {'seq'}, dimensions={0}, use_global_device_ids=true | all-gather | bytes 4352 | tf_op jit(solution)/shard_map/all_gather | solution.py:228
  403.9 211.0 %all-gather.18.cloned.1.call-done = bf16[2048,5632]{1,0:T(8,128)(2,1)} async-done(((bf16[128,5632]{1,0:T(8,128)(2,1)}), bf16[2048,5632]{1,0:T(8,128)(2,1)}) %all-gather.18.cloned.1.call-update) | async-done | bytes 23068688 | tf_op jit(solution)/shard_map/all_gather | solution.py:229
  615.0 12.3 fusion.104
  627.3 239.0 %all-gather.20.cloned.1.call-done = bf16[2048,5632]{1,0:T(8,128)(2,1)} async-done(((bf16[128,5632]{1,0:T(8,128)(2,1)}), bf16[2048,5632]{1,0:T(8,128)(2,1)}) %all-gather.20.cloned.1.call-update) | async-done | bytes 23068688 | tf_op jit(solution)/shard_map/all_gather | solution.py:230
  866.3 12.3 fusion.105
  878.6 239.1 %all-gather.22.cloned.1.call-done = bf16[5632,2048]{1,0:T(8,128)(2,1)} async-done(((bf16[352,2048]{1,0:T(8,128)(2,1)}), bf16[5632,2048]{1,0:T(8,128)(2,1)}) %all-gather.22.cloned.1.call-update) | async-done | bytes 23068688 | tf_op jit(solution)/shard_map/all_gather | solution.py:231
  1117.7 14.9 multiply_convert_fusion.1
  1132.6 12.4 fusion.106
  1145.0 13.8 fusion.64
  1170.4 12.3 reduce.19
  1189.0 12.3 all-to-all-done.4
  1208.5 96.5 %while.29 = (s32[]{:T(128)}, f32[1,2048,2,64]{1,3,2,0:T(8,128)S(1)}, f32[1,2048,2,64]{1,3,2,0:T(8,128)}, bf16[4,1,512,128]{3,2,0,1:T(8,128)(2,1)}, s32[4]{0:T(12...) while((s32[]{:T(128)}, ...), condition=%wide.region_9.10_spmd.clone, body=%wide.region_7.9_spmd.clone.sunk | while | flops 1376124416 | bytes 157974848 | solution.py:139
  1317.9 17.8 all_to_all.102
  1341.8 12.6 reduce.22
  1354.5 18.6 all_to_all.104
  1403.7 20.7 all_to_all.103
  1434.7 12.2 convolution_convert_fusion.2
  1447.0 12.3 convolution_convert_fusion.1
  1460.3 12.6 convolution_convert_fusion
  1473.0 14.3 reduce-scatter.12.cloned.1.call-done
  1487.3 187.0 %reduce-scatter.14.cloned.1.call-done = bf16[128,2048]{1,0:T(8,128)(2,1)} async-done(((bf16[2048,2048]{1,0:T(8,128)(2,1)}), bf16[128,2048]{1,0:T(8,128)(2,1)}) %reduce-scatter.14.cloned.1.call-update) | async-done | bytes 524304 | tf_op jit(solution)/shard_map/reduce_scatter | solution.py:366
  1674.3 182.6 %reduce-scatter.8.cloned.1.call-done = bf16[128,2048]{1,0:T(8,128)(2,1)} async-done(((bf16[2048,2048]{1,0:T(8,128)(2,1)}), bf16[128,2048]{1,0:T(8,128)(2,1)}) %reduce-scatter.8.cloned.1.call-update) | async-done | bytes 524304 | tf_op jit(solution)/shard_map/reduce_scatter | solution.py:357
  1856.9 476.0 %reduce-scatter.16.cloned.1.call-done = bf16[128,5632]{1,0:T(8,128)(2,1)} async-done(((bf16[2048,5632]{1,0:T(8,128)(2,1)}), bf16[128,5632]{1,0:T(8,128)(2,1)}) %reduce-scatter.16.cloned.1.call-update) | async-done | bytes 1441808 | tf_op jit(solution)/shard_map/reduce_scatter | solution.py:286
  2333.0 482.2 %reduce-scatter.18.cloned.1.call-done = bf16[128,5632]{1,0:T(8,128)(2,1)} async-done(((bf16[2048,5632]{1,0:T(8,128)(2,1)}), bf16[128,5632]{1,0:T(8,128)(2,1)}) %reduce-scatter.18.cloned.1.call-update) | async-done | bytes 1441808 | tf_op jit(solution)/shard_map/reduce_scatter | solution.py:289
  2815.1 482.0 %reduce-scatter.20.cloned.1.call-done = bf16[352,2048]{1,0:T(8,128)(2,1)} async-done(((bf16[5632,2048]{1,0:T(8,128)(2,1)}), bf16[352,2048]{1,0:T(8,128)(2,1)}) %reduce-scatter.20.cloned.1.call-update) | async-done | bytes 1441808 | tf_op jit(solution)/shard_map/reduce_scatter | solution.py:292
  3319.2 41.3 %all-reduce.2 = (bf16[2048]{0:T(1024)(128)(2,1)S(1)}, bf16[2048]{0:T(1024)(128)(2,1)S(1)}) all-reduce(bf16[2048]{0:T(1024)(128)(2,1)S(1)} %get-tuple-element.171, bf16[2048]{0:T(1024)(128)(2,1)S(1)} %copy-done.34), channel_id=2, replica_groups=mesh['dp'=2,'seq'=16] {'seq'}, use_global_device_ids=true, to_apply=%region_14.15.clone | all-reduce | flops 4096 | bytes 16384
  (351 shorter events, 402.5 us)
Async XLA Ops:
  7.2 58.8 %all-gather.12.cloned.1.call-start = ((), (), s32[]{:S(2)}) async-start(), calls=%async_computation.16 | async-start | bytes 1114112 | tf_op jit(solution)/shard_map/all_gather | solution.py:223
  7.9 117.0 %all-gather.14.cloned.1.call-start = ((), (), s32[]{:S(2)}) async-start(), calls=%async_computation.17 | async-start | bytes 1114112 | tf_op jit(solution)/shard_map/all_gather | solution.py:224
  8.7 235.0 %all-gather.10.cloned.1.call-start = ((), (), s32[]{:S(2)}) async-start(), calls=%async_computation.15 | async-start | bytes 8912896 | tf_op jit(solution)/shard_map/all_gather | solution.py:222
  9.4 389.4 %all-gather.16.cloned.1.call-start = ((), (), s32[]{:S(2)}) async-start(), calls=%async_computation.18 | async-start | bytes 8912896 | tf_op jit(solution)/shard_map/all_gather | solution.py:225
  10.0 605.0 %all-gather.18.cloned.1.call-start = ((), (), s32[]{:S(2)}) async-start(), calls=%async_computation.19 | async-start | bytes 24510464 | tf_op jit(solution)/shard_map/all_gather | solution.py:229
  10.6 855.7 %all-gather.20.cloned.1.call-start = ((), (), s32[]{:S(2)}) async-start(), calls=%async_computation.20 | async-start | bytes 24510464 | tf_op jit(solution)/shard_map/all_gather | solution.py:230
  11.1 1106.6 %all-gather.22.cloned.1.call-start = ((), (), s32[]{:S(2)}) async-start(), calls=%async_computation.21 | async-start | bytes 24510464 | tf_op jit(solution)/shard_map/all_gather | solution.py:231
  46.6 197.0 %copy-start.28 = (f32[16,1,128]{2,1,0:T(1,128)}, f32[16,1,128]{2,1,0:T(1,128)S(1)}, u32[]{:S(2)}) copy-start(f32[16,1,128]{2,1,0:T(1,128)S(1)} %convert_element_type.427) | copy-start | bytes 24580
  47.5 79.0 %copy-start.23 = (f32[128,64]{0,1:T(8,128)}, f32[128,64]{0,1:T(8,128)S(1)}, u32[]{:S(2)}) copy-start(f32[128,64]{0,1:T(8,128)S(1)} %get-tuple-element.237) | copy-start | bytes 98308
  47.5 79.0 %copy-start.30 = (f32[128,64]{0,1:T(8,128)}, f32[128,64]{0,1:T(8,128)S(1)}, u32[]{:S(2)}) copy-start(f32[128,64]{0,1:T(8,128)S(1)} %get-tuple-element.238) | copy-start | bytes 98308
  48.7 194.9 %copy-start.32 = (f32[128]{0:T(128)}, f32[128]{0:T(128)S(1)}, u32[]{:S(2)}) copy-start(f32[128]{0:T(128)S(1)} %add_rsqrt_fusion.1) | copy-start | bytes 1540
  89.2 58.5 %all-to-all-start.1 = ((bf16[16,2,8192]{2,1,0:T(2,128)(2,1)}), bf16[16,2,8192]{2,1,0:T(2,128)(2,1)S(1)}, u32[]{:S(2)}, u32[]{:S(2)}) async-start(bf16[16,2,8192]{2,1,0:T(2,128)(2,1)} %reshape.787), calls=%async_computation.1 | async-start | bytes 1048576 | tf_op jit(solution)/shard_map/all_to_all | solution.py:170
  147.7 100.6 %copy-start.20 = (bf16[16,2,8192]{2,1,0:T(2,128)(2,1)}, bf16[16,2,8192]{2,1,0:T(2,128)(2,1)S(1)}, u32[]{:S(2)}) copy-start(bf16[16,2,8192]{2,1,0:T(2,128)(2,1)S(1)} %all-to-all-done.1) | copy-start | bytes 1572868
  147.7 117.8 %all-to-all-start.2 = ((bf16[16,2,8192]{2,1,0:T(2,128)(2,1)}), bf16[16,2,8192]{2,1,0:T(2,128)(2,1)}, u32[]{:S(2)}, u32[]{:S(2)}) async-start(bf16[16,2,8192]{2,1,0:T(2,128)(2,1)} %reshape.789), calls=%async_computation.2 | async-start | bytes 1048576 | tf_op jit(solution)/shard_map/all_to_all | solution.py:171
  265.6 20.2 all-to-all-start
  290.3 105.3 %copy-start.38 = (s32[1,128]{1,0:T(1,128)S(1)}, s32[1,128]{1,0:T(1,128)}, u32[]{:S(2)}) copy-start(s32[1,128]{1,0:T(1,128)} %param.19) | copy-start | bytes 1540
  347.8 47.8 %all-to-all-start.3 = ((bf16[16,2,8192]{2,1,0:T(2,128)(2,1)}), bf16[16,2,8192]{2,1,0:T(2,128)(2,1)S(1)}, u32[]{:S(2)}, u32[]{:S(2)}) async-start(bf16[16,2,8192]{2,1,0:T(2,128)(2,1)} %reshape.791), calls=%async_computation.3 | async-start | bytes 1048576 | tf_op jit(solution)/shard_map/all_to_all | solution.py:174
  395.6 763.2 %copy-start.35 = (f32[128]{0:T(128)}, f32[128]{0:T(128)S(1)}, u32[]{:S(2)}) copy-start(f32[128]{0:T(128)S(1)} %convert_bitcast_fusion.2) | copy-start | bytes 1540
  403.8 755.0 %copy-start.5 = (f32[1,128,2048]{2,1,0:T(8,128)}, f32[1,128,2048]{2,1,0:T(8,128)S(1)}, u32[]{:S(2)}) copy-start(f32[1,128,2048]{2,1,0:T(8,128)S(1)} %get-tuple-element.240) | copy-start | bytes 3145732
  403.9 462.3 %copy-start.11 = (bf16[128,2048]{1,0:T(8,128)(2,1)}, bf16[128,2048]{1,0:T(8,128)(2,1)S(1)}, u32[]{:S(2)}) copy-start(bf16[128,2048]{1,0:T(8,128)(2,1)S(1)} %fusion.71) | copy-start | bytes 1572868
  627.3 490.4 %copy-start.18 = (bf16[1,128,2048]{2,1,0:T(8,128)(2,1)S(1)}, bf16[1,128,2048]{2,1,0:T(8,128)(2,1)}, u32[]{:S(2)}) copy-start(bf16[1,128,2048]{2,1,0:T(8,128)(2,1)} %param.20) | copy-start | bytes 1572868
  1184.6 16.6 all-to-all-start.4
  1188.9 284.1 %reduce-scatter.10.cloned.1.call-start = ((), (), s32[]{:S(2)}) async-start(), calls=%async_computation.23 | async-start | bytes 1114112 | tf_op jit(solution)/shard_map/reduce_scatter | solution.py:360
  1338.5 148.8 %reduce-scatter.12.cloned.1.call-start = ((), (), s32[]{:S(2)}) async-start(), calls=%async_computation.24 | async-start | bytes 1114112 | tf_op jit(solution)/shard_map/reduce_scatter | solution.py:363
  1378.1 296.2 %reduce-scatter.14.cloned.1.call-start = ((), (), s32[]{:S(2)}) async-start(), calls=%async_computation.25 | async-start | bytes 8912896 | tf_op jit(solution)/shard_map/reduce_scatter | solution.py:366
  1383.8 473.1 %reduce-scatter.8.cloned.1.call-start = ((), (), s32[]{:S(2)}) async-start(), calls=%async_computation.22 | async-start | bytes 8912896 | tf_op jit(solution)/shard_map/reduce_scatter | solution.py:357
  1434.7 898.3 %reduce-scatter.16.cloned.1.call-start = ((), (), s32[]{:S(2)}) async-start(), calls=%async_computation.26 | async-start | bytes 24510464 | tf_op jit(solution)/shard_map/reduce_scatter | solution.py:286
  1446.9 1368.2 %reduce-scatter.18.cloned.1.call-start = ((), (), s32[]{:S(2)}) async-start(), calls=%async_computation.27 | async-start | bytes 24510464 | tf_op jit(solution)/shard_map/reduce_scatter | solution.py:289
  1459.3 1837.9 %reduce-scatter.20.cloned.1.call-start = ((), (), s32[]{:S(2)}) async-start(), calls=%async_computation.28 | async-start | bytes 24510464 | tf_op jit(solution)/shard_map/reduce_scatter | solution.py:292
  1472.9 1824.3 %copy-start.39 = (u32[32]{0:T(128)S(1)}, u32[32]{0:T(128)}, u32[]{:S(2)}) copy-start(u32[32]{0:T(128)} %constant.75) | copy-start | bytes 388
  1472.9 1825.6 %copy-start.6 = (f32[1,128,2048]{2,1,0:T(8,128)S(1)}, f32[1,128,2048]{2,1,0:T(8,128)}, u32[]{:S(2)}) copy-start(f32[1,128,2048]{2,1,0:T(8,128)} %copy-done.5) | copy-start | bytes 3145732
  1472.9 1901.2 %all-reduce.7.cloned.1.call-start = ((), (), s32[]{:S(2)}) async-start(), calls=%async_computation.29 | async-start | bytes 11010048 | tf_op jit(solution)/shard_map/psum | solution.py:372
  (37 other events, 626.6 us)
Sparse Core Ops, SparseCore 0:
  10.7 55.1 all-gather.11
  68.7 56.1 all-gather.13
  127.7 115.8 all-gather.9
  246.3 116.4 all-gather.15
  365.3 249.6 all-gather.17
  617.5 248.6 all-gather.19
  869.0 248.6 all-gather.21
  1338.7 70.0 reduce-scatter.9
  1411.6 75.7 reduce-scatter.11
  1489.4 184.8 reduce-scatter.13
  1676.6 180.2 reduce-scatter.7
  1859.1 473.8 reduce-scatter.15
  2335.3 479.8 reduce-scatter.17
  2817.3 479.8 reduce-scatter.19
  3300.3 40.3 all-reduce.6
where the time goes:
time: 3410 us; the launch traced here: 3400 us
  waiting for transfers between devices  2680 us (79%)
  matrix products  243 us (7%)
  blocking collectives  178 us (5%)
  other arithmetic  154 us (5%)
  local copies, waits for them, and re-layouts  88.3 us (3%)
    reduce_scatter x1, waiting for transfers between devices, body(): lax.psum_scatter(grad_up_weight.astype(jnp.bfloat16), 'seq', scatter_dime...  482 us
    reduce_scatter x1, waiting for transfers between devices, body(): lax.psum_scatter(grad_down.astype(jnp.bfloat16), 'seq', scatter_dimension...  482 us
    reduce_scatter x1, waiting for transfers between devices, body(): lax.psum_scatter(grad_gate_weight.astype(jnp.bfloat16), 'seq', scatter_di...  476 us
    all_gather x1, waiting for transfers between devices, body(): lax.all_gather(w_down, 'seq', axis=0, tiled=True)  239 us
    all_gather x1, waiting for transfers between devices, body(): lax.all_gather(w_up, 'seq', axis=0, tiled=True)  239 us
    all_gather x1, waiting for transfers between devices, body(): lax.all_gather(w_gate, 'seq', axis=0, tiled=True)  211 us
    reduce_scatter x1, waiting for transfers between devices, body(): lax.psum_scatter(grad_out_weight.astype(jnp.bfloat16), 'seq', scatter_dim...  187 us
    reduce_scatter x1, waiting for transfers between devices, body(): lax.psum_scatter(grad_query_weight.astype(jnp.bfloat16), 'seq', scatter_d...  183 us
  transfers between devices with their start and end apart: 20, of which 14 were waited for; matrix products, arithmetic and copies ran while one was open for 8% of the time, Pallas kernels for 0%

commit v1 on v0

v1 whole, which is shorter than its diff:
```python
import functools

import jax
import jax.numpy as jnp
from jax import lax
from jax.experimental import pallas as pl
from jax.experimental.pallas import tpu as pltpu
from jax.sharding import PartitionSpec as P

HEADS = 32
KV_HEADS = 4
HEAD_DIM = 64
GROUP = KV_HEADS
GROUP_HEADS = HEADS // GROUP
PAIR = 2 * HEAD_DIM

epsilon = 1e-05
rope_base = 10000.0
masked_score = -1e30

f32 = jnp.float32
bf16 = jnp.bfloat16


def dot(left, right, contract=((1,), (0,))):
    return lax.dot_general(left, right, (contract, ((), ())), preferred_element_type=f32)


def stack_heads(block, rows):
    lane = lax.broadcasted_iota(jnp.int32, (rows, PAIR), 1)
    parts = []
    for pair in range(GROUP_HEADS // 2):
        both = block[:, pair * PAIR : (pair + 1) * PAIR]
        parts.append(jnp.where(lane < HEAD_DIM, both, jnp.zeros_like(both)))
        parts.append(jnp.where(lane >= HEAD_DIM, both, jnp.zeros_like(both)))
    return jnp.concatenate(parts, axis=0)


def unstack_heads(stacked, rows):
    lane = lax.broadcasted_iota(jnp.int32, (rows, PAIR), 1)
    parts = []
    for pair in range(GROUP_HEADS // 2):
        low = stacked[2 * pair * rows : (2 * pair + 1) * rows]
        high = stacked[(2 * pair + 1) * rows : (2 * pair + 2) * rows]
        parts.append(jnp.where(lane < HEAD_DIM, low, high))
    return jnp.concatenate(parts, axis=1)


def as_row(column):
    wide = jnp.broadcast_to(column, (column.shape[0], 128))
    return jnp.transpose(wide)[:8]


def attend_kernel(seen_ref, q_ref, kk_ref, vv_ref, qpos_ref, kpos_ref, o_ref, lse_ref):
    rows = q_ref.shape[0]
    stacked = stack_heads(q_ref[...], rows)
    qpos = jnp.concatenate([qpos_ref[...]] * GROUP_HEADS, axis=0)

    def unit(index, carry, masked):
        top, total, acc = carry
        scores = dot(stacked, kk_ref[index], ((1,), (1,)))
        if masked:
            scores = jnp.where(kpos_ref[...] <= qpos, scores, masked_score)
        new_top = jnp.maximum(top, jnp.max(scores, axis=1, keepdims=True))
        weights = jnp.exp(scores - new_top)
        keep = jnp.exp(top - new_top)
        total = total * keep + jnp.sum(weights, axis=1, keepdims=True)
        acc = acc * keep + dot(weights.astype(bf16), vv_ref[index])
        return new_top, total, acc

    count = GROUP_HEADS * rows
    start = (
        jnp.full((count, 1), masked_score, f32),
        jnp.zeros((count, 1), f32),
        jnp.zeros((count, PAIR), f32),
    )
    carry = unit(0, start, True)
    top, total, acc = lax.fori_loop(1, seen_ref[0], lambda i, c: unit(i, c, False), carry)
    o_ref[...] = unstack_heads(acc / total, rows).astype(bf16)
    lse_ref[...] = as_row(top + jnp.log(total))


def attend_back_kernel(
    seen_ref, q_ref, do_ref, o_ref, kk_ref, vv_ref, lse_ref, qpos_ref, kpos_ref,
    dq_ref, dkk_ref, dvv_ref, qs_ref, dos_ref, delta_ref, dqs_ref,
):
    rows = q_ref.shape[0]

    @pl.when(pl.program_id(0) == 0)
    def _():
        dkk_ref[...] = jnp.zeros_like(dkk_ref)
        dvv_ref[...] = jnp.zeros_like(dvv_ref)

    qs_ref[...] = stack_heads(q_ref[...], rows)
    grads = stack_heads(do_ref[...], rows)
    dos_ref[...] = grads
    outs = stack_heads(o_ref[...], rows)
    delta_ref[...] = as_row(jnp.sum(grads.astype(f32) * outs.astype(f32), axis=1, keepdims=True))

    def unit(index, masked):
        keys = kk_ref[index]
        scores = dot(keys, qs_ref[...], ((1,), (1,)))
        if masked:
            qpos = jnp.concatenate([qpos_ref[0:1, :]] * GROUP_HEADS, axis=1)
            scores = jnp.where(kpos_ref[...] <= qpos, scores, masked_score)
        probs = jnp.exp(scores - lse_ref[0:1, :])
        prob_grad = dot(vv_ref[index], dos_ref[...], ((1,), (1,)))
        score_grad = (probs * (prob_grad - delta_ref[0:1, :])).astype(bf16)
        dvv_ref[index] += dot(probs.astype(bf16), dos_ref[...])
        dkk_ref[index] += dot(score_grad, qs_ref[...])
        return dot(score_grad, keys, ((0,), (0,)))

    dqs_ref[...] = unit(0, True)

    @pl.loop(1, seen_ref[0])
    def _(index):
        dqs_ref[...] += unit(index, False)

    dq_ref[...] = unstack_heads(dqs_ref[...], rows)


def block_rows(length):
    return min(128, length)


def whole(shape):
    zeros = (0,) * len(shape)
    return pl.BlockSpec(shape, lambda i, seen: zeros)


def attend(seen, q, kk, vv, order):
    length, width = q.shape
    rows = block_rows(length)
    stacked = GROUP_HEADS * rows
    steps = length // rows
    return pl.pallas_call(
        attend_kernel,
        out_shape=(
            jax.ShapeDtypeStruct((length, width), bf16),
            jax.ShapeDtypeStruct((steps, 8, stacked), f32),
        ),
        grid_spec=pltpu.PrefetchScalarGridSpec(
            num_scalar_prefetch=1,
            grid=(steps,),
            in_specs=[
                pl.BlockSpec((rows, width), lambda i, seen: (i, 0)),
                whole(kk.shape),
                whole(vv.shape),
                pl.BlockSpec((rows, 1), lambda i, seen: (i, 0)),
                whole((1, length)),
            ],
            out_specs=[
                pl.BlockSpec((rows, width), lambda i, seen: (i, 0)),
                pl.BlockSpec((pl.Squeezed(), 8, stacked), lambda i, seen: (i, 0, 0)),
            ],
        ),
        name="attend",
    )(seen, q, kk, vv, order[:, None], order[None, :])


def attend_back(seen, q, do, o, kk, vv, lse, order):
    length, width = q.shape
    rows = block_rows(length)
    stacked = GROUP_HEADS * rows
    steps = length // rows
    return pl.pallas_call(
        attend_back_kernel,
        out_shape=(
            jax.ShapeDtypeStruct((length, width), f32),
            jax.ShapeDtypeStruct(kk.shape, f32),
            jax.ShapeDtypeStruct(vv.shape, f32),
        ),
        grid_spec=pltpu.PrefetchScalarGridSpec(
            num_scalar_prefetch=1,
            grid=(steps,),
            in_specs=[
                pl.BlockSpec((rows, width), lambda i, seen: (i, 0)),
                pl.BlockSpec((rows, width), lambda i, seen: (i, 0)),
                pl.BlockSpec((rows, width), lambda i, seen: (i, 0)),
                whole(kk.shape),
                whole(vv.shape),
                pl.BlockSpec((pl.Squeezed(), 8, stacked), lambda i, seen: (i, 0, 0)),
                pl.BlockSpec((8, rows), lambda i, seen: (0, i)),
                whole((length, 1)),
            ],
            out_specs=[
                pl.BlockSpec((rows, width), lambda i, seen: (i, 0)),
                whole(kk.shape),
                whole(vv.shape),
            ],
            scratch_shapes=[
                pltpu.VMEM((stacked, PAIR), bf16),
                pltpu.VMEM((stacked, PAIR), bf16),
                pltpu.VMEM((8, stacked), f32),
                pltpu.VMEM((stacked, PAIR), f32),
            ],
        ),
        name="attend_back",
    )(seen, q, do, o, kk, vv, lse, jnp.broadcast_to(order[None, :], (8, length)), order[:, None])


def normalize(values):
    inverse = lax.rsqrt(jnp.mean(values * values, axis=-1, keepdims=True) + epsilon)
    return values * inverse, inverse


def norm_back(inner, normed, inverse):
    return inverse * (inner - normed * jnp.mean(inner * normed, axis=-1, keepdims=True))


def rope_tables(positions):
    half_dim = HEAD_DIM // 2
    frequency = rope_base ** (-(jnp.arange(half_dim).astype(f32) * 2.0 / HEAD_DIM))
    angles = positions.astype(f32)[:, None] * frequency
    angles = jnp.concatenate([angles, angles], axis=-1)
    return jnp.cos(angles)[:, None, :], jnp.sin(angles)[:, None, :]


def turn(values):
    half_dim = HEAD_DIM // 2
    return jnp.concatenate([-values[..., half_dim:], values[..., :half_dim]], axis=-1)


def rotate(values, cosine, sine):
    return values * cosine + turn(values) * sine


def unrotate(grads, cosine, sine):
    return grads * cosine - turn(grads * sine)


def solution(mesh):
    n_dp = mesh.shape["dp"]
    n_seq = mesh.shape["seq"]
    planes = n_seq // GROUP
    halves = n_dp // 2
    both = ("dp", "seq")

    in_plane = [[GROUP * p + w for w in range(GROUP)] for p in range(planes)]
    across_dp = [
        [c * n_seq + GROUP * p + w for c in range(n_dp) for p in range(planes)] for w in range(GROUP)
    ]
    in_plane_dp = [
        [c * n_seq + GROUP * p + w for c in range(n_dp) for w in range(GROUP)] for p in range(planes)
    ]
    across = [[GROUP * p + w for p in range(planes)] for w in range(GROUP)]

    def xor_w(value, j):
        return lax.ppermute(value, "seq", [(s, s ^ j) for s in range(n_seq)])

    def shift_z(value, t):
        return lax.ppermute(value, "seq", [(s, (s + GROUP * t) % n_seq) for s in range(n_seq)])

    def shift_dp(value, t):
        return lax.ppermute(value, "dp", [(c, (c + t) % n_dp) for c in range(n_dp)])

    def gather_w(value):
        first = xor_w(value, 1)
        second = xor_w(value, 2)
        half = value.shape[0] // 2
        third = jnp.concatenate([xor_w(first[:half], 2), xor_w(second[half:], 1)], axis=0)
        return jnp.concatenate([value, first, second, third], axis=0)

    def scatter_w(slots):
        got = [xor_w(slots[j], j) for j in range(1, GROUP)]
        return functools.reduce(jnp.add, [g.astype(f32) for g in got], slots[0].astype(f32))

    def gather_z(value):
        return [value] + [shift_z(value, t) for t in range(1, planes)]

    def scatter_z(slots):
        got = [shift_z(slots[t], -t) for t in range(1, planes)]
        return functools.reduce(jnp.add, [g.astype(f32) for g in got], slots[0].astype(f32))

    def gather_dp(value):
        return jnp.concatenate([value] + [shift_dp(value, t) for t in range(1, n_dp)], axis=0)

    def pick(value, index, count, axis):
        size = value.shape[axis] // count
        return lax.dynamic_slice_in_dim(value, index * size, size, axis)

    def exchange_dp(value, c, axis):
        parts = [pick(value, c, n_dp, axis)]
        for t in range(1, n_dp):
            parts.append(shift_dp(pick(value, (c + t) % n_dp, n_dp, axis), t))
        return jnp.concatenate(parts, axis=0)

    def collect_dp(value, c):
        out = jnp.zeros((n_dp,) + value.shape, value.dtype)
        out = lax.dynamic_update_index_in_dim(out, value, c, 0)
        for t in range(1, n_dp):
            out = lax.dynamic_update_index_in_dim(out, shift_dp(value, t), (c - t) % n_dp, 0)
        return out

    def body(
        inputs, positions, select, cotangent, gain_attn, w_query, w_key, w_value, w_out, gain_mlp,
        w_gate, w_up, w_down,
    ):
        seqs, rows, width = inputs.shape
        tokens = seqs * rows
        shard = w_query.shape[0]
        ff_rows = w_down.shape[0]
        ff_block = w_gate.shape[1] // planes
        q_width = GROUP_HEADS * HEAD_DIM
        s = lax.axis_index("seq")
        c = lax.axis_index("dp")
        p = s // GROUP
        w = s % GROUP

        gain_one = gain_attn.astype(f32)[:, None]
        gain_two = gain_mlp.astype(f32)[:, None]

        def scaled(weight, gain):
            return (weight.astype(f32) * gain).astype(bf16)

        q_cols = scaled(w_query, gain_one).reshape(shard, GROUP, n_dp, q_width // n_dp)
        kv_cols = jnp.concatenate(
            [
                scaled(w_key, gain_one).reshape(shard, GROUP, HEAD_DIM),
                scaled(w_value, gain_one).reshape(shard, GROUP, HEAD_DIM),
            ],
            axis=-1,
        ).reshape(shard, GROUP, n_dp, PAIR // n_dp)
        qkv_cols = jnp.concatenate([q_cols, kv_cols], axis=-1)
        qkv_part = lax.dynamic_index_in_dim(qkv_cols, c, 2, keepdims=False)
        qkv_part = lax.all_to_all(
            jnp.transpose(qkv_part, (1, 0, 2)), "seq", 0, 0, axis_index_groups=in_plane, tiled=True
        )
        part_width = (q_width + PAIR) // n_dp
        qkv_part = qkv_part.reshape(GROUP * shard, part_width)
        qkv_full = lax.all_gather(qkv_part, both, axis_index_groups=across_dp, tiled=False)
        qkv_full = qkv_full.reshape(n_dp, width, part_width)

        out_part = pick(w_out, c, n_dp, 1)
        out_part = lax.ppermute(
            out_part, "seq", [(i, GROUP * (i % planes) + i // planes) for i in range(n_seq)]
        )
        out_full = lax.all_gather(out_part, both, axis_index_groups=across_dp, tiled=False)
        out_full = out_full.reshape(n_dp, planes * shard, width // n_dp)

        piece = shard // halves
        gate_up = jnp.where(c // halves == 0, scaled(w_gate, gain_two), scaled(w_up, gain_two))
        gate_up = pick(gate_up, c % halves, halves, 0)
        gate_up_part = jnp.zeros((planes, piece, ff_block), bf16)
        for t in range(planes):
            block = pick(gate_up, (p + t) % planes, planes, 1)
            block = shift_z(block, t) if t else block
            gate_up_part = lax.dynamic_update_index_in_dim(gate_up_part, block, (p - t) % planes, 0)
        gate_up_full = lax.all_gather(gate_up_part, both, axis_index_groups=in_plane_dp, tiled=False)
        gate_up_full = gate_up_full.reshape(2, width, ff_block)
        gate_full = gate_up_full[0]
        up_full = gate_up_full[1]

        down_full = lax.all_gather(
            pick(w_down, c, n_dp, 1), both, axis_index_groups=in_plane_dp, tiled=False
        )
        down_full = down_full.reshape(n_dp, ff_block, width // n_dp)

        def reorder(value):
            value = value.reshape(tokens, planes, GROUP, halves, piece)
            return jnp.transpose(value, (0, 3, 2, 1, 4)).reshape(tokens, width)

        def order_back(value):
            value = value.reshape(tokens, halves, GROUP, planes, piece)
            return jnp.transpose(value, (0, 3, 2, 1, 4)).reshape(tokens, width)

        x_in = inputs.reshape(tokens, width).astype(f32)
        normed_one, inverse_one = normalize(x_in)
        low_one = gather_w(normed_one.astype(bf16))
        own_pos = positions.reshape(1, tokens)
        plane_pos = jnp.concatenate([own_pos] + [xor_w(own_pos, j) for j in range(1, GROUP)], axis=1)
        cosine, sine = rope_tables(plane_pos.reshape(GROUP * tokens))

        grad_y = (
            cotangent.astype(f32) * select.astype(f32)[..., None]
        ).reshape(tokens, width)
        grad_y_all = jnp.concatenate(gather_z(grad_y.astype(bf16)), axis=0)

        projected = [dot(low_one, qkv_full[i]) for i in range(n_dp)]
        cut = q_width // n_dp
        q = jnp.concatenate([one[:, :cut] for one in projected], axis=1)
        kv = jnp.concatenate([one[:, cut:] for one in projected], axis=1)
        plane_tokens = GROUP * tokens
        q = rotate(q.reshape(plane_tokens, GROUP_HEADS, HEAD_DIM), cosine, sine)
        q = (q.astype(bf16).astype(f32) * HEAD_DIM ** (-0.5)).astype(bf16).reshape(plane_tokens, q_width)
        k = rotate(kv[:, None, :HEAD_DIM], cosine, sine)[:, 0]
        kv_low = jnp.concatenate([k, kv[:, HEAD_DIM:]], axis=1).astype(bf16)
        kv_all = jnp.stack(gather_z(kv_low))
        kk = jnp.concatenate([kv_all[..., :HEAD_DIM]] * 2, axis=-1)
        vv = jnp.concatenate([kv_all[..., HEAD_DIM:]] * 2, axis=-1)

        def by_seq(value, axis):
            shape = value.shape
            value = value.reshape(shape[:axis] + (GROUP, seqs, rows) + shape[axis + 1 :])
            value = jnp.moveaxis(value, axis + 1, 0)
            return value.reshape((seqs,) + shape[:axis] + (GROUP * rows,) + shape[axis + 1 :])

        def from_seq(value, axis):
            shape = value.shape[1:]
            value = value.reshape((seqs,) + shape[:axis] + (GROUP, rows) + shape[axis + 1 :])
            value = jnp.moveaxis(value, 0, axis + 1)
            return value.reshape(shape[:axis] + (GROUP * seqs * rows,) + shape[axis + 1 :])

        order = jnp.concatenate([(w ^ j) * rows + jnp.arange(rows) for j in range(GROUP)])
        order = order.astype(jnp.int32)
        seen = (p + 1).astype(jnp.int32).reshape(1)
        q_seq = by_seq(q, 0)
        kk_seq = by_seq(kk, 1)
        vv_seq = by_seq(vv, 1)
        pieces = [attend(seen, q_seq[i], kk_seq[i], vv_seq[i], order) for i in range(seqs)]
        o_seq = [one[0] for one in pieces]
        lse_seq = [one[1] for one in pieces]
        o = from_seq(jnp.stack(o_seq), 0)

        branch = jnp.concatenate([dot(o, out_full[i]).astype(bf16) for i in range(n_dp)], axis=1)
        branch = scatter_w([branch[j * tokens : (j + 1) * tokens] for j in range(GROUP)])
        x_mid = x_in + branch

        normed_two, inverse_two = normalize(x_mid)
        low_two = jnp.concatenate(gather_z(reorder(normed_two.astype(bf16))), axis=0)
        gate = dot(low_two, gate_full)
        up_part = dot(low_two, up_full)
        sigmoid_gate = 1.0 / (1.0 + jnp.exp(-gate))
        hidden = (gate * sigmoid_gate * up_part).astype(bf16)

        grad_hidden = functools.reduce(
            jnp.add,
            [
                dot(pick(grad_y_all, i, n_dp, 1), down_full[i], ((1,), (1,)))
                for i in range(n_dp)
            ],
        )
        grad_gate = (
            grad_hidden * up_part * sigmoid_gate * (1.0 + gate * (1.0 - sigmoid_gate))
        ).astype(bf16)
        grad_up = (grad_hidden * gate * sigmoid_gate).astype(bf16)
        grad_low_two = dot(grad_gate, gate_full, ((1,), (1,))) + dot(
            grad_up, up_full, ((1,), (1,))
        )
        grad_low_two = grad_low_two.astype(bf16)
        inner_two = scatter_z([grad_low_two[t * tokens : (t + 1) * tokens] for t in range(planes)])
        grad_x_mid = grad_y + norm_back(order_back(inner_two), normed_two, inverse_two)

        mixed = jnp.concatenate([dot(hidden, down_full[i]).astype(bf16) for i in range(n_dp)], axis=1)
        mixed = scatter_z([mixed[t * tokens : (t + 1) * tokens] for t in range(planes)])
        outputs = (x_mid + mixed).astype(bf16).reshape(seqs, rows, width)

        hidden_all = gather_dp(hidden)
        down_sum = dot(hidden_all, exchange_dp(grad_y_all, c, 1), ((0,), (0,))).astype(bf16)
        down_sum = lax.psum_scatter(down_sum, "seq", axis_index_groups=in_plane, tiled=True)
        down_sum = collect_dp(down_sum, c)
        grad_w_down = jnp.moveaxis(down_sum, 0, 1).reshape(ff_rows, width).astype(f32)

        low_two_all = gather_dp(low_two)
        if halves > 1:
            low_two_all = pick(low_two_all, c % halves, halves, 1)

        def of_member(member):
            return jnp.where(member // halves == 0, grad_gate, grad_up)

        gate_up_grads = [of_member(c)]
        for t in range(1, n_dp):
            gate_up_grads.append(shift_dp(of_member((c + t) % n_dp), t))
        gate_up_sum = dot(low_two_all, jnp.concatenate(gate_up_grads, axis=0), ((0,), (0,)))
        gate_up_sum = lax.psum_scatter(
            gate_up_sum.astype(bf16), "seq", axis_index_groups=in_plane, tiled=True
        ).reshape(planes, piece, ff_block)
        gate_up_rows = jnp.zeros((piece, planes, ff_block), bf16)
        for t in range(planes):
            block = lax.dynamic_index_in_dim(gate_up_sum, (p + t) % planes, 0, keepdims=False)
            block = shift_z(block, t) if t else block
            gate_up_rows = lax.dynamic_update_index_in_dim(gate_up_rows, block, (p - t) % planes, 1)
        gate_up_rows = collect_dp(gate_up_rows.reshape(piece, planes * ff_block), c)
        gate_up_rows = gate_up_rows.reshape(2, shard, planes * ff_block).astype(f32)
        grad_w_gate = gate_up_rows[0] * gain_two
        grad_w_up = gate_up_rows[1] * gain_two
        grad_gain_mlp = jnp.sum(
            gate_up_rows[0] * w_gate.astype(f32) + gate_up_rows[1] * w_up.astype(f32), axis=1
        )

        grad_branch = gather_w(grad_x_mid.astype(bf16))
        grad_o = functools.reduce(
            jnp.add,
            [dot(pick(grad_branch, i, n_dp, 1), out_full[i], ((1,), (1,))) for i in range(n_dp)],
        ).astype(bf16)

        out_sum = dot(gather_dp(o), exchange_dp(grad_branch, c, 1), ((0,), (0,))).astype(bf16)
        out_sum = lax.psum_scatter(out_sum, "seq", axis_index_groups=across, tiled=True)
        out_sum = lax.ppermute(
            out_sum, "seq", [(GROUP * (i % planes) + i // planes, i) for i in range(n_seq)]
        )
        grad_w_out = jnp.moveaxis(collect_dp(out_sum, c), 0, 1).reshape(shard, width).astype(f32)

        grad_o_seq = by_seq(grad_o, 0)
        pieces = [
            attend_back(
                seen, q_seq[i], grad_o_seq[i], o_seq[i], kk_seq[i], vv_seq[i], lse_seq[i], order
            )
            for i in range(seqs)
        ]
        grad_q = from_seq(jnp.stack([one[0] for one in pieces]), 0) * HEAD_DIM ** (-0.5)
        grad_kk = from_seq(jnp.stack([one[1] for one in pieces]), 1)
        grad_vv = from_seq(jnp.stack([one[2] for one in pieces]), 1)
        grad_kv = jnp.concatenate(
            [
                grad_kk[..., :HEAD_DIM] + grad_kk[..., HEAD_DIM:],
                grad_vv[..., :HEAD_DIM] + grad_vv[..., HEAD_DIM:],
            ],
            axis=-1,
        ).astype(bf16)
        grad_kv = scatter_z([grad_kv[t] for t in range(planes)])
        query_pre = unrotate(grad_q.reshape(plane_tokens, GROUP_HEADS, HEAD_DIM), cosine, sine)
        query_pre = query_pre.reshape(plane_tokens, q_width).astype(bf16)
        key_pre = unrotate(grad_kv[:, None, :HEAD_DIM], cosine, sine)[:, 0]
        kv_pre = jnp.concatenate([key_pre, grad_kv[:, HEAD_DIM:]], axis=1).astype(bf16)
        pre = [
            jnp.concatenate(
                [query_pre[:, i * cut : (i + 1) * cut], pick(kv_pre, i, n_dp, 1)], axis=1
            )
            for i in range(n_dp)
        ]
        grad_low_one = functools.reduce(
            jnp.add, [dot(pre[i], qkv_full[i], ((1,), (1,))) for i in range(n_dp)]
        ).astype(bf16)
        inner_one = scatter_w([grad_low_one[j * tokens : (j + 1) * tokens] for j in range(GROUP)])
        grad_inputs = grad_x_mid + norm_back(inner_one, normed_one, inverse_one)
        grad_inputs = grad_inputs.reshape(seqs, rows, width)

        qkv_sum = dot(
            gather_dp(low_one), exchange_dp(jnp.concatenate(pre, axis=1), c, 1), ((0,), (0,))
        ).astype(bf16)
        qkv_sum = lax.psum_scatter(qkv_sum, "seq", axis_index_groups=across, tiled=True)
        qkv_sum = qkv_sum.reshape(GROUP, shard, part_width)
        qkv_sum = lax.all_to_all(qkv_sum, "seq", 0, 0, axis_index_groups=in_plane, tiled=True)
        qkv_sum = collect_dp(qkv_sum, c).astype(f32)
        q_sum = jnp.transpose(qkv_sum[..., :cut], (2, 1, 0, 3)).reshape(shard, width)
        kv_sum = jnp.transpose(qkv_sum[..., cut:], (2, 1, 0, 3)).reshape(shard, GROUP, PAIR)
        k_sum = kv_sum[..., :HEAD_DIM].reshape(shard, GROUP * HEAD_DIM)
        v_sum = kv_sum[..., HEAD_DIM:].reshape(shard, GROUP * HEAD_DIM)
        grad_gain_attn = (
            jnp.sum(q_sum * w_query.astype(f32), axis=1)
            + jnp.sum(k_sum * w_key.astype(f32), axis=1)
            + jnp.sum(v_sum * w_value.astype(f32), axis=1)
        )

        return (
            outputs,
            grad_inputs,
            grad_gain_attn,
            q_sum * gain_one,
            k_sum * gain_one,
            v_sum * gain_one,
            grad_w_out,
            grad_gain_mlp,
            grad_w_gate,
            grad_w_up,
            grad_w_down,
        )

    tokens_spec = P("dp", "seq", None)
    in_specs = (
        tokens_spec,
        P("dp", "seq"),
        P("dp", "seq"),
        tokens_spec,
        P("seq"),
        P("seq", None),
        P("seq", None),
        P("seq", None),
        P("seq", None),
        P("seq"),
        P("seq", None),
        P("seq", None),
        P("seq", None),
    )
    out_specs = (
        tokens_spec,
        tokens_spec,
        P("seq"),
        P("seq", None),
        P("seq", None),
        P("seq", None),
        P("seq", None),
        P("seq"),
        P("seq", None),
        P("seq", None),
        P("seq", None),
    )
    return jax.shard_map(body, mesh=mesh, in_specs=in_specs, out_specs=out_specs, check_vma=False)
```

time: 3410 us -> 771 us (0.23)
  the two profiles are of different devices: /device:TPU:1 before, /device:TPU:25 now
where the time goes in v1:
time: 771 us; the launch traced here: 759 us
  waiting for transfers between devices  290 us (38%)
  local copies, waits for them, and re-layouts  174 us (23%)
  starting transfers between devices  89.5 us (12%)
  matrix products  72.9 us (9%)
  other arithmetic  55.8 us (7%)
  Pallas kernels  51.2 us (7%)
  between operations  16.2 us (2%)
  blocking collectives  8.8 us (1%)
    ppermute x24, waiting for transfers between devices, shift_z(): lax.ppermute(value, 'seq', [(s, (s + GROUP * t) % n_seq) for s in range(n...  125 us
    dot_general x20, matrix products, dot(): lax.dot_general(left, right, (contract, ((), ())), preferred_element_type...  72.9 us
    ppermute x17, waiting for transfers between devices, xor_w(): return lax.ppermute(value, 'seq', [(s, s ^ j) for s in range(n_seq)])  70.2 us
    reduce_scatter x1, waiting for transfers between devices, body(): lax.psum_scatter(gate_up_sum.astype(bf16), 'seq', axis_index_groups=in_pl...  46.5 us
    ppermute x24, starting transfers between devices, shift_z(): lax.ppermute(value, 'seq', [(s, (s + GROUP * t) % n_seq) for s in range(n...  44.5 us
    dynamic_update_slice x4, local copies, waits for them, and re-layouts, body(): lax.dynamic_update_index_in_dim(gate_up_rows, block, (p - t) % planes, 1)  43 us
    unnamed x156, local copies, waits for them, and re-layouts  31.1 us
    pallas_call x1, Pallas kernels, attend_back(): pl.pallas_call(attend_back_kernel, out_shape=(jax.ShapeDtypeStruct((lengt...  29.1 us
  transfers between devices with their start and end apart: 64, of which 22 were waited for; matrix products, arithmetic and copies ran while one was open for 32% of the time, Pallas kernels for 7%

profile of v1, /device:TPU:25, one launch (start us, length us, event | category | flops | bytes accessed | tf_op | source)
XLA Modules:
  0.0 758.8 jit_solution(11300002881033346901)
XLA Ops:
  9.9 8.8 %all_to_all.10 = bf16[4,128,320]{1,2,0:T(8,128)(2,1)S(1)} all-to-all(bf16[4,128,320]{1,2,0:T(8,128)(2,1)S(1)} %fusion.78), channel_id=1, replica_groups={{0,1,2,3},{4,5,6,7},{8,9,10,11},{12,13,14,15},{16,17,18,19},{20,21,22,2..., dimensions={0} | all-to-all | bytes 655360 | tf_op jit(solution)/shard_map/all_to_all | solution.py:326
  23.3 9.4 %collective-permute-done.10 = bf16[128,1024]{1,0:T(8,128)(2,1)S(1)} collective-permute-done((bf16[128,1024]{1,0:T(8,128)(2,1)S(1)}, bf16[128,1024]{1,0:T(8,128)(2,1)S(1)}, u32[]{:S(2)}, u32[]{:S(2)}) %collective-permute-start.10) | collective-permute-done | bytes 262176 | tf_op jit(solution)/shard_map/ppermute | solution.py:335
  38.3 12.8 %collective-permute-start.18 = (bf16[128,1408]{1,0:T(8,128)(2,1)}, bf16[128,1408]{1,0:T(8,128)(2,1)}, u32[]{:S(2)}, u32[]{:S(2)}) collective-permute-start(bf16[128,1408]{1,0:T(8,128)(2,1)} %get-tuple-element.92), channel_id=1, source_target_pairs={{0,8},{1,9},{2,10},{3,11},{4,12},{5,13},{6,14},{7,15},{8,0},{9,1},... | collective-permute-start | bytes 1081352 | tf_op jit(solution)/shard_map/ppermute | solution.py:252
  58.0 24.2 %collective-permute-done.18 = bf16[128,1408]{1,0:T(8,128)(2,1)} collective-permute-done((bf16[128,1408]{1,0:T(8,128)(2,1)}, bf16[128,1408]{1,0:T(8,128)(2,1)}, u32[]{:S(2)}, u32[]{:S(2)}) %collective-permute-start.18) | collective-permute-done | bytes 360480 | tf_op jit(solution)/shard_map/ppermute | solution.py:252
  139.7 8.5 %collective-permute-done.8 = bf16[512,128]{1,0:T(8,128)(2,1)} collective-permute-done((bf16[512,128]{1,0:T(8,128)(2,1)}, bf16[512,128]{1,0:T(8,128)(2,1)}, u32[]{:S(2)}, u32[]{:S(2)}) %collective-permute-start.8) | collective-permute-done | bytes 131104 | tf_op jit(solution)/shard_map/ppermute | solution.py:252
  151.1 22.1 %attend.1 = (bf16[512,512]{1,0:T(8,128)(2,1)}, f32[4,8,1024]{2,1,0:T(8,128)}) custom-call(s32[1]{0:T(128)} %bitcast.1.seen_ref, bf16[512,512]{1,0:T(8,128)(2,1)} %multiply_convert_fusion.3.q_ref, bf16[4,512,128]{2,1,0:T(8,128)(2,1)} %get-tuple-element.138.kk_ref, bf16[4,512,128]{2,1,0:T(8,128)(2,1)} %get-tuple-element.139.vv_ref, ...), custom_call_target="tpu_custom_call" | custom-call | tf_op jit(solution)/shard_map/attend/pallas_call | solution.py:136
  183.2 6.8 collective-permute-done.13
  190.0 21.6 %collective-permute-done.12 = bf16[128,2048]{1,0:T(8,128)(2,1)S(1)} collective-permute-done((bf16[128,2048]{1,0:T(8,128)(2,1)S(1)}, bf16[128,2048]{1,0:T(8,128)(2,1)S(1)}, u32[]{:S(2)}, u32[]{:S(2)}) %collective-permute-start.12) | collective-permute-done | bytes 524320 | tf_op jit(solution)/shard_map/ppermute | solution.py:249
  214.9 14.1 %collective-permute-start.16 = (bf16[128,2048]{0,1:T(8,128)(2,1)S(1)}, bf16[128,2048]{0,1:T(8,128)(2,1)}, u32[]{:S(2)}, u32[]{:S(2)}) collective-permute-start(bf16[128,2048]{0,1:T(8,128)(2,1)S(1)} %bitcast.183), channel_id=1, source_target_pairs={{0,12},{1,13},{2,14},{3,15},{4,0},{5,1},{6,2},{7,3},{8,4},{9,5},{1... | collective-permute-start | bytes 1572872 | tf_op jit(solution)/shard_map/ppermute | solution.py:252
  231.4 6.7 fusion.14
  238.1 28.7 %all-gather.9.cloned.1.call-done = bf16[8,4,128,1408]{3,2,1,0:T(8,128)(2,1)} async-done(((bf16[1,4,128,1408]{3,2,1,0:T(8,128)(2,1)}), bf16[8,4,128,1408]{3,2,1,0:T(8,128)(2,1)}) %all-gather.9.cloned.1.call-update) | async-done | bytes 11534352 | tf_op jit(solution)/shard_map/all_gather | solution.py:349
  266.8 10.1 %fusion.108 = (bf16[4,4,128,1408]{3,2,1,0:T(8,128)(2,1)}, bf16[4,4,128,1408]{3,2,1,0:T(8,128)(2,1)}) fusion(bf16[8,4,128,1408]{3,2,1,0:T(8,128)(2,1)} %all-gather.9.cloned.1.call-done), kind=kLoop, calls=%fused_computation.262 | loop fusion | bytes 23068672 | tf_op jit(solution)/shard_map/slice | solution.py:351
  276.9 6.2 fusion.106
  283.2 7.7 %multiply_convert_fusion.2 = (bf16[512,1408]{1,0:T(8,128)(2,1)S(1)}, f32[512,1408]{1,0:T(8,128)}) fusion(f32[512,1408]{1,0:T(8,128)S(1)} %fusion.106, bf16[2048,1408]{1,0:T(8,128)(2,1)S(1)} %bitcast.173, bf16[128,2048]{0,1:T(8,128)(2,1)} %collective-permute-done.16, bf16[128,2048]{0,1:T(8,128)(2,1)} %collective-permute-done.15, ...), kind=kOutput, calls=%fused_computation.23 | convolution fusion | flops 2965504000 | bytes 15073280 | tf_op jit(solution)/shard_map/dot_general | solution.py:26
  291.0 6.7 broadcast_select_fusion.1
  302.8 5.3 add_convert_fusion.1
  321.8 33.4 %collective-permute-done.27 = bf16[128,2048]{1,0:T(8,128)(2,1)S(1)} collective-permute-done((bf16[128,2048]{1,0:T(8,128)(2,1)S(1)}, bf16[128,2048]{1,0:T(8,128)(2,1)S(1)}, u32[]{:S(2)}, u32[]{:S(2)}) %collective-permute-start.27) | collective-permute-done | bytes 524320 | tf_op jit(solution)/shard_map/ppermute | solution.py:252
  364.5 35.8 %collective-permute-done.21 = bf16[128,2048]{1,0:T(8,128)(2,1)} collective-permute-done((bf16[128,2048]{1,0:T(8,128)(2,1)}, bf16[128,2048]{1,0:T(8,128)(2,1)}, u32[]{:S(2)}, u32[]{:S(2)}) %collective-permute-start.21) | collective-permute-done | bytes 524320 | tf_op jit(solution)/shard_map/ppermute | solution.py:252
  408.3 9.4 %collective-permute-done.29 = bf16[128,2048]{1,0:T(8,128)(2,1)S(1)} collective-permute-done((bf16[128,2048]{1,0:T(8,128)(2,1)}, bf16[128,2048]{1,0:T(8,128)(2,1)S(1)}, u32[]{:S(2)}, u32[]{:S(2)}) %collective-permute-start.29) | collective-permute-done | bytes 524320 | tf_op jit(solution)/shard_map/ppermute | solution.py:249
  429.5 29.1 %attend_back.1 = (f32[512,512]{1,0:T(8,128)}, f32[4,512,128]{2,1,0:T(8,128)}, f32[4,512,128]{2,1,0:T(8,128)}) custom-call(s32[1]{0:T(128)} %bitcast.1.seen_ref, bf16[512,512]{1,0:T(8,128)(2,1)} %multiply_convert_fusion.3.q_ref, bf16[512,512]{1,0:T(8,128)(2,1)} %fusion.39.do_ref, bf16[512,512]{1,0:T(8,128)(2,1)} %get-tuple-element.16.o_ref, ...), custom_call_target="tpu_custom_call" | custom-call | tf_op jit(solution)/shard_map/attend_back/pallas_call | solution.py:166
  504.1 10.4 %convolution_convert_fusion = bf16[2048,1408]{1,0:T(8,128)(2,1)} fusion(bf16[1024,2048]{0,1:T(8,128)(2,1)} %constant_dynamic-update-slice_fusion.16, bf16[512,1408]{1,0:T(8,128)(2,1)} %collective-permute-done.47, bf16[512,1408]{1,0:T(8,128)(2,1)S(1)} %copy-done.63), kind=kOutput, calls=%fused_computation | convolution fusion | flops 5914230784 | bytes 12845056 | tf_op jit(solution)/shard_map/dot_general | solution.py:26
  532.4 11.7 %collective-permute-done.38 = bf16[128,2048]{1,0:T(8,128)(2,1)S(1)} collective-permute-done((bf16[128,2048]{1,0:T(8,128)(2,1)}, bf16[128,2048]{1,0:T(8,128)(2,1)S(1)}, u32[]{:S(2)}, u32[]{:S(2)}) %collective-permute-start.38) | collective-permute-done | bytes 524320 | tf_op jit(solution)/shard_map/ppermute | solution.py:249
  544.1 11.9 %collective-permute-done.37 = bf16[128,2048]{1,0:T(8,128)(2,1)} collective-permute-done((bf16[128,2048]{1,0:T(8,128)(2,1)}, bf16[128,2048]{1,0:T(8,128)(2,1)}, u32[]{:S(2)}, u32[]{:S(2)}) %collective-permute-start.37) | collective-permute-done | bytes 524320 | tf_op jit(solution)/shard_map/ppermute | solution.py:249
  563.9 5.7 collective-permute-start.44
  572.6 5.8 all-to-all-done.1
  582.6 46.5 %reduce-scatter.9.cloned.1.call-done = bf16[512,1408]{1,0:T(8,128)(2,1)} async-done(((bf16[2048,1408]{1,0:T(8,128)(2,1)}), bf16[512,1408]{1,0:T(8,128)(2,1)}) %reduce-scatter.9.cloned.1.call-update) | async-done | bytes 1441808 | tf_op jit(solution)/shard_map/reduce_scatter | solution.py:465
  637.4 10.1 %dynamic_update_slice.66 = bf16[128,4,1408]{2,1,0:T(4,128)(2,1)S(1)} dynamic-update-slice(bf16[128,4,1408]{2,1,0:T(4,128)(2,1)S(1)} %broadcast_in_dim.101, bf16[128,1,1408]{2,1,0:T(2,128)(2,1)S(1)} %copy.137, s32[]{:T(128)} %constant.217.clone.1, s32[]{:T(128)S(6)} %select_n.188, s32[]{:T(128)} %constant.217.clone.1) | dynamic-update-slice | bytes 720900 | tf_op jit(solution)/shard_map/jit(dynamic_update_index_in_dim)/dynamic_update_slice | solution.py:472
  649.1 14.9 %collective-permute-done.49 = bf16[128,1408]{1,0:T(8,128)(2,1)} collective-permute-done((bf16[128,1408]{1,0:T(8,128)(2,1)S(1)}, bf16[128,1408]{1,0:T(8,128)(2,1)}, u32[]{:S(2)}, u32[]{:S(2)}) %collective-permute-start.49) | collective-permute-done | bytes 360480 | tf_op jit(solution)/shard_map/ppermute | solution.py:252
  668.0 9.8 %dynamic_update_slice.67 = bf16[128,4,1408]{2,1,0:T(4,128)(2,1)S(1)} dynamic-update-slice(bf16[128,4,1408]{2,1,0:T(4,128)(2,1)S(1)} %dynamic_update_slice.66, bf16[128,1,1408]{2,1,0:T(2,128)(2,1)S(1)} %copy.138, s32[]{:T(128)} %constant.217.clone.1, s32[]{:T(128)S(6)} %select_n.192, s32[]{:T(128)} %constant.217.clone.1) | dynamic-update-slice | bytes 720900 | tf_op jit(solution)/shard_map/jit(dynamic_update_index_in_dim)/dynamic_update_slice | solution.py:472
  677.8 9.9 %dynamic_update_slice.68 = bf16[128,4,1408]{2,1,0:T(4,128)(2,1)S(1)} dynamic-update-slice(bf16[128,4,1408]{2,1,0:T(4,128)(2,1)S(1)} %dynamic_update_slice.67, bf16[128,1,1408]{2,1,0:T(2,128)(2,1)S(1)} %copy.139, s32[]{:T(128)} %constant.217.clone.1, s32[]{:T(128)S(6)} %select_n.196, s32[]{:T(128)} %constant.217.clone.1) | dynamic-update-slice | bytes 720900 | tf_op jit(solution)/shard_map/jit(dynamic_update_index_in_dim)/dynamic_update_slice | solution.py:472
  687.7 13.2 %dynamic_update_slice.69 = bf16[128,4,1408]{2,1,0:T(4,128)(2,1)S(1)} dynamic-update-slice(bf16[128,4,1408]{2,1,0:T(4,128)(2,1)S(1)} %dynamic_update_slice.68, bf16[128,1,1408]{2,1,0:T(2,128)(2,1)} %copy.140, s32[]{:T(128)} %constant.217.clone.1, s32[]{:T(128)S(6)} %select_n.200, s32[]{:T(128)} %constant.217.clone.1) | dynamic-update-slice | bytes 720900 | tf_op jit(solution)/shard_map/jit(dynamic_update_index_in_dim)/dynamic_update_slice | solution.py:472
  717.7 21.6 %dynamic_update_slice.73 = bf16[2,352,1024]{2,0,1:T(2,128)(2,1)S(1)} dynamic-update-slice(bf16[2,352,1024]{2,0,1:T(2,128)(2,1)S(1)} %copy.141, bf16[1,352,1024]{2,0,1:T(2,128)(2,1)} %copy.142, s32[]{:T(128)S(6)} %select_n.205, s32[]{:T(128)} %constant.217.clone.1, s32[]{:T(128)} %constant.217.clone.1) | dynamic-update-slice | bytes 1441796 | tf_op jit(solution)/shard_map/jit(dynamic_update_index_in_dim)/dynamic_update_slice | solution.py:292
  (427 shorter events, 263.6 us)
Async XLA Ops:
  7.2 104.5 %all-gather.7.cloned.1.call-start = ((), (), s32[]{:S(2)}) async-start(), calls=%async_computation.6 | async-start | bytes 2949120 | tf_op jit(solution)/shard_map/all_gather | solution.py:331
  19.8 153.3 %all-gather.11.cloned.1.call-start = ((), (), s32[]{:S(2)}) async-start(), calls=%async_computation.12 | async-start | bytes 2359296 | tf_op jit(solution)/shard_map/all_gather | solution.py:338
  33.4 197.9 %all-gather.13.cloned.1.call-start = ((), (), s32[]{:S(2)}) async-start(), calls=%async_computation.13 | async-start | bytes 6488064 | tf_op jit(solution)/shard_map/all_gather | solution.py:354
  34.4 232.3 %all-gather.9.cloned.1.call-start = ((), (), s32[]{:S(2)}) async-start(), calls=%async_computation.7 | async-start | bytes 12976128 | tf_op jit(solution)/shard_map/all_gather | solution.py:349
  38.3 43.9 %collective-permute-start.18 = (bf16[128,1408]{1,0:T(8,128)(2,1)}, bf16[128,1408]{1,0:T(8,128)(2,1)}, u32[]{:S(2)}, u32[]{:S(2)}) collective-permute-start(bf16[128,1408]{1,0:T(8,128)(2,1)} %get-tuple-element.92), channel_id=1, source_target_pairs={{0,8},{1,9},{2,10},{3,11},{4,12},{5,13},{6,14},{7,15},{8,0},{9,1},... | collective-permute-start | bytes 1081352 | tf_op jit(solution)/shard_map/ppermute | solution.py:252
  51.1 32.1 %collective-permute-start.19 = (bf16[128,1408]{1,0:T(8,128)(2,1)S(1)}, bf16[128,1408]{1,0:T(8,128)(2,1)}, u32[]{:S(2)}, u32[]{:S(2)}) collective-permute-start(bf16[128,1408]{1,0:T(8,128)(2,1)S(1)} %get-tuple-element.91), channel_id=1, source_target_pairs={{0,12},{1,13},{2,14},{3,15},{4,0},{5,1},{6,2},{7,3},{8,4},{9,5},{1... | collective-permute-start | bytes 1081352 | tf_op jit(solution)/shard_map/ppermute | solution.py:252
  85.4 472.5 %reduce-scatter.5.cloned.1.call-start = ((), (), s32[]{:S(2)}) async-start(), calls=%async_computation.8 | async-start | bytes 1638400 | tf_op jit(solution)/shard_map/reduce_scatter | solution.py:532
  103.1 76.5 %collective-permute-start.25 = (bf16[128,2048]{1,0:T(8,128)(2,1)}, bf16[128,2048]{1,0:T(8,128)(2,1)}, u32[]{:S(2)}, u32[]{:S(2)}) collective-permute-start(bf16[128,2048]{1,0:T(8,128)(2,1)} %bitcast_convert_fusion), channel_id=1, source_target_pairs={{0,12},{1,13},{2,14},{3,15},{4,0},{5,1},{6,2},{7,3},{8,4},{9,5},{1... | collective-permute-start | bytes 1572872 | tf_op jit(solution)/shard_map/ppermute | solution.py:252
  103.1 77.0 %collective-permute-start.24 = (bf16[128,2048]{1,0:T(8,128)(2,1)}, bf16[128,2048]{1,0:T(8,128)(2,1)}, u32[]{:S(2)}, u32[]{:S(2)}) collective-permute-start(bf16[128,2048]{1,0:T(8,128)(2,1)} %bitcast_convert_fusion), channel_id=1, source_target_pairs={{0,8},{1,9},{2,10},{3,11},{4,12},{5,13},{6,14},{7,15},{8,0},{9,1},... | collective-permute-start | bytes 1572872 | tf_op jit(solution)/shard_map/ppermute | solution.py:252
  124.5 23.7 %collective-permute-start.8 = (bf16[512,128]{1,0:T(8,128)(2,1)}, bf16[512,128]{1,0:T(8,128)(2,1)}, u32[]{:S(2)}, u32[]{:S(2)}) collective-permute-start(bf16[512,128]{1,0:T(8,128)(2,1)} %pad_maximum_fusion.13), channel_id=1, source_target_pairs={{0,8},{1,9},{2,10},{3,11},{4,12},{5,13},{6,14},{7,15},{8,0},{9,1},... | collective-permute-start | bytes 393224 | tf_op jit(solution)/shard_map/ppermute | solution.py:252
  138.0 42.1 %collective-permute-start.23 = (bf16[128,2048]{1,0:T(8,128)(2,1)}, bf16[128,2048]{1,0:T(8,128)(2,1)}, u32[]{:S(2)}, u32[]{:S(2)}) collective-permute-start(bf16[128,2048]{1,0:T(8,128)(2,1)} %bitcast_convert_fusion), channel_id=1, source_target_pairs={{0,4},{1,5},{2,6},{3,7},{4,8},{5,9},{6,10},{7,11},{8,12},{9,13},{1... | collective-permute-start | bytes 1572872 | tf_op jit(solution)/shard_map/ppermute | solution.py:252
  179.4 32.2 %collective-permute-start.12 = (bf16[128,2048]{1,0:T(8,128)(2,1)S(1)}, bf16[128,2048]{1,0:T(8,128)(2,1)S(1)}, u32[]{:S(2)}, u32[]{:S(2)}) collective-permute-start(bf16[128,2048]{1,0:T(8,128)(2,1)S(1)} %get-tuple-element.86), channel_id=1, source_target_pairs={{0,2},{1,3},{2,0},{3,1},{4,6},{5,7},{6,4},{7,5},{8,10},{9,11},{10,... | collective-permute-start | bytes 1572872 | tf_op jit(solution)/shard_map/ppermute | solution.py:249
  179.6 32.0 %collective-permute-start.11 = (bf16[128,2048]{1,0:T(8,128)(2,1)S(1)}, bf16[128,2048]{1,0:T(8,128)(2,1)S(1)}, u32[]{:S(2)}, u32[]{:S(2)}) collective-permute-start(bf16[128,2048]{1,0:T(8,128)(2,1)S(1)} %get-tuple-element.84), channel_id=1, source_target_pairs={{0,1},{1,0},{2,3},{3,2},{4,5},{5,4},{6,7},{7,6},{8,9},{9,8},{10,11... | collective-permute-start | bytes 1572872 | tf_op jit(solution)/shard_map/ppermute | solution.py:249
  214.9 61.9 %collective-permute-start.16 = (bf16[128,2048]{0,1:T(8,128)(2,1)S(1)}, bf16[128,2048]{0,1:T(8,128)(2,1)}, u32[]{:S(2)}, u32[]{:S(2)}) collective-permute-start(bf16[128,2048]{0,1:T(8,128)(2,1)S(1)} %bitcast.183), channel_id=1, source_target_pairs={{0,12},{1,13},{2,14},{3,15},{4,0},{5,1},{6,2},{7,3},{8,4},{9,5},{1... | collective-permute-start | bytes 1572872 | tf_op jit(solution)/shard_map/ppermute | solution.py:252
  229.0 47.9 %collective-permute-start.15 = (bf16[128,2048]{0,1:T(8,128)(2,1)S(1)}, bf16[128,2048]{0,1:T(8,128)(2,1)}, u32[]{:S(2)}, u32[]{:S(2)}) collective-permute-start(bf16[128,2048]{0,1:T(8,128)(2,1)S(1)} %bitcast.184), channel_id=1, source_target_pairs={{0,8},{1,9},{2,10},{3,11},{4,12},{5,13},{6,14},{7,15},{8,0},{9,1},... | collective-permute-start | bytes 1572872 | tf_op jit(solution)/shard_map/ppermute | solution.py:252
  229.0 47.9 %collective-permute-start.14 = (bf16[128,2048]{0,1:T(8,128)(2,1)S(1)}, bf16[128,2048]{0,1:T(8,128)(2,1)}, u32[]{:S(2)}, u32[]{:S(2)}) collective-permute-start(bf16[128,2048]{0,1:T(8,128)(2,1)S(1)} %bitcast.185), channel_id=1, source_target_pairs={{0,4},{1,5},{2,6},{3,7},{4,8},{5,9},{6,10},{7,11},{8,12},{9,13},{1... | collective-permute-start | bytes 1572872 | tf_op jit(solution)/shard_map/ppermute | solution.py:252
  308.5 46.7 %collective-permute-start.27 = (bf16[128,2048]{1,0:T(8,128)(2,1)S(1)}, bf16[128,2048]{1,0:T(8,128)(2,1)S(1)}, u32[]{:S(2)}, u32[]{:S(2)}) collective-permute-start(bf16[128,2048]{1,0:T(8,128)(2,1)S(1)} %get-tuple-element.80), channel_id=1, source_target_pairs={{0,8},{1,9},{2,10},{3,11},{4,12},{5,13},{6,14},{7,15},{8,0},{9,1},... | collective-permute-start | bytes 1572872 | tf_op jit(solution)/shard_map/ppermute | solution.py:252
  309.7 45.5 %collective-permute-start.26 = (bf16[128,2048]{1,0:T(8,128)(2,1)S(1)}, bf16[128,2048]{1,0:T(8,128)(2,1)S(1)}, u32[]{:S(2)}, u32[]{:S(2)}) collective-permute-start(bf16[128,2048]{1,0:T(8,128)(2,1)S(1)} %get-tuple-element.78), channel_id=1, source_target_pairs={{0,12},{1,13},{2,14},{3,15},{4,0},{5,1},{6,2},{7,3},{8,4},{9,5},{1... | collective-permute-start | bytes 1572872 | tf_op jit(solution)/shard_map/ppermute | solution.py:252
  315.5 49.0 %collective-permute-start.22 = (bf16[128,2048]{1,0:T(8,128)(2,1)}, bf16[128,2048]{1,0:T(8,128)(2,1)}, u32[]{:S(2)}, u32[]{:S(2)}) collective-permute-start(bf16[128,2048]{1,0:T(8,128)(2,1)} %get-tuple-element.82), channel_id=1, source_target_pairs={{0,4},{1,5},{2,6},{3,7},{4,8},{5,9},{6,10},{7,11},{8,12},{9,13},{1... | collective-permute-start | bytes 1572872 | tf_op jit(solution)/shard_map/ppermute | solution.py:252
  318.5 81.8 %collective-permute-start.21 = (bf16[128,2048]{1,0:T(8,128)(2,1)}, bf16[128,2048]{1,0:T(8,128)(2,1)}, u32[]{:S(2)}, u32[]{:S(2)}) collective-permute-start(bf16[128,2048]{1,0:T(8,128)(2,1)} %get-tuple-element.83), channel_id=1, source_target_pairs={{0,8},{1,9},{2,10},{3,11},{4,12},{5,13},{6,14},{7,15},{8,0},{9,1},... | collective-permute-start | bytes 1572872 | tf_op jit(solution)/shard_map/ppermute | solution.py:252
  321.5 78.8 %collective-permute-start.20 = (bf16[128,2048]{1,0:T(8,128)(2,1)}, bf16[128,2048]{1,0:T(8,128)(2,1)}, u32[]{:S(2)}, u32[]{:S(2)}) collective-permute-start(bf16[128,2048]{1,0:T(8,128)(2,1)} %get-tuple-element.81), channel_id=1, source_target_pairs={{0,12},{1,13},{2,14},{3,15},{4,0},{5,1},{6,2},{7,3},{8,4},{9,5},{1... | collective-permute-start | bytes 1572872 | tf_op jit(solution)/shard_map/ppermute | solution.py:252
  406.6 75.3 %collective-permute-start.39 = (bf16[512,2048]{1,0:T(8,128)(2,1)}, bf16[512,2048]{1,0:T(8,128)(2,1)}, u32[]{:S(2)}, u32[]{:S(2)}) collective-permute-start(bf16[512,2048]{1,0:T(8,128)(2,1)} %get-tuple-element.118), channel_id=1, source_target_pairs={{0,16},{16,0},{1,17},{17,1},{2,18},{18,2},{3,19},{19,3},{4,20},{20... | collective-permute-start | bytes 6291464 | tf_op jit(solution)/shard_map/ppermute | solution.py:255
  486.4 77.5 %reduce-scatter.7.cloned.1.call-start = ((), (), s32[]{:S(2)}) async-start(), calls=%async_computation.9 | async-start | bytes 1310720 | tf_op jit(solution)/shard_map/reduce_scatter | solution.py:488
  498.9 130.2 %reduce-scatter.9.cloned.1.call-start = ((), (), s32[]{:S(2)}) async-start(), calls=%async_computation.10 | async-start | bytes 7208960 | tf_op jit(solution)/shard_map/reduce_scatter | solution.py:465
  514.6 189.2 %reduce-scatter.11.cloned.1.call-start = ((), (), s32[]{:S(2)}) async-start(), calls=%async_computation.11 | async-start | bytes 3604480 | tf_op jit(solution)/shard_map/reduce_scatter | solution.py:450
  531.2 24.9 %collective-permute-start.37 = (bf16[128,2048]{1,0:T(8,128)(2,1)}, bf16[128,2048]{1,0:T(8,128)(2,1)}, u32[]{:S(2)}, u32[]{:S(2)}) collective-permute-start(bf16[128,2048]{1,0:T(8,128)(2,1)} %get-tuple-element.77), channel_id=1, source_target_pairs={{0,2},{1,3},{2,0},{3,1},{4,6},{5,7},{6,4},{7,5},{8,10},{9,11},{10,... | collective-permute-start | bytes 1572872 | tf_op jit(solution)/shard_map/ppermute | solution.py:249
  532.0 24.1 %collective-permute-start.36 = (bf16[128,2048]{1,0:T(8,128)(2,1)}, bf16[128,2048]{1,0:T(8,128)(2,1)}, u32[]{:S(2)}, u32[]{:S(2)}) collective-permute-start(bf16[128,2048]{1,0:T(8,128)(2,1)} %get-tuple-element.75), channel_id=1, source_target_pairs={{0,1},{1,0},{2,3},{3,2},{4,5},{5,4},{6,7},{7,6},{8,9},{9,8},{10,11... | collective-permute-start | bytes 1572872 | tf_op jit(solution)/shard_map/ppermute | solution.py:249
  578.4 54.7 %collective-permute-start.41 = (bf16[4,128,320]{1,2,0:T(8,128)(2,1)}, bf16[4,128,320]{1,2,0:T(8,128)(2,1)S(1)}, u32[]{:S(2)}, u32[]{:S(2)}) collective-permute-start(bf16[4,128,320]{1,2,0:T(8,128)(2,1)} %all-to-all-done.1), channel_id=1, source_target_pairs={{0,16},{16,0},{1,17},{17,1},{2,18},{18,2},{3,19},{19,3},{4,20},{20... | collective-permute-start | bytes 983048 | tf_op jit(solution)/shard_map/ppermute | solution.py:255
  582.5 123.5 %collective-permute-start.45 = (bf16[128,1024]{1,0:T(8,128)(2,1)}, bf16[128,1024]{1,0:T(8,128)(2,1)}, u32[]{:S(2)}, u32[]{:S(2)}) collective-permute-start(bf16[128,1024]{1,0:T(8,128)(2,1)} %collective-permute-done.44), channel_id=1, source_target_pairs={{0,16},{16,0},{1,17},{17,1},{2,18},{18,2},{3,19},{19,3},{4,20},{20... | collective-permute-start | bytes 786440 | tf_op jit(solution)/shard_map/ppermute | solution.py:255
  631.6 32.4 %collective-permute-start.49 = (bf16[128,1408]{1,0:T(8,128)(2,1)S(1)}, bf16[128,1408]{1,0:T(8,128)(2,1)}, u32[]{:S(2)}, u32[]{:S(2)}) collective-permute-start(bf16[128,1408]{1,0:T(8,128)(2,1)S(1)} %get-tuple-element.88), channel_id=1, source_target_pairs={{0,8},{1,9},{2,10},{3,11},{4,12},{5,13},{6,14},{7,15},{8,0},{9,1},... | collective-permute-start | bytes 1081352 | tf_op jit(solution)/shard_map/ppermute | solution.py:252
  632.8 32.8 %collective-permute-start.50 = (bf16[128,1408]{1,0:T(8,128)(2,1)}, bf16[128,1408]{1,0:T(8,128)(2,1)}, u32[]{:S(2)}, u32[]{:S(2)}) collective-permute-start(bf16[128,1408]{1,0:T(8,128)(2,1)} %get-tuple-element.87), channel_id=1, source_target_pairs={{0,12},{1,13},{2,14},{3,15},{4,0},{5,1},{6,2},{7,3},{8,4},{9,5},{1... | collective-permute-start | bytes 1081352 | tf_op jit(solution)/shard_map/ppermute | solution.py:252
  702.2 42.0 %collective-permute-start.51 = (bf16[128,5632]{1,0:T(8,128)(2,1)}, bf16[128,5632]{1,0:T(8,128)(2,1)}, u32[]{:S(2)}, u32[]{:S(2)}) collective-permute-start(bf16[128,5632]{1,0:T(8,128)(2,1)} %bitcast.87), channel_id=1, source_target_pairs={{0,16},{16,0},{1,17},{17,1},{2,18},{18,2},{3,19},{19,3},{4,20},{20... | collective-permute-start | bytes 4325384 | tf_op jit(solution)/shard_map/ppermute | solution.py:255
  (100 other events, 945.3 us)
Sparse Core Ops, SparseCore 0:
  20.0 39.2 all-gather.6
  61.4 53.9 all-gather.10
  117.8 63.3 all-gather.12
  183.5 83.1 all-gather.8
  486.5 29.6 reduce-scatter.4
  518.9 25.5 reduce-scatter.6
  547.5 81.5 reduce-scatter.8
  632.7 41.7 reduce-scatter.10

commit v2 on v1

--- a/solution.py
+++ b/solution.py
@@ -229,6 +229,10 @@
     return grads * cosine - turn(grads * sine)
 
 
+def after(value, *earlier):
+    return lax.optimization_barrier((value,) + earlier)[0]
+
+
 def solution(mesh):
     n_dp = mesh.shape["dp"]
     n_seq = mesh.shape["seq"]
@@ -286,10 +290,13 @@
         return jnp.concatenate(parts, axis=0)
 
     def collect_dp(value, c):
-        out = jnp.zeros((n_dp,) + value.shape, value.dtype)
-        out = lax.dynamic_update_index_in_dim(out, value, c, 0)
-        for t in range(1, n_dp):
-            out = lax.dynamic_update_index_in_dim(out, shift_dp(value, t), (c - t) % n_dp, 0)
+        slots = [value] + [shift_dp(value, t) for t in range(1, n_dp)]
+        out = []
+        for member in range(n_dp):
+            chosen = slots[0]
+            for t in range(1, n_dp):
+                chosen = jnp.where((c - t) % n_dp == member, slots[t], chosen)
+            out.append(chosen)
         return out
 
     def body(
@@ -331,7 +338,11 @@
         qkv_full = lax.all_gather(qkv_part, both, axis_index_groups=across_dp, tiled=False)
         qkv_full = qkv_full.reshape(n_dp, width, part_width)
 
-        out_part = pick(w_out, c, n_dp, 1)
+        x_in = inputs.reshape(tokens, width).astype(f32)
+        normed_one, inverse_one = normalize(x_in)
+        low_one = gather_w(after(normed_one.astype(bf16), qkv_part))
+
+        out_part = after(pick(w_out, c, n_dp, 1), low_one)
         out_part = lax.ppermute(
             out_part, "seq", [(i, GROUP * (i % planes) + i // planes) for i in range(n_seq)]
         )
@@ -340,7 +351,7 @@
 
         piece = shard // halves
         gate_up = jnp.where(c // halves == 0, scaled(w_gate, gain_two), scaled(w_up, gain_two))
-        gate_up = pick(gate_up, c % halves, halves, 0)
+        gate_up = after(pick(gate_up, c % halves, halves, 0), low_one, qkv_full)
         gate_up_part = jnp.zeros((planes, piece, ff_block), bf16)
         for t in range(planes):
             block = pick(gate_up, (p + t) % planes, planes, 1)
@@ -352,21 +363,24 @@
         up_full = gate_up_full[1]
 
         down_full = lax.all_gather(
-            pick(w_down, c, n_dp, 1), both, axis_index_groups=in_plane_dp, tiled=False
+            after(pick(w_down, c, n_dp, 1), gate_up_part), both, axis_index_groups=in_plane_dp, tiled=False
         )
         down_full = down_full.reshape(n_dp, ff_block, width // n_dp)
 
+        blocks = [
+            (i * GROUP + j) * halves + h
+            for h in range(halves) for j in range(GROUP) for i in range(planes)
+        ]
+
+        def column_blocks(value, which):
+            return jnp.concatenate([value[:, i * piece : (i + 1) * piece] for i in which], axis=1)
+
         def reorder(value):
-            value = value.reshape(tokens, planes, GROUP, halves, piece)
-            return jnp.transpose(value, (0, 3, 2, 1, 4)).reshape(tokens, width)
+            return column_blocks(value, blocks)
 
         def order_back(value):
-            value = value.reshape(tokens, halves, GROUP, planes, piece)
-            return jnp.transpose(value, (0, 3, 2, 1, 4)).reshape(tokens, width)
-
-        x_in = inputs.reshape(tokens, width).astype(f32)
-        normed_one, inverse_one = normalize(x_in)
-        low_one = gather_w(normed_one.astype(bf16))
+            return column_blocks(value, [blocks.index(i) for i in range(len(blocks))])
+
         own_pos = positions.reshape(1, tokens)
         plane_pos = jnp.concatenate([own_pos] + [xor_w(own_pos, j) for j in range(1, GROUP)], axis=1)
         cosine, sine = rope_tables(plane_pos.reshape(GROUP * tokens))
@@ -374,8 +388,6 @@
         grad_y = (
             cotangent.astype(f32) * select.astype(f32)[..., None]
         ).reshape(tokens, width)
-        grad_y_all = jnp.concatenate(gather_z(grad_y.astype(bf16)), axis=0)
-
         projected = [dot(low_one, qkv_full[i]) for i in range(n_dp)]
         cut = q_width // n_dp
         q = jnp.concatenate([one[:, :cut] for one in projected], axis=1)
@@ -386,6 +398,7 @@
         k = rotate(kv[:, None, :HEAD_DIM], cosine, sine)[:, 0]
         kv_low = jnp.concatenate([k, kv[:, HEAD_DIM:]], axis=1).astype(bf16)
         kv_all = jnp.stack(gather_z(kv_low))
+        grad_y_all = jnp.concatenate(gather_z(after(grad_y.astype(bf16), kv_all)), axis=0)
         kk = jnp.concatenate([kv_all[..., :HEAD_DIM]] * 2, axis=-1)
         vv = jnp.concatenate([kv_all[..., HEAD_DIM:]] * 2, axis=-1)
 
@@ -439,17 +452,10 @@
         )
         grad_low_two = grad_low_two.astype(bf16)
         inner_two = scatter_z([grad_low_two[t * tokens : (t + 1) * tokens] for t in range(planes)])
-        grad_x_mid = grad_y + norm_back(order_back(inner_two), normed_two, inverse_two)
-
-        mixed = jnp.concatenate([dot(hidden, down_full[i]).astype(bf16) for i in range(n_dp)], axis=1)
-        mixed = scatter_z([mixed[t * tokens : (t + 1) * tokens] for t in range(planes)])
-        outputs = (x_mid + mixed).astype(bf16).reshape(seqs, rows, width)
-
-        hidden_all = gather_dp(hidden)
+
+        hidden_later = after(hidden, grad_low_two)
+        hidden_all = gather_dp(hidden_later)
         down_sum = dot(hidden_all, exchange_dp(grad_y_all, c, 1), ((0,), (0,))).astype(bf16)
-        down_sum = lax.psum_scatter(down_sum, "seq", axis_index_groups=in_plane, tiled=True)
-        down_sum = collect_dp(down_sum, c)
-        grad_w_down = jnp.moveaxis(down_sum, 0, 1).reshape(ff_rows, width).astype(f32)
 
         low_two_all = gather_dp(low_two)
         if halves > 1:
@@ -461,22 +467,21 @@
         gate_up_grads = [of_member(c)]
         for t in range(1, n_dp):
             gate_up_grads.append(shift_dp(of_member((c + t) % n_dp), t))
-        gate_up_sum = dot(low_two_all, jnp.concatenate(gate_up_grads, axis=0), ((0,), (0,)))
+        gate_up_grads = after(jnp.concatenate(gate_up_grads, axis=0), grad_low_two)
+        gate_up_sum = dot(low_two_all, gate_up_grads, ((0,), (0,))).astype(bf16)
+
+        mixed = jnp.concatenate(
+            [dot(hidden_later, down_full[i]).astype(bf16) for i in range(n_dp)], axis=1
+        )
+        inner_two = after(inner_two, down_sum, gate_up_sum, mixed)
+        grad_x_mid = grad_y + norm_back(order_back(inner_two), normed_two, inverse_two)
+
+        mixed = after(mixed, inner_two)
+        mixed = scatter_z([mixed[t * tokens : (t + 1) * tokens] for t in range(planes)])
+        down_sum = lax.psum_scatter(down_sum, "seq", axis_index_groups=in_plane, tiled=True)
         gate_up_sum = lax.psum_scatter(
-            gate_up_sum.astype(bf16), "seq", axis_index_groups=in_plane, tiled=True
+            gate_up_sum, "seq", axis_index_groups=in_plane, tiled=True
         ).reshape(planes, piece, ff_block)
-        gate_up_rows = jnp.zeros((piece, planes, ff_block), bf16)
-        for t in range(planes):
-            block = lax.dynamic_index_in_dim(gate_up_sum, (p + t) % planes, 0, keepdims=False)
-            block = shift_z(block, t) if t else block
-            gate_up_rows = lax.dynamic_update_index_in_dim(gate_up_rows, block, (p - t) % planes, 1)
-        gate_up_rows = collect_dp(gate_up_rows.reshape(piece, planes * ff_block), c)
-        gate_up_rows = gate_up_rows.reshape(2, shard, planes * ff_block).astype(f32)
-        grad_w_gate = gate_up_rows[0] * gain_two
-        grad_w_up = gate_up_rows[1] * gain_two
-        grad_gain_mlp = jnp.sum(
-            gate_up_rows[0] * w_gate.astype(f32) + gate_up_rows[1] * w_up.astype(f32), axis=1
-        )
 
         grad_branch = gather_w(grad_x_mid.astype(bf16))
         grad_o = functools.reduce(
@@ -484,14 +489,15 @@
             [dot(pick(grad_branch, i, n_dp, 1), out_full[i], ((1,), (1,))) for i in range(n_dp)],
         ).astype(bf16)
 
-        out_sum = dot(gather_dp(o), exchange_dp(grad_branch, c, 1), ((0,), (0,))).astype(bf16)
-        out_sum = lax.psum_scatter(out_sum, "seq", axis_index_groups=across, tiled=True)
+        out_part_sum = dot(gather_dp(o), exchange_dp(grad_branch, c, 1), ((0,), (0,))).astype(bf16)
+        out_sum = lax.psum_scatter(out_part_sum, "seq", axis_index_groups=across, tiled=True)
         out_sum = lax.ppermute(
             out_sum, "seq", [(GROUP * (i % planes) + i // planes, i) for i in range(n_seq)]
         )
-        grad_w_out = jnp.moveaxis(collect_dp(out_sum, c), 0, 1).reshape(shard, width).astype(f32)
+        grad_w_out = jnp.concatenate(collect_dp(out_sum, c), axis=1).astype(f32)
 
         grad_o_seq = by_seq(grad_o, 0)
+        grad_o_seq = after(grad_o_seq, out_part_sum)
         pieces = [
             attend_back(
                 seen, q_seq[i], grad_o_seq[i], o_seq[i], kk_seq[i], vv_seq[i], lse_seq[i], order
@@ -519,6 +525,9 @@
             )
             for i in range(n_dp)
         ]
+        mixed = after(mixed, kv_pre)
+        outputs = (x_mid + mixed).astype(bf16).reshape(seqs, rows, width)
+
         grad_low_one = functools.reduce(
             jnp.add, [dot(pre[i], qkv_full[i], ((1,), (1,))) for i in range(n_dp)]
         ).astype(bf16)
@@ -527,16 +536,42 @@
         grad_inputs = grad_inputs.reshape(seqs, rows, width)
 
         qkv_sum = dot(
-            gather_dp(low_one), exchange_dp(jnp.concatenate(pre, axis=1), c, 1), ((0,), (0,))
+            gather_dp(low_one),
+            exchange_dp(after(jnp.concatenate(pre, axis=1), grad_low_one), c, 1),
+            ((0,), (0,)),
         ).astype(bf16)
         qkv_sum = lax.psum_scatter(qkv_sum, "seq", axis_index_groups=across, tiled=True)
         qkv_sum = qkv_sum.reshape(GROUP, shard, part_width)
         qkv_sum = lax.all_to_all(qkv_sum, "seq", 0, 0, axis_index_groups=in_plane, tiled=True)
-        qkv_sum = collect_dp(qkv_sum, c).astype(f32)
-        q_sum = jnp.transpose(qkv_sum[..., :cut], (2, 1, 0, 3)).reshape(shard, width)
-        kv_sum = jnp.transpose(qkv_sum[..., cut:], (2, 1, 0, 3)).reshape(shard, GROUP, PAIR)
+        qkv_sum = collect_dp(qkv_sum, c)
+        q_sum = jnp.concatenate(
+            [one[j][:, :cut] for j in range(GROUP) for one in qkv_sum], axis=1
+        ).astype(f32)
+        kv_sum = jnp.concatenate(
+            [one[j][:, cut:] for j in range(GROUP) for one in qkv_sum], axis=1
+        ).astype(f32).reshape(shard, GROUP, PAIR)
         k_sum = kv_sum[..., :HEAD_DIM].reshape(shard, GROUP * HEAD_DIM)
         v_sum = kv_sum[..., HEAD_DIM:].reshape(shard, GROUP * HEAD_DIM)
+
+        grad_w_down = jnp.concatenate(collect_dp(down_sum, c), axis=1).astype(f32)
+        gate_up_rows = jnp.zeros((planes, piece, ff_block), bf16)
+        for t in range(planes):
+            block = lax.dynamic_index_in_dim(gate_up_sum, (p + t) % planes, 0, keepdims=False)
+            block = shift_z(block, t) if t else block
+            gate_up_rows = lax.dynamic_update_index_in_dim(gate_up_rows, block, (p - t) % planes, 0)
+        gate_up_rows = collect_dp(gate_up_rows, c)
+
+        def rows_of(members):
+            wide = [jnp.concatenate([one[i] for i in range(planes)], axis=1) for one in members]
+            return jnp.concatenate(wide, axis=0).astype(f32)
+
+        gate_rows = rows_of(gate_up_rows[:halves])
+        up_rows = rows_of(gate_up_rows[halves:])
+        grad_w_gate = gate_rows * gain_two
+        grad_w_up = up_rows * gain_two
+        grad_gain_mlp = jnp.sum(
+            gate_rows * w_gate.astype(f32) + up_rows * w_up.astype(f32), axis=1
+        )
         grad_gain_attn = (
             jnp.sum(q_sum * w_query.astype(f32), axis=1)
             + jnp.sum(k_sum * w_key.astype(f32), axis=1)

time: 771 us -> 840 us (1.089)
  the two profiles are of different devices: /device:TPU:25 before, /device:TPU:1 now
where the time goes in v2:
time: 840 us; the launch traced here: 831 us
  waiting for transfers between devices  410 us (49%)
  starting transfers between devices  148 us (18%)
  local copies, waits for them, and re-layouts  95 us (11%)
  matrix products  80.2 us (10%)
  other arithmetic  54.2 us (6%)
  Pallas kernels  17.9 us (2%)
  between operations  16.4 us (2%)
  blocking collectives  9.61 us (1%)
    ppermute x24, waiting for transfers between devices, shift_z(): lax.ppermute(value, 'seq', [(s, (s + GROUP * t) % n_seq) for s in range(n...  219 us
    ppermute x24, starting transfers between devices, shift_z(): lax.ppermute(value, 'seq', [(s, (s + GROUP * t) % n_seq) for s in range(n...  96.4 us
    ppermute x17, waiting for transfers between devices, xor_w(): return lax.ppermute(value, 'seq', [(s, s ^ j) for s in range(n_seq)])  82.5 us
    dot_general x20, matrix products, dot(): lax.dot_general(left, right, (contract, ((), ())), preferred_element_type...  80.2 us
    reduce_scatter x1, waiting for transfers between devices, body(): lax.psum_scatter(gate_up_sum, 'seq', axis_index_groups=in_plane, tiled=True)  65.9 us
    unnamed x192, local copies, waits for them, and re-layouts  47.5 us
    reduce_scatter x1, waiting for transfers between devices, body(): lax.psum_scatter(down_sum, 'seq', axis_index_groups=in_plane, tiled=True)  30.7 us
    ppermute x12, starting transfers between devices, shift_dp(): return lax.ppermute(value, 'dp', [(c, (c + t) % n_dp) for c in range(n_dp)])  26.6 us
  transfers between devices with their start and end apart: 64, of which 30 were waited for; matrix products, arithmetic and copies ran while one was open for 22% of the time, Pallas kernels for 2%

profile of v2, /device:TPU:1, one launch (start us, length us, event | category | flops | bytes accessed | tf_op | source)
XLA Modules:
  0.0 831.1 jit_solution(17563278563423913384)
XLA Ops:
  11.6 9.6 %all_to_all.10 = bf16[4,128,320]{1,2,0:T(8,128)(2,1)S(1)} all-to-all(bf16[4,128,320]{1,2,0:T(8,128)(2,1)S(1)} %fusion.71), channel_id=1, replica_groups={{0,1,2,3},{4,5,6,7},{8,9,10,11},{12,13,14,15},{16,17,18,19},{20,21,22,2..., dimensions={0} | all-to-all | bytes 655360 | tf_op jit(solution)/shard_map/all_to_all | solution.py:333
  25.0 9.3 %collective-permute-done.1 = bf16[128,2048]{1,0:T(8,128)(2,1)S(1)} collective-permute-done((bf16[128,2048]{1,0:T(8,128)(2,1)S(1)}, bf16[128,2048]{1,0:T(8,128)(2,1)S(1)}, u32[]{:S(2)}, u32[]{:S(2)}) %collective-permute-start.1) | collective-permute-done | bytes 524320 | tf_op jit(solution)/shard_map/ppermute | solution.py:253
  47.1 34.7 %collective-permute-start.17 = (bf16[128,1408]{1,0:T(8,128)(2,1)S(1)}, bf16[128,1408]{1,0:T(8,128)(2,1)S(1)}, u32[]{:S(2)}, u32[]{:S(2)}) collective-permute-start(bf16[128,1408]{1,0:T(8,128)(2,1)S(1)} %get-tuple-element.123), channel_id=1, source_target_pairs={{0,4},{1,5},{2,6},{3,7},{4,8},{5,9},{6,10},{7,11},{8,12},{9,13},{1... | collective-permute-start | bytes 1081352 | tf_op jit(solution)/shard_map/ppermute | solution.py:256
  85.1 7.0 collective-permute-done.17
  92.1 31.7 %collective-permute-done.18 = bf16[128,1408]{1,0:T(8,128)(2,1)S(1)} collective-permute-done((bf16[128,1408]{1,0:T(8,128)(2,1)S(1)}, bf16[128,1408]{1,0:T(8,128)(2,1)S(1)}, u32[]{:S(2)}, u32[]{:S(2)}) %collective-permute-start.18) | collective-permute-done | bytes 360480 | tf_op jit(solution)/shard_map/ppermute | solution.py:256
  164.1 7.6 attend.1
  177.6 6.7 collective-permute-done.11
  184.4 21.2 %collective-permute-done.13 = bf16[128,2048]{1,0:T(8,128)(2,1)S(1)} collective-permute-done((bf16[128,2048]{1,0:T(8,128)(2,1)S(1)}, bf16[128,2048]{1,0:T(8,128)(2,1)S(1)}, u32[]{:S(2)}, u32[]{:S(2)}) %collective-permute-start.13) | collective-permute-done | bytes 524320 | tf_op jit(solution)/shard_map/ppermute | solution.py:253
  216.4 21.4 %collective-permute-start.16 = (bf16[128,2048]{1,0:T(8,128)(2,1)S(1)}, bf16[128,2048]{1,0:T(8,128)(2,1)S(1)}, u32[]{:S(2)}, u32[]{:S(2)}) collective-permute-start(bf16[128,2048]{1,0:T(8,128)(2,1)S(1)} %get-tuple-element.150), channel_id=1, source_target_pairs={{0,12},{1,13},{2,14},{3,15},{4,0},{5,1},{6,2},{7,3},{8,4},{9,5},{1... | collective-permute-start | bytes 1572872 | tf_op jit(solution)/shard_map/ppermute | solution.py:256
  247.4 56.3 %collective-permute-done.15 = bf16[128,2048]{1,0:T(8,128)(2,1)S(1)} collective-permute-done((bf16[128,2048]{1,0:T(8,128)(2,1)S(1)}, bf16[128,2048]{1,0:T(8,128)(2,1)S(1)}, u32[]{:S(2)}, u32[]{:S(2)}) %collective-permute-start.15) | collective-permute-done | bytes 524320 | tf_op jit(solution)/shard_map/ppermute | solution.py:256
  310.3 12.1 %collective-permute-done.21 = bf16[128,2048]{1,0:T(8,128)(2,1)} collective-permute-done((bf16[128,2048]{1,0:T(8,128)(2,1)}, bf16[128,2048]{1,0:T(8,128)(2,1)}, u32[]{:S(2)}, u32[]{:S(2)}) %collective-permute-start.21) | collective-permute-done | bytes 524320 | tf_op jit(solution)/shard_map/ppermute | solution.py:256
  323.5 9.4 %collective-permute-done.22 = bf16[128,2048]{1,0:T(8,128)(2,1)S(1)} collective-permute-done((bf16[128,2048]{1,0:T(8,128)(2,1)}, bf16[128,2048]{1,0:T(8,128)(2,1)S(1)}, u32[]{:S(2)}, u32[]{:S(2)}) %collective-permute-start.22) | collective-permute-done | bytes 524320 | tf_op jit(solution)/shard_map/ppermute | solution.py:256
  346.7 10.1 %fusion.99 = (bf16[16,128,1408]{2,1,0:T(8,128)(2,1)}, bf16[16,128,1408]{2,1,0:T(8,128)(2,1)}) fusion(bf16[32,128,1408]{2,1,0:T(8,128)(2,1)} %all-gather.12.cloned.1.call-done), kind=kLoop, calls=%fused_computation.340 | loop fusion | bytes 23068672 | tf_op jit(solution)/shard_map/slice | solution.py:362
  356.9 7.3 fusion.98
  364.3 6.7 multiply_convert_fusion.2
  400.2 12.2 %collective-permute-start.26 = (bf16[512,1408]{1,0:T(8,128)(2,1)}, bf16[512,1408]{1,0:T(8,128)(2,1)}, u32[]{:S(2)}, u32[]{:S(2)}) collective-permute-start(bf16[512,1408]{1,0:T(8,128)(2,1)} %get-tuple-element.31), channel_id=1, source_target_pairs={{0,16},{16,0},{1,17},{17,1},{2,18},{18,2},{3,19},{19,3},{4,20},{20... | collective-permute-start | bytes 4325384 | tf_op jit(solution)/shard_map/ppermute | solution.py:259
  412.4 22.0 %collective-permute-done.24 = bf16[128,2048]{1,0:T(8,128)(2,1)S(1)} collective-permute-done((bf16[128,2048]{1,0:T(8,128)(2,1)S(1)}, bf16[128,2048]{1,0:T(8,128)(2,1)S(1)}, u32[]{:S(2)}, u32[]{:S(2)}) %collective-permute-start.24) | collective-permute-done | bytes 524320 | tf_op jit(solution)/shard_map/ppermute | solution.py:256
  436.0 10.9 %convolution_convert_fusion = bf16[2048,1408]{1,0:T(8,128)(2,1)} fusion(bf16[1024,2048]{1,0:T(8,128)(2,1)} %constant_dynamic-update-slice_fusion.25, bf16[1024,1408]{1,0:T(8,128)(2,1)S(1)} %pad_maximum_fusion), kind=kOutput, calls=%fused_computation | convolution fusion | flops 5908463616 | bytes 12845056 | tf_op jit(solution)/shard_map/dot_general | solution.py:26
  446.8 7.2 convolution_convert_fusion.1
  472.9 7.6 collective-permute-done.30
  480.5 12.2 %collective-permute-done.32 = bf16[128,2048]{1,0:T(8,128)(2,1)S(1)} collective-permute-done((bf16[128,2048]{1,0:T(8,128)(2,1)S(1)}, bf16[128,2048]{1,0:T(8,128)(2,1)S(1)}, u32[]{:S(2)}, u32[]{:S(2)}) %collective-permute-start.32) | collective-permute-done | bytes 524320 | tf_op jit(solution)/shard_map/ppermute | solution.py:256
  492.8 20.5 %collective-permute-done.31 = bf16[128,2048]{1,0:T(8,128)(2,1)S(1)} collective-permute-done((bf16[128,2048]{1,0:T(8,128)(2,1)S(1)}, bf16[128,2048]{1,0:T(8,128)(2,1)S(1)}, u32[]{:S(2)}, u32[]{:S(2)}) %collective-permute-start.31) | collective-permute-done | bytes 524320 | tf_op jit(solution)/shard_map/ppermute | solution.py:256
  517.7 11.4 %collective-permute-done.34 = bf16[128,2048]{1,0:T(8,128)(2,1)S(1)} collective-permute-done((bf16[128,2048]{1,0:T(8,128)(2,1)S(1)}, bf16[128,2048]{1,0:T(8,128)(2,1)S(1)}, u32[]{:S(2)}, u32[]{:S(2)}) %collective-permute-start.34) | collective-permute-done | bytes 524320 | tf_op jit(solution)/shard_map/ppermute | solution.py:253
  551.5 10.3 %attend_back.1 = (f32[512,512]{1,0:T(8,128)}, f32[4,512,128]{2,1,0:T(8,128)}, f32[4,512,128]{2,1,0:T(8,128)}) custom-call(s32[1]{0:T(128)} %bitcast.1.seen_ref, bf16[512,512]{1,0:T(8,128)(2,1)} %multiply_convert_fusion.3.q_ref, bf16[512,512]{1,0:T(8,128)(2,1)} %bitcast.180, bf16[512,512]{1,0:T(8,128)(2,1)} %get-tuple-element.26.o_ref, ...), custom_call_target="tpu_custom_call" | custom-call | tf_op jit(solution)/shard_map/attend_back/pallas_call | solution.py:166
  565.1 21.0 %collective-permute-start.39 = (bf16[512,128]{1,0:T(8,128)(2,1)}, bf16[512,128]{1,0:T(8,128)(2,1)S(1)}, u32[]{:S(2)}, u32[]{:S(2)}) collective-permute-start(bf16[512,128]{1,0:T(8,128)(2,1)} %get-tuple-element.126), channel_id=1, source_target_pairs={{0,12},{1,13},{2,14},{3,15},{4,0},{5,1},{6,2},{7,3},{8,4},{9,5},{1... | collective-permute-start | bytes 393224 | tf_op jit(solution)/shard_map/ppermute | solution.py:256
  621.5 10.0 %collective-permute-done.42 = bf16[128,2048]{1,0:T(8,128)(2,1)S(1)} collective-permute-done((bf16[128,2048]{1,0:T(8,128)(2,1)}, bf16[128,2048]{1,0:T(8,128)(2,1)S(1)}, u32[]{:S(2)}, u32[]{:S(2)}) %collective-permute-start.42) | collective-permute-done | bytes 524320 | tf_op jit(solution)/shard_map/ppermute | solution.py:253
  631.4 15.6 %collective-permute-done.44 = bf16[128,2048]{1,0:T(8,128)(2,1)S(1)} collective-permute-done((bf16[128,2048]{1,0:T(8,128)(2,1)}, bf16[128,2048]{1,0:T(8,128)(2,1)S(1)}, u32[]{:S(2)}, u32[]{:S(2)}) %collective-permute-start.44) | collective-permute-done | bytes 524320 | tf_op jit(solution)/shard_map/ppermute | solution.py:253
  649.9 7.9 reduce-scatter.5.cloned.1.call-done
  672.3 30.7 %reduce-scatter.11.cloned.1.call-done = bf16[352,1024]{1,0:T(8,128)(2,1)} async-done(((bf16[1408,1024]{1,0:T(8,128)(2,1)}), bf16[352,1024]{1,0:T(8,128)(2,1)}) %reduce-scatter.11.cloned.1.call-update) | async-done | bytes 720912 | tf_op jit(solution)/shard_map/reduce_scatter | solution.py:481
  705.7 65.9 %reduce-scatter.9.cloned.1.call-done = bf16[512,1408]{1,0:T(8,128)(2,1)} async-done(((bf16[2048,1408]{1,0:T(8,128)(2,1)}), bf16[512,1408]{1,0:T(8,128)(2,1)}) %reduce-scatter.9.cloned.1.call-update) | async-done | bytes 1441808 | tf_op jit(solution)/shard_map/reduce_scatter | solution.py:482
  777.3 7.0 collective-permute-done.50
  784.3 24.3 %collective-permute-done.51 = bf16[128,1408]{1,0:T(8,128)(2,1)S(1)} collective-permute-done((bf16[128,1408]{1,0:T(8,128)(2,1)S(1)}, bf16[128,1408]{1,0:T(8,128)(2,1)S(1)}, u32[]{:S(2)}, u32[]{:S(2)}) %collective-permute-start.51) | collective-permute-done | bytes 360480 | tf_op jit(solution)/shard_map/ppermute | solution.py:256
  (445 shorter events, 267.0 us)
Async XLA Ops:
  7.2 125.7 %all-gather.8.cloned.1.call-start = ((), (), s32[]{:S(2)}) async-start(), calls=%async_computation.6 | async-start | bytes 2949120 | tf_op jit(solution)/shard_map/all_gather | solution.py:338
  22.4 149.3 %all-gather.10.cloned.1.call-start = ((), (), s32[]{:S(2)}) async-start(), calls=%async_computation.11 | async-start | bytes 2359296 | tf_op jit(solution)/shard_map/all_gather | solution.py:349
  43.6 297.6 %all-gather.14.cloned.1.call-start = ((), (), s32[]{:S(2)}) async-start(), calls=%async_computation.13 | async-start | bytes 6488064 | tf_op jit(solution)/shard_map/all_gather | solution.py:365
  47.1 45.0 %collective-permute-start.17 = (bf16[128,1408]{1,0:T(8,128)(2,1)S(1)}, bf16[128,1408]{1,0:T(8,128)(2,1)S(1)}, u32[]{:S(2)}, u32[]{:S(2)}) collective-permute-start(bf16[128,1408]{1,0:T(8,128)(2,1)S(1)} %get-tuple-element.123), channel_id=1, source_target_pairs={{0,4},{1,5},{2,6},{3,7},{4,8},{5,9},{6,10},{7,11},{8,12},{9,13},{1... | collective-permute-start | bytes 1081352 | tf_op jit(solution)/shard_map/ppermute | solution.py:256
  82.7 41.1 %collective-permute-start.19 = (bf16[128,1408]{1,0:T(8,128)(2,1)S(1)}, bf16[128,1408]{1,0:T(8,128)(2,1)S(1)}, u32[]{:S(2)}, u32[]{:S(2)}) collective-permute-start(bf16[128,1408]{1,0:T(8,128)(2,1)S(1)} %get-tuple-element.121), channel_id=1, source_target_pairs={{0,12},{1,13},{2,14},{3,15},{4,0},{5,1},{6,2},{7,3},{8,4},{9,5},{1... | collective-permute-start | bytes 1081352 | tf_op jit(solution)/shard_map/ppermute | solution.py:256
  82.7 41.0 %collective-permute-start.18 = (bf16[128,1408]{1,0:T(8,128)(2,1)S(1)}, bf16[128,1408]{1,0:T(8,128)(2,1)S(1)}, u32[]{:S(2)}, u32[]{:S(2)}) collective-permute-start(bf16[128,1408]{1,0:T(8,128)(2,1)S(1)} %get-tuple-element.122), channel_id=1, source_target_pairs={{0,8},{1,9},{2,10},{3,11},{4,12},{5,13},{6,14},{7,15},{8,0},{9,1},... | collective-permute-start | bytes 1081352 | tf_op jit(solution)/shard_map/ppermute | solution.py:256
  123.9 222.9 %all-gather.12.cloned.1.call-start = ((), (), s32[]{:S(2)}) async-start(), calls=%async_computation.12 | async-start | bytes 12976128 | tf_op jit(solution)/shard_map/all_gather | solution.py:360
  125.0 492.9 %reduce-scatter.7.cloned.1.call-start = ((), (), s32[]{:S(2)}) async-start(), calls=%async_computation.8 | async-start | bytes 1310720 | tf_op jit(solution)/shard_map/reduce_scatter | solution.py:493
  176.2 29.4 %collective-permute-start.13 = (bf16[128,2048]{1,0:T(8,128)(2,1)S(1)}, bf16[128,2048]{1,0:T(8,128)(2,1)S(1)}, u32[]{:S(2)}, u32[]{:S(2)}) collective-permute-start(bf16[128,2048]{1,0:T(8,128)(2,1)S(1)} %get-tuple-element.102), channel_id=1, source_target_pairs={{0,3},{1,2},{2,1},{3,0},{4,7},{5,6},{6,5},{7,4},{8,11},{9,10},{10,... | collective-permute-start | bytes 1572872 | tf_op jit(solution)/shard_map/ppermute | solution.py:253
  177.4 28.1 %collective-permute-start.12 = (bf16[128,2048]{1,0:T(8,128)(2,1)S(1)}, bf16[128,2048]{1,0:T(8,128)(2,1)S(1)}, u32[]{:S(2)}, u32[]{:S(2)}) collective-permute-start(bf16[128,2048]{1,0:T(8,128)(2,1)S(1)} %get-tuple-element.103), channel_id=1, source_target_pairs={{0,2},{1,3},{2,0},{3,1},{4,6},{5,7},{6,4},{7,5},{8,10},{9,11},{10,... | collective-permute-start | bytes 1572872 | tf_op jit(solution)/shard_map/ppermute | solution.py:253
  216.4 31.0 %collective-permute-start.16 = (bf16[128,2048]{1,0:T(8,128)(2,1)S(1)}, bf16[128,2048]{1,0:T(8,128)(2,1)S(1)}, u32[]{:S(2)}, u32[]{:S(2)}) collective-permute-start(bf16[128,2048]{1,0:T(8,128)(2,1)S(1)} %get-tuple-element.150), channel_id=1, source_target_pairs={{0,12},{1,13},{2,14},{3,15},{4,0},{5,1},{6,2},{7,3},{8,4},{9,5},{1... | collective-permute-start | bytes 1572872 | tf_op jit(solution)/shard_map/ppermute | solution.py:256
  237.9 65.8 %collective-permute-start.15 = (bf16[128,2048]{1,0:T(8,128)(2,1)S(1)}, bf16[128,2048]{1,0:T(8,128)(2,1)S(1)}, u32[]{:S(2)}, u32[]{:S(2)}) collective-permute-start(bf16[128,2048]{1,0:T(8,128)(2,1)S(1)} %get-tuple-element.150), channel_id=1, source_target_pairs={{0,8},{1,9},{2,10},{3,11},{4,12},{5,13},{6,14},{7,15},{8,0},{9,1},... | collective-permute-start | bytes 1572872 | tf_op jit(solution)/shard_map/ppermute | solution.py:256
  237.9 65.8 %collective-permute-start.14 = (bf16[128,2048]{1,0:T(8,128)(2,1)S(1)}, bf16[128,2048]{1,0:T(8,128)(2,1)S(1)}, u32[]{:S(2)}, u32[]{:S(2)}) collective-permute-start(bf16[128,2048]{1,0:T(8,128)(2,1)S(1)} %get-tuple-element.150), channel_id=1, source_target_pairs={{0,4},{1,5},{2,6},{3,7},{4,8},{5,9},{6,10},{7,11},{8,12},{9,13},{1... | collective-permute-start | bytes 1572872 | tf_op jit(solution)/shard_map/ppermute | solution.py:256
  239.4 69.8 %collective-permute-start.20 = (bf16[128,2048]{1,0:T(8,128)(2,1)}, bf16[128,2048]{1,0:T(8,128)(2,1)}, u32[]{:S(2)}, u32[]{:S(2)}) collective-permute-start(bf16[128,2048]{1,0:T(8,128)(2,1)} %bitcast_convert_fusion), channel_id=1, source_target_pairs={{0,4},{1,5},{2,6},{3,7},{4,8},{5,9},{6,10},{7,11},{8,12},{9,13},{1... | collective-permute-start | bytes 1572872 | tf_op jit(solution)/shard_map/ppermute | solution.py:256
  305.4 32.7 %collective-permute-start.28 = (bf16[512,2048]{1,0:T(8,128)(2,1)}, bf16[512,2048]{1,0:T(8,128)(2,1)}, u32[]{:S(2)}, u32[]{:S(2)}) collective-permute-start(bf16[512,2048]{1,0:T(8,128)(2,1)} %pad_maximum_fusion.1), channel_id=1, source_target_pairs={{0,16},{16,0},{1,17},{17,1},{2,18},{18,2},{3,19},{19,3},{4,20},{20... | collective-permute-start | bytes 6291464 | tf_op jit(solution)/shard_map/ppermute | solution.py:259
  334.5 112.4 %collective-permute-start.27 = (bf16[512,1024]{1,0:T(8,128)(2,1)}, bf16[512,1024]{1,0:T(8,128)(2,1)}, u32[]{:S(2)}, u32[]{:S(2)}) collective-permute-start(bf16[512,1024]{1,0:T(8,128)(2,1)} %get-tuple-element.97), channel_id=1, source_target_pairs={{0,16},{16,0},{1,17},{17,1},{2,18},{18,2},{3,19},{19,3},{4,20},{20... | collective-permute-start | bytes 3145736 | tf_op jit(solution)/shard_map/ppermute | solution.py:259
  387.0 48.7 %collective-permute-start.29 = (bf16[512,1408]{1,0:T(8,128)(2,1)S(1)}, bf16[512,1408]{1,0:T(8,128)(2,1)S(1)}, u32[]{:S(2)}, u32[]{:S(2)}) collective-permute-start(bf16[512,1408]{1,0:T(8,128)(2,1)S(1)} %broadcast_select_fusion.2), channel_id=1, source_target_pairs={{0,16},{16,0},{1,17},{17,1},{2,18},{18,2},{3,19},{19,3},{4,20},{20... | collective-permute-start | bytes 4325384 | tf_op jit(solution)/shard_map/ppermute | solution.py:259
  388.8 45.7 %collective-permute-start.24 = (bf16[128,2048]{1,0:T(8,128)(2,1)S(1)}, bf16[128,2048]{1,0:T(8,128)(2,1)S(1)}, u32[]{:S(2)}, u32[]{:S(2)}) collective-permute-start(bf16[128,2048]{1,0:T(8,128)(2,1)S(1)} %get-tuple-element.100), channel_id=1, source_target_pairs={{0,8},{1,9},{2,10},{3,11},{4,12},{5,13},{6,14},{7,15},{8,0},{9,1},... | collective-permute-start | bytes 1572872 | tf_op jit(solution)/shard_map/ppermute | solution.py:256
  400.2 46.7 %collective-permute-start.26 = (bf16[512,1408]{1,0:T(8,128)(2,1)}, bf16[512,1408]{1,0:T(8,128)(2,1)}, u32[]{:S(2)}, u32[]{:S(2)}) collective-permute-start(bf16[512,1408]{1,0:T(8,128)(2,1)} %get-tuple-element.31), channel_id=1, source_target_pairs={{0,16},{16,0},{1,17},{17,1},{2,18},{18,2},{3,19},{19,3},{4,20},{20... | collective-permute-start | bytes 4325384 | tf_op jit(solution)/shard_map/ppermute | solution.py:259
  470.0 43.2 %collective-permute-start.31 = (bf16[128,2048]{1,0:T(8,128)(2,1)S(1)}, bf16[128,2048]{1,0:T(8,128)(2,1)S(1)}, u32[]{:S(2)}, u32[]{:S(2)}) collective-permute-start(bf16[128,2048]{1,0:T(8,128)(2,1)S(1)} %get-tuple-element.95), channel_id=1, source_target_pairs={{0,8},{1,9},{2,10},{3,11},{4,12},{5,13},{6,14},{7,15},{8,0},{9,1},... | collective-permute-start | bytes 1572872 | tf_op jit(solution)/shard_map/ppermute | solution.py:256
  541.1 65.7 %collective-permute-start.45 = (bf16[512,2048]{1,0:T(8,128)(2,1)}, bf16[512,2048]{1,0:T(8,128)(2,1)}, u32[]{:S(2)}, u32[]{:S(2)}) collective-permute-start(bf16[512,2048]{1,0:T(8,128)(2,1)} %copy-done.44), channel_id=1, source_target_pairs={{0,16},{16,0},{1,17},{17,1},{2,18},{18,2},{3,19},{19,3},{4,20},{20... | collective-permute-start | bytes 6291464 | tf_op jit(solution)/shard_map/ppermute | solution.py:259
  550.8 106.9 %reduce-scatter.5.cloned.1.call-start = ((), (), s32[]{:S(2)}) async-start(), calls=%async_computation.7 | async-start | bytes 1638400 | tf_op jit(solution)/shard_map/reduce_scatter | solution.py:543
  565.1 32.2 %collective-permute-start.39 = (bf16[512,128]{1,0:T(8,128)(2,1)}, bf16[512,128]{1,0:T(8,128)(2,1)S(1)}, u32[]{:S(2)}, u32[]{:S(2)}) collective-permute-start(bf16[512,128]{1,0:T(8,128)(2,1)} %get-tuple-element.126), channel_id=1, source_target_pairs={{0,12},{1,13},{2,14},{3,15},{4,0},{5,1},{6,2},{7,3},{8,4},{9,5},{1... | collective-permute-start | bytes 393224 | tf_op jit(solution)/shard_map/ppermute | solution.py:256
  611.2 91.8 %reduce-scatter.11.cloned.1.call-start = ((), (), s32[]{:S(2)}) async-start(), calls=%async_computation.10 | async-start | bytes 3604480 | tf_op jit(solution)/shard_map/reduce_scatter | solution.py:481
  611.9 159.7 %reduce-scatter.9.cloned.1.call-start = ((), (), s32[]{:S(2)}) async-start(), calls=%async_computation.9 | async-start | bytes 7208960 | tf_op jit(solution)/shard_map/reduce_scatter | solution.py:482
  616.4 30.6 %collective-permute-start.44 = (bf16[128,2048]{1,0:T(8,128)(2,1)}, bf16[128,2048]{1,0:T(8,128)(2,1)S(1)}, u32[]{:S(2)}, u32[]{:S(2)}) collective-permute-start(bf16[128,2048]{1,0:T(8,128)(2,1)} %get-tuple-element.89), channel_id=1, source_target_pairs={{0,3},{1,2},{2,1},{3,0},{4,7},{5,6},{6,5},{7,4},{8,11},{9,10},{10,... | collective-permute-start | bytes 1572872 | tf_op jit(solution)/shard_map/ppermute | solution.py:253
  617.8 29.2 %collective-permute-start.43 = (bf16[128,2048]{1,0:T(8,128)(2,1)}, bf16[128,2048]{1,0:T(8,128)(2,1)S(1)}, u32[]{:S(2)}, u32[]{:S(2)}) collective-permute-start(bf16[128,2048]{1,0:T(8,128)(2,1)} %get-tuple-element.90), channel_id=1, source_target_pairs={{0,2},{1,3},{2,0},{3,1},{4,6},{5,7},{6,4},{7,5},{8,10},{9,11},{10,... | collective-permute-start | bytes 1572872 | tf_op jit(solution)/shard_map/ppermute | solution.py:253
  617.9 30.6 %collective-permute-start.48 = (bf16[128,1024]{1,0:T(8,128)(2,1)}, bf16[128,1024]{1,0:T(8,128)(2,1)}, u32[]{:S(2)}, u32[]{:S(2)}) collective-permute-start(bf16[128,1024]{1,0:T(8,128)(2,1)} %reduce-scatter.7.cloned.1.call-done), channel_id=1, source_target_pairs={{0,0},{4,1},{8,2},{12,3},{1,4},{5,5},{9,6},{13,7},{2,8},{6,9},{10,... | collective-permute-start | bytes 786440 | tf_op jit(solution)/shard_map/ppermute | solution.py:494
  667.3 36.5 %collective-permute-start.47 = (bf16[4,128,320]{1,2,0:T(8,128)(2,1)S(1)}, bf16[4,128,320]{1,2,0:T(8,128)(2,1)S(1)}, u32[]{:S(2)}, u32[]{:S(2)}) collective-permute-start(bf16[4,128,320]{1,2,0:T(8,128)(2,1)S(1)} %all-to-all-done.1), channel_id=1, source_target_pairs={{0,16},{16,0},{1,17},{17,1},{2,18},{18,2},{3,19},{19,3},{4,20},{20... | collective-permute-start | bytes 983048 | tf_op jit(solution)/shard_map/ppermute | solution.py:259
  703.0 108.5 %collective-permute-start.54 = (bf16[352,1024]{1,0:T(8,128)(2,1)}, bf16[352,1024]{1,0:T(8,128)(2,1)}, u32[]{:S(2)}, u32[]{:S(2)}) collective-permute-start(bf16[352,1024]{1,0:T(8,128)(2,1)} %reduce-scatter.11.cloned.1.call-done), channel_id=1, source_target_pairs={{0,16},{16,0},{1,17},{17,1},{2,18},{18,2},{3,19},{19,3},{4,20},{20... | collective-permute-start | bytes 2162696 | tf_op jit(solution)/shard_map/ppermute | solution.py:259
  774.6 34.1 %collective-permute-start.52 = (bf16[128,1408]{1,0:T(8,128)(2,1)S(1)}, bf16[128,1408]{1,0:T(8,128)(2,1)S(1)}, u32[]{:S(2)}, u32[]{:S(2)}) collective-permute-start(bf16[128,1408]{1,0:T(8,128)(2,1)S(1)} %get-tuple-element.117), channel_id=1, source_target_pairs={{0,12},{1,13},{2,14},{3,15},{4,0},{5,1},{6,2},{7,3},{8,4},{9,5},{1... | collective-permute-start | bytes 1081352 | tf_op jit(solution)/shard_map/ppermute | solution.py:256
  777.0 31.7 %collective-permute-start.51 = (bf16[128,1408]{1,0:T(8,128)(2,1)S(1)}, bf16[128,1408]{1,0:T(8,128)(2,1)S(1)}, u32[]{:S(2)}, u32[]{:S(2)}) collective-permute-start(bf16[128,1408]{1,0:T(8,128)(2,1)S(1)} %get-tuple-element.118), channel_id=1, source_target_pairs={{0,8},{1,9},{2,10},{3,11},{4,12},{5,13},{6,14},{7,15},{8,0},{9,1},... | collective-permute-start | bytes 1081352 | tf_op jit(solution)/shard_map/ppermute | solution.py:256
  (95 other events, 1137.6 us)
Sparse Core Ops, SparseCore 0:
  22.5 56.7 all-gather.7
  80.9 41.2 all-gather.9
  124.6 48.7 all-gather.13
  175.7 88.1 all-gather.11
  551.0 26.0 reduce-scatter.6
  611.3 46.3 reduce-scatter.4
  661.4 41.5 reduce-scatter.10
  705.9 65.6 reduce-scatter.8

commit v3 on v2

--- a/solution.py
+++ b/solution.py
@@ -335,23 +335,28 @@
         )
         part_width = (q_width + PAIR) // n_dp
         qkv_part = qkv_part.reshape(GROUP * shard, part_width)
-        qkv_full = lax.all_gather(qkv_part, both, axis_index_groups=across_dp, tiled=False)
-        qkv_full = qkv_full.reshape(n_dp, width, part_width)
+        ring = [qkv_part] + [shift_z(qkv_part, -t) for t in range(1, planes)]
+        qkv_ring = jnp.concatenate(ring + ring[: planes - 1], axis=0)
+        qkv_mine = lax.dynamic_slice_in_dim(
+            qkv_ring, ((planes - p) % planes) * GROUP * shard, width, 0
+        )
+        qkv_full = collect_dp(qkv_mine, c)
 
         x_in = inputs.reshape(tokens, width).astype(f32)
         normed_one, inverse_one = normalize(x_in)
-        low_one = gather_w(after(normed_one.astype(bf16), qkv_part))
-
-        out_part = after(pick(w_out, c, n_dp, 1), low_one)
+        low_one = gather_w(normed_one.astype(bf16))
+
         out_part = lax.ppermute(
-            out_part, "seq", [(i, GROUP * (i % planes) + i // planes) for i in range(n_seq)]
+            pick(w_out, c, n_dp, 1),
+            "seq",
+            [(i, GROUP * (i % planes) + i // planes) for i in range(n_seq)],
         )
         out_full = lax.all_gather(out_part, both, axis_index_groups=across_dp, tiled=False)
         out_full = out_full.reshape(n_dp, planes * shard, width // n_dp)
 
         piece = shard // halves
         gate_up = jnp.where(c // halves == 0, scaled(w_gate, gain_two), scaled(w_up, gain_two))
-        gate_up = after(pick(gate_up, c % halves, halves, 0), low_one, qkv_full)
+        gate_up = after(pick(gate_up, c % halves, halves, 0), low_one, qkv_mine)
         gate_up_part = jnp.zeros((planes, piece, ff_block), bf16)
         for t in range(planes):
             block = pick(gate_up, (p + t) % planes, planes, 1)
@@ -363,7 +368,7 @@
         up_full = gate_up_full[1]
 
         down_full = lax.all_gather(
-            after(pick(w_down, c, n_dp, 1), gate_up_part), both, axis_index_groups=in_plane_dp, tiled=False
+            pick(w_down, c, n_dp, 1), both, axis_index_groups=in_plane_dp, tiled=False
         )
         down_full = down_full.reshape(n_dp, ff_block, width // n_dp)
 
@@ -398,7 +403,7 @@
         k = rotate(kv[:, None, :HEAD_DIM], cosine, sine)[:, 0]
         kv_low = jnp.concatenate([k, kv[:, HEAD_DIM:]], axis=1).astype(bf16)
         kv_all = jnp.stack(gather_z(kv_low))
-        grad_y_all = jnp.concatenate(gather_z(after(grad_y.astype(bf16), kv_all)), axis=0)
+        grad_y_all = jnp.concatenate(gather_z(after(grad_y.astype(bf16), kv_all, gate_up_part)), axis=0)
         kk = jnp.concatenate([kv_all[..., :HEAD_DIM]] * 2, axis=-1)
         vv = jnp.concatenate([kv_all[..., HEAD_DIM:]] * 2, axis=-1)
 
@@ -430,7 +435,8 @@
         x_mid = x_in + branch
 
         normed_two, inverse_two = normalize(x_mid)
-        low_two = jnp.concatenate(gather_z(reorder(normed_two.astype(bf16))), axis=0)
+        low_two = reorder(normed_two.astype(bf16))
+        low_two = jnp.concatenate(gather_z(after(low_two, grad_y_all)), axis=0)
         gate = dot(low_two, gate_full)
         up_part = dot(low_two, up_full)
         sigmoid_gate = 1.0 / (1.0 + jnp.exp(-gate))
@@ -478,10 +484,11 @@
 
         mixed = after(mixed, inner_two)
         mixed = scatter_z([mixed[t * tokens : (t + 1) * tokens] for t in range(planes)])
-        down_sum = lax.psum_scatter(down_sum, "seq", axis_index_groups=in_plane, tiled=True)
-        gate_up_sum = lax.psum_scatter(
-            gate_up_sum, "seq", axis_index_groups=in_plane, tiled=True
-        ).reshape(planes, piece, ff_block)
+        gate_up_sum = lax.psum_scatter(gate_up_sum, "seq", axis_index_groups=in_plane, tiled=True)
+        down_sum = lax.psum_scatter(
+            after(down_sum, gate_up_sum), "seq", axis_index_groups=in_plane, tiled=True
+        )
+        gate_up_sum = gate_up_sum.reshape(planes, piece, ff_block)
 
         grad_branch = gather_w(grad_x_mid.astype(bf16))
         grad_o = functools.reduce(
@@ -490,7 +497,9 @@
         ).astype(bf16)
 
         out_part_sum = dot(gather_dp(o), exchange_dp(grad_branch, c, 1), ((0,), (0,))).astype(bf16)
-        out_sum = lax.psum_scatter(out_part_sum, "seq", axis_index_groups=across, tiled=True)
+        out_sum = lax.psum_scatter(
+            after(out_part_sum, down_sum), "seq", axis_index_groups=across, tiled=True
+        )
         out_sum = lax.ppermute(
             out_sum, "seq", [(GROUP * (i % planes) + i // planes, i) for i in range(n_seq)]
         )
@@ -540,7 +549,9 @@
             exchange_dp(after(jnp.concatenate(pre, axis=1), grad_low_one), c, 1),
             ((0,), (0,)),
         ).astype(bf16)
-        qkv_sum = lax.psum_scatter(qkv_sum, "seq", axis_index_groups=across, tiled=True)
+        qkv_sum = lax.psum_scatter(
+            after(qkv_sum, out_sum), "seq", axis_index_groups=across, tiled=True
+        )
         qkv_sum = qkv_sum.reshape(GROUP, shard, part_width)
         qkv_sum = lax.all_to_all(qkv_sum, "seq", 0, 0, axis_index_groups=in_plane, tiled=True)
         qkv_sum = collect_dp(qkv_sum, c)

time: 840 us -> 691 us (0.82)
  waiting for transfers between devices: 410 us -> 291 us
  starting transfers between devices: 148 us -> 135 us
  blocking collectives: 9.61 us -> 0 us
    reduce_scatter x1, waiting for transfers between devices: 65.9 us -> 0.01 us  [body(): lax.psum_scatter(gate_up_sum, 'seq', axis_index_groups=in_plane, tiled=True)]
    ppermute x17, waiting for transfers between devices: 82.5 us -> 28.7 us  [xor_w(): return lax.ppermute(value, 'seq', [(s, s ^ j) for s in range(n_seq)])]
    ppermute x24 -> x27, starting transfers between devices: 96.4 us -> 71.5 us  [shift_z(): lax.ppermute(value, 'seq', [(s, (s + GROUP * t) % n_seq) for s in range(n...]
    ppermute x17, starting transfers between devices: 15.4 us -> 36.9 us  [xor_w(): return lax.ppermute(value, 'seq', [(s, s ^ j) for s in range(n_seq)])]
    ppermute x12 -> x13, starting transfers between devices: 26.6 us -> 14.4 us  [shift_dp(): return lax.ppermute(value, 'dp', [(c, (c + t) % n_dp) for c in range(n_dp)])]
    unnamed x192 -> x201, local copies, waits for them, and re-layouts: 47.5 us -> 35.8 us
    all_to_all x1 -> x0, blocking collectives: 9.61 us -> none  [body(): lax.all_to_all(jnp.transpose(qkv_part, (1, 0, 2)), 'seq', 0, 0, axis_inde...]
    ppermute x24 -> x27, waiting for transfers between devices: 219 us -> 220 us  [shift_z(): lax.ppermute(value, 'seq', [(s, (s + GROUP * t) % n_seq) for s in range(n...]
  transfers between devices with their start and end apart: 64 -> 68, of which waited for: 30 -> 26; matrix products, arithmetic and copies ran while one was open for 22% -> 24% of each run, Pallas kernels for 2% -> 3%
where the time goes in v3:
time: 691 us; the launch traced here: 681 us
  waiting for transfers between devices  291 us (42%)
  starting transfers between devices  135 us (20%)
  local copies, waits for them, and re-layouts  91.2 us (13%)
  matrix products  74.2 us (11%)
  other arithmetic  55.5 us (8%)
  Pallas kernels  17.9 us (3%)
  between operations  16.3 us (2%)
    ppermute x27, waiting for transfers between devices, shift_z(): lax.ppermute(value, 'seq', [(s, (s + GROUP * t) % n_seq) for s in range(n...  220 us
    dot_general x20, matrix products, dot(): lax.dot_general(left, right, (contract, ((), ())), preferred_element_type...  74.2 us
    ppermute x27, starting transfers between devices, shift_z(): lax.ppermute(value, 'seq', [(s, (s + GROUP * t) % n_seq) for s in range(n...  71.5 us
    ppermute x17, starting transfers between devices, xor_w(): return lax.ppermute(value, 'seq', [(s, s ^ j) for s in range(n_seq)])  36.9 us
    unnamed x201, local copies, waits for them, and re-layouts  35.8 us
    reduce_scatter x1, waiting for transfers between devices, body(): lax.psum_scatter(after(qkv_sum, out_sum), 'seq', axis_index_groups=across...  33.2 us
    ppermute x17, waiting for transfers between devices, xor_w(): return lax.ppermute(value, 'seq', [(s, s ^ j) for s in range(n_seq)])  28.7 us
    ppermute x13, starting transfers between devices, shift_dp(): return lax.ppermute(value, 'dp', [(c, (c + t) % n_dp) for c in range(n_dp)])  14.4 us
  transfers between devices with their start and end apart: 68, of which 26 were waited for; matrix products, arithmetic and copies ran while one was open for 24% of the time, Pallas kernels for 3%

profile of v3, /device:TPU:1, one launch (start us, length us, event | category | flops | bytes accessed | tf_op | source)
XLA Modules:
  0.0 681.2 jit_solution(5474267342630552454)
XLA Ops:
  12.2 18.0 %collective-permute-start.1 = (bf16[128,2048]{1,0:T(8,128)(2,1)}, bf16[128,2048]{1,0:T(8,128)(2,1)}, u32[]{:S(2)}, u32[]{:S(2)}) collective-permute-start(bf16[128,2048]{1,0:T(8,128)(2,1)} %get-tuple-element.68), channel_id=1, source_target_pairs={{0,2},{1,3},{2,0},{3,1},{4,6},{5,7},{6,4},{7,5},{8,10},{9,11},{10,... | collective-permute-start | bytes 1572872 | tf_op jit(solution)/shard_map/ppermute | solution.py:253
  64.3 13.8 %collective-permute-done.4 = bf16[512,320]{0,1:T(8,128)(2,1)S(1)} collective-permute-done((bf16[512,320]{0,1:T(8,128)(2,1)S(1)}, bf16[512,320]{0,1:T(8,128)(2,1)S(1)}, u32[]{:S(2)}, u32[]{:S(2)}) %collective-permute-start.4) | collective-permute-done | bytes 327712 | tf_op jit(solution)/shard_map/ppermute | solution.py:256
  85.7 7.4 %collective-permute-start.18 = (bf16[128,1408]{1,0:T(8,128)(2,1)}, bf16[128,1408]{1,0:T(8,128)(2,1)}, u32[]{:S(2)}, u32[]{:S(2)}) collective-permute-start(bf16[128,1408]{1,0:T(8,128)(2,1)} %get-tuple-element.116), channel_id=1, source_target_pairs={{0,4},{1,5},{2,6},{3,7},{4,8},{5,9},{6,10},{7,11},{8,12},{9,13},{1... | collective-permute-start | bytes 1081352 | tf_op jit(solution)/shard_map/ppermute | solution.py:256
  96.2 5.0 collective-permute-done.18
  102.9 22.4 %collective-permute-done.19 = bf16[128,1408]{1,0:T(8,128)(2,1)S(1)} collective-permute-done((bf16[128,1408]{1,0:T(8,128)(2,1)}, bf16[128,1408]{1,0:T(8,128)(2,1)S(1)}, u32[]{:S(2)}, u32[]{:S(2)}) %collective-permute-start.19) | collective-permute-done | bytes 360480 | tf_op jit(solution)/shard_map/ppermute | solution.py:256
  171.4 7.6 %attend.1 = (bf16[512,512]{1,0:T(8,128)(2,1)}, f32[4,8,1024]{2,1,0:T(8,128)}) custom-call(s32[1]{0:T(128)} %bitcast.1.seen_ref, bf16[512,512]{1,0:T(8,128)(2,1)} %multiply_convert_fusion.3.q_ref, bf16[4,512,128]{2,1,0:T(8,128)(2,1)} %get-tuple-element.181.kk_ref, bf16[4,512,128]{2,1,0:T(8,128)(2,1)} %get-tuple-element.182.vv_ref, ...), custom_call_target="tpu_custom_call" | custom-call | tf_op jit(solution)/shard_map/attend/pallas_call | solution.py:136
  186.5 16.1 %collective-permute-done.21 = bf16[128,2048]{1,0:T(8,128)(2,1)} collective-permute-done((bf16[128,2048]{1,0:T(8,128)(2,1)}, bf16[128,2048]{1,0:T(8,128)(2,1)}, u32[]{:S(2)}, u32[]{:S(2)}) %collective-permute-start.21) | collective-permute-done | bytes 524320 | tf_op jit(solution)/shard_map/ppermute | solution.py:256
  205.7 7.6 %collective-permute-done.22 = bf16[128,2048]{1,0:T(8,128)(2,1)S(1)} collective-permute-done((bf16[128,2048]{1,0:T(8,128)(2,1)}, bf16[128,2048]{1,0:T(8,128)(2,1)S(1)}, u32[]{:S(2)}, u32[]{:S(2)}) %collective-permute-start.22) | collective-permute-done | bytes 524320 | tf_op jit(solution)/shard_map/ppermute | solution.py:256
  215.3 11.7 %collective-permute-done.16 = bf16[128,2048]{1,0:T(8,128)(2,1)S(1)} collective-permute-done((bf16[128,2048]{1,0:T(8,128)(2,1)S(1)}, bf16[128,2048]{1,0:T(8,128)(2,1)S(1)}, u32[]{:S(2)}, u32[]{:S(2)}) %collective-permute-start.16) | collective-permute-done | bytes 524320 | tf_op jit(solution)/shard_map/ppermute | solution.py:253
  229.0 5.3 collective-permute-start.25
  237.9 5.0 collective-permute-done.24
  243.9 22.4 %collective-permute-done.25 = bf16[128,2048]{1,0:T(8,128)(2,1)S(1)} collective-permute-done((bf16[128,2048]{1,0:T(8,128)(2,1)S(1)}, bf16[128,2048]{1,0:T(8,128)(2,1)S(1)}, u32[]{:S(2)}, u32[]{:S(2)}) %collective-permute-start.25) | collective-permute-done | bytes 524320 | tf_op jit(solution)/shard_map/ppermute | solution.py:256
  277.9 5.5 fusion.7
  283.4 10.1 %fusion.100 = (bf16[16,128,1408]{2,1,0:T(8,128)(2,1)}, bf16[16,128,1408]{2,1,0:T(8,128)(2,1)}) fusion(bf16[32,128,1408]{2,1,0:T(8,128)(2,1)} %all-gather.9.cloned.1.call-done), kind=kLoop, calls=%fused_computation.337 | loop fusion | bytes 23068672 | tf_op jit(solution)/shard_map/slice | solution.py:367
  293.6 6.5 fusion.107
  300.2 8.2 %multiply_convert_fusion.2 = (bf16[512,1408]{1,0:T(8,128)(2,1)}, f32[512,1408]{1,0:T(8,128)}) fusion(f32[512,1408]{1,0:T(8,128)S(1)} %fusion.107, bf16[512,2048]{1,0:T(8,128)(2,1)} %get-tuple-element.141, bf16[2048,1408]{1,0:T(8,128)(2,1)S(1)} %bitcast.165), kind=kOutput, calls=%fused_computation.21 | convolution fusion | flops 2957115392 | bytes 15073280 | tf_op jit(solution)/shard_map/dot_general | solution.py:26
  308.4 5.5 broadcast_select_fusion.3
  324.8 8.8 %convolution_convert_fusion = bf16[2048,1408]{1,0:T(8,128)(2,1)} fusion(bf16[1024,2048]{1,0:T(8,128)(2,1)S(1)} %copy-done.44, bf16[1024,1408]{1,0:T(8,128)(2,1)S(1)} %pad_maximum_fusion), kind=kOutput, calls=%fused_computation | convolution fusion | flops 5908463616 | bytes 12845056 | tf_op jit(solution)/shard_map/dot_general | solution.py:26
  336.5 16.4 %collective-permute-start.27 = (bf16[128,2048]{1,0:T(8,128)(2,1)S(1)}, bf16[128,2048]{1,0:T(8,128)(2,1)S(1)}, u32[]{:S(2)}, u32[]{:S(2)}) collective-permute-start(bf16[128,2048]{1,0:T(8,128)(2,1)S(1)} %get-tuple-element.91), channel_id=1, source_target_pairs={{0,12},{1,13},{2,14},{3,15},{4,0},{5,1},{6,2},{7,3},{8,4},{9,5},{1... | collective-permute-start | bytes 1572872 | tf_op jit(solution)/shard_map/ppermute | solution.py:256
  365.7 10.6 %collective-permute-done.29 = bf16[128,2048]{1,0:T(8,128)(2,1)S(1)} collective-permute-done((bf16[128,2048]{1,0:T(8,128)(2,1)S(1)}, bf16[128,2048]{1,0:T(8,128)(2,1)S(1)}, u32[]{:S(2)}, u32[]{:S(2)}) %collective-permute-start.29) | collective-permute-done | bytes 524320 | tf_op jit(solution)/shard_map/ppermute | solution.py:256
  376.4 20.5 %collective-permute-done.28 = bf16[128,2048]{1,0:T(8,128)(2,1)S(1)} collective-permute-done((bf16[128,2048]{1,0:T(8,128)(2,1)S(1)}, bf16[128,2048]{1,0:T(8,128)(2,1)S(1)}, u32[]{:S(2)}, u32[]{:S(2)}) %collective-permute-start.28) | collective-permute-done | bytes 524320 | tf_op jit(solution)/shard_map/ppermute | solution.py:256
  407.1 11.5 %collective-permute-done.34 = bf16[128,2048]{1,0:T(8,128)(2,1)S(1)} collective-permute-done((bf16[128,2048]{1,0:T(8,128)(2,1)S(1)}, bf16[128,2048]{1,0:T(8,128)(2,1)S(1)}, u32[]{:S(2)}, u32[]{:S(2)}) %collective-permute-start.34) | collective-permute-done | bytes 524320 | tf_op jit(solution)/shard_map/ppermute | solution.py:256
  418.6 10.2 %collective-permute-done.36 = bf16[128,2048]{1,0:T(8,128)(2,1)S(1)} collective-permute-done((bf16[128,2048]{1,0:T(8,128)(2,1)S(1)}, bf16[128,2048]{1,0:T(8,128)(2,1)S(1)}, u32[]{:S(2)}, u32[]{:S(2)}) %collective-permute-start.36) | collective-permute-done | bytes 524320 | tf_op jit(solution)/shard_map/ppermute | solution.py:256
  428.8 20.5 %collective-permute-done.35 = bf16[128,2048]{1,0:T(8,128)(2,1)S(1)} collective-permute-done((bf16[128,2048]{1,0:T(8,128)(2,1)S(1)}, bf16[128,2048]{1,0:T(8,128)(2,1)S(1)}, u32[]{:S(2)}, u32[]{:S(2)}) %collective-permute-start.35) | collective-permute-done | bytes 524320 | tf_op jit(solution)/shard_map/ppermute | solution.py:256
  454.5 10.0 %collective-permute-done.38 = bf16[128,2048]{1,0:T(8,128)(2,1)S(1)} collective-permute-done((bf16[128,2048]{1,0:T(8,128)(2,1)S(1)}, bf16[128,2048]{1,0:T(8,128)(2,1)S(1)}, u32[]{:S(2)}, u32[]{:S(2)}) %collective-permute-start.38) | collective-permute-done | bytes 524320 | tf_op jit(solution)/shard_map/ppermute | solution.py:253
  466.1 5.2 collective-permute-done.39
  487.4 10.4 %attend_back.1 = (f32[512,512]{1,0:T(8,128)}, f32[4,512,128]{2,1,0:T(8,128)}, f32[4,512,128]{2,1,0:T(8,128)}) custom-call(s32[1]{0:T(128)} %bitcast.1.seen_ref, bf16[512,512]{1,0:T(8,128)(2,1)} %multiply_convert_fusion.3.q_ref, bf16[512,512]{1,0:T(8,128)(2,1)} %bitcast.180, bf16[512,512]{1,0:T(8,128)(2,1)} %get-tuple-element.28.o_ref, ...), custom_call_target="tpu_custom_call" | custom-call | tf_op jit(solution)/shard_map/attend_back/pallas_call | solution.py:166
  501.8 22.1 %collective-permute-start.43 = (bf16[512,128]{1,0:T(8,128)(2,1)}, bf16[512,128]{1,0:T(8,128)(2,1)}, u32[]{:S(2)}, u32[]{:S(2)}) collective-permute-start(bf16[512,128]{1,0:T(8,128)(2,1)} %get-tuple-element.119), channel_id=1, source_target_pairs={{0,12},{1,13},{2,14},{3,15},{4,0},{5,1},{6,2},{7,3},{8,4},{9,5},{1... | collective-permute-start | bytes 393224 | tf_op jit(solution)/shard_map/ppermute | solution.py:256
  556.6 32.7 %collective-permute-done.55 = bf16[128,1408]{1,0:T(8,128)(2,1)S(1)} collective-permute-done((bf16[128,1408]{1,0:T(8,128)(2,1)}, bf16[128,1408]{1,0:T(8,128)(2,1)S(1)}, u32[]{:S(2)}, u32[]{:S(2)}) %collective-permute-start.55) | collective-permute-done | bytes 360480 | tf_op jit(solution)/shard_map/ppermute | solution.py:256
  589.7 9.0 %collective-permute-done.56 = bf16[128,1408]{1,0:T(8,128)(2,1)S(1)} collective-permute-done((bf16[128,1408]{1,0:T(8,128)(2,1)S(1)}, bf16[128,1408]{1,0:T(8,128)(2,1)S(1)}, u32[]{:S(2)}, u32[]{:S(2)}) %collective-permute-start.56) | collective-permute-done | bytes 360480 | tf_op jit(solution)/shard_map/ppermute | solution.py:256
  616.2 5.5 convert_multiply_fusion
  621.9 33.2 %reduce-scatter.11.cloned.1.call-done = bf16[512,320]{0,1:T(8,128)(2,1)} async-done(((bf16[2048,320]{0,1:T(8,128)(2,1)}), bf16[512,320]{0,1:T(8,128)(2,1)}) %reduce-scatter.11.cloned.1.call-update) | async-done | bytes 327696 | tf_op jit(solution)/shard_map/reduce_scatter | solution.py:552
  (460 shorter events, 260.3 us)
Async XLA Ops:
  7.2 173.7 %all-gather.7.cloned.1.call-start = ((), (), s32[]{:S(2)}) async-start(), calls=%async_computation.10 | async-start | bytes 2359296 | tf_op jit(solution)/shard_map/all_gather | solution.py:354
  9.8 268.1 %all-gather.11.cloned.1.call-start = ((), (), s32[]{:S(2)}) async-start(), calls=%async_computation.12 | async-start | bytes 6488064 | tf_op jit(solution)/shard_map/all_gather | solution.py:370
  12.2 44.4 %collective-permute-start.1 = (bf16[128,2048]{1,0:T(8,128)(2,1)}, bf16[128,2048]{1,0:T(8,128)(2,1)}, u32[]{:S(2)}, u32[]{:S(2)}) collective-permute-start(bf16[128,2048]{1,0:T(8,128)(2,1)} %get-tuple-element.68), channel_id=1, source_target_pairs={{0,2},{1,3},{2,0},{3,1},{4,6},{5,7},{6,4},{7,5},{8,10},{9,11},{10,... | collective-permute-start | bytes 1572872 | tf_op jit(solution)/shard_map/ppermute | solution.py:253
  30.1 28.2 %collective-permute-start = (bf16[128,2048]{1,0:T(8,128)(2,1)}, bf16[128,2048]{1,0:T(8,128)(2,1)}, u32[]{:S(2)}, u32[]{:S(2)}) collective-permute-start(bf16[128,2048]{1,0:T(8,128)(2,1)} %get-tuple-element.68), channel_id=1, source_target_pairs={{0,1},{1,0},{2,3},{3,2},{4,5},{5,4},{6,7},{7,6},{8,9},{9,8},{10,11... | collective-permute-start | bytes 1572872 | tf_op jit(solution)/shard_map/ppermute | solution.py:253
  44.3 239.2 %all-gather.9.cloned.1.call-start = ((), (), s32[]{:S(2)}) async-start(), calls=%async_computation.11 | async-start | bytes 12976128 | tf_op jit(solution)/shard_map/all_gather | solution.py:365
  50.7 31.0 %collective-permute-start.6 = (bf16[512,320]{0,1:T(8,128)(2,1)S(1)}, bf16[512,320]{0,1:T(8,128)(2,1)S(1)}, u32[]{:S(2)}, u32[]{:S(2)}) collective-permute-start(bf16[512,320]{0,1:T(8,128)(2,1)S(1)} %copy_bitcast_fusion), channel_id=1, source_target_pairs={{0,4},{1,5},{2,6},{3,7},{4,8},{5,9},{6,10},{7,11},{8,12},{9,13},{1... | collective-permute-start | bytes 983048 | tf_op jit(solution)/shard_map/ppermute | solution.py:256
  50.8 30.9 %collective-permute-start.5 = (bf16[512,320]{0,1:T(8,128)(2,1)S(1)}, bf16[512,320]{0,1:T(8,128)(2,1)S(1)}, u32[]{:S(2)}, u32[]{:S(2)}) collective-permute-start(bf16[512,320]{0,1:T(8,128)(2,1)S(1)} %copy_bitcast_fusion), channel_id=1, source_target_pairs={{0,8},{1,9},{2,10},{3,11},{4,12},{5,13},{6,14},{7,15},{8,0},{9,1},... | collective-permute-start | bytes 983048 | tf_op jit(solution)/shard_map/ppermute | solution.py:256
  93.1 33.1 %collective-permute-start.20 = (bf16[128,1408]{1,0:T(8,128)(2,1)}, bf16[128,1408]{1,0:T(8,128)(2,1)S(1)}, u32[]{:S(2)}, u32[]{:S(2)}) collective-permute-start(bf16[128,1408]{1,0:T(8,128)(2,1)} %get-tuple-element.114), channel_id=1, source_target_pairs={{0,12},{1,13},{2,14},{3,15},{4,0},{5,1},{6,2},{7,3},{8,4},{9,5},{1... | collective-permute-start | bytes 1081352 | tf_op jit(solution)/shard_map/ppermute | solution.py:256
  93.1 32.3 %collective-permute-start.19 = (bf16[128,1408]{1,0:T(8,128)(2,1)}, bf16[128,1408]{1,0:T(8,128)(2,1)S(1)}, u32[]{:S(2)}, u32[]{:S(2)}) collective-permute-start(bf16[128,1408]{1,0:T(8,128)(2,1)} %get-tuple-element.115), channel_id=1, source_target_pairs={{0,8},{1,9},{2,10},{3,11},{4,12},{5,13},{6,14},{7,15},{8,0},{9,1},... | collective-permute-start | bytes 1081352 | tf_op jit(solution)/shard_map/ppermute | solution.py:256
  126.9 350.2 %reduce-scatter.5.cloned.1.call-start = ((), (), s32[]{:S(2)}) async-start(), calls=%async_computation.6 | async-start | bytes 7208960 | tf_op jit(solution)/shard_map/reduce_scatter | solution.py:487
  165.8 47.6 %collective-permute-start.23 = (bf16[128,2048]{1,0:T(8,128)(2,1)}, bf16[128,2048]{1,0:T(8,128)(2,1)S(1)}, u32[]{:S(2)}, u32[]{:S(2)}) collective-permute-start(bf16[128,2048]{1,0:T(8,128)(2,1)} %bitcast_convert_fusion), channel_id=1, source_target_pairs={{0,12},{1,13},{2,14},{3,15},{4,0},{5,1},{6,2},{7,3},{8,4},{9,5},{1... | collective-permute-start | bytes 1572872 | tf_op jit(solution)/shard_map/ppermute | solution.py:256
  168.9 44.4 %collective-permute-start.22 = (bf16[128,2048]{1,0:T(8,128)(2,1)}, bf16[128,2048]{1,0:T(8,128)(2,1)S(1)}, u32[]{:S(2)}, u32[]{:S(2)}) collective-permute-start(bf16[128,2048]{1,0:T(8,128)(2,1)} %bitcast_convert_fusion), channel_id=1, source_target_pairs={{0,8},{1,9},{2,10},{3,11},{4,12},{5,13},{6,14},{7,15},{8,0},{9,1},... | collective-permute-start | bytes 1572872 | tf_op jit(solution)/shard_map/ppermute | solution.py:256
  169.3 33.3 %collective-permute-start.21 = (bf16[128,2048]{1,0:T(8,128)(2,1)}, bf16[128,2048]{1,0:T(8,128)(2,1)}, u32[]{:S(2)}, u32[]{:S(2)}) collective-permute-start(bf16[128,2048]{1,0:T(8,128)(2,1)} %bitcast_convert_fusion), channel_id=1, source_target_pairs={{0,4},{1,5},{2,6},{3,7},{4,8},{5,9},{6,10},{7,11},{8,12},{9,13},{1... | collective-permute-start | bytes 1572872 | tf_op jit(solution)/shard_map/ppermute | solution.py:256
  184.0 29.4 %collective-permute-start.15 = (bf16[128,2048]{1,0:T(8,128)(2,1)S(1)}, bf16[128,2048]{1,0:T(8,128)(2,1)S(1)}, u32[]{:S(2)}, u32[]{:S(2)}) collective-permute-start(bf16[128,2048]{1,0:T(8,128)(2,1)S(1)} %get-tuple-element.94), channel_id=1, source_target_pairs={{0,1},{1,0},{2,3},{3,2},{4,5},{5,4},{6,7},{7,6},{8,9},{9,8},{10,11... | collective-permute-start | bytes 1572872 | tf_op jit(solution)/shard_map/ppermute | solution.py:253
  185.2 30.0 %collective-permute-start.17 = (bf16[128,2048]{1,0:T(8,128)(2,1)S(1)}, bf16[128,2048]{1,0:T(8,128)(2,1)S(1)}, u32[]{:S(2)}, u32[]{:S(2)}) collective-permute-start(bf16[128,2048]{1,0:T(8,128)(2,1)S(1)} %get-tuple-element.95), channel_id=1, source_target_pairs={{0,3},{1,2},{2,1},{3,0},{4,7},{5,6},{6,5},{7,4},{8,11},{9,10},{10,... | collective-permute-start | bytes 1572872 | tf_op jit(solution)/shard_map/ppermute | solution.py:253
  229.0 37.2 %collective-permute-start.25 = (bf16[128,2048]{1,0:T(8,128)(2,1)S(1)}, bf16[128,2048]{1,0:T(8,128)(2,1)S(1)}, u32[]{:S(2)}, u32[]{:S(2)}) collective-permute-start(bf16[128,2048]{1,0:T(8,128)(2,1)S(1)} %constant_dynamic-update-slice_fusion.12), channel_id=1, source_target_pairs={{0,8},{1,9},{2,10},{3,11},{4,12},{5,13},{6,14},{7,15},{8,0},{9,1},... | collective-permute-start | bytes 1572872 | tf_op jit(solution)/shard_map/ppermute | solution.py:256
  234.3 32.9 %collective-permute-start.26 = (bf16[128,2048]{1,0:T(8,128)(2,1)S(1)}, bf16[128,2048]{1,0:T(8,128)(2,1)S(1)}, u32[]{:S(2)}, u32[]{:S(2)}) collective-permute-start(bf16[128,2048]{1,0:T(8,128)(2,1)S(1)} %constant_dynamic-update-slice_fusion.12), channel_id=1, source_target_pairs={{0,12},{1,13},{2,14},{3,15},{4,0},{5,1},{6,2},{7,3},{8,4},{9,5},{1... | collective-permute-start | bytes 1572872 | tf_op jit(solution)/shard_map/ppermute | solution.py:256
  333.6 213.1 %reduce-scatter.7.cloned.1.call-start = ((), (), s32[]{:S(2)}) async-start(), calls=%async_computation.7 | async-start | bytes 3604480 | tf_op jit(solution)/shard_map/reduce_scatter | solution.py:488
  335.6 62.5 %collective-permute-start.31 = (bf16[512,1024]{1,0:T(8,128)(2,1)S(1)}, bf16[512,1024]{1,0:T(8,128)(2,1)S(1)}, u32[]{:S(2)}, u32[]{:S(2)}) collective-permute-start(bf16[512,1024]{1,0:T(8,128)(2,1)S(1)} %get-tuple-element.90), channel_id=1, source_target_pairs={{0,16},{16,0},{1,17},{17,1},{2,18},{18,2},{3,19},{19,3},{4,20},{20... | collective-permute-start | bytes 3145736 | tf_op jit(solution)/shard_map/ppermute | solution.py:259
  335.8 62.4 %collective-permute-start.30 = (bf16[512,1408]{1,0:T(8,128)(2,1)S(1)}, bf16[512,1408]{1,0:T(8,128)(2,1)S(1)}, u32[]{:S(2)}, u32[]{:S(2)}) collective-permute-start(bf16[512,1408]{1,0:T(8,128)(2,1)S(1)} %copy-done.54), channel_id=1, source_target_pairs={{0,16},{16,0},{1,17},{17,1},{2,18},{18,2},{3,19},{19,3},{4,20},{20... | collective-permute-start | bytes 4325384 | tf_op jit(solution)/shard_map/ppermute | solution.py:259
  352.9 43.9 %collective-permute-start.28 = (bf16[128,2048]{1,0:T(8,128)(2,1)S(1)}, bf16[128,2048]{1,0:T(8,128)(2,1)S(1)}, u32[]{:S(2)}, u32[]{:S(2)}) collective-permute-start(bf16[128,2048]{1,0:T(8,128)(2,1)S(1)} %get-tuple-element.93), channel_id=1, source_target_pairs={{0,8},{1,9},{2,10},{3,11},{4,12},{5,13},{6,14},{7,15},{8,0},{9,1},... | collective-permute-start | bytes 1572872 | tf_op jit(solution)/shard_map/ppermute | solution.py:256
  364.1 113.3 %collective-permute-start.49 = (bf16[512,2048]{1,0:T(8,128)(2,1)}, bf16[512,2048]{1,0:T(8,128)(2,1)}, u32[]{:S(2)}, u32[]{:S(2)}) collective-permute-start(bf16[512,2048]{1,0:T(8,128)(2,1)} %get-tuple-element.159), channel_id=1, source_target_pairs={{0,16},{16,0},{1,17},{17,1},{2,18},{18,2},{3,19},{19,3},{4,20},{20... | collective-permute-start | bytes 6291464 | tf_op jit(solution)/shard_map/ppermute | solution.py:259
  406.5 42.8 %collective-permute-start.35 = (bf16[128,2048]{1,0:T(8,128)(2,1)S(1)}, bf16[128,2048]{1,0:T(8,128)(2,1)S(1)}, u32[]{:S(2)}, u32[]{:S(2)}) collective-permute-start(bf16[128,2048]{1,0:T(8,128)(2,1)S(1)} %get-tuple-element.88), channel_id=1, source_target_pairs={{0,8},{1,9},{2,10},{3,11},{4,12},{5,13},{6,14},{7,15},{8,0},{9,1},... | collective-permute-start | bytes 1572872 | tf_op jit(solution)/shard_map/ppermute | solution.py:256
  477.2 125.8 %reduce-scatter.9.cloned.1.call-start = ((), (), s32[]{:S(2)}) async-start(), calls=%async_computation.8 | async-start | bytes 1310720 | tf_op jit(solution)/shard_map/reduce_scatter | solution.py:500
  501.8 31.2 %collective-permute-start.43 = (bf16[512,128]{1,0:T(8,128)(2,1)}, bf16[512,128]{1,0:T(8,128)(2,1)}, u32[]{:S(2)}, u32[]{:S(2)}) collective-permute-start(bf16[512,128]{1,0:T(8,128)(2,1)} %get-tuple-element.119), channel_id=1, source_target_pairs={{0,12},{1,13},{2,14},{3,15},{4,0},{5,1},{6,2},{7,3},{8,4},{9,5},{1... | collective-permute-start | bytes 393224 | tf_op jit(solution)/shard_map/ppermute | solution.py:256
  546.8 108.2 %reduce-scatter.11.cloned.1.call-start = ((), (), s32[]{:S(2)}) async-start(), calls=%async_computation.9 | async-start | bytes 1638400 | tf_op jit(solution)/shard_map/reduce_scatter | solution.py:552
  547.5 52.8 %collective-permute-start.50 = (bf16[512,320]{1,0:T(8,128)(2,1)S(1)}, bf16[512,320]{1,0:T(8,128)(2,1)S(1)}, u32[]{:S(2)}, u32[]{:S(2)}) collective-permute-start(bf16[512,320]{1,0:T(8,128)(2,1)S(1)} %get-tuple-element.129), channel_id=1, source_target_pairs={{0,16},{16,0},{1,17},{17,1},{2,18},{18,2},{3,19},{19,3},{4,20},{20... | collective-permute-start | bytes 983048 | tf_op jit(solution)/shard_map/ppermute | solution.py:259
  549.1 57.8 %collective-permute-start.46 = (bf16[128,2048]{1,0:T(8,128)(2,1)}, bf16[128,2048]{1,0:T(8,128)(2,1)S(1)}, u32[]{:S(2)}, u32[]{:S(2)}) collective-permute-start(bf16[128,2048]{1,0:T(8,128)(2,1)} %get-tuple-element.81), channel_id=1, source_target_pairs={{0,1},{1,0},{2,3},{3,2},{4,5},{5,4},{6,7},{7,6},{8,9},{9,8},{10,11... | collective-permute-start | bytes 1572872 | tf_op jit(solution)/shard_map/ppermute | solution.py:253
  549.4 57.5 %collective-permute-start.48 = (bf16[128,2048]{1,0:T(8,128)(2,1)}, bf16[128,2048]{1,0:T(8,128)(2,1)}, u32[]{:S(2)}, u32[]{:S(2)}) collective-permute-start(bf16[128,2048]{1,0:T(8,128)(2,1)} %get-tuple-element.82), channel_id=1, source_target_pairs={{0,3},{1,2},{2,1},{3,0},{4,7},{5,6},{6,5},{7,4},{8,11},{9,10},{10,... | collective-permute-start | bytes 1572872 | tf_op jit(solution)/shard_map/ppermute | solution.py:253
  551.0 56.0 %collective-permute-start.47 = (bf16[128,2048]{1,0:T(8,128)(2,1)}, bf16[128,2048]{1,0:T(8,128)(2,1)}, u32[]{:S(2)}, u32[]{:S(2)}) collective-permute-start(bf16[128,2048]{1,0:T(8,128)(2,1)} %get-tuple-element.83), channel_id=1, source_target_pairs={{0,2},{1,3},{2,0},{3,1},{4,6},{5,7},{6,4},{7,5},{8,10},{9,11},{10,... | collective-permute-start | bytes 1572872 | tf_op jit(solution)/shard_map/ppermute | solution.py:253
  555.6 33.7 %collective-permute-start.55 = (bf16[128,1408]{1,0:T(8,128)(2,1)}, bf16[128,1408]{1,0:T(8,128)(2,1)S(1)}, u32[]{:S(2)}, u32[]{:S(2)}) collective-permute-start(bf16[128,1408]{1,0:T(8,128)(2,1)} %get-tuple-element.111), channel_id=1, source_target_pairs={{0,8},{1,9},{2,10},{3,11},{4,12},{5,13},{6,14},{7,15},{8,0},{9,1},... | collective-permute-start | bytes 1081352 | tf_op jit(solution)/shard_map/ppermute | solution.py:256
  621.8 45.3 %collective-permute-start.53 = (bf16[128,1024]{1,0:T(8,128)(2,1)}, bf16[128,1024]{1,0:T(8,128)(2,1)S(1)}, u32[]{:S(2)}, u32[]{:S(2)}) collective-permute-start(bf16[128,1024]{1,0:T(8,128)(2,1)} %collective-permute-done.51), channel_id=1, source_target_pairs={{0,16},{16,0},{1,17},{17,1},{2,18},{18,2},{3,19},{19,3},{4,20},{20... | collective-permute-start | bytes 786440 | tf_op jit(solution)/shard_map/ppermute | solution.py:259
  (101 other events, 995.4 us)
Sparse Core Ops, SparseCore 0:
  9.9 68.3 all-gather.6
  80.8 41.9 all-gather.10
  127.0 72.0 all-gather.8
  333.8 78.2 reduce-scatter.4
  477.3 42.0 reduce-scatter.6
  546.9 40.0 reduce-scatter.8
  608.9 46.0 reduce-scatter.10

commit v4 on v3

--- a/solution.py
+++ b/solution.py
@@ -344,33 +344,30 @@
 
         x_in = inputs.reshape(tokens, width).astype(f32)
         normed_one, inverse_one = normalize(x_in)
-        low_one = gather_w(normed_one.astype(bf16))
+        low_one = gather_w(after(normed_one.astype(bf16), qkv_part))
 
         out_part = lax.ppermute(
-            pick(w_out, c, n_dp, 1),
+            after(pick(w_out, c, n_dp, 1), low_one, qkv_mine),
             "seq",
             [(i, GROUP * (i % planes) + i // planes) for i in range(n_seq)],
         )
-        out_full = lax.all_gather(out_part, both, axis_index_groups=across_dp, tiled=False)
+        down_full = lax.all_gather(
+            pick(w_down, c, n_dp, 1), both, axis_index_groups=in_plane_dp, tiled=False
+        )
+        down_full = down_full.reshape(n_dp, ff_block, width // n_dp)
+        out_full = lax.all_gather(
+            after(out_part, down_full), both, axis_index_groups=across_dp, tiled=False
+        )
         out_full = out_full.reshape(n_dp, planes * shard, width // n_dp)
 
         piece = shard // halves
         gate_up = jnp.where(c // halves == 0, scaled(w_gate, gain_two), scaled(w_up, gain_two))
         gate_up = after(pick(gate_up, c % halves, halves, 0), low_one, qkv_mine)
-        gate_up_part = jnp.zeros((planes, piece, ff_block), bf16)
-        for t in range(planes):
-            block = pick(gate_up, (p + t) % planes, planes, 1)
-            block = shift_z(block, t) if t else block
-            gate_up_part = lax.dynamic_update_index_in_dim(gate_up_part, block, (p - t) % planes, 0)
-        gate_up_full = lax.all_gather(gate_up_part, both, axis_index_groups=in_plane_dp, tiled=False)
-        gate_up_full = gate_up_full.reshape(2, width, ff_block)
-        gate_full = gate_up_full[0]
-        up_full = gate_up_full[1]
-
-        down_full = lax.all_gather(
-            pick(w_down, c, n_dp, 1), both, axis_index_groups=in_plane_dp, tiled=False
-        )
-        down_full = down_full.reshape(n_dp, ff_block, width // n_dp)
+        gate_up_sent = [
+            shift_z(pick(gate_up, (p + t) % planes, planes, 1), t) if t
+            else pick(gate_up, p, planes, 1)
+            for t in range(planes)
+        ]
 
         blocks = [
             (i * GROUP + j) * halves + h
@@ -402,7 +399,19 @@
         q = (q.astype(bf16).astype(f32) * HEAD_DIM ** (-0.5)).astype(bf16).reshape(plane_tokens, q_width)
         k = rotate(kv[:, None, :HEAD_DIM], cosine, sine)[:, 0]
         kv_low = jnp.concatenate([k, kv[:, HEAD_DIM:]], axis=1).astype(bf16)
-        kv_all = jnp.stack(gather_z(kv_low))
+        kv_sent = gather_z(kv_low)
+        gate_up_part = jnp.zeros((planes, piece, ff_block), bf16)
+        for t in range(planes):
+            gate_up_part = lax.dynamic_update_index_in_dim(
+                gate_up_part, after(gate_up_sent[t], kv_low), (p - t) % planes, 0
+            )
+        gate_up_full = lax.all_gather(
+            after(gate_up_part, out_part), both, axis_index_groups=in_plane_dp, tiled=False
+        )
+        gate_up_full = gate_up_full.reshape(2, width, ff_block)
+        gate_full = gate_up_full[0]
+        up_full = gate_up_full[1]
+        kv_all = jnp.stack(kv_sent)
         grad_y_all = jnp.concatenate(gather_z(after(grad_y.astype(bf16), kv_all, gate_up_part)), axis=0)
         kk = jnp.concatenate([kv_all[..., :HEAD_DIM]] * 2, axis=-1)
         vv = jnp.concatenate([kv_all[..., HEAD_DIM:]] * 2, axis=-1)
@@ -482,11 +491,11 @@
         inner_two = after(inner_two, down_sum, gate_up_sum, mixed)
         grad_x_mid = grad_y + norm_back(order_back(inner_two), normed_two, inverse_two)
 
-        mixed = after(mixed, inner_two)
-        mixed = scatter_z([mixed[t * tokens : (t + 1) * tokens] for t in range(planes)])
+        mixed = after(mixed, grad_x_mid)
+        mixed_sent = [shift_z(mixed[t * tokens : (t + 1) * tokens], -t) for t in range(1, planes)]
         gate_up_sum = lax.psum_scatter(gate_up_sum, "seq", axis_index_groups=in_plane, tiled=True)
         down_sum = lax.psum_scatter(
-            after(down_sum, gate_up_sum), "seq", axis_index_groups=in_plane, tiled=True
+            down_sum, "seq", axis_index_groups=in_plane, tiled=True
         )
         gate_up_sum = gate_up_sum.reshape(planes, piece, ff_block)
 
@@ -498,7 +507,7 @@
 
         out_part_sum = dot(gather_dp(o), exchange_dp(grad_branch, c, 1), ((0,), (0,))).astype(bf16)
         out_sum = lax.psum_scatter(
-            after(out_part_sum, down_sum), "seq", axis_index_groups=across, tiled=True
+            after(out_part_sum, down_sum, gate_up_sum), "seq", axis_index_groups=across, tiled=True
         )
         out_sum = lax.ppermute(
             out_sum, "seq", [(GROUP * (i % planes) + i // planes, i) for i in range(n_seq)]
@@ -506,7 +515,12 @@
         grad_w_out = jnp.concatenate(collect_dp(out_sum, c), axis=1).astype(f32)
 
         grad_o_seq = by_seq(grad_o, 0)
-        grad_o_seq = after(grad_o_seq, out_part_sum)
+        mixed = functools.reduce(
+            jnp.add,
+            [after(g, grad_branch).astype(f32) for g in mixed_sent],
+            mixed[:tokens].astype(f32),
+        )
+        grad_o_seq = after(grad_o_seq, out_part_sum, mixed)
         pieces = [
             attend_back(
                 seen, q_seq[i], grad_o_seq[i], o_seq[i], kk_seq[i], vv_seq[i], lse_seq[i], order
@@ -549,6 +563,7 @@
             exchange_dp(after(jnp.concatenate(pre, axis=1), grad_low_one), c, 1),
             ((0,), (0,)),
         ).astype(bf16)
+        gate_up_late = after(gate_up_sum, qkv_sum)
         qkv_sum = lax.psum_scatter(
             after(qkv_sum, out_sum), "seq", axis_index_groups=across, tiled=True
         )
@@ -566,10 +581,15 @@
 
         grad_w_down = jnp.concatenate(collect_dp(down_sum, c), axis=1).astype(f32)
         gate_up_rows = jnp.zeros((planes, piece, ff_block), bf16)
+        sent = []
         for t in range(planes):
-            block = lax.dynamic_index_in_dim(gate_up_sum, (p + t) % planes, 0, keepdims=False)
-            block = shift_z(block, t) if t else block
-            gate_up_rows = lax.dynamic_update_index_in_dim(gate_up_rows, block, (p - t) % planes, 0)
+            block = lax.dynamic_index_in_dim(gate_up_late, (p + t) % planes, 0, keepdims=False)
+            sent.append(shift_z(block, t) if t else block)
+        sent = lax.optimization_barrier(tuple(sent))
+        for t in range(planes):
+            gate_up_rows = lax.dynamic_update_index_in_dim(
+                gate_up_rows, sent[t], (p - t) % planes, 0
+            )
         gate_up_rows = collect_dp(gate_up_rows, c)
 
         def rows_of(members):

time: 691 us -> 708 us (1.025)
  starting transfers between devices: 135 us -> 151 us
  waiting for transfers between devices: 291 us -> 281 us
  other arithmetic: 55.5 us -> 62.9 us
    ppermute x27, waiting for transfers between devices: 220 us -> 186 us  [shift_z(): lax.ppermute(value, 'seq', [(s, (s + GROUP * t) % n_seq) for s in range(n...]
    ppermute x17, waiting for transfers between devices: 28.7 us -> 51.2 us  [xor_w(): return lax.ppermute(value, 'seq', [(s, s ^ j) for s in range(n_seq)])]
    ppermute x27, starting transfers between devices: 71.5 us -> 81.6 us  [shift_z(): lax.ppermute(value, 'seq', [(s, (s + GROUP * t) % n_seq) for s in range(n...]
    unnamed x201 -> x203, local copies, waits for them, and re-layouts: 35.8 us -> 39.1 us
  transfers between devices with their start and end apart: 68 -> 68, of which waited for: 26 -> 24; matrix products, arithmetic and copies ran while one was open for 24% -> 25% of each run, Pallas kernels for 3% -> 3%
where the time goes in v4:
time: 708 us; the launch traced here: 698 us
  waiting for transfers between devices  281 us (40%)
  starting transfers between devices  151 us (21%)
  local copies, waits for them, and re-layouts  89.5 us (13%)
  matrix products  79.2 us (11%)
  other arithmetic  62.9 us (9%)
  Pallas kernels  18 us (3%)
  between operations  16.5 us (2%)
    ppermute x27, waiting for transfers between devices, shift_z(): lax.ppermute(value, 'seq', [(s, (s + GROUP * t) % n_seq) for s in range(n...  186 us
    ppermute x27, starting transfers between devices, shift_z(): lax.ppermute(value, 'seq', [(s, (s + GROUP * t) % n_seq) for s in range(n...  81.6 us
    dot_general x20, matrix products, dot(): lax.dot_general(left, right, (contract, ((), ())), preferred_element_type...  79.2 us
    ppermute x17, waiting for transfers between devices, xor_w(): return lax.ppermute(value, 'seq', [(s, s ^ j) for s in range(n_seq)])  51.2 us
    ppermute x17, starting transfers between devices, xor_w(): return lax.ppermute(value, 'seq', [(s, s ^ j) for s in range(n_seq)])  40.4 us
    unnamed x203, local copies, waits for them, and re-layouts  39.1 us
    reduce_scatter x1, waiting for transfers between devices, body(): lax.psum_scatter(after(qkv_sum, out_sum), 'seq', axis_index_groups=across...  34.8 us
    ppermute x13, starting transfers between devices, shift_dp(): return lax.ppermute(value, 'dp', [(c, (c + t) % n_dp) for c in range(n_dp)])  16.8 us
  transfers between devices with their start and end apart: 68, of which 24 were waited for; matrix products, arithmetic and copies ran while one was open for 25% of the time, Pallas kernels for 3%

profile of v4, /device:TPU:1, one launch (start us, length us, event | category | flops | bytes accessed | tf_op | source)
XLA Modules:
  0.0 698.1 jit_solution(765029531104981123)
XLA Ops:
  28.8 13.5 %collective-permute-done.4 = bf16[512,320]{0,1:T(8,128)(2,1)S(1)} collective-permute-done((bf16[512,320]{0,1:T(8,128)(2,1)S(1)}, bf16[512,320]{0,1:T(8,128)(2,1)S(1)}, u32[]{:S(2)}, u32[]{:S(2)}) %collective-permute-start.4) | collective-permute-done | bytes 327712 | tf_op jit(solution)/shard_map/ppermute | solution.py:256
  49.2 6.4 collective-permute-done.2
  59.5 16.6 %collective-permute-start.9 = (s32[1,128]{1,0:T(1,128)S(1)}, s32[1,128]{1,0:T(1,128)S(1)}, u32[]{:S(2)}, u32[]{:S(2)}) collective-permute-start(s32[1,128]{1,0:T(1,128)S(1)} %copy-done.54), channel_id=1, source_target_pairs={{0,2},{1,3},{2,0},{3,1},{4,6},{5,7},{6,4},{7,5},{8,10},{9,11},{10,... | collective-permute-start | bytes 1544 | tf_op jit(solution)/shard_map/ppermute | solution.py:253
  76.1 6.5 collective-permute-start.8
  99.3 11.8 %collective-permute-done.20 = bf16[128,1408]{1,0:T(8,128)(2,1)S(1)} collective-permute-done((bf16[128,1408]{1,0:T(8,128)(2,1)S(1)}, bf16[128,1408]{1,0:T(8,128)(2,1)S(1)}, u32[]{:S(2)}, u32[]{:S(2)}) %collective-permute-start.20) | collective-permute-done | bytes 360480 | tf_op jit(solution)/shard_map/ppermute | solution.py:256
  111.1 25.5 %collective-permute-done.19 = bf16[128,1408]{1,0:T(8,128)(2,1)S(1)} collective-permute-done((bf16[128,1408]{1,0:T(8,128)(2,1)S(1)}, bf16[128,1408]{1,0:T(8,128)(2,1)S(1)}, u32[]{:S(2)}, u32[]{:S(2)}) %collective-permute-start.19) | collective-permute-done | bytes 360480 | tf_op jit(solution)/shard_map/ppermute | solution.py:256
  171.1 7.6 %attend.1 = (bf16[512,512]{1,0:T(8,128)(2,1)}, f32[4,8,1024]{2,1,0:T(8,128)}) custom-call(s32[1]{0:T(128)} %bitcast.1.seen_ref, bf16[512,512]{1,0:T(8,128)(2,1)} %multiply_convert_fusion.3.q_ref, bf16[4,512,128]{2,1,0:T(8,128)(2,1)} %get-tuple-element.208.kk_ref, bf16[4,512,128]{2,1,0:T(8,128)(2,1)} %get-tuple-element.209.vv_ref, ...), custom_call_target="tpu_custom_call" | custom-call | tf_op jit(solution)/shard_map/attend/pallas_call | solution.py:136
  186.5 15.6 %collective-permute-done.21 = bf16[128,2048]{1,0:T(8,128)(2,1)} collective-permute-done((bf16[128,2048]{1,0:T(8,128)(2,1)}, bf16[128,2048]{1,0:T(8,128)(2,1)}, u32[]{:S(2)}, u32[]{:S(2)}) %collective-permute-start.21) | collective-permute-done | bytes 524320 | tf_op jit(solution)/shard_map/ppermute | solution.py:256
  204.4 8.3 %collective-permute-done.22 = bf16[128,2048]{1,0:T(8,128)(2,1)} collective-permute-done((bf16[128,2048]{1,0:T(8,128)(2,1)}, bf16[128,2048]{1,0:T(8,128)(2,1)}, u32[]{:S(2)}, u32[]{:S(2)}) %collective-permute-start.22) | collective-permute-done | bytes 524320 | tf_op jit(solution)/shard_map/ppermute | solution.py:256
  215.0 6.3 collective-permute-done.17
  221.3 10.5 %collective-permute-done.16 = bf16[128,2048]{1,0:T(8,128)(2,1)S(1)} collective-permute-done((bf16[128,2048]{1,0:T(8,128)(2,1)S(1)}, bf16[128,2048]{1,0:T(8,128)(2,1)S(1)}, u32[]{:S(2)}, u32[]{:S(2)}) %collective-permute-start.16) | collective-permute-done | bytes 524320 | tf_op jit(solution)/shard_map/ppermute | solution.py:253
  232.9 11.9 %collective-permute-start.24 = (bf16[128,2048]{1,0:T(8,128)(2,1)S(1)}, bf16[128,2048]{1,0:T(8,128)(2,1)S(1)}, u32[]{:S(2)}, u32[]{:S(2)}) collective-permute-start(bf16[128,2048]{1,0:T(8,128)(2,1)S(1)} %constant_dynamic-update-slice_fusion.12), channel_id=1, source_target_pairs={{0,4},{1,5},{2,6},{3,7},{4,8},{5,9},{6,10},{7,11},{8,12},{9,13},{1... | collective-permute-start | bytes 1572872 | tf_op jit(solution)/shard_map/ppermute | solution.py:256
  252.5 16.7 %collective-permute-done.25 = bf16[128,2048]{1,0:T(8,128)(2,1)S(1)} collective-permute-done((bf16[128,2048]{1,0:T(8,128)(2,1)S(1)}, bf16[128,2048]{1,0:T(8,128)(2,1)S(1)}, u32[]{:S(2)}, u32[]{:S(2)}) %collective-permute-start.25) | collective-permute-done | bytes 524320 | tf_op jit(solution)/shard_map/ppermute | solution.py:256
  275.1 5.5 fusion.7
  280.6 10.1 %fusion.99 = (bf16[16,128,1408]{2,1,0:T(8,128)(2,1)}, bf16[16,128,1408]{2,1,0:T(8,128)(2,1)}) fusion(bf16[32,128,1408]{2,1,0:T(8,128)(2,1)} %all-gather.9.cloned.1.call-done), kind=kLoop, calls=%fused_computation.339 | loop fusion | bytes 23068672 | tf_op jit(solution)/shard_map/slice | solution.py:412
  290.8 7.0 fusion.106
  297.8 8.2 %multiply_convert_fusion.2 = (bf16[512,1408]{1,0:T(8,128)(2,1)}, f32[512,1408]{1,0:T(8,128)}) fusion(f32[512,1408]{1,0:T(8,128)S(1)} %fusion.106, bf16[512,2048]{1,0:T(8,128)(2,1)} %get-tuple-element.168, bf16[2048,1408]{1,0:T(8,128)(2,1)S(1)} %bitcast.168), kind=kOutput, calls=%fused_computation.21 | convolution fusion | flops 2957115392 | bytes 15073280 | tf_op jit(solution)/shard_map/dot_general | solution.py:26
  306.0 5.8 broadcast_select_fusion.3
  333.0 6.3 convolution_convert_fusion.1
  344.9 18.5 %collective-permute-start.27 = (bf16[128,2048]{1,0:T(8,128)(2,1)S(1)}, bf16[128,2048]{1,0:T(8,128)(2,1)S(1)}, u32[]{:S(2)}, u32[]{:S(2)}) collective-permute-start(bf16[128,2048]{1,0:T(8,128)(2,1)S(1)} %get-tuple-element.117), channel_id=1, source_target_pairs={{0,12},{1,13},{2,14},{3,15},{4,0},{5,1},{6,2},{7,3},{8,4},{9,5},{1... | collective-permute-start | bytes 1572872 | tf_op jit(solution)/shard_map/ppermute | solution.py:256
  374.6 12.3 %collective-permute-done.29 = bf16[128,2048]{1,0:T(8,128)(2,1)S(1)} collective-permute-done((bf16[128,2048]{1,0:T(8,128)(2,1)S(1)}, bf16[128,2048]{1,0:T(8,128)(2,1)S(1)}, u32[]{:S(2)}, u32[]{:S(2)}) %collective-permute-start.29) | collective-permute-done | bytes 524320 | tf_op jit(solution)/shard_map/ppermute | solution.py:256
  386.9 20.5 %collective-permute-done.28 = bf16[128,2048]{1,0:T(8,128)(2,1)S(1)} collective-permute-done((bf16[128,2048]{1,0:T(8,128)(2,1)S(1)}, bf16[128,2048]{1,0:T(8,128)(2,1)S(1)}, u32[]{:S(2)}, u32[]{:S(2)}) %collective-permute-start.28) | collective-permute-done | bytes 524320 | tf_op jit(solution)/shard_map/ppermute | solution.py:256
  408.9 10.9 %convolution_convert_fusion = bf16[2048,1408]{1,0:T(8,128)(2,1)} fusion(bf16[1024,2048]{1,0:T(8,128)(2,1)} %constant_dynamic-update-slice_fusion.36, bf16[1024,1408]{1,0:T(8,128)(2,1)S(1)} %pad_maximum_fusion), kind=kOutput, calls=%fused_computation | convolution fusion | flops 5908463616 | bytes 12845056 | tf_op jit(solution)/shard_map/dot_general | solution.py:26
  445.2 15.9 %collective-permute-done.36 = bf16[128,2048]{1,0:T(8,128)(2,1)S(1)} collective-permute-done((bf16[128,2048]{1,0:T(8,128)(2,1)S(1)}, bf16[128,2048]{1,0:T(8,128)(2,1)S(1)}, u32[]{:S(2)}, u32[]{:S(2)}) %collective-permute-start.36) | collective-permute-done | bytes 524320 | tf_op jit(solution)/shard_map/ppermute | solution.py:253
  465.3 12.0 %collective-permute-done.37 = bf16[64,2048]{1,0:T(8,128)(2,1)S(1)} collective-permute-done((bf16[64,2048]{1,0:T(8,128)(2,1)S(1)}, bf16[64,2048]{1,0:T(8,128)(2,1)S(1)}, u32[]{:S(2)}, u32[]{:S(2)}) %collective-permute-start.37) | collective-permute-done | bytes 262176 | tf_op jit(solution)/shard_map/ppermute | solution.py:253
  479.7 7.3 %collective-permute-done.39 = bf16[128,2048]{1,0:T(8,128)(2,1)S(1)} collective-permute-done((bf16[128,2048]{1,0:T(8,128)(2,1)S(1)}, bf16[128,2048]{1,0:T(8,128)(2,1)S(1)}, u32[]{:S(2)}, u32[]{:S(2)}) %collective-permute-start.39) | collective-permute-done | bytes 524320 | tf_op jit(solution)/shard_map/ppermute | solution.py:256
  496.4 10.4 %attend_back.1 = (f32[512,512]{1,0:T(8,128)}, f32[4,512,128]{2,1,0:T(8,128)}, f32[4,512,128]{2,1,0:T(8,128)}) custom-call(s32[1]{0:T(128)} %bitcast.1.seen_ref, bf16[512,512]{1,0:T(8,128)(2,1)} %multiply_convert_fusion.3.q_ref, bf16[512,512]{1,0:T(8,128)(2,1)} %bitcast.183, bf16[512,512]{1,0:T(8,128)(2,1)} %get-tuple-element.43.o_ref, ...), custom_call_target="tpu_custom_call" | custom-call | tf_op jit(solution)/shard_map/attend_back/pallas_call | solution.py:166
  510.5 22.3 %collective-permute-start.43 = (bf16[512,128]{1,0:T(8,128)(2,1)}, bf16[512,128]{1,0:T(8,128)(2,1)S(1)}, u32[]{:S(2)}, u32[]{:S(2)}) collective-permute-start(bf16[512,128]{1,0:T(8,128)(2,1)} %get-tuple-element.146), channel_id=1, source_target_pairs={{0,12},{1,13},{2,14},{3,15},{4,0},{5,1},{6,2},{7,3},{8,4},{9,5},{1... | collective-permute-start | bytes 393224 | tf_op jit(solution)/shard_map/ppermute | solution.py:256
  568.6 11.8 %collective-permute-done.56 = bf16[128,1408]{1,0:T(8,128)(2,1)S(1)} collective-permute-done((bf16[128,1408]{1,0:T(8,128)(2,1)S(1)}, bf16[128,1408]{1,0:T(8,128)(2,1)S(1)}, u32[]{:S(2)}, u32[]{:S(2)}) %collective-permute-start.56) | collective-permute-done | bytes 360480 | tf_op jit(solution)/shard_map/ppermute | solution.py:256
  580.4 32.9 %collective-permute-done.55 = bf16[128,1408]{1,0:T(8,128)(2,1)S(1)} collective-permute-done((bf16[128,1408]{1,0:T(8,128)(2,1)S(1)}, bf16[128,1408]{1,0:T(8,128)(2,1)S(1)}, u32[]{:S(2)}, u32[]{:S(2)}) %collective-permute-start.55) | collective-permute-done | bytes 360480 | tf_op jit(solution)/shard_map/ppermute | solution.py:256
  629.3 34.8 %reduce-scatter.11.cloned.1.call-done = bf16[512,320]{0,1:T(8,128)(2,1)} async-done(((bf16[2048,320]{0,1:T(8,128)(2,1)}), bf16[512,320]{0,1:T(8,128)(2,1)}) %reduce-scatter.11.cloned.1.call-update) | async-done | bytes 327696 | tf_op jit(solution)/shard_map/reduce_scatter | solution.py:567
  670.3 6.2 convert_multiply_fusion
  (464 shorter events, 265.7 us)
Async XLA Ops:
  16.5 164.1 %all-gather.7.cloned.1.call-start = ((), (), s32[]{:S(2)}) async-start(), calls=%async_computation.10 | async-start | bytes 2359296 | tf_op jit(solution)/shard_map/all_gather | solution.py:358
  58.4 216.6 %all-gather.11.cloned.1.call-start = ((), (), s32[]{:S(2)}) async-start(), calls=%async_computation.12 | async-start | bytes 6488064 | tf_op jit(solution)/shard_map/all_gather | solution.py:354
  59.5 221.2 %all-gather.9.cloned.1.call-start = ((), (), s32[]{:S(2)}) async-start(), calls=%async_computation.11 | async-start | bytes 12976128 | tf_op jit(solution)/shard_map/all_gather | solution.py:408
  59.5 27.9 %collective-permute-start.9 = (s32[1,128]{1,0:T(1,128)S(1)}, s32[1,128]{1,0:T(1,128)S(1)}, u32[]{:S(2)}, u32[]{:S(2)}) collective-permute-start(s32[1,128]{1,0:T(1,128)S(1)} %copy-done.54), channel_id=1, source_target_pairs={{0,2},{1,3},{2,0},{3,1},{4,6},{5,7},{6,4},{7,5},{8,10},{9,11},{10,... | collective-permute-start | bytes 1544 | tf_op jit(solution)/shard_map/ppermute | solution.py:253
  91.3 45.2 %collective-permute-start.19 = (bf16[128,1408]{1,0:T(8,128)(2,1)S(1)}, bf16[128,1408]{1,0:T(8,128)(2,1)S(1)}, u32[]{:S(2)}, u32[]{:S(2)}) collective-permute-start(bf16[128,1408]{1,0:T(8,128)(2,1)S(1)} %get-tuple-element.141), channel_id=1, source_target_pairs={{0,8},{1,9},{2,10},{3,11},{4,12},{5,13},{6,14},{7,15},{8,0},{9,1},... | collective-permute-start | bytes 1081352 | tf_op jit(solution)/shard_map/ppermute | solution.py:256
  91.3 45.2 %collective-permute-start.18 = (bf16[128,1408]{1,0:T(8,128)(2,1)S(1)}, bf16[128,1408]{1,0:T(8,128)(2,1)S(1)}, u32[]{:S(2)}, u32[]{:S(2)}) collective-permute-start(bf16[128,1408]{1,0:T(8,128)(2,1)S(1)} %get-tuple-element.142), channel_id=1, source_target_pairs={{0,4},{1,5},{2,6},{3,7},{4,8},{5,9},{6,10},{7,11},{8,12},{9,13},{1... | collective-permute-start | bytes 1081352 | tf_op jit(solution)/shard_map/ppermute | solution.py:256
  138.0 421.0 %reduce-scatter.5.cloned.1.call-start = ((), (), s32[]{:S(2)}) async-start(), calls=%async_computation.6 | async-start | bytes 3604480 | tf_op jit(solution)/shard_map/reduce_scatter | solution.py:497
  167.3 46.6 %collective-permute-start.23 = (bf16[128,2048]{1,0:T(8,128)(2,1)}, bf16[128,2048]{1,0:T(8,128)(2,1)}, u32[]{:S(2)}, u32[]{:S(2)}) collective-permute-start(bf16[128,2048]{1,0:T(8,128)(2,1)} %bitcast_convert_fusion), channel_id=1, source_target_pairs={{0,12},{1,13},{2,14},{3,15},{4,0},{5,1},{6,2},{7,3},{8,4},{9,5},{1... | collective-permute-start | bytes 1572872 | tf_op jit(solution)/shard_map/ppermute | solution.py:256
  168.8 44.0 %collective-permute-start.22 = (bf16[128,2048]{1,0:T(8,128)(2,1)}, bf16[128,2048]{1,0:T(8,128)(2,1)}, u32[]{:S(2)}, u32[]{:S(2)}) collective-permute-start(bf16[128,2048]{1,0:T(8,128)(2,1)} %bitcast_convert_fusion), channel_id=1, source_target_pairs={{0,8},{1,9},{2,10},{3,11},{4,12},{5,13},{6,14},{7,15},{8,0},{9,1},... | collective-permute-start | bytes 1572872 | tf_op jit(solution)/shard_map/ppermute | solution.py:256
  168.8 33.3 %collective-permute-start.21 = (bf16[128,2048]{1,0:T(8,128)(2,1)}, bf16[128,2048]{1,0:T(8,128)(2,1)}, u32[]{:S(2)}, u32[]{:S(2)}) collective-permute-start(bf16[128,2048]{1,0:T(8,128)(2,1)} %bitcast_convert_fusion), channel_id=1, source_target_pairs={{0,4},{1,5},{2,6},{3,7},{4,8},{5,9},{6,10},{7,11},{8,12},{9,13},{1... | collective-permute-start | bytes 1572872 | tf_op jit(solution)/shard_map/ppermute | solution.py:256
  183.8 31.2 %collective-permute-start.15 = (bf16[128,2048]{1,0:T(8,128)(2,1)S(1)}, bf16[128,2048]{1,0:T(8,128)(2,1)S(1)}, u32[]{:S(2)}, u32[]{:S(2)}) collective-permute-start(bf16[128,2048]{1,0:T(8,128)(2,1)S(1)} %get-tuple-element.120), channel_id=1, source_target_pairs={{0,1},{1,0},{2,3},{3,2},{4,5},{5,4},{6,7},{7,6},{8,9},{9,8},{10,11... | collective-permute-start | bytes 1572872 | tf_op jit(solution)/shard_map/ppermute | solution.py:253
  185.0 36.3 %collective-permute-start.17 = (bf16[128,2048]{1,0:T(8,128)(2,1)S(1)}, bf16[128,2048]{1,0:T(8,128)(2,1)S(1)}, u32[]{:S(2)}, u32[]{:S(2)}) collective-permute-start(bf16[128,2048]{1,0:T(8,128)(2,1)S(1)} %get-tuple-element.121), channel_id=1, source_target_pairs={{0,3},{1,2},{2,1},{3,0},{4,7},{5,6},{6,5},{7,4},{8,11},{9,10},{10,... | collective-permute-start | bytes 1572872 | tf_op jit(solution)/shard_map/ppermute | solution.py:253
  202.1 29.8 %collective-permute-start.16 = (bf16[128,2048]{1,0:T(8,128)(2,1)S(1)}, bf16[128,2048]{1,0:T(8,128)(2,1)S(1)}, u32[]{:S(2)}, u32[]{:S(2)}) collective-permute-start(bf16[128,2048]{1,0:T(8,128)(2,1)S(1)} %get-tuple-element.122), channel_id=1, source_target_pairs={{0,2},{1,3},{2,0},{3,1},{4,6},{5,7},{6,4},{7,5},{8,10},{9,11},{10,... | collective-permute-start | bytes 1572872 | tf_op jit(solution)/shard_map/ppermute | solution.py:253
  247.9 26.1 %collective-permute-start.26 = (bf16[128,2048]{1,0:T(8,128)(2,1)S(1)}, bf16[128,2048]{1,0:T(8,128)(2,1)S(1)}, u32[]{:S(2)}, u32[]{:S(2)}) collective-permute-start(bf16[128,2048]{1,0:T(8,128)(2,1)S(1)} %constant_dynamic-update-slice_fusion.12), channel_id=1, source_target_pairs={{0,12},{1,13},{2,14},{3,15},{4,0},{5,1},{6,2},{7,3},{8,4},{9,5},{1... | collective-permute-start | bytes 1572872 | tf_op jit(solution)/shard_map/ppermute | solution.py:256
  339.4 219.7 %reduce-scatter.7.cloned.1.call-start = ((), (), s32[]{:S(2)}) async-start(), calls=%async_computation.7 | async-start | bytes 7208960 | tf_op jit(solution)/shard_map/reduce_scatter | solution.py:496
  339.4 100.6 %collective-permute-start.49 = (bf16[512,2048]{1,0:T(8,128)(2,1)}, bf16[512,2048]{1,0:T(8,128)(2,1)}, u32[]{:S(2)}, u32[]{:S(2)}) collective-permute-start(bf16[512,2048]{1,0:T(8,128)(2,1)} %copy-done.44), channel_id=1, source_target_pairs={{0,16},{16,0},{1,17},{17,1},{2,18},{18,2},{3,19},{19,3},{4,20},{20... | collective-permute-start | bytes 6291464 | tf_op jit(solution)/shard_map/ppermute | solution.py:259
  343.3 65.3 %collective-permute-start.33 = (bf16[512,1408]{1,0:T(8,128)(2,1)S(1)}, bf16[512,1408]{1,0:T(8,128)(2,1)S(1)}, u32[]{:S(2)}, u32[]{:S(2)}) collective-permute-start(bf16[512,1408]{1,0:T(8,128)(2,1)S(1)} %broadcast_select_fusion.2), channel_id=1, source_target_pairs={{0,16},{16,0},{1,17},{17,1},{2,18},{18,2},{3,19},{19,3},{4,20},{20... | collective-permute-start | bytes 4325384 | tf_op jit(solution)/shard_map/ppermute | solution.py:259
  344.9 29.7 %collective-permute-start.27 = (bf16[128,2048]{1,0:T(8,128)(2,1)S(1)}, bf16[128,2048]{1,0:T(8,128)(2,1)S(1)}, u32[]{:S(2)}, u32[]{:S(2)}) collective-permute-start(bf16[128,2048]{1,0:T(8,128)(2,1)S(1)} %get-tuple-element.117), channel_id=1, source_target_pairs={{0,12},{1,13},{2,14},{3,15},{4,0},{5,1},{6,2},{7,3},{8,4},{9,5},{1... | collective-permute-start | bytes 1572872 | tf_op jit(solution)/shard_map/ppermute | solution.py:256
  363.6 43.8 %collective-permute-start.28 = (bf16[128,2048]{1,0:T(8,128)(2,1)S(1)}, bf16[128,2048]{1,0:T(8,128)(2,1)S(1)}, u32[]{:S(2)}, u32[]{:S(2)}) collective-permute-start(bf16[128,2048]{1,0:T(8,128)(2,1)S(1)} %get-tuple-element.119), channel_id=1, source_target_pairs={{0,8},{1,9},{2,10},{3,11},{4,12},{5,13},{6,14},{7,15},{8,0},{9,1},... | collective-permute-start | bytes 1572872 | tf_op jit(solution)/shard_map/ppermute | solution.py:256
  419.8 195.2 %reduce-scatter.9.cloned.1.call-start = ((), (), s32[]{:S(2)}) async-start(), calls=%async_computation.8 | async-start | bytes 1310720 | tf_op jit(solution)/shard_map/reduce_scatter | solution.py:509
  437.5 26.2 %collective-permute-start.35 = (bf16[128,2048]{1,0:T(8,128)(2,1)S(1)}, bf16[128,2048]{1,0:T(8,128)(2,1)S(1)}, u32[]{:S(2)}, u32[]{:S(2)}) collective-permute-start(bf16[128,2048]{1,0:T(8,128)(2,1)S(1)} %get-tuple-element.96), channel_id=1, source_target_pairs={{0,1},{1,0},{2,3},{3,2},{4,5},{5,4},{6,7},{7,6},{8,9},{9,8},{10,11... | collective-permute-start | bytes 1572872 | tf_op jit(solution)/shard_map/ppermute | solution.py:253
  442.8 36.9 %collective-permute-start.34 = (bf16[128,2048]{1,0:T(8,128)(2,1)S(1)}, bf16[128,2048]{1,0:T(8,128)(2,1)S(1)}, u32[]{:S(2)}, u32[]{:S(2)}) collective-permute-start(bf16[128,2048]{1,0:T(8,128)(2,1)S(1)} %get-tuple-element.112), channel_id=1, source_target_pairs={{0,12},{1,13},{2,14},{3,15},{4,0},{5,1},{6,2},{7,3},{8,4},{9,5},{1... | collective-permute-start | bytes 1572872 | tf_op jit(solution)/shard_map/ppermute | solution.py:256
  444.7 35.0 %collective-permute-start.40 = (bf16[128,2048]{1,0:T(8,128)(2,1)S(1)}, bf16[128,2048]{1,0:T(8,128)(2,1)S(1)}, u32[]{:S(2)}, u32[]{:S(2)}) collective-permute-start(bf16[128,2048]{1,0:T(8,128)(2,1)S(1)} %get-tuple-element.113), channel_id=1, source_target_pairs={{0,4},{1,5},{2,6},{3,7},{4,8},{5,9},{6,10},{7,11},{8,12},{9,13},{1... | collective-permute-start | bytes 1572872 | tf_op jit(solution)/shard_map/ppermute | solution.py:256
  444.9 42.1 %collective-permute-start.39 = (bf16[128,2048]{1,0:T(8,128)(2,1)S(1)}, bf16[128,2048]{1,0:T(8,128)(2,1)S(1)}, u32[]{:S(2)}, u32[]{:S(2)}) collective-permute-start(bf16[128,2048]{1,0:T(8,128)(2,1)S(1)} %get-tuple-element.114), channel_id=1, source_target_pairs={{0,8},{1,9},{2,10},{3,11},{4,12},{5,13},{6,14},{7,15},{8,0},{9,1},... | collective-permute-start | bytes 1572872 | tf_op jit(solution)/shard_map/ppermute | solution.py:256
  510.5 33.9 %collective-permute-start.43 = (bf16[512,128]{1,0:T(8,128)(2,1)}, bf16[512,128]{1,0:T(8,128)(2,1)S(1)}, u32[]{:S(2)}, u32[]{:S(2)}) collective-permute-start(bf16[512,128]{1,0:T(8,128)(2,1)} %get-tuple-element.146), channel_id=1, source_target_pairs={{0,12},{1,13},{2,14},{3,15},{4,0},{5,1},{6,2},{7,3},{8,4},{9,5},{1... | collective-permute-start | bytes 393224 | tf_op jit(solution)/shard_map/ppermute | solution.py:256
  559.0 105.1 %reduce-scatter.11.cloned.1.call-start = ((), (), s32[]{:S(2)}) async-start(), calls=%async_computation.9 | async-start | bytes 1638400 | tf_op jit(solution)/shard_map/reduce_scatter | solution.py:567
  563.4 49.9 %collective-permute-start.55 = (bf16[128,1408]{1,0:T(8,128)(2,1)S(1)}, bf16[128,1408]{1,0:T(8,128)(2,1)S(1)}, u32[]{:S(2)}, u32[]{:S(2)}) collective-permute-start(bf16[128,1408]{1,0:T(8,128)(2,1)S(1)} %get-tuple-element.137), channel_id=1, source_target_pairs={{0,8},{1,9},{2,10},{3,11},{4,12},{5,13},{6,14},{7,15},{8,0},{9,1},... | collective-permute-start | bytes 1081352 | tf_op jit(solution)/shard_map/ppermute | solution.py:256
  565.2 48.1 %collective-permute-start.54 = (bf16[128,1408]{1,0:T(8,128)(2,1)S(1)}, bf16[128,1408]{1,0:T(8,128)(2,1)S(1)}, u32[]{:S(2)}, u32[]{:S(2)}) collective-permute-start(bf16[128,1408]{1,0:T(8,128)(2,1)S(1)} %get-tuple-element.138), channel_id=1, source_target_pairs={{0,4},{1,5},{2,6},{3,7},{4,8},{5,9},{6,10},{7,11},{8,12},{9,13},{1... | collective-permute-start | bytes 1081352 | tf_op jit(solution)/shard_map/ppermute | solution.py:256
  567.7 48.8 %collective-permute-start.46 = (bf16[128,2048]{1,0:T(8,128)(2,1)}, bf16[128,2048]{1,0:T(8,128)(2,1)}, u32[]{:S(2)}, u32[]{:S(2)}) collective-permute-start(bf16[128,2048]{1,0:T(8,128)(2,1)} %get-tuple-element.107), channel_id=1, source_target_pairs={{0,1},{1,0},{2,3},{3,2},{4,5},{5,4},{6,7},{7,6},{8,9},{9,8},{10,11... | collective-permute-start | bytes 1572872 | tf_op jit(solution)/shard_map/ppermute | solution.py:253
  567.8 48.8 %collective-permute-start.48 = (bf16[128,2048]{1,0:T(8,128)(2,1)}, bf16[128,2048]{1,0:T(8,128)(2,1)}, u32[]{:S(2)}, u32[]{:S(2)}) collective-permute-start(bf16[128,2048]{1,0:T(8,128)(2,1)} %get-tuple-element.108), channel_id=1, source_target_pairs={{0,3},{1,2},{2,1},{3,0},{4,7},{5,6},{6,5},{7,4},{8,11},{9,10},{10,... | collective-permute-start | bytes 1572872 | tf_op jit(solution)/shard_map/ppermute | solution.py:253
  580.4 36.1 %collective-permute-start.47 = (bf16[128,2048]{1,0:T(8,128)(2,1)}, bf16[128,2048]{1,0:T(8,128)(2,1)}, u32[]{:S(2)}, u32[]{:S(2)}) collective-permute-start(bf16[128,2048]{1,0:T(8,128)(2,1)} %get-tuple-element.109), channel_id=1, source_target_pairs={{0,2},{1,3},{2,0},{3,1},{4,6},{5,7},{6,4},{7,5},{8,10},{9,11},{10,... | collective-permute-start | bytes 1572872 | tf_op jit(solution)/shard_map/ppermute | solution.py:253
  629.0 48.6 %collective-permute-start.53 = (bf16[128,1024]{1,0:T(8,128)(2,1)S(1)}, bf16[128,1024]{1,0:T(8,128)(2,1)}, u32[]{:S(2)}, u32[]{:S(2)}) collective-permute-start(bf16[128,1024]{1,0:T(8,128)(2,1)S(1)} %collective-permute-done.51), channel_id=1, source_target_pairs={{0,16},{16,0},{1,17},{17,1},{2,18},{18,2},{3,19},{19,3},{4,20},{20... | collective-permute-start | bytes 786440 | tf_op jit(solution)/shard_map/ppermute | solution.py:259
  (102 other events, 1253.1 us)
Sparse Core Ops, SparseCore 0:
  58.6 76.6 all-gather.6
  137.7 40.9 all-gather.10
  181.3 82.4 all-gather.8
  339.5 60.0 reduce-scatter.4
  419.9 85.5 reduce-scatter.6
  559.2 47.3 reduce-scatter.8
  618.9 45.1 reduce-scatter.10

commit v5 on v4

--- a/solution.py
+++ b/solution.py
@@ -229,8 +229,8 @@
     return grads * cosine - turn(grads * sine)
 
 
-def after(value, *earlier):
-    return lax.optimization_barrier((value,) + earlier)[0]
+def tie(*values):
+    return lax.optimization_barrier(values)
 
 
 def solution(mesh):
@@ -335,39 +335,40 @@
         )
         part_width = (q_width + PAIR) // n_dp
         qkv_part = qkv_part.reshape(GROUP * shard, part_width)
+        own_pos = positions.reshape(1, tokens)
+        plane_pos = jnp.concatenate([own_pos] + [xor_w(own_pos, j) for j in range(1, GROUP)], axis=1)
+        x_in = inputs.reshape(tokens, width).astype(f32)
+        normed_one, inverse_one = normalize(x_in)
+        low_one, qkv_part, plane_pos = tie(normed_one.astype(bf16), qkv_part, plane_pos)
+
         ring = [qkv_part] + [shift_z(qkv_part, -t) for t in range(1, planes)]
         qkv_ring = jnp.concatenate(ring + ring[: planes - 1], axis=0)
         qkv_mine = lax.dynamic_slice_in_dim(
             qkv_ring, ((planes - p) % planes) * GROUP * shard, width, 0
         )
-        qkv_full = collect_dp(qkv_mine, c)
-
-        x_in = inputs.reshape(tokens, width).astype(f32)
-        normed_one, inverse_one = normalize(x_in)
-        low_one = gather_w(after(normed_one.astype(bf16), qkv_part))
-
-        out_part = lax.ppermute(
-            after(pick(w_out, c, n_dp, 1), low_one, qkv_mine),
-            "seq",
-            [(i, GROUP * (i % planes) + i // planes) for i in range(n_seq)],
-        )
-        down_full = lax.all_gather(
-            pick(w_down, c, n_dp, 1), both, axis_index_groups=in_plane_dp, tiled=False
-        )
-        down_full = down_full.reshape(n_dp, ff_block, width // n_dp)
-        out_full = lax.all_gather(
-            after(out_part, down_full), both, axis_index_groups=across_dp, tiled=False
-        )
-        out_full = out_full.reshape(n_dp, planes * shard, width // n_dp)
+        low_one = gather_w(low_one)
 
         piece = shard // halves
         gate_up = jnp.where(c // halves == 0, scaled(w_gate, gain_two), scaled(w_up, gain_two))
-        gate_up = after(pick(gate_up, c % halves, halves, 0), low_one, qkv_mine)
+        out_part, gate_up, qkv_mine = tie(
+            pick(w_out, c, n_dp, 1), pick(gate_up, c % halves, halves, 0), qkv_mine
+        )
+        qkv_full = collect_dp(qkv_mine, c)
+        out_part = lax.ppermute(
+            out_part, "seq", [(i, GROUP * (i % planes) + i // planes) for i in range(n_seq)]
+        )
         gate_up_sent = [
             shift_z(pick(gate_up, (p + t) % planes, planes, 1), t) if t
             else pick(gate_up, p, planes, 1)
             for t in range(planes)
         ]
+        down_full = lax.all_gather(
+            pick(w_down, c, n_dp, 1), both, axis_index_groups=in_plane_dp, tiled=False
+        )
+        out_part, down_full = tie(out_part, down_full)
+        down_full = down_full.reshape(n_dp, ff_block, width // n_dp)
+        out_full = lax.all_gather(out_part, both, axis_index_groups=across_dp, tiled=False)
+        out_full = out_full.reshape(n_dp, planes * shard, width // n_dp)
 
         blocks = [
             (i * GROUP + j) * halves + h
@@ -383,8 +384,6 @@
         def order_back(value):
             return column_blocks(value, [blocks.index(i) for i in range(len(blocks))])
 
-        own_pos = positions.reshape(1, tokens)
-        plane_pos = jnp.concatenate([own_pos] + [xor_w(own_pos, j) for j in range(1, GROUP)], axis=1)
         cosine, sine = rope_tables(plane_pos.reshape(GROUP * tokens))
 
         grad_y = (
@@ -399,20 +398,21 @@
         q = (q.astype(bf16).astype(f32) * HEAD_DIM ** (-0.5)).astype(bf16).reshape(plane_tokens, q_width)
         k = rotate(kv[:, None, :HEAD_DIM], cosine, sine)[:, 0]
         kv_low = jnp.concatenate([k, kv[:, HEAD_DIM:]], axis=1).astype(bf16)
-        kv_sent = gather_z(kv_low)
+        kv_all = jnp.stack(gather_z(kv_low))
+        grad_y_low, kv_all = tie(grad_y.astype(bf16), kv_all)
+        *gate_up_sent, q = tie(*gate_up_sent, q)
         gate_up_part = jnp.zeros((planes, piece, ff_block), bf16)
         for t in range(planes):
             gate_up_part = lax.dynamic_update_index_in_dim(
-                gate_up_part, after(gate_up_sent[t], kv_low), (p - t) % planes, 0
+                gate_up_part, gate_up_sent[t], (p - t) % planes, 0
             )
         gate_up_full = lax.all_gather(
-            after(gate_up_part, out_part), both, axis_index_groups=in_plane_dp, tiled=False
+            gate_up_part, both, axis_index_groups=in_plane_dp, tiled=False
         )
         gate_up_full = gate_up_full.reshape(2, width, ff_block)
         gate_full = gate_up_full[0]
         up_full = gate_up_full[1]
-        kv_all = jnp.stack(kv_sent)
-        grad_y_all = jnp.concatenate(gather_z(after(grad_y.astype(bf16), kv_all, gate_up_part)), axis=0)
+        grad_y_all = jnp.concatenate(gather_z(grad_y_low), axis=0)
         kk = jnp.concatenate([kv_all[..., :HEAD_DIM]] * 2, axis=-1)
         vv = jnp.concatenate([kv_all[..., HEAD_DIM:]] * 2, axis=-1)
 
@@ -445,7 +445,8 @@
 
         normed_two, inverse_two = normalize(x_mid)
         low_two = reorder(normed_two.astype(bf16))
-        low_two = jnp.concatenate(gather_z(after(low_two, grad_y_all)), axis=0)
+        low_two, grad_y_all = tie(low_two, grad_y_all)
+        low_two = jnp.concatenate(gather_z(low_two), axis=0)
         gate = dot(low_two, gate_full)
         up_part = dot(low_two, up_full)
         sigmoid_gate = 1.0 / (1.0 + jnp.exp(-gate))
@@ -466,9 +467,13 @@
             grad_up, up_full, ((1,), (1,))
         )
         grad_low_two = grad_low_two.astype(bf16)
-        inner_two = scatter_z([grad_low_two[t * tokens : (t + 1) * tokens] for t in range(planes)])
-
-        hidden_later = after(hidden, grad_low_two)
+        hidden_later, grad_gate_later, grad_up_later, grad_low_two = tie(
+            hidden, grad_gate, grad_up, grad_low_two
+        )
+        inner_sent = [
+            shift_z(grad_low_two[t * tokens : (t + 1) * tokens], -t) for t in range(1, planes)
+        ]
+
         hidden_all = gather_dp(hidden_later)
         down_sum = dot(hidden_all, exchange_dp(grad_y_all, c, 1), ((0,), (0,))).astype(bf16)
 
@@ -477,21 +482,25 @@
             low_two_all = pick(low_two_all, c % halves, halves, 1)
 
         def of_member(member):
-            return jnp.where(member // halves == 0, grad_gate, grad_up)
+            return jnp.where(member // halves == 0, grad_gate_later, grad_up_later)
 
         gate_up_grads = [of_member(c)]
         for t in range(1, n_dp):
             gate_up_grads.append(shift_dp(of_member((c + t) % n_dp), t))
-        gate_up_grads = after(jnp.concatenate(gate_up_grads, axis=0), grad_low_two)
+        gate_up_grads = jnp.concatenate(gate_up_grads, axis=0)
         gate_up_sum = dot(low_two_all, gate_up_grads, ((0,), (0,))).astype(bf16)
 
+        hidden_last, down_sum, gate_up_sum = tie(hidden_later, down_sum, gate_up_sum)
         mixed = jnp.concatenate(
-            [dot(hidden_later, down_full[i]).astype(bf16) for i in range(n_dp)], axis=1
-        )
-        inner_two = after(inner_two, down_sum, gate_up_sum, mixed)
+            [dot(hidden_last, down_full[i]).astype(bf16) for i in range(n_dp)], axis=1
+        )
+        *inner_sent, mixed = tie(*inner_sent, mixed)
+        inner_two = functools.reduce(
+            jnp.add, [g.astype(f32) for g in inner_sent], grad_low_two[:tokens].astype(f32)
+        )
         grad_x_mid = grad_y + norm_back(order_back(inner_two), normed_two, inverse_two)
 
-        mixed = after(mixed, grad_x_mid)
+        mixed, grad_x_low = tie(mixed, grad_x_mid.astype(bf16))
         mixed_sent = [shift_z(mixed[t * tokens : (t + 1) * tokens], -t) for t in range(1, planes)]
         gate_up_sum = lax.psum_scatter(gate_up_sum, "seq", axis_index_groups=in_plane, tiled=True)
         down_sum = lax.psum_scatter(
@@ -499,28 +508,25 @@
         )
         gate_up_sum = gate_up_sum.reshape(planes, piece, ff_block)
 
-        grad_branch = gather_w(grad_x_mid.astype(bf16))
+        grad_branch = gather_w(grad_x_low)
+        mixed_sent[0], grad_branch = tie(mixed_sent[0], grad_branch)
         grad_o = functools.reduce(
             jnp.add,
             [dot(pick(grad_branch, i, n_dp, 1), out_full[i], ((1,), (1,))) for i in range(n_dp)],
         ).astype(bf16)
 
         out_part_sum = dot(gather_dp(o), exchange_dp(grad_branch, c, 1), ((0,), (0,))).astype(bf16)
-        out_sum = lax.psum_scatter(
-            after(out_part_sum, down_sum, gate_up_sum), "seq", axis_index_groups=across, tiled=True
-        )
+        grad_o_seq = by_seq(grad_o, 0)
+        *mixed_sent, grad_o_seq, out_part_sum = tie(*mixed_sent, grad_o_seq, out_part_sum)
+        out_sum = lax.psum_scatter(out_part_sum, "seq", axis_index_groups=across, tiled=True)
         out_sum = lax.ppermute(
             out_sum, "seq", [(GROUP * (i % planes) + i // planes, i) for i in range(n_seq)]
         )
         grad_w_out = jnp.concatenate(collect_dp(out_sum, c), axis=1).astype(f32)
 
-        grad_o_seq = by_seq(grad_o, 0)
         mixed = functools.reduce(
-            jnp.add,
-            [after(g, grad_branch).astype(f32) for g in mixed_sent],
-            mixed[:tokens].astype(f32),
-        )
-        grad_o_seq = after(grad_o_seq, out_part_sum, mixed)
+            jnp.add, [g.astype(f32) for g in mixed_sent], mixed[:tokens].astype(f32)
+        )
         pieces = [
             attend_back(
                 seen, q_seq[i], grad_o_seq[i], o_seq[i], kk_seq[i], vv_seq[i], lse_seq[i], order
@@ -548,7 +554,6 @@
             )
             for i in range(n_dp)
         ]
-        mixed = after(mixed, kv_pre)
         outputs = (x_mid + mixed).astype(bf16).reshape(seqs, rows, width)
 
         grad_low_one = functools.reduce(
@@ -560,12 +565,12 @@
 
         qkv_sum = dot(
             gather_dp(low_one),
-            exchange_dp(after(jnp.concatenate(pre, axis=1), grad_low_one), c, 1),
+            exchange_dp(jnp.concatenate(pre, axis=1), c, 1),
             ((0,), (0,)),
         ).astype(bf16)
-        gate_up_late = after(gate_up_sum, qkv_sum)
+        gate_up_late, qkv_sum = tie(gate_up_sum, qkv_sum)
         qkv_sum = lax.psum_scatter(
-            after(qkv_sum, out_sum), "seq", axis_index_groups=across, tiled=True
+            qkv_sum, "seq", axis_index_groups=across, tiled=True
         )
         qkv_sum = qkv_sum.reshape(GROUP, shard, part_width)
         qkv_sum = lax.all_to_all(qkv_sum, "seq", 0, 0, axis_index_groups=in_plane, tiled=True)

time: 708 us -> 667 us (0.942)
  waiting for transfers between devices: 281 us -> 232 us
  starting transfers between devices: 151 us -> 172 us
    ppermute x27, waiting for transfers between devices: 186 us -> 110 us  [shift_z(): lax.ppermute(value, 'seq', [(s, (s + GROUP * t) % n_seq) for s in range(n...]
    reduce_scatter x1, waiting for transfers between devices: 0.01 us -> 41.1 us  [body(): lax.psum_scatter(gate_up_sum, 'seq', axis_index_groups=in_plane, tiled=True)]
    reduce_scatter x1, waiting for transfers between devices: 0.01 us -> 37.4 us  [body(): lax.psum_scatter(down_sum, 'seq', axis_index_groups=in_plane, tiled=True)]
    ppermute x17, waiting for transfers between devices: 51.2 us -> 17.3 us  [xor_w(): return lax.ppermute(value, 'seq', [(s, s ^ j) for s in range(n_seq)])]
    ppermute x27, starting transfers between devices: 81.6 us -> 107 us  [shift_z(): lax.ppermute(value, 'seq', [(s, (s + GROUP * t) % n_seq) for s in range(n...]
    reduce_scatter x2, waiting for transfers between devices: 34.8 us -> 18.7 us  [the longest x1 18.7 us: body(): lax.psum_scatter(qkv_sum, 'seq', axis_index_groups=across, tiled=True)]
    ppermute x17, starting transfers between devices: 40.4 us -> 24.5 us  [xor_w(): return lax.ppermute(value, 'seq', [(s, s ^ j) for s in range(n_seq)])]
    unnamed x203 -> x207, local copies, waits for them, and re-layouts: 39.1 us -> 25.5 us
  transfers between devices with their start and end apart: 68 -> 68, of which waited for: 24 -> 19; matrix products, arithmetic and copies ran while one was open for 25% -> 29% of each run, Pallas kernels for 3% -> 3%
where the time goes in v5:
time: 667 us; the launch traced here: 658 us
  waiting for transfers between devices  232 us (35%)
  starting transfers between devices  172 us (26%)
  local copies, waits for them, and re-layouts  86.3 us (13%)
  matrix products  72.6 us (11%)
  other arithmetic  60.5 us (9%)
  Pallas kernels  17.9 us (3%)
  between operations  16.7 us (3%)
    ppermute x27, waiting for transfers between devices, shift_z(): lax.ppermute(value, 'seq', [(s, (s + GROUP * t) % n_seq) for s in range(n...  110 us
    ppermute x27, starting transfers between devices, shift_z(): lax.ppermute(value, 'seq', [(s, (s + GROUP * t) % n_seq) for s in range(n...  107 us
    dot_general x20, matrix products, dot(): lax.dot_general(left, right, (contract, ((), ())), preferred_element_type...  72.6 us
    reduce_scatter x1, waiting for transfers between devices, body(): lax.psum_scatter(gate_up_sum, 'seq', axis_index_groups=in_plane, tiled=True)  41.1 us
    reduce_scatter x1, waiting for transfers between devices, body(): lax.psum_scatter(down_sum, 'seq', axis_index_groups=in_plane, tiled=True)  37.4 us
    ppermute x13, starting transfers between devices, shift_dp(): return lax.ppermute(value, 'dp', [(c, (c + t) % n_dp) for c in range(n_dp)])  29.1 us
    unnamed x207, local copies, waits for them, and re-layouts  25.5 us
    ppermute x17, starting transfers between devices, xor_w(): return lax.ppermute(value, 'seq', [(s, s ^ j) for s in range(n_seq)])  24.5 us
  transfers between devices with their start and end apart: 68, of which 19 were waited for; matrix products, arithmetic and copies ran while one was open for 29% of the time, Pallas kernels for 3%

profile of v5, /device:TPU:1, one launch (start us, length us, event | category | flops | bytes accessed | tf_op | source)
XLA Modules:
  0.0 657.7 jit_solution(13365524398888002753)
XLA Ops:
  32.7 9.6 %collective-permute-done.3 = bf16[512,320]{0,1:T(8,128)(2,1)S(1)} collective-permute-done((bf16[512,320]{0,1:T(8,128)(2,1)S(1)}, bf16[512,320]{0,1:T(8,128)(2,1)S(1)}, u32[]{:S(2)}, u32[]{:S(2)}) %collective-permute-start.3) | collective-permute-done | bytes 327712 | tf_op jit(solution)/shard_map/ppermute | solution.py:256
  42.3 7.6 %collective-permute-done.4 = bf16[512,320]{0,1:T(8,128)(2,1)S(1)} collective-permute-done((bf16[512,320]{0,1:T(8,128)(2,1)S(1)}, bf16[512,320]{0,1:T(8,128)(2,1)S(1)}, u32[]{:S(2)}, u32[]{:S(2)}) %collective-permute-start.4) | collective-permute-done | bytes 327712 | tf_op jit(solution)/shard_map/ppermute | solution.py:256
  54.1 8.8 %collective-permute-start.8 = (bf16[128,1408]{1,0:T(8,128)(2,1)}, bf16[128,1408]{1,0:T(8,128)(2,1)}, u32[]{:S(2)}, u32[]{:S(2)}) collective-permute-start(bf16[128,1408]{1,0:T(8,128)(2,1)} %get-tuple-element.177), channel_id=1, source_target_pairs={{0,12},{1,13},{2,14},{3,15},{4,0},{5,1},{6,2},{7,3},{8,4},{9,5},{1... | collective-permute-start | bytes 1081352 | tf_op jit(solution)/shard_map/ppermute | solution.py:256
  66.7 8.5 %collective-permute-done.11 = bf16[64,2048]{1,0:T(8,128)(2,1)S(1)} collective-permute-done((bf16[64,2048]{1,0:T(8,128)(2,1)S(1)}, bf16[64,2048]{1,0:T(8,128)(2,1)S(1)}, u32[]{:S(2)}, u32[]{:S(2)}) %collective-permute-start.11) | collective-permute-done | bytes 262176 | tf_op jit(solution)/shard_map/ppermute | solution.py:253
  116.9 5.7 collective-permute-done.16
  122.6 8.6 %collective-permute-done.15 = bf16[512,128]{1,0:T(8,128)(2,1)S(1)} collective-permute-done((bf16[512,128]{1,0:T(8,128)(2,1)S(1)}, bf16[512,128]{1,0:T(8,128)(2,1)S(1)}, u32[]{:S(2)}, u32[]{:S(2)}) %collective-permute-start.15) | collective-permute-done | bytes 131104 | tf_op jit(solution)/shard_map/ppermute | solution.py:256
  134.8 7.6 %attend.1 = (bf16[512,512]{1,0:T(8,128)(2,1)}, f32[4,8,1024]{2,1,0:T(8,128)}) custom-call(s32[1]{0:T(128)} %bitcast.1.seen_ref, bf16[512,512]{1,0:T(8,128)(2,1)} %multiply_convert_fusion.3.q_ref, bf16[4,512,128]{2,1,0:T(8,128)(2,1)} %get-tuple-element.243.kk_ref, bf16[4,512,128]{2,1,0:T(8,128)(2,1)} %get-tuple-element.244.vv_ref, ...), custom_call_target="tpu_custom_call" | custom-call | tf_op jit(solution)/shard_map/attend/pallas_call | solution.py:136
  145.6 7.8 %collective-permute-start.18 = (bf16[128,2048]{1,0:T(8,128)(2,1)S(1)}, bf16[128,2048]{1,0:T(8,128)(2,1)S(1)}, u32[]{:S(2)}, u32[]{:S(2)}) collective-permute-start(bf16[128,2048]{1,0:T(8,128)(2,1)S(1)} %get-tuple-element.157), channel_id=1, source_target_pairs={{0,1},{1,0},{2,3},{3,2},{4,5},{5,4},{6,7},{7,6},{8,9},{9,8},{10,11... | collective-permute-start | bytes 1572872 | tf_op jit(solution)/shard_map/ppermute | solution.py:253
  154.6 21.6 %collective-permute-done.22 = bf16[128,2048]{1,0:T(8,128)(2,1)} collective-permute-done((bf16[128,2048]{1,0:T(8,128)(2,1)S(1)}, bf16[128,2048]{1,0:T(8,128)(2,1)}, u32[]{:S(2)}, u32[]{:S(2)}) %collective-permute-start.22) | collective-permute-done | bytes 524320 | tf_op jit(solution)/shard_map/ppermute | solution.py:256
  181.3 30.0 %collective-permute-start.26 = (bf16[128,2048]{1,0:T(8,128)(2,1)S(1)}, bf16[128,2048]{1,0:T(8,128)(2,1)S(1)}, u32[]{:S(2)}, u32[]{:S(2)}) collective-permute-start(bf16[128,2048]{1,0:T(8,128)(2,1)S(1)} %constant_dynamic-update-slice_fusion.12), channel_id=1, source_target_pairs={{0,12},{1,13},{2,14},{3,15},{4,0},{5,1},{6,2},{7,3},{8,4},{9,5},{1... | collective-permute-start | bytes 1572872 | tf_op jit(solution)/shard_map/ppermute | solution.py:256
  216.4 17.8 %collective-permute-done.24 = bf16[128,2048]{1,0:T(8,128)(2,1)S(1)} collective-permute-done((bf16[128,2048]{1,0:T(8,128)(2,1)S(1)}, bf16[128,2048]{1,0:T(8,128)(2,1)S(1)}, u32[]{:S(2)}, u32[]{:S(2)}) %collective-permute-start.24) | collective-permute-done | bytes 524320 | tf_op jit(solution)/shard_map/ppermute | solution.py:256
  238.9 19.6 %collective-permute-start.32 = (bf16[512,2048]{1,0:T(8,128)(2,1)}, bf16[512,2048]{1,0:T(8,128)(2,1)}, u32[]{:S(2)}, u32[]{:S(2)}) collective-permute-start(bf16[512,2048]{1,0:T(8,128)(2,1)} %get-tuple-element.205), channel_id=1, source_target_pairs={{0,16},{16,0},{1,17},{17,1},{2,18},{18,2},{3,19},{19,3},{4,20},{20... | collective-permute-start | bytes 6291464 | tf_op jit(solution)/shard_map/ppermute | solution.py:259
  258.5 10.0 %fusion.92 = (bf16[4,4,128,1408]{3,2,1,0:T(8,128)(2,1)}, bf16[4,4,128,1408]{3,2,1,0:T(8,128)(2,1)}) fusion(bf16[8,4,128,1408]{3,2,1,0:T(8,128)(2,1)} %all-gather.6.cloned.1.call-done), kind=kLoop, calls=%fused_computation.333 | loop fusion | bytes 23068672 | tf_op jit(solution)/shard_map/slice | solution.py:413
  268.6 6.5 fusion.101
  275.1 6.7 %fusion.100 = f32[512,1408]{1,0:T(8,128)} fusion(bf16[512,2048]{1,0:T(8,128)(2,1)} %get-tuple-element.205, bf16[2048,1408]{1,0:T(8,128)(2,1)S(1)} %bitcast.173), kind=kOutput, calls=%fused_computation.342 | convolution fusion | flops 2952790016 | bytes 10747904 | tf_op jit(solution)/shard_map/dot_general | solution.py:26
  281.9 5.5 multiply_convert_fusion
  290.9 4.6 add_convert_fusion.1
  312.9 10.0 %convolution_convert_fusion = bf16[2048,1408]{1,0:T(8,128)(2,1)} fusion(bf16[1024,2048]{1,0:T(8,128)(2,1)S(1)} %constant_dynamic-update-slice_fusion.32, bf16[512,1408]{1,0:T(8,128)(2,1)} %collective-permute-done.33, bf16[512,1408]{1,0:T(8,128)(2,1)S(1)} %copy-done.32), kind=kOutput, calls=%fused_computation | convolution fusion | flops 5914230784 | bytes 12845056 | tf_op jit(solution)/shard_map/dot_general | solution.py:26
  322.8 7.2 %convolution_convert_fusion.1 = bf16[1408,1024]{1,0:T(8,128)(2,1)} fusion(bf16[512,1408]{1,0:T(8,128)(2,1)} %collective-permute-done.30, bf16[512,1408]{1,0:T(8,128)(2,1)} %get-tuple-element.81, bf16[512,1024]{1,0:T(8,128)(2,1)} %collective-permute-done.31, bf16[512,1024]{1,0:T(8,128)(2,1)} %get-tuple-element.152), kind=kOutput, calls=%fused_computation.3 | convolution fusion | flops 2964193280 | bytes 7864320 | tf_op jit(solution)/shard_map/dot_general | solution.py:26
  337.6 5.5 collective-permute-done.28
  351.5 15.5 %collective-permute-start.34 = (bf16[128,2048]{1,0:T(8,128)(2,1)S(1)}, bf16[128,2048]{1,0:T(8,128)(2,1)}, u32[]{:S(2)}, u32[]{:S(2)}) collective-permute-start(bf16[128,2048]{1,0:T(8,128)(2,1)S(1)} %get-tuple-element.151), channel_id=1, source_target_pairs={{0,12},{1,13},{2,14},{3,15},{4,0},{5,1},{6,2},{7,3},{8,4},{9,5},{1... | collective-permute-start | bytes 1572872 | tf_op jit(solution)/shard_map/ppermute | solution.py:256
  367.4 5.6 collective-permute-done.37
  379.5 5.1 collective-permute-start.40
  392.2 7.8 %collective-permute-done.40 = bf16[128,2048]{1,0:T(8,128)(2,1)} collective-permute-done((bf16[128,2048]{1,0:T(8,128)(2,1)}, bf16[128,2048]{1,0:T(8,128)(2,1)}, u32[]{:S(2)}, u32[]{:S(2)}) %collective-permute-start.40) | collective-permute-done | bytes 524320 | tf_op jit(solution)/shard_map/ppermute | solution.py:256
  400.0 22.6 %collective-permute-done.39 = bf16[128,2048]{1,0:T(8,128)(2,1)} collective-permute-done((bf16[128,2048]{1,0:T(8,128)(2,1)}, bf16[128,2048]{1,0:T(8,128)(2,1)}, u32[]{:S(2)}, u32[]{:S(2)}) %collective-permute-start.39) | collective-permute-done | bytes 524320 | tf_op jit(solution)/shard_map/ppermute | solution.py:256
  432.4 10.3 %attend_back.1 = (f32[512,512]{1,0:T(8,128)}, f32[4,512,128]{2,1,0:T(8,128)}, f32[4,512,128]{2,1,0:T(8,128)}) custom-call(s32[1]{0:T(128)} %bitcast.1.seen_ref, bf16[512,512]{1,0:T(8,128)(2,1)} %multiply_convert_fusion.3.q_ref, bf16[512,512]{1,0:T(8,128)(2,1)} %bitcast.188, bf16[512,512]{1,0:T(8,128)(2,1)} %get-tuple-element.66.o_ref, ...), custom_call_target="tpu_custom_call" | custom-call | tf_op jit(solution)/shard_map/attend_back/pallas_call | solution.py:166
  446.9 18.0 %collective-permute-start.43 = (bf16[512,128]{1,0:T(8,128)(2,1)}, bf16[512,128]{1,0:T(8,128)(2,1)}, u32[]{:S(2)}, u32[]{:S(2)}) collective-permute-start(bf16[512,128]{1,0:T(8,128)(2,1)} %get-tuple-element.183), channel_id=1, source_target_pairs={{0,12},{1,13},{2,14},{3,15},{4,0},{5,1},{6,2},{7,3},{8,4},{9,5},{1... | collective-permute-start | bytes 393224 | tf_op jit(solution)/shard_map/ppermute | solution.py:256
  496.2 41.1 %reduce-scatter.5.cloned.1.call-done = bf16[512,1408]{1,0:T(8,128)(2,1)} async-done(((bf16[2048,1408]{1,0:T(8,128)(2,1)}), bf16[512,1408]{1,0:T(8,128)(2,1)}) %reduce-scatter.5.cloned.1.call-update) | async-done | bytes 1441808 | tf_op jit(solution)/shard_map/reduce_scatter | solution.py:505
  539.8 5.9 collective-permute-start.55
  548.6 37.4 %reduce-scatter.11.cloned.1.call-done = bf16[352,1024]{1,0:T(8,128)(2,1)} async-done(((bf16[1408,1024]{1,0:T(8,128)(2,1)}), bf16[352,1024]{1,0:T(8,128)(2,1)}) %reduce-scatter.11.cloned.1.call-update) | async-done | bytes 720912 | tf_op jit(solution)/shard_map/reduce_scatter | solution.py:506
  601.3 18.7 %reduce-scatter.7.cloned.1.call-done = bf16[512,320]{0,1:T(8,128)(2,1)} async-done(((bf16[2048,320]{0,1:T(8,128)(2,1)}), bf16[512,320]{0,1:T(8,128)(2,1)}) %reduce-scatter.7.cloned.1.call-update) | async-done | bytes 327696 | tf_op jit(solution)/shard_map/reduce_scatter | solution.py:572
  633.0 6.2 convert_multiply_fusion
  (467 shorter events, 237.7 us)
Async XLA Ops:
  7.2 78.2 %all-gather.8.cloned.1.call-start = ((), (), s32[]{:S(2)}) async-start(), calls=%async_computation.11 | async-start | bytes 6488064 | tf_op jit(solution)/shard_map/all_gather | solution.py:365
  18.3 124.1 %all-gather.10.cloned.1.call-start = ((), (), s32[]{:S(2)}) async-start(), calls=%async_computation.12 | async-start | bytes 2359296 | tf_op jit(solution)/shard_map/all_gather | solution.py:370
  28.9 34.0 %collective-permute-start.10 = (bf16[128,2048]{1,0:T(8,128)(2,1)}, bf16[128,2048]{1,0:T(8,128)(2,1)S(1)}, u32[]{:S(2)}, u32[]{:S(2)}) collective-permute-start(bf16[128,2048]{1,0:T(8,128)(2,1)} %fusion.22), channel_id=1, source_target_pairs={{0,2},{1,3},{2,0},{3,1},{4,6},{5,7},{6,4},{7,5},{8,10},{9,11},{10,... | collective-permute-start | bytes 1572872 | tf_op jit(solution)/shard_map/ppermute | solution.py:253
  30.3 36.1 %collective-permute-start.9 = (bf16[128,2048]{1,0:T(8,128)(2,1)}, bf16[128,2048]{1,0:T(8,128)(2,1)S(1)}, u32[]{:S(2)}, u32[]{:S(2)}) collective-permute-start(bf16[128,2048]{1,0:T(8,128)(2,1)} %fusion.22), channel_id=1, source_target_pairs={{0,1},{1,0},{2,3},{3,2},{4,5},{5,4},{6,7},{7,6},{8,9},{9,8},{10,11... | collective-permute-start | bytes 1572872 | tf_op jit(solution)/shard_map/ppermute | solution.py:253
  50.2 31.1 %collective-permute-start.13 = (bf16[2048,320]{0,1:T(8,128)(2,1)S(1)}, bf16[2048,320]{0,1:T(8,128)(2,1)S(1)}, u32[]{:S(2)}, u32[]{:S(2)}) collective-permute-start(bf16[2048,320]{0,1:T(8,128)(2,1)S(1)} %constant_dynamic-slice_fusion.11), channel_id=1, source_target_pairs={{0,16},{16,0},{1,17},{17,1},{2,18},{18,2},{3,19},{19,3},{4,20},{20... | collective-permute-start | bytes 3932168 | tf_op jit(solution)/shard_map/ppermute | solution.py:259
  51.7 33.8 %collective-permute-start.17 = (bf16[128,1024]{1,0:T(8,128)(2,1)S(1)}, bf16[128,1024]{1,0:T(8,128)(2,1)}, u32[]{:S(2)}, u32[]{:S(2)}) collective-permute-start(bf16[128,1024]{1,0:T(8,128)(2,1)S(1)} %constant_dynamic-slice_fusion.12), channel_id=1, source_target_pairs={{0,0},{1,4},{2,8},{3,12},{4,1},{5,5},{6,9},{7,13},{8,2},{9,6},{10,... | collective-permute-start | bytes 786440 | tf_op jit(solution)/shard_map/ppermute | solution.py:357
  54.1 52.6 %collective-permute-start.8 = (bf16[128,1408]{1,0:T(8,128)(2,1)}, bf16[128,1408]{1,0:T(8,128)(2,1)}, u32[]{:S(2)}, u32[]{:S(2)}) collective-permute-start(bf16[128,1408]{1,0:T(8,128)(2,1)} %get-tuple-element.177), channel_id=1, source_target_pairs={{0,12},{1,13},{2,14},{3,15},{4,0},{5,1},{6,2},{7,3},{8,4},{9,5},{1... | collective-permute-start | bytes 1081352 | tf_op jit(solution)/shard_map/ppermute | solution.py:256
  75.2 31.5 %collective-permute-start.7 = (bf16[128,1408]{1,0:T(8,128)(2,1)}, bf16[128,1408]{1,0:T(8,128)(2,1)}, u32[]{:S(2)}, u32[]{:S(2)}) collective-permute-start(bf16[128,1408]{1,0:T(8,128)(2,1)} %get-tuple-element.178), channel_id=1, source_target_pairs={{0,8},{1,9},{2,10},{3,11},{4,12},{5,13},{6,14},{7,15},{8,0},{9,1},... | collective-permute-start | bytes 1081352 | tf_op jit(solution)/shard_map/ppermute | solution.py:256
  78.7 28.0 %collective-permute-start.6 = (bf16[128,1408]{1,0:T(8,128)(2,1)}, bf16[128,1408]{1,0:T(8,128)(2,1)}, u32[]{:S(2)}, u32[]{:S(2)}) collective-permute-start(bf16[128,1408]{1,0:T(8,128)(2,1)} %get-tuple-element.179), channel_id=1, source_target_pairs={{0,4},{1,5},{2,6},{3,7},{4,8},{5,9},{6,10},{7,11},{8,12},{9,13},{1... | collective-permute-start | bytes 1081352 | tf_op jit(solution)/shard_map/ppermute | solution.py:256
  85.4 173.1 %all-gather.6.cloned.1.call-start = ((), (), s32[]{:S(2)}) async-start(), calls=%async_computation.6 | async-start | bytes 12976128 | tf_op jit(solution)/shard_map/all_gather | solution.py:409
  111.2 383.4 %reduce-scatter.9.cloned.1.call-start = ((), (), s32[]{:S(2)}) async-start(), calls=%async_computation.9 | async-start | bytes 1310720 | tf_op jit(solution)/shard_map/reduce_scatter | solution.py:521
  131.4 44.8 %collective-permute-start.22 = (bf16[128,2048]{1,0:T(8,128)(2,1)S(1)}, bf16[128,2048]{1,0:T(8,128)(2,1)}, u32[]{:S(2)}, u32[]{:S(2)}) collective-permute-start(bf16[128,2048]{1,0:T(8,128)(2,1)S(1)} %bitcast_convert_fusion), channel_id=1, source_target_pairs={{0,8},{1,9},{2,10},{3,11},{4,12},{5,13},{6,14},{7,15},{8,0},{9,1},... | collective-permute-start | bytes 1572872 | tf_op jit(solution)/shard_map/ppermute | solution.py:256
  131.5 44.7 %collective-permute-start.21 = (bf16[128,2048]{1,0:T(8,128)(2,1)S(1)}, bf16[128,2048]{1,0:T(8,128)(2,1)}, u32[]{:S(2)}, u32[]{:S(2)}) collective-permute-start(bf16[128,2048]{1,0:T(8,128)(2,1)S(1)} %bitcast_convert_fusion), channel_id=1, source_target_pairs={{0,4},{1,5},{2,6},{3,7},{4,8},{5,9},{6,10},{7,11},{8,12},{9,13},{1... | collective-permute-start | bytes 1572872 | tf_op jit(solution)/shard_map/ppermute | solution.py:256
  145.6 34.6 %collective-permute-start.18 = (bf16[128,2048]{1,0:T(8,128)(2,1)S(1)}, bf16[128,2048]{1,0:T(8,128)(2,1)S(1)}, u32[]{:S(2)}, u32[]{:S(2)}) collective-permute-start(bf16[128,2048]{1,0:T(8,128)(2,1)S(1)} %get-tuple-element.157), channel_id=1, source_target_pairs={{0,1},{1,0},{2,3},{3,2},{4,5},{5,4},{6,7},{7,6},{8,9},{9,8},{10,11... | collective-permute-start | bytes 1572872 | tf_op jit(solution)/shard_map/ppermute | solution.py:253
  181.3 54.7 %collective-permute-start.26 = (bf16[128,2048]{1,0:T(8,128)(2,1)S(1)}, bf16[128,2048]{1,0:T(8,128)(2,1)S(1)}, u32[]{:S(2)}, u32[]{:S(2)}) collective-permute-start(bf16[128,2048]{1,0:T(8,128)(2,1)S(1)} %constant_dynamic-update-slice_fusion.12), channel_id=1, source_target_pairs={{0,12},{1,13},{2,14},{3,15},{4,0},{5,1},{6,2},{7,3},{8,4},{9,5},{1... | collective-permute-start | bytes 1572872 | tf_op jit(solution)/shard_map/ppermute | solution.py:256
  238.9 62.2 %collective-permute-start.32 = (bf16[512,2048]{1,0:T(8,128)(2,1)}, bf16[512,2048]{1,0:T(8,128)(2,1)}, u32[]{:S(2)}, u32[]{:S(2)}) collective-permute-start(bf16[512,2048]{1,0:T(8,128)(2,1)} %get-tuple-element.205), channel_id=1, source_target_pairs={{0,16},{16,0},{1,17},{17,1},{2,18},{18,2},{3,19},{19,3},{4,20},{20... | collective-permute-start | bytes 6291464 | tf_op jit(solution)/shard_map/ppermute | solution.py:259
  304.5 33.1 %collective-permute-start.29 = (bf16[128,2048]{1,0:T(8,128)(2,1)}, bf16[128,2048]{1,0:T(8,128)(2,1)S(1)}, u32[]{:S(2)}, u32[]{:S(2)}) collective-permute-start(bf16[128,2048]{1,0:T(8,128)(2,1)} %get-tuple-element.154), channel_id=1, source_target_pairs={{0,4},{1,5},{2,6},{3,7},{4,8},{5,9},{6,10},{7,11},{8,12},{9,13},{1... | collective-permute-start | bytes 1572872 | tf_op jit(solution)/shard_map/ppermute | solution.py:256
  308.5 34.6 %collective-permute-start.28 = (bf16[128,2048]{1,0:T(8,128)(2,1)}, bf16[128,2048]{1,0:T(8,128)(2,1)}, u32[]{:S(2)}, u32[]{:S(2)}) collective-permute-start(bf16[128,2048]{1,0:T(8,128)(2,1)} %get-tuple-element.155), channel_id=1, source_target_pairs={{0,8},{1,9},{2,10},{3,11},{4,12},{5,13},{6,14},{7,15},{8,0},{9,1},... | collective-permute-start | bytes 1572872 | tf_op jit(solution)/shard_map/ppermute | solution.py:256
  310.6 32.6 %collective-permute-start.27 = (bf16[128,2048]{1,0:T(8,128)(2,1)}, bf16[128,2048]{1,0:T(8,128)(2,1)}, u32[]{:S(2)}, u32[]{:S(2)}) collective-permute-start(bf16[128,2048]{1,0:T(8,128)(2,1)} %get-tuple-element.156), channel_id=1, source_target_pairs={{0,12},{1,13},{2,14},{3,15},{4,0},{5,1},{6,2},{7,3},{8,4},{9,5},{1... | collective-permute-start | bytes 1572872 | tf_op jit(solution)/shard_map/ppermute | solution.py:256
  384.5 38.0 %collective-permute-start.39 = (bf16[128,2048]{1,0:T(8,128)(2,1)}, bf16[128,2048]{1,0:T(8,128)(2,1)}, u32[]{:S(2)}, u32[]{:S(2)}) collective-permute-start(bf16[128,2048]{1,0:T(8,128)(2,1)} %get-tuple-element.150), channel_id=1, source_target_pairs={{0,8},{1,9},{2,10},{3,11},{4,12},{5,13},{6,14},{7,15},{8,0},{9,1},... | collective-permute-start | bytes 1572872 | tf_op jit(solution)/shard_map/ppermute | solution.py:256
  422.6 114.7 %reduce-scatter.5.cloned.1.call-start = ((), (), s32[]{:S(2)}) async-start(), calls=%async_computation.7 | async-start | bytes 7208960 | tf_op jit(solution)/shard_map/reduce_scatter | solution.py:505
  423.2 162.7 %reduce-scatter.11.cloned.1.call-start = ((), (), s32[]{:S(2)}) async-start(), calls=%async_computation.10 | async-start | bytes 3604480 | tf_op jit(solution)/shard_map/reduce_scatter | solution.py:506
  431.1 188.9 %reduce-scatter.7.cloned.1.call-start = ((), (), s32[]{:S(2)}) async-start(), calls=%async_computation.8 | async-start | bytes 1638400 | tf_op jit(solution)/shard_map/reduce_scatter | solution.py:572
  446.9 32.5 %collective-permute-start.43 = (bf16[512,128]{1,0:T(8,128)(2,1)}, bf16[512,128]{1,0:T(8,128)(2,1)}, u32[]{:S(2)}, u32[]{:S(2)}) collective-permute-start(bf16[512,128]{1,0:T(8,128)(2,1)} %get-tuple-element.183), channel_id=1, source_target_pairs={{0,12},{1,13},{2,14},{3,15},{4,0},{5,1},{6,2},{7,3},{8,4},{9,5},{1... | collective-permute-start | bytes 393224 | tf_op jit(solution)/shard_map/ppermute | solution.py:256
  489.2 50.6 %collective-permute-start.46 = (bf16[128,2048]{1,0:T(8,128)(2,1)}, bf16[128,2048]{1,0:T(8,128)(2,1)S(1)}, u32[]{:S(2)}, u32[]{:S(2)}) collective-permute-start(bf16[128,2048]{1,0:T(8,128)(2,1)} %get-tuple-element.144), channel_id=1, source_target_pairs={{0,1},{1,0},{2,3},{3,2},{4,5},{5,4},{6,7},{7,6},{8,9},{9,8},{10,11... | collective-permute-start | bytes 1572872 | tf_op jit(solution)/shard_map/ppermute | solution.py:253
  490.1 55.6 %collective-permute-start.48 = (bf16[128,2048]{1,0:T(8,128)(2,1)S(1)}, bf16[128,2048]{1,0:T(8,128)(2,1)S(1)}, u32[]{:S(2)}, u32[]{:S(2)}) collective-permute-start(bf16[128,2048]{1,0:T(8,128)(2,1)S(1)} %get-tuple-element.145), channel_id=1, source_target_pairs={{0,3},{1,2},{2,1},{3,0},{4,7},{5,6},{6,5},{7,4},{8,11},{9,10},{10,... | collective-permute-start | bytes 1572872 | tf_op jit(solution)/shard_map/ppermute | solution.py:253
  491.5 54.2 %collective-permute-start.47 = (bf16[128,2048]{1,0:T(8,128)(2,1)S(1)}, bf16[128,2048]{1,0:T(8,128)(2,1)S(1)}, u32[]{:S(2)}, u32[]{:S(2)}) collective-permute-start(bf16[128,2048]{1,0:T(8,128)(2,1)S(1)} %get-tuple-element.146), channel_id=1, source_target_pairs={{0,2},{1,3},{2,0},{3,1},{4,6},{5,7},{6,4},{7,5},{8,10},{9,11},{10,... | collective-permute-start | bytes 1572872 | tf_op jit(solution)/shard_map/ppermute | solution.py:253
  494.5 52.7 %collective-permute-start.52 = (bf16[128,1024]{1,0:T(8,128)(2,1)}, bf16[128,1024]{1,0:T(8,128)(2,1)S(1)}, u32[]{:S(2)}, u32[]{:S(2)}) collective-permute-start(bf16[128,1024]{1,0:T(8,128)(2,1)} %reduce-scatter.9.cloned.1.call-done), channel_id=1, source_target_pairs={{0,0},{4,1},{8,2},{12,3},{1,4},{5,5},{9,6},{13,7},{2,8},{6,9},{10,... | collective-permute-start | bytes 786440 | tf_op jit(solution)/shard_map/ppermute | solution.py:522
  539.8 47.0 %collective-permute-start.56 = (bf16[128,1408]{1,0:T(8,128)(2,1)}, bf16[128,1408]{1,0:T(8,128)(2,1)}, u32[]{:S(2)}, u32[]{:S(2)}) collective-permute-start(bf16[128,1408]{1,0:T(8,128)(2,1)} %get-tuple-element.173), channel_id=1, source_target_pairs={{0,12},{1,13},{2,14},{3,15},{4,0},{5,1},{6,2},{7,3},{8,4},{9,5},{1... | collective-permute-start | bytes 1081352 | tf_op jit(solution)/shard_map/ppermute | solution.py:256
  539.8 47.0 %collective-permute-start.55 = (bf16[128,1408]{1,0:T(8,128)(2,1)}, bf16[128,1408]{1,0:T(8,128)(2,1)}, u32[]{:S(2)}, u32[]{:S(2)}) collective-permute-start(bf16[128,1408]{1,0:T(8,128)(2,1)} %get-tuple-element.174), channel_id=1, source_target_pairs={{0,8},{1,9},{2,10},{3,11},{4,12},{5,13},{6,14},{7,15},{8,0},{9,1},... | collective-permute-start | bytes 1081352 | tf_op jit(solution)/shard_map/ppermute | solution.py:256
  545.7 41.1 %collective-permute-start.54 = (bf16[128,1408]{1,0:T(8,128)(2,1)}, bf16[128,1408]{1,0:T(8,128)(2,1)S(1)}, u32[]{:S(2)}, u32[]{:S(2)}) collective-permute-start(bf16[128,1408]{1,0:T(8,128)(2,1)} %get-tuple-element.175), channel_id=1, source_target_pairs={{0,4},{1,5},{2,6},{3,7},{4,8},{5,9},{6,10},{7,11},{8,12},{9,13},{1... | collective-permute-start | bytes 1081352 | tf_op jit(solution)/shard_map/ppermute | solution.py:256
  547.3 46.3 %collective-permute-start.53 = (bf16[128,1024]{1,0:T(8,128)(2,1)S(1)}, bf16[128,1024]{1,0:T(8,128)(2,1)}, u32[]{:S(2)}, u32[]{:S(2)}) collective-permute-start(bf16[128,1024]{1,0:T(8,128)(2,1)S(1)} %collective-permute-done.52), channel_id=1, source_target_pairs={{0,16},{16,0},{1,17},{17,1},{2,18},{18,2},{3,19},{19,3},{4,20},{20... | collective-permute-start | bytes 786440 | tf_op jit(solution)/shard_map/ppermute | solution.py:259
  (105 other events, 1071.8 us)
Sparse Core Ops, SparseCore 0:
  10.5 51.6 all-gather.7
  85.6 37.7 all-gather.9
  125.8 86.6 all-gather.5
  422.7 23.8 reduce-scatter.8
  449.5 87.8 reduce-scatter.4
  540.8 45.0 reduce-scatter.10
  588.8 31.1 reduce-scatter.6

commit v6 on v5

--- a/solution.py
+++ b/solution.py
@@ -490,18 +490,18 @@
         gate_up_grads = jnp.concatenate(gate_up_grads, axis=0)
         gate_up_sum = dot(low_two_all, gate_up_grads, ((0,), (0,))).astype(bf16)
 
-        hidden_last, down_sum, gate_up_sum = tie(hidden_later, down_sum, gate_up_sum)
+        inner_sent[0], gate_up_sum = tie(inner_sent[0], gate_up_sum)
+        *inner_rest, down_sum = tie(*inner_sent[1:], down_sum)
+        inner_sent = [inner_sent[0]] + inner_rest
+        inner_two = functools.reduce(
+            jnp.add, [g.astype(f32) for g in inner_sent], grad_low_two[:tokens].astype(f32)
+        )
+        grad_x_mid = grad_y + norm_back(order_back(inner_two), normed_two, inverse_two)
+
+        hidden_last, grad_x_low = tie(hidden_later, grad_x_mid.astype(bf16))
         mixed = jnp.concatenate(
             [dot(hidden_last, down_full[i]).astype(bf16) for i in range(n_dp)], axis=1
         )
-        *inner_sent, mixed = tie(*inner_sent, mixed)
-        inner_two = functools.reduce(
-            jnp.add, [g.astype(f32) for g in inner_sent], grad_low_two[:tokens].astype(f32)
-        )
-        grad_x_mid = grad_y + norm_back(order_back(inner_two), normed_two, inverse_two)
-
-        mixed, grad_x_low = tie(mixed, grad_x_mid.astype(bf16))
-        mixed_sent = [shift_z(mixed[t * tokens : (t + 1) * tokens], -t) for t in range(1, planes)]
         gate_up_sum = lax.psum_scatter(gate_up_sum, "seq", axis_index_groups=in_plane, tiled=True)
         down_sum = lax.psum_scatter(
             down_sum, "seq", axis_index_groups=in_plane, tiled=True
@@ -509,7 +509,8 @@
         gate_up_sum = gate_up_sum.reshape(planes, piece, ff_block)
 
         grad_branch = gather_w(grad_x_low)
-        mixed_sent[0], grad_branch = tie(mixed_sent[0], grad_branch)
+        mixed, grad_branch = tie(mixed, grad_branch)
+        mixed_sent = [shift_z(mixed[t * tokens : (t + 1) * tokens], -t) for t in range(1, planes)]
         grad_o = functools.reduce(
             jnp.add,
             [dot(pick(grad_branch, i, n_dp, 1), out_full[i], ((1,), (1,))) for i in range(n_dp)],
@@ -517,23 +518,19 @@
 
         out_part_sum = dot(gather_dp(o), exchange_dp(grad_branch, c, 1), ((0,), (0,))).astype(bf16)
         grad_o_seq = by_seq(grad_o, 0)
-        *mixed_sent, grad_o_seq, out_part_sum = tie(*mixed_sent, grad_o_seq, out_part_sum)
+        gate_up_sum, out_part_sum = tie(gate_up_sum, out_part_sum)
         out_sum = lax.psum_scatter(out_part_sum, "seq", axis_index_groups=across, tiled=True)
-        out_sum = lax.ppermute(
-            out_sum, "seq", [(GROUP * (i % planes) + i // planes, i) for i in range(n_seq)]
-        )
-        grad_w_out = jnp.concatenate(collect_dp(out_sum, c), axis=1).astype(f32)
-
-        mixed = functools.reduce(
-            jnp.add, [g.astype(f32) for g in mixed_sent], mixed[:tokens].astype(f32)
-        )
         pieces = [
             attend_back(
                 seen, q_seq[i], grad_o_seq[i], o_seq[i], kk_seq[i], vv_seq[i], lse_seq[i], order
             )
             for i in range(seqs)
         ]
-        grad_q = from_seq(jnp.stack([one[0] for one in pieces]), 0) * HEAD_DIM ** (-0.5)
+        *mixed_sent, grad_q = tie(*mixed_sent, jnp.stack([one[0] for one in pieces]))
+        mixed = functools.reduce(
+            jnp.add, [g.astype(f32) for g in mixed_sent], mixed[:tokens].astype(f32)
+        )
+        grad_q = from_seq(grad_q, 0) * HEAD_DIM ** (-0.5)
         grad_kk = from_seq(jnp.stack([one[1] for one in pieces]), 1)
         grad_vv = from_seq(jnp.stack([one[2] for one in pieces]), 1)
         grad_kv = jnp.concatenate(
@@ -568,7 +565,12 @@
             exchange_dp(jnp.concatenate(pre, axis=1), c, 1),
             ((0,), (0,)),
         ).astype(bf16)
-        gate_up_late, qkv_sum = tie(gate_up_sum, qkv_sum)
+        gate_up_late, down_sum, out_sum, qkv_sum = tie(gate_up_sum, down_sum, out_sum, qkv_sum)
+        out_sum = lax.ppermute(
+            out_sum, "seq", [(GROUP * (i % planes) + i // planes, i) for i in range(n_seq)]
+        )
+        grad_w_out = jnp.concatenate(collect_dp(out_sum, c), axis=1).astype(f32)
+
         qkv_sum = lax.psum_scatter(
             qkv_sum, "seq", axis_index_groups=across, tiled=True
         )

time: 667 us -> 664 us (level)
  starting transfers between devices: 172 us -> 154 us
  waiting for transfers between devices: 232 us -> 245 us
    ppermute x27, waiting for transfers between devices: 110 us -> 202 us  [shift_z(): lax.ppermute(value, 'seq', [(s, (s + GROUP * t) % n_seq) for s in range(n...]
    reduce_scatter x1, waiting for transfers between devices: 41.1 us -> 0.01 us  [body(): lax.psum_scatter(gate_up_sum, 'seq', axis_index_groups=in_plane, tiled=True)]
    reduce_scatter x1, waiting for transfers between devices: 37.4 us -> 0.01 us  [body(): lax.psum_scatter(down_sum, 'seq', axis_index_groups=in_plane, tiled=True)]
    ppermute x27, starting transfers between devices: 107 us -> 86.3 us  [shift_z(): lax.ppermute(value, 'seq', [(s, (s + GROUP * t) % n_seq) for s in range(n...]
    reduce_scatter x1, waiting for transfers between devices: 18.7 us -> 0.01 us  [body(): lax.psum_scatter(qkv_sum, 'seq', axis_index_groups=across, tiled=True)]
    reduce_scatter x1, waiting for transfers between devices: 0.01 us -> 12.2 us  [body(): lax.psum_scatter(out_part_sum, 'seq', axis_index_groups=across, tiled=True)]
    ppermute x17, waiting for transfers between devices: 17.3 us -> 27 us  [xor_w(): return lax.ppermute(value, 'seq', [(s, s ^ j) for s in range(n_seq)])]
    unnamed x207 -> x217, local copies, waits for them, and re-layouts: 25.5 us -> 26.6 us
  transfers between devices with their start and end apart: 68 -> 68, of which waited for: 19 -> 21; matrix products, arithmetic and copies ran while one was open for 29% -> 30% of each run, Pallas kernels for 3% -> 3%
where the time goes in v6:
time: 664 us; the launch traced here: 654 us
  waiting for transfers between devices  245 us (37%)
  starting transfers between devices  154 us (23%)
  local copies, waits for them, and re-layouts  92.5 us (14%)
  matrix products  71.4 us (11%)
  other arithmetic  57.3 us (9%)
  Pallas kernels  17.9 us (3%)
  between operations  16.6 us (3%)
    ppermute x27, waiting for transfers between devices, shift_z(): lax.ppermute(value, 'seq', [(s, (s + GROUP * t) % n_seq) for s in range(n...  202 us
    ppermute x27, starting transfers between devices, shift_z(): lax.ppermute(value, 'seq', [(s, (s + GROUP * t) % n_seq) for s in range(n...  86.3 us
    dot_general x20, matrix products, dot(): lax.dot_general(left, right, (contract, ((), ())), preferred_element_type...  71.4 us
    ppermute x13, starting transfers between devices, shift_dp(): return lax.ppermute(value, 'dp', [(c, (c + t) % n_dp) for c in range(n_dp)])  28.3 us
    ppermute x17, starting transfers between devices, xor_w(): return lax.ppermute(value, 'seq', [(s, s ^ j) for s in range(n_seq)])  28.2 us
    ppermute x17, waiting for transfers between devices, xor_w(): return lax.ppermute(value, 'seq', [(s, s ^ j) for s in range(n_seq)])  27 us
    unnamed x217, local copies, waits for them, and re-layouts  26.6 us
  transfers between devices with their start and end apart: 68, of which 21 were waited for; matrix products, arithmetic and copies ran while one was open for 30% of the time, Pallas kernels for 3%

profile of v6, /device:TPU:1, one launch (start us, length us, event | category | flops | bytes accessed | tf_op | source)
XLA Modules:
  0.0 654.4 jit_solution(11284599998853779610)
XLA Ops:
  32.7 9.6 %collective-permute-done.3 = bf16[512,320]{0,1:T(8,128)(2,1)S(1)} collective-permute-done((bf16[512,320]{0,1:T(8,128)(2,1)S(1)}, bf16[512,320]{0,1:T(8,128)(2,1)S(1)}, u32[]{:S(2)}, u32[]{:S(2)}) %collective-permute-start.3) | collective-permute-done | bytes 327712 | tf_op jit(solution)/shard_map/ppermute | solution.py:256
  42.3 7.6 %collective-permute-done.4 = bf16[512,320]{0,1:T(8,128)(2,1)S(1)} collective-permute-done((bf16[512,320]{0,1:T(8,128)(2,1)S(1)}, bf16[512,320]{0,1:T(8,128)(2,1)S(1)}, u32[]{:S(2)}, u32[]{:S(2)}) %collective-permute-start.4) | collective-permute-done | bytes 327712 | tf_op jit(solution)/shard_map/ppermute | solution.py:256
  54.1 8.8 %collective-permute-start.8 = (bf16[128,1408]{1,0:T(8,128)(2,1)}, bf16[128,1408]{1,0:T(8,128)(2,1)}, u32[]{:S(2)}, u32[]{:S(2)}) collective-permute-start(bf16[128,1408]{1,0:T(8,128)(2,1)} %get-tuple-element.179), channel_id=1, source_target_pairs={{0,12},{1,13},{2,14},{3,15},{4,0},{5,1},{6,2},{7,3},{8,4},{9,5},{1... | collective-permute-start | bytes 1081352 | tf_op jit(solution)/shard_map/ppermute | solution.py:256
  66.7 8.5 %collective-permute-done.11 = bf16[64,2048]{1,0:T(8,128)(2,1)S(1)} collective-permute-done((bf16[64,2048]{1,0:T(8,128)(2,1)S(1)}, bf16[64,2048]{1,0:T(8,128)(2,1)S(1)}, u32[]{:S(2)}, u32[]{:S(2)}) %collective-permute-start.11) | collective-permute-done | bytes 262176 | tf_op jit(solution)/shard_map/ppermute | solution.py:253
  116.9 5.8 collective-permute-done.16
  122.6 8.6 %collective-permute-done.15 = bf16[512,128]{1,0:T(8,128)(2,1)S(1)} collective-permute-done((bf16[512,128]{1,0:T(8,128)(2,1)S(1)}, bf16[512,128]{1,0:T(8,128)(2,1)S(1)}, u32[]{:S(2)}, u32[]{:S(2)}) %collective-permute-start.15) | collective-permute-done | bytes 131104 | tf_op jit(solution)/shard_map/ppermute | solution.py:256
  134.8 7.6 %attend.1 = (bf16[512,512]{1,0:T(8,128)(2,1)}, f32[4,8,1024]{2,1,0:T(8,128)}) custom-call(s32[1]{0:T(128)} %bitcast.1.seen_ref, bf16[512,512]{1,0:T(8,128)(2,1)} %multiply_convert_fusion.3.q_ref, bf16[4,512,128]{2,1,0:T(8,128)(2,1)} %get-tuple-element.247.kk_ref, bf16[4,512,128]{2,1,0:T(8,128)(2,1)} %get-tuple-element.248.vv_ref, ...), custom_call_target="tpu_custom_call" | custom-call | tf_op jit(solution)/shard_map/attend/pallas_call | solution.py:136
  146.7 7.7 %collective-permute-start.18 = (bf16[128,2048]{1,0:T(8,128)(2,1)S(1)}, bf16[128,2048]{1,0:T(8,128)(2,1)S(1)}, u32[]{:S(2)}, u32[]{:S(2)}) collective-permute-start(bf16[128,2048]{1,0:T(8,128)(2,1)S(1)} %get-tuple-element.159), channel_id=1, source_target_pairs={{0,1},{1,0},{2,3},{3,2},{4,5},{5,4},{6,7},{7,6},{8,9},{9,8},{10,11... | collective-permute-start | bytes 1572872 | tf_op jit(solution)/shard_map/ppermute | solution.py:253
  155.7 20.4 %collective-permute-done.22 = bf16[128,2048]{1,0:T(8,128)(2,1)S(1)} collective-permute-done((bf16[128,2048]{1,0:T(8,128)(2,1)S(1)}, bf16[128,2048]{1,0:T(8,128)(2,1)S(1)}, u32[]{:S(2)}, u32[]{:S(2)}) %collective-permute-start.22) | collective-permute-done | bytes 524320 | tf_op jit(solution)/shard_map/ppermute | solution.py:256
  180.7 31.4 %collective-permute-start.26 = (bf16[128,2048]{1,0:T(8,128)(2,1)S(1)}, bf16[128,2048]{1,0:T(8,128)(2,1)S(1)}, u32[]{:S(2)}, u32[]{:S(2)}) collective-permute-start(bf16[128,2048]{1,0:T(8,128)(2,1)S(1)} %constant_dynamic-update-slice_fusion.12), channel_id=1, source_target_pairs={{0,12},{1,13},{2,14},{3,15},{4,0},{5,1},{6,2},{7,3},{8,4},{9,5},{1... | collective-permute-start | bytes 1572872 | tf_op jit(solution)/shard_map/ppermute | solution.py:256
  217.1 18.6 %collective-permute-done.24 = bf16[128,2048]{1,0:T(8,128)(2,1)S(1)} collective-permute-done((bf16[128,2048]{1,0:T(8,128)(2,1)S(1)}, bf16[128,2048]{1,0:T(8,128)(2,1)S(1)}, u32[]{:S(2)}, u32[]{:S(2)}) %collective-permute-start.24) | collective-permute-done | bytes 524320 | tf_op jit(solution)/shard_map/ppermute | solution.py:256
  240.4 18.8 %collective-permute-start.28 = (bf16[512,2048]{1,0:T(8,128)(2,1)}, bf16[512,2048]{1,0:T(8,128)(2,1)}, u32[]{:S(2)}, u32[]{:S(2)}) collective-permute-start(bf16[512,2048]{1,0:T(8,128)(2,1)} %get-tuple-element.207), channel_id=1, source_target_pairs={{0,16},{16,0},{1,17},{17,1},{2,18},{18,2},{3,19},{19,3},{4,20},{20... | collective-permute-start | bytes 6291464 | tf_op jit(solution)/shard_map/ppermute | solution.py:259
  259.2 10.1 %fusion.93 = (bf16[4,4,128,1408]{3,2,1,0:T(8,128)(2,1)}, bf16[4,4,128,1408]{3,2,1,0:T(8,128)(2,1)}) fusion(bf16[8,4,128,1408]{3,2,1,0:T(8,128)(2,1)} %all-gather.6.cloned.1.call-done), kind=kLoop, calls=%fused_computation.334 | loop fusion | bytes 23068672 | tf_op jit(solution)/shard_map/slice | solution.py:413
  269.3 6.5 fusion.102
  275.9 6.7 %fusion.101 = f32[512,1408]{1,0:T(8,128)} fusion(bf16[512,2048]{1,0:T(8,128)(2,1)} %get-tuple-element.207, bf16[2048,1408]{1,0:T(8,128)(2,1)S(1)} %bitcast.177), kind=kOutput, calls=%fused_computation.343 | convolution fusion | flops 2952790016 | bytes 10747904 | tf_op jit(solution)/shard_map/dot_general | solution.py:26
  282.6 5.6 multiply_convert_fusion
  301.5 8.6 %convolution_convert_fusion = bf16[2048,1408]{1,0:T(8,128)(2,1)} fusion(bf16[1024,2048]{1,0:T(8,128)(2,1)S(1)} %constant_dynamic-update-slice_fusion.32, bf16[512,1408]{1,0:T(8,128)(2,1)S(1)} %collective-permute-done.29, bf16[512,1408]{1,0:T(8,128)(2,1)S(1)} %get-tuple-element.144), kind=kOutput, calls=%fused_computation | convolution fusion | flops 5914230784 | bytes 12845056 | tf_op jit(solution)/shard_map/dot_general | solution.py:26
  310.1 7.7 %collective-permute-done.27 = bf16[128,2048]{1,0:T(8,128)(2,1)S(1)} collective-permute-done((bf16[128,2048]{1,0:T(8,128)(2,1)}, bf16[128,2048]{1,0:T(8,128)(2,1)S(1)}, u32[]{:S(2)}, u32[]{:S(2)}) %collective-permute-start.27) | collective-permute-done | bytes 524320 | tf_op jit(solution)/shard_map/ppermute | solution.py:256
  330.2 6.4 convolution_convert_fusion.1
  337.4 23.2 %collective-permute-done.30 = bf16[128,2048]{1,0:T(8,128)(2,1)} collective-permute-done((bf16[128,2048]{1,0:T(8,128)(2,1)}, bf16[128,2048]{1,0:T(8,128)(2,1)}, u32[]{:S(2)}, u32[]{:S(2)}) %collective-permute-start.30) | collective-permute-done | bytes 524320 | tf_op jit(solution)/shard_map/ppermute | solution.py:256
  376.8 12.0 %collective-permute-done.35 = bf16[128,2048]{1,0:T(8,128)(2,1)} collective-permute-done((bf16[128,2048]{1,0:T(8,128)(2,1)S(1)}, bf16[128,2048]{1,0:T(8,128)(2,1)}, u32[]{:S(2)}, u32[]{:S(2)}) %collective-permute-start.35) | collective-permute-done | bytes 524320 | tf_op jit(solution)/shard_map/ppermute | solution.py:253
  403.4 10.3 %attend_back.1 = (f32[512,512]{1,0:T(8,128)}, f32[4,512,128]{2,1,0:T(8,128)}, f32[4,512,128]{2,1,0:T(8,128)}) custom-call(s32[1]{0:T(128)} %bitcast.1.seen_ref, bf16[512,512]{1,0:T(8,128)(2,1)} %multiply_convert_fusion.3.q_ref, bf16[512,512]{1,0:T(8,128)(2,1)} %fusion.24.do_ref, bf16[512,512]{1,0:T(8,128)(2,1)} %get-tuple-element.67.o_ref, ...), custom_call_target="tpu_custom_call" | custom-call | tf_op jit(solution)/shard_map/attend_back/pallas_call | solution.py:166
  416.4 20.3 %collective-permute-start.41 = (bf16[512,128]{1,0:T(8,128)(2,1)S(1)}, bf16[512,128]{1,0:T(8,128)(2,1)S(1)}, u32[]{:S(2)}, u32[]{:S(2)}) collective-permute-start(bf16[512,128]{1,0:T(8,128)(2,1)S(1)} %get-tuple-element.185), channel_id=1, source_target_pairs={{0,12},{1,13},{2,14},{3,15},{4,0},{5,1},{6,2},{7,3},{8,4},{9,5},{1... | collective-permute-start | bytes 393224 | tf_op jit(solution)/shard_map/ppermute | solution.py:256
  445.4 24.9 %collective-permute-done.42 = bf16[512,128]{1,0:T(8,128)(2,1)S(1)} collective-permute-done((bf16[512,128]{1,0:T(8,128)(2,1)S(1)}, bf16[512,128]{1,0:T(8,128)(2,1)S(1)}, u32[]{:S(2)}, u32[]{:S(2)}) %collective-permute-start.42) | collective-permute-done | bytes 131104 | tf_op jit(solution)/shard_map/ppermute | solution.py:256
  473.9 7.8 %collective-permute-done.39 = bf16[128,2048]{1,0:T(8,128)(2,1)} collective-permute-done((bf16[128,2048]{1,0:T(8,128)(2,1)}, bf16[128,2048]{1,0:T(8,128)(2,1)}, u32[]{:S(2)}, u32[]{:S(2)}) %collective-permute-start.39) | collective-permute-done | bytes 524320 | tf_op jit(solution)/shard_map/ppermute | solution.py:256
  481.7 12.1 %collective-permute-done.38 = bf16[128,2048]{1,0:T(8,128)(2,1)} collective-permute-done((bf16[128,2048]{1,0:T(8,128)(2,1)}, bf16[128,2048]{1,0:T(8,128)(2,1)}, u32[]{:S(2)}, u32[]{:S(2)}) %collective-permute-start.38) | collective-permute-done | bytes 524320 | tf_op jit(solution)/shard_map/ppermute | solution.py:256
  522.5 12.2 %reduce-scatter.9.cloned.1.call-done = bf16[128,1024]{1,0:T(8,128)(2,1)} async-done(((bf16[512,1024]{1,0:T(8,128)(2,1)}), bf16[128,1024]{1,0:T(8,128)(2,1)}) %reduce-scatter.9.cloned.1.call-update) | async-done | bytes 262160 | tf_op jit(solution)/shard_map/reduce_scatter | solution.py:522
  538.6 5.4 collective-permute-start.56
  548.4 32.2 %collective-permute-done.56 = bf16[128,1408]{1,0:T(8,128)(2,1)} collective-permute-done((bf16[128,1408]{1,0:T(8,128)(2,1)}, bf16[128,1408]{1,0:T(8,128)(2,1)}, u32[]{:S(2)}, u32[]{:S(2)}) %collective-permute-start.56) | collective-permute-done | bytes 360480 | tf_op jit(solution)/shard_map/ppermute | solution.py:256
  580.6 22.7 %collective-permute-done.55 = bf16[128,1408]{1,0:T(8,128)(2,1)} collective-permute-done((bf16[128,1408]{1,0:T(8,128)(2,1)}, bf16[128,1408]{1,0:T(8,128)(2,1)}, u32[]{:S(2)}, u32[]{:S(2)}) %collective-permute-start.55) | collective-permute-done | bytes 360480 | tf_op jit(solution)/shard_map/ppermute | solution.py:256
  618.7 4.1 all-to-all-start.1
  629.7 6.2 convert_multiply_fusion
  (477 shorter events, 239.5 us)
Async XLA Ops:
  7.2 78.2 %all-gather.8.cloned.1.call-start = ((), (), s32[]{:S(2)}) async-start(), calls=%async_computation.11 | async-start | bytes 6488064 | tf_op jit(solution)/shard_map/all_gather | solution.py:365
  18.4 124.0 %all-gather.10.cloned.1.call-start = ((), (), s32[]{:S(2)}) async-start(), calls=%async_computation.12 | async-start | bytes 2359296 | tf_op jit(solution)/shard_map/all_gather | solution.py:370
  28.9 34.0 %collective-permute-start.10 = (bf16[128,2048]{1,0:T(8,128)(2,1)}, bf16[128,2048]{1,0:T(8,128)(2,1)S(1)}, u32[]{:S(2)}, u32[]{:S(2)}) collective-permute-start(bf16[128,2048]{1,0:T(8,128)(2,1)} %fusion.22), channel_id=1, source_target_pairs={{0,2},{1,3},{2,0},{3,1},{4,6},{5,7},{6,4},{7,5},{8,10},{9,11},{10,... | collective-permute-start | bytes 1572872 | tf_op jit(solution)/shard_map/ppermute | solution.py:253
  30.3 36.1 %collective-permute-start.9 = (bf16[128,2048]{1,0:T(8,128)(2,1)}, bf16[128,2048]{1,0:T(8,128)(2,1)S(1)}, u32[]{:S(2)}, u32[]{:S(2)}) collective-permute-start(bf16[128,2048]{1,0:T(8,128)(2,1)} %fusion.22), channel_id=1, source_target_pairs={{0,1},{1,0},{2,3},{3,2},{4,5},{5,4},{6,7},{7,6},{8,9},{9,8},{10,11... | collective-permute-start | bytes 1572872 | tf_op jit(solution)/shard_map/ppermute | solution.py:253
  50.2 31.1 %collective-permute-start.13 = (bf16[2048,320]{0,1:T(8,128)(2,1)S(1)}, bf16[2048,320]{0,1:T(8,128)(2,1)S(1)}, u32[]{:S(2)}, u32[]{:S(2)}) collective-permute-start(bf16[2048,320]{0,1:T(8,128)(2,1)S(1)} %constant_dynamic-slice_fusion.11), channel_id=1, source_target_pairs={{0,16},{16,0},{1,17},{17,1},{2,18},{18,2},{3,19},{19,3},{4,20},{20... | collective-permute-start | bytes 3932168 | tf_op jit(solution)/shard_map/ppermute | solution.py:259
  51.7 33.8 %collective-permute-start.17 = (bf16[128,1024]{1,0:T(8,128)(2,1)S(1)}, bf16[128,1024]{1,0:T(8,128)(2,1)}, u32[]{:S(2)}, u32[]{:S(2)}) collective-permute-start(bf16[128,1024]{1,0:T(8,128)(2,1)S(1)} %constant_dynamic-slice_fusion.12), channel_id=1, source_target_pairs={{0,0},{1,4},{2,8},{3,12},{4,1},{5,5},{6,9},{7,13},{8,2},{9,6},{10,... | collective-permute-start | bytes 786440 | tf_op jit(solution)/shard_map/ppermute | solution.py:357
  54.1 52.6 %collective-permute-start.8 = (bf16[128,1408]{1,0:T(8,128)(2,1)}, bf16[128,1408]{1,0:T(8,128)(2,1)}, u32[]{:S(2)}, u32[]{:S(2)}) collective-permute-start(bf16[128,1408]{1,0:T(8,128)(2,1)} %get-tuple-element.179), channel_id=1, source_target_pairs={{0,12},{1,13},{2,14},{3,15},{4,0},{5,1},{6,2},{7,3},{8,4},{9,5},{1... | collective-permute-start | bytes 1081352 | tf_op jit(solution)/shard_map/ppermute | solution.py:256
  75.2 31.5 %collective-permute-start.7 = (bf16[128,1408]{1,0:T(8,128)(2,1)}, bf16[128,1408]{1,0:T(8,128)(2,1)}, u32[]{:S(2)}, u32[]{:S(2)}) collective-permute-start(bf16[128,1408]{1,0:T(8,128)(2,1)} %get-tuple-element.180), channel_id=1, source_target_pairs={{0,8},{1,9},{2,10},{3,11},{4,12},{5,13},{6,14},{7,15},{8,0},{9,1},... | collective-permute-start | bytes 1081352 | tf_op jit(solution)/shard_map/ppermute | solution.py:256
  85.5 173.8 %all-gather.6.cloned.1.call-start = ((), (), s32[]{:S(2)}) async-start(), calls=%async_computation.6 | async-start | bytes 12976128 | tf_op jit(solution)/shard_map/all_gather | solution.py:409
  111.1 398.4 %reduce-scatter.5.cloned.1.call-start = ((), (), s32[]{:S(2)}) async-start(), calls=%async_computation.7 | async-start | bytes 7208960 | tf_op jit(solution)/shard_map/reduce_scatter | solution.py:505
  131.4 44.7 %collective-permute-start.22 = (bf16[128,2048]{1,0:T(8,128)(2,1)S(1)}, bf16[128,2048]{1,0:T(8,128)(2,1)S(1)}, u32[]{:S(2)}, u32[]{:S(2)}) collective-permute-start(bf16[128,2048]{1,0:T(8,128)(2,1)S(1)} %bitcast_convert_fusion), channel_id=1, source_target_pairs={{0,8},{1,9},{2,10},{3,11},{4,12},{5,13},{6,14},{7,15},{8,0},{9,1},... | collective-permute-start | bytes 1572872 | tf_op jit(solution)/shard_map/ppermute | solution.py:256
  131.5 44.6 %collective-permute-start.21 = (bf16[128,2048]{1,0:T(8,128)(2,1)S(1)}, bf16[128,2048]{1,0:T(8,128)(2,1)}, u32[]{:S(2)}, u32[]{:S(2)}) collective-permute-start(bf16[128,2048]{1,0:T(8,128)(2,1)S(1)} %bitcast_convert_fusion), channel_id=1, source_target_pairs={{0,4},{1,5},{2,6},{3,7},{4,8},{5,9},{6,10},{7,11},{8,12},{9,13},{1... | collective-permute-start | bytes 1572872 | tf_op jit(solution)/shard_map/ppermute | solution.py:256
  146.7 32.9 %collective-permute-start.18 = (bf16[128,2048]{1,0:T(8,128)(2,1)S(1)}, bf16[128,2048]{1,0:T(8,128)(2,1)S(1)}, u32[]{:S(2)}, u32[]{:S(2)}) collective-permute-start(bf16[128,2048]{1,0:T(8,128)(2,1)S(1)} %get-tuple-element.159), channel_id=1, source_target_pairs={{0,1},{1,0},{2,3},{3,2},{4,5},{5,4},{6,7},{7,6},{8,9},{9,8},{10,11... | collective-permute-start | bytes 1572872 | tf_op jit(solution)/shard_map/ppermute | solution.py:253
  180.7 56.9 %collective-permute-start.26 = (bf16[128,2048]{1,0:T(8,128)(2,1)S(1)}, bf16[128,2048]{1,0:T(8,128)(2,1)S(1)}, u32[]{:S(2)}, u32[]{:S(2)}) collective-permute-start(bf16[128,2048]{1,0:T(8,128)(2,1)S(1)} %constant_dynamic-update-slice_fusion.12), channel_id=1, source_target_pairs={{0,12},{1,13},{2,14},{3,15},{4,0},{5,1},{6,2},{7,3},{8,4},{9,5},{1... | collective-permute-start | bytes 1572872 | tf_op jit(solution)/shard_map/ppermute | solution.py:256
  240.4 55.3 %collective-permute-start.28 = (bf16[512,2048]{1,0:T(8,128)(2,1)}, bf16[512,2048]{1,0:T(8,128)(2,1)}, u32[]{:S(2)}, u32[]{:S(2)}) collective-permute-start(bf16[512,2048]{1,0:T(8,128)(2,1)} %get-tuple-element.207), channel_id=1, source_target_pairs={{0,16},{16,0},{1,17},{17,1},{2,18},{18,2},{3,19},{19,3},{4,20},{20... | collective-permute-start | bytes 6291464 | tf_op jit(solution)/shard_map/ppermute | solution.py:259
  317.9 204.6 %reduce-scatter.7.cloned.1.call-start = ((), (), s32[]{:S(2)}) async-start(), calls=%async_computation.8 | async-start | bytes 3604480 | tf_op jit(solution)/shard_map/reduce_scatter | solution.py:506
  322.1 183.6 %collective-permute-start.47 = (bf16[512,512]{1,0:T(8,128)(2,1)}, bf16[512,512]{1,0:T(8,128)(2,1)}, u32[]{:S(2)}, u32[]{:S(2)}) collective-permute-start(bf16[512,512]{1,0:T(8,128)(2,1)} %get-tuple-element.67.o_ref), channel_id=1, source_target_pairs={{0,16},{16,0},{1,17},{17,1},{2,18},{18,2},{3,19},{19,3},{4,20},{20... | collective-permute-start | bytes 1572872 | tf_op jit(solution)/shard_map/ppermute | solution.py:259
  324.4 36.2 %collective-permute-start.30 = (bf16[128,2048]{1,0:T(8,128)(2,1)}, bf16[128,2048]{1,0:T(8,128)(2,1)}, u32[]{:S(2)}, u32[]{:S(2)}) collective-permute-start(bf16[128,2048]{1,0:T(8,128)(2,1)} %get-tuple-element.156), channel_id=1, source_target_pairs={{0,8},{1,9},{2,10},{3,11},{4,12},{5,13},{6,14},{7,15},{8,0},{9,1},... | collective-permute-start | bytes 1572872 | tf_op jit(solution)/shard_map/ppermute | solution.py:256
  373.4 161.3 %reduce-scatter.9.cloned.1.call-start = ((), (), s32[]{:S(2)}) async-start(), calls=%async_computation.9 | async-start | bytes 1310720 | tf_op jit(solution)/shard_map/reduce_scatter | solution.py:522
  436.8 33.5 %collective-permute-start.42 = (bf16[512,128]{1,0:T(8,128)(2,1)S(1)}, bf16[512,128]{1,0:T(8,128)(2,1)S(1)}, u32[]{:S(2)}, u32[]{:S(2)}) collective-permute-start(bf16[512,128]{1,0:T(8,128)(2,1)S(1)} %get-tuple-element.187), channel_id=1, source_target_pairs={{0,8},{1,9},{2,10},{3,11},{4,12},{5,13},{6,14},{7,15},{8,0},{9,1},... | collective-permute-start | bytes 393224 | tf_op jit(solution)/shard_map/ppermute | solution.py:256
  438.6 67.1 %collective-permute-start.48 = (bf16[512,1024]{1,0:T(8,128)(2,1)}, bf16[512,1024]{1,0:T(8,128)(2,1)}, u32[]{:S(2)}, u32[]{:S(2)}) collective-permute-start(bf16[512,1024]{1,0:T(8,128)(2,1)} %get-tuple-element.147), channel_id=1, source_target_pairs={{0,16},{16,0},{1,17},{17,1},{2,18},{18,2},{3,19},{19,3},{4,20},{20... | collective-permute-start | bytes 3145736 | tf_op jit(solution)/shard_map/ppermute | solution.py:259
  441.9 31.9 %collective-permute-start.40 = (bf16[128,2048]{1,0:T(8,128)(2,1)}, bf16[128,2048]{1,0:T(8,128)(2,1)}, u32[]{:S(2)}, u32[]{:S(2)}) collective-permute-start(bf16[128,2048]{1,0:T(8,128)(2,1)} %get-tuple-element.151), channel_id=1, source_target_pairs={{0,4},{1,5},{2,6},{3,7},{4,8},{5,9},{6,10},{7,11},{8,12},{9,13},{1... | collective-permute-start | bytes 1572872 | tf_op jit(solution)/shard_map/ppermute | solution.py:256
  445.4 36.3 %collective-permute-start.39 = (bf16[128,2048]{1,0:T(8,128)(2,1)}, bf16[128,2048]{1,0:T(8,128)(2,1)}, u32[]{:S(2)}, u32[]{:S(2)}) collective-permute-start(bf16[128,2048]{1,0:T(8,128)(2,1)} %get-tuple-element.152), channel_id=1, source_target_pairs={{0,8},{1,9},{2,10},{3,11},{4,12},{5,13},{6,14},{7,15},{8,0},{9,1},... | collective-permute-start | bytes 1572872 | tf_op jit(solution)/shard_map/ppermute | solution.py:256
  509.6 107.2 %reduce-scatter.11.cloned.1.call-start = ((), (), s32[]{:S(2)}) async-start(), calls=%async_computation.10 | async-start | bytes 1638400 | tf_op jit(solution)/shard_map/reduce_scatter | solution.py:574
  513.5 30.5 %collective-permute-start.44 = (bf16[128,2048]{1,0:T(8,128)(2,1)}, bf16[128,2048]{1,0:T(8,128)(2,1)S(1)}, u32[]{:S(2)}, u32[]{:S(2)}) collective-permute-start(bf16[128,2048]{1,0:T(8,128)(2,1)} %get-tuple-element.148), channel_id=1, source_target_pairs={{0,1},{1,0},{2,3},{3,2},{4,5},{5,4},{6,7},{7,6},{8,9},{9,8},{10,11... | collective-permute-start | bytes 1572872 | tf_op jit(solution)/shard_map/ppermute | solution.py:253
  514.8 29.2 %collective-permute-start.46 = (bf16[128,2048]{1,0:T(8,128)(2,1)}, bf16[128,2048]{1,0:T(8,128)(2,1)S(1)}, u32[]{:S(2)}, u32[]{:S(2)}) collective-permute-start(bf16[128,2048]{1,0:T(8,128)(2,1)} %get-tuple-element.149), channel_id=1, source_target_pairs={{0,3},{1,2},{2,1},{3,0},{4,7},{5,6},{6,5},{7,4},{8,11},{9,10},{10,... | collective-permute-start | bytes 1572872 | tf_op jit(solution)/shard_map/ppermute | solution.py:253
  514.8 29.9 %collective-permute-start.45 = (bf16[128,2048]{1,0:T(8,128)(2,1)}, bf16[128,2048]{1,0:T(8,128)(2,1)S(1)}, u32[]{:S(2)}, u32[]{:S(2)}) collective-permute-start(bf16[128,2048]{1,0:T(8,128)(2,1)} %get-tuple-element.150), channel_id=1, source_target_pairs={{0,2},{1,3},{2,0},{3,1},{4,6},{5,7},{6,4},{7,5},{8,10},{9,11},{10,... | collective-permute-start | bytes 1572872 | tf_op jit(solution)/shard_map/ppermute | solution.py:253
  538.6 42.0 %collective-permute-start.56 = (bf16[128,1408]{1,0:T(8,128)(2,1)}, bf16[128,1408]{1,0:T(8,128)(2,1)}, u32[]{:S(2)}, u32[]{:S(2)}) collective-permute-start(bf16[128,1408]{1,0:T(8,128)(2,1)} %get-tuple-element.175), channel_id=1, source_target_pairs={{0,12},{1,13},{2,14},{3,15},{4,0},{5,1},{6,2},{7,3},{8,4},{9,5},{1... | collective-permute-start | bytes 1081352 | tf_op jit(solution)/shard_map/ppermute | solution.py:256
  544.0 59.2 %collective-permute-start.55 = (bf16[128,1408]{1,0:T(8,128)(2,1)}, bf16[128,1408]{1,0:T(8,128)(2,1)}, u32[]{:S(2)}, u32[]{:S(2)}) collective-permute-start(bf16[128,1408]{1,0:T(8,128)(2,1)} %get-tuple-element.176), channel_id=1, source_target_pairs={{0,8},{1,9},{2,10},{3,11},{4,12},{5,13},{6,14},{7,15},{8,0},{9,1},... | collective-permute-start | bytes 1081352 | tf_op jit(solution)/shard_map/ppermute | solution.py:256
  544.0 59.2 %collective-permute-start.54 = (bf16[128,1408]{1,0:T(8,128)(2,1)S(1)}, bf16[128,1408]{1,0:T(8,128)(2,1)}, u32[]{:S(2)}, u32[]{:S(2)}) collective-permute-start(bf16[128,1408]{1,0:T(8,128)(2,1)S(1)} %get-tuple-element.177), channel_id=1, source_target_pairs={{0,4},{1,5},{2,6},{3,7},{4,8},{5,9},{6,10},{7,11},{8,12},{9,13},{1... | collective-permute-start | bytes 1081352 | tf_op jit(solution)/shard_map/ppermute | solution.py:256
  546.4 65.9 %collective-permute-start.58 = (bf16[352,1024]{1,0:T(8,128)(2,1)}, bf16[352,1024]{1,0:T(8,128)(2,1)S(1)}, u32[]{:S(2)}, u32[]{:S(2)}) collective-permute-start(bf16[352,1024]{1,0:T(8,128)(2,1)} %reduce-scatter.7.cloned.1.call-done), channel_id=1, source_target_pairs={{0,16},{16,0},{1,17},{17,1},{2,18},{18,2},{3,19},{19,3},{4,20},{20... | collective-permute-start | bytes 2162696 | tf_op jit(solution)/shard_map/ppermute | solution.py:259
  548.3 62.8 %collective-permute-start.53 = (bf16[128,1024]{1,0:T(8,128)(2,1)S(1)}, bf16[128,1024]{1,0:T(8,128)(2,1)S(1)}, u32[]{:S(2)}, u32[]{:S(2)}) collective-permute-start(bf16[128,1024]{1,0:T(8,128)(2,1)S(1)} %collective-permute-done.52), channel_id=1, source_target_pairs={{0,16},{16,0},{1,17},{17,1},{2,18},{18,2},{3,19},{19,3},{4,20},{20... | collective-permute-start | bytes 786440 | tf_op jit(solution)/shard_map/ppermute | solution.py:259
  (110 other events, 1203.4 us)
Sparse Core Ops, SparseCore 0:
  10.5 51.6 all-gather.7
  85.6 37.7 all-gather.9
  125.9 86.9 all-gather.5
  318.0 80.2 reduce-scatter.4
  401.8 42.5 reduce-scatter.6
  509.7 24.9 reduce-scatter.8
  546.5 53.0 reduce-scatter.10

commit v7 on v6

--- a/solution.py
+++ b/solution.py
@@ -493,15 +493,17 @@
         inner_sent[0], gate_up_sum = tie(inner_sent[0], gate_up_sum)
         *inner_rest, down_sum = tie(*inner_sent[1:], down_sum)
         inner_sent = [inner_sent[0]] + inner_rest
+        mixed = jnp.concatenate(
+            [dot(hidden_later, down_full[i]).astype(bf16) for i in range(n_dp)], axis=1
+        )
+        *inner_sent, mixed = tie(*inner_sent, mixed)
         inner_two = functools.reduce(
             jnp.add, [g.astype(f32) for g in inner_sent], grad_low_two[:tokens].astype(f32)
         )
         grad_x_mid = grad_y + norm_back(order_back(inner_two), normed_two, inverse_two)
 
-        hidden_last, grad_x_low = tie(hidden_later, grad_x_mid.astype(bf16))
-        mixed = jnp.concatenate(
-            [dot(hidden_last, down_full[i]).astype(bf16) for i in range(n_dp)], axis=1
-        )
+        mixed, grad_x_low = tie(mixed, grad_x_mid.astype(bf16))
+        mixed_sent = [shift_z(mixed[t * tokens : (t + 1) * tokens], -t) for t in range(1, planes)]
         gate_up_sum = lax.psum_scatter(gate_up_sum, "seq", axis_index_groups=in_plane, tiled=True)
         down_sum = lax.psum_scatter(
             down_sum, "seq", axis_index_groups=in_plane, tiled=True
@@ -509,8 +511,8 @@
         gate_up_sum = gate_up_sum.reshape(planes, piece, ff_block)
 
         grad_branch = gather_w(grad_x_low)
-        mixed, grad_branch = tie(mixed, grad_branch)
-        mixed_sent = [shift_z(mixed[t * tokens : (t + 1) * tokens], -t) for t in range(1, planes)]
+        early = planes - 2
+        *mixed_sent[:early], grad_branch = tie(*mixed_sent[:early], grad_branch)
         grad_o = functools.reduce(
             jnp.add,
             [dot(pick(grad_branch, i, n_dp, 1), out_full[i], ((1,), (1,))) for i in range(n_dp)],
@@ -518,6 +520,8 @@
 
         out_part_sum = dot(gather_dp(o), exchange_dp(grad_branch, c, 1), ((0,), (0,))).astype(bf16)
         grad_o_seq = by_seq(grad_o, 0)
+        *late, grad_o_seq, out_part_sum = tie(*mixed_sent[early:], grad_o_seq, out_part_sum)
+        mixed_sent = mixed_sent[:early] + list(late)
         gate_up_sum, out_part_sum = tie(gate_up_sum, out_part_sum)
         out_sum = lax.psum_scatter(out_part_sum, "seq", axis_index_groups=across, tiled=True)
         pieces = [
@@ -526,7 +530,7 @@
             )
             for i in range(seqs)
         ]
-        *mixed_sent, grad_q = tie(*mixed_sent, jnp.stack([one[0] for one in pieces]))
+        grad_q = jnp.stack([one[0] for one in pieces])
         mixed = functools.reduce(
             jnp.add, [g.astype(f32) for g in mixed_sent], mixed[:tokens].astype(f32)
         )
@@ -541,8 +545,14 @@
             axis=-1,
         ).astype(bf16)
         grad_kv = scatter_z([grad_kv[t] for t in range(planes)])
+        grad_kv, gate_up_late = tie(grad_kv, gate_up_sum)
+        gate_up_sent = []
+        for t in range(planes):
+            block = lax.dynamic_index_in_dim(gate_up_late, (p + t) % planes, 0, keepdims=False)
+            gate_up_sent.append(shift_z(block, t) if t else block)
         query_pre = unrotate(grad_q.reshape(plane_tokens, GROUP_HEADS, HEAD_DIM), cosine, sine)
         query_pre = query_pre.reshape(plane_tokens, q_width).astype(bf16)
+        query_pre, out_sum = tie(query_pre, out_sum)
         key_pre = unrotate(grad_kv[:, None, :HEAD_DIM], cosine, sine)[:, 0]
         kv_pre = jnp.concatenate([key_pre, grad_kv[:, HEAD_DIM:]], axis=1).astype(bf16)
         pre = [
@@ -565,7 +575,7 @@
             exchange_dp(jnp.concatenate(pre, axis=1), c, 1),
             ((0,), (0,)),
         ).astype(bf16)
-        gate_up_late, down_sum, out_sum, qkv_sum = tie(gate_up_sum, down_sum, out_sum, qkv_sum)
+        *gate_up_sent, down_sum, qkv_sum = tie(*gate_up_sent, down_sum, qkv_sum)
         out_sum = lax.ppermute(
             out_sum, "seq", [(GROUP * (i % planes) + i // planes, i) for i in range(n_seq)]
         )
@@ -588,14 +598,9 @@
 
         grad_w_down = jnp.concatenate(collect_dp(down_sum, c), axis=1).astype(f32)
         gate_up_rows = jnp.zeros((planes, piece, ff_block), bf16)
-        sent = []
-        for t in range(planes):
-            block = lax.dynamic_index_in_dim(gate_up_late, (p + t) % planes, 0, keepdims=False)
-            sent.append(shift_z(block, t) if t else block)
-        sent = lax.optimization_barrier(tuple(sent))
         for t in range(planes):
             gate_up_rows = lax.dynamic_update_index_in_dim(
-                gate_up_rows, sent[t], (p - t) % planes, 0
+                gate_up_rows, gate_up_sent[t], (p - t) % planes, 0
             )
         gate_up_rows = collect_dp(gate_up_rows, c)
 

time: 664 us -> 602 us (0.907)
  waiting for transfers between devices: 245 us -> 185 us
    ppermute x27, waiting for transfers between devices: 202 us -> 121 us  [shift_z(): lax.ppermute(value, 'seq', [(s, (s + GROUP * t) % n_seq) for s in range(n...]
    ppermute x17, waiting for transfers between devices: 27 us -> 48.5 us  [xor_w(): return lax.ppermute(value, 'seq', [(s, s ^ j) for s in range(n_seq)])]
    reduce_scatter x1, waiting for transfers between devices: 0.01 us -> 12.4 us  [body(): lax.psum_scatter(qkv_sum, 'seq', axis_index_groups=across, tiled=True)]
    reduce_scatter x1, waiting for transfers between devices: 12.2 us -> 0.02 us  [body(): lax.psum_scatter(out_part_sum, 'seq', axis_index_groups=across, tiled=True)]
  transfers between devices with their start and end apart: 68 -> 68, of which waited for: 21 -> 19; matrix products, arithmetic and copies ran while one was open for 30% -> 32% of each run, Pallas kernels for 3% -> 3%
where the time goes in v7:
time: 602 us; the launch traced here: 593 us
  waiting for transfers between devices  185 us (31%)
  starting transfers between devices  159 us (26%)
  local copies, waits for them, and re-layouts  89 us (15%)
  matrix products  69.8 us (12%)
  other arithmetic  55.8 us (9%)
  Pallas kernels  17.9 us (3%)
  between operations  16.6 us (3%)
    ppermute x27, waiting for transfers between devices, shift_z(): lax.ppermute(value, 'seq', [(s, (s + GROUP * t) % n_seq) for s in range(n...  121 us
    ppermute x27, starting transfers between devices, shift_z(): lax.ppermute(value, 'seq', [(s, (s + GROUP * t) % n_seq) for s in range(n...  84 us
    dot_general x20, matrix products, dot(): lax.dot_general(left, right, (contract, ((), ())), preferred_element_type...  69.8 us
    ppermute x17, waiting for transfers between devices, xor_w(): return lax.ppermute(value, 'seq', [(s, s ^ j) for s in range(n_seq)])  48.5 us
    ppermute x13, starting transfers between devices, shift_dp(): return lax.ppermute(value, 'dp', [(c, (c + t) % n_dp) for c in range(n_dp)])  34.1 us
    unnamed x217, local copies, waits for them, and re-layouts  29.6 us
    ppermute x17, starting transfers between devices, xor_w(): return lax.ppermute(value, 'seq', [(s, s ^ j) for s in range(n_seq)])  27.3 us
    reduce_scatter x1, waiting for transfers between devices, body(): lax.psum_scatter(qkv_sum, 'seq', axis_index_groups=across, tiled=True)  12.4 us
  transfers between devices with their start and end apart: 68, of which 19 were waited for; matrix products, arithmetic and copies ran while one was open for 32% of the time, Pallas kernels for 3%

profile of v7, /device:TPU:1, one launch (start us, length us, event | category | flops | bytes accessed | tf_op | source)
XLA Modules:
  0.0 592.6 jit_solution(18335204002802698875)
XLA Ops:
  33.4 8.8 %collective-permute-done.3 = bf16[512,320]{0,1:T(8,128)(2,1)S(1)} collective-permute-done((bf16[512,320]{0,1:T(8,128)(2,1)S(1)}, bf16[512,320]{0,1:T(8,128)(2,1)S(1)}, u32[]{:S(2)}, u32[]{:S(2)}) %collective-permute-start.3) | collective-permute-done | bytes 327712 | tf_op jit(solution)/shard_map/ppermute | solution.py:256
  42.3 7.6 %collective-permute-done.4 = bf16[512,320]{0,1:T(8,128)(2,1)S(1)} collective-permute-done((bf16[512,320]{0,1:T(8,128)(2,1)S(1)}, bf16[512,320]{0,1:T(8,128)(2,1)S(1)}, u32[]{:S(2)}, u32[]{:S(2)}) %collective-permute-start.4) | collective-permute-done | bytes 327712 | tf_op jit(solution)/shard_map/ppermute | solution.py:256
  54.1 8.8 %collective-permute-start.8 = (bf16[128,1408]{1,0:T(8,128)(2,1)}, bf16[128,1408]{1,0:T(8,128)(2,1)}, u32[]{:S(2)}, u32[]{:S(2)}) collective-permute-start(bf16[128,1408]{1,0:T(8,128)(2,1)} %get-tuple-element.191), channel_id=1, source_target_pairs={{0,12},{1,13},{2,14},{3,15},{4,0},{5,1},{6,2},{7,3},{8,4},{9,5},{1... | collective-permute-start | bytes 1081352 | tf_op jit(solution)/shard_map/ppermute | solution.py:256
  68.2 7.0 %collective-permute-done.11 = bf16[64,2048]{1,0:T(8,128)(2,1)S(1)} collective-permute-done((bf16[64,2048]{1,0:T(8,128)(2,1)S(1)}, bf16[64,2048]{1,0:T(8,128)(2,1)S(1)}, u32[]{:S(2)}, u32[]{:S(2)}) %collective-permute-start.11) | collective-permute-done | bytes 262176 | tf_op jit(solution)/shard_map/ppermute | solution.py:253
  81.9 5.3 fusion.56
  122.5 8.8 %collective-permute-done.15 = bf16[512,128]{1,0:T(8,128)(2,1)S(1)} collective-permute-done((bf16[512,128]{1,0:T(8,128)(2,1)S(1)}, bf16[512,128]{1,0:T(8,128)(2,1)S(1)}, u32[]{:S(2)}, u32[]{:S(2)}) %collective-permute-start.15) | collective-permute-done | bytes 131104 | tf_op jit(solution)/shard_map/ppermute | solution.py:256
  134.9 7.6 %attend.1 = (bf16[512,512]{1,0:T(8,128)(2,1)}, f32[4,8,1024]{2,1,0:T(8,128)}) custom-call(s32[1]{0:T(128)} %bitcast.1.seen_ref, bf16[512,512]{1,0:T(8,128)(2,1)} %multiply_convert_fusion.3.q_ref, bf16[4,512,128]{2,1,0:T(8,128)(2,1)} %get-tuple-element.257.kk_ref, bf16[4,512,128]{2,1,0:T(8,128)(2,1)} %get-tuple-element.258.vv_ref, ...), custom_call_target="tpu_custom_call" | custom-call | tf_op jit(solution)/shard_map/attend/pallas_call | solution.py:136
  145.6 7.8 %collective-permute-start.18 = (bf16[128,2048]{1,0:T(8,128)(2,1)S(1)}, bf16[128,2048]{1,0:T(8,128)(2,1)S(1)}, u32[]{:S(2)}, u32[]{:S(2)}) collective-permute-start(bf16[128,2048]{1,0:T(8,128)(2,1)S(1)} %get-tuple-element.171), channel_id=1, source_target_pairs={{0,1},{1,0},{2,3},{3,2},{4,5},{5,4},{6,7},{7,6},{8,9},{9,8},{10,11... | collective-permute-start | bytes 1572872 | tf_op jit(solution)/shard_map/ppermute | solution.py:253
  154.6 21.7 %collective-permute-done.22 = bf16[128,2048]{1,0:T(8,128)(2,1)} collective-permute-done((bf16[128,2048]{1,0:T(8,128)(2,1)S(1)}, bf16[128,2048]{1,0:T(8,128)(2,1)}, u32[]{:S(2)}, u32[]{:S(2)}) %collective-permute-start.22) | collective-permute-done | bytes 524320 | tf_op jit(solution)/shard_map/ppermute | solution.py:256
  181.4 29.9 %collective-permute-start.26 = (bf16[128,2048]{1,0:T(8,128)(2,1)S(1)}, bf16[128,2048]{1,0:T(8,128)(2,1)S(1)}, u32[]{:S(2)}, u32[]{:S(2)}) collective-permute-start(bf16[128,2048]{1,0:T(8,128)(2,1)S(1)} %constant_dynamic-update-slice_fusion.12), channel_id=1, source_target_pairs={{0,12},{1,13},{2,14},{3,15},{4,0},{5,1},{6,2},{7,3},{8,4},{9,5},{1... | collective-permute-start | bytes 1572872 | tf_op jit(solution)/shard_map/ppermute | solution.py:256
  216.4 17.8 %collective-permute-done.24 = bf16[128,2048]{1,0:T(8,128)(2,1)S(1)} collective-permute-done((bf16[128,2048]{1,0:T(8,128)(2,1)S(1)}, bf16[128,2048]{1,0:T(8,128)(2,1)S(1)}, u32[]{:S(2)}, u32[]{:S(2)}) %collective-permute-start.24) | collective-permute-done | bytes 524320 | tf_op jit(solution)/shard_map/ppermute | solution.py:256
  238.9 19.6 %collective-permute-start.28 = (bf16[512,2048]{1,0:T(8,128)(2,1)}, bf16[512,2048]{1,0:T(8,128)(2,1)}, u32[]{:S(2)}, u32[]{:S(2)}) collective-permute-start(bf16[512,2048]{1,0:T(8,128)(2,1)} %get-tuple-element.219), channel_id=1, source_target_pairs={{0,16},{16,0},{1,17},{17,1},{2,18},{18,2},{3,19},{19,3},{4,20},{20... | collective-permute-start | bytes 6291464 | tf_op jit(solution)/shard_map/ppermute | solution.py:259
  258.5 10.1 %fusion.92 = (bf16[4,4,128,1408]{3,2,1,0:T(8,128)(2,1)}, bf16[4,4,128,1408]{3,2,1,0:T(8,128)(2,1)}) fusion(bf16[8,4,128,1408]{3,2,1,0:T(8,128)(2,1)} %all-gather.6.cloned.1.call-done), kind=kLoop, calls=%fused_computation.333 | loop fusion | bytes 23068672 | tf_op jit(solution)/shard_map/slice | solution.py:413
  268.6 6.5 %fusion.101 = f32[512,1408]{1,0:T(8,128)S(1)} fusion(bf16[512,2048]{1,0:T(8,128)(2,1)} %get-tuple-element.219, bf16[2048,1408]{1,0:T(8,128)(2,1)} %bitcast.169), kind=kOutput, calls=%fused_computation.343 | convolution fusion | flops 2952790016 | bytes 10747904 | tf_op jit(solution)/shard_map/dot_general | solution.py:26
  275.2 6.7 %fusion.100 = f32[512,1408]{1,0:T(8,128)} fusion(bf16[512,2048]{1,0:T(8,128)(2,1)} %get-tuple-element.219, bf16[2048,1408]{1,0:T(8,128)(2,1)S(1)} %bitcast.173), kind=kOutput, calls=%fused_computation.342 | convolution fusion | flops 2952790016 | bytes 10747904 | tf_op jit(solution)/shard_map/dot_general | solution.py:26
  281.9 5.6 multiply_convert_fusion
  300.8 8.6 %convolution_convert_fusion = bf16[2048,1408]{1,0:T(8,128)(2,1)} fusion(bf16[1024,2048]{1,0:T(8,128)(2,1)S(1)} %constant_dynamic-update-slice_fusion.32, bf16[512,1408]{1,0:T(8,128)(2,1)S(1)} %collective-permute-done.29, bf16[512,1408]{1,0:T(8,128)(2,1)S(1)} %get-tuple-element.156), kind=kOutput, calls=%fused_computation | convolution fusion | flops 5914230784 | bytes 12845056 | tf_op jit(solution)/shard_map/dot_general | solution.py:26
  309.4 7.7 %collective-permute-done.27 = bf16[128,2048]{1,0:T(8,128)(2,1)S(1)} collective-permute-done((bf16[128,2048]{1,0:T(8,128)(2,1)}, bf16[128,2048]{1,0:T(8,128)(2,1)S(1)}, u32[]{:S(2)}, u32[]{:S(2)}) %collective-permute-start.27) | collective-permute-done | bytes 524320 | tf_op jit(solution)/shard_map/ppermute | solution.py:256
  329.9 5.9 convolution_convert_fusion.1
  335.8 22.5 %collective-permute-done.30 = bf16[128,2048]{1,0:T(8,128)(2,1)} collective-permute-done((bf16[128,2048]{1,0:T(8,128)(2,1)}, bf16[128,2048]{1,0:T(8,128)(2,1)}, u32[]{:S(2)}, u32[]{:S(2)}) %collective-permute-start.30) | collective-permute-done | bytes 524320 | tf_op jit(solution)/shard_map/ppermute | solution.py:256
  368.2 16.1 %collective-permute-done.37 = bf16[128,2048]{1,0:T(8,128)(2,1)S(1)} collective-permute-done((bf16[128,2048]{1,0:T(8,128)(2,1)S(1)}, bf16[128,2048]{1,0:T(8,128)(2,1)S(1)}, u32[]{:S(2)}, u32[]{:S(2)}) %collective-permute-start.37) | collective-permute-done | bytes 524320 | tf_op jit(solution)/shard_map/ppermute | solution.py:253
  388.1 8.1 %collective-permute-done.38 = bf16[64,2048]{1,0:T(8,128)(2,1)S(1)} collective-permute-done((bf16[64,2048]{1,0:T(8,128)(2,1)S(1)}, bf16[64,2048]{1,0:T(8,128)(2,1)S(1)}, u32[]{:S(2)}, u32[]{:S(2)}) %collective-permute-start.38) | collective-permute-done | bytes 262176 | tf_op jit(solution)/shard_map/ppermute | solution.py:253
  409.4 10.0 %collective-permute-done.40 = bf16[128,2048]{1,0:T(8,128)(2,1)} collective-permute-done((bf16[128,2048]{1,0:T(8,128)(2,1)}, bf16[128,2048]{1,0:T(8,128)(2,1)}, u32[]{:S(2)}, u32[]{:S(2)}) %collective-permute-start.40) | collective-permute-done | bytes 524320 | tf_op jit(solution)/shard_map/ppermute | solution.py:256
  424.0 10.4 %attend_back.1 = (f32[512,512]{1,0:T(8,128)}, f32[4,512,128]{2,1,0:T(8,128)}, f32[4,512,128]{2,1,0:T(8,128)}) custom-call(s32[1]{0:T(128)} %bitcast.1.seen_ref, bf16[512,512]{1,0:T(8,128)(2,1)} %multiply_convert_fusion.3.q_ref, bf16[512,512]{1,0:T(8,128)(2,1)} %bitcast.188, bf16[512,512]{1,0:T(8,128)(2,1)} %get-tuple-element.73.o_ref, ...), custom_call_target="tpu_custom_call" | custom-call | tf_op jit(solution)/shard_map/attend_back/pallas_call | solution.py:166
  438.5 19.9 %collective-permute-start.43 = (bf16[512,128]{1,0:T(8,128)(2,1)}, bf16[512,128]{1,0:T(8,128)(2,1)}, u32[]{:S(2)}, u32[]{:S(2)}) collective-permute-start(bf16[512,128]{1,0:T(8,128)(2,1)} %get-tuple-element.197), channel_id=1, source_target_pairs={{0,12},{1,13},{2,14},{3,15},{4,0},{5,1},{6,2},{7,3},{8,4},{9,5},{1... | collective-permute-start | bytes 393224 | tf_op jit(solution)/shard_map/ppermute | solution.py:256
  480.7 4.0 collective-permute-start.55
  501.1 12.8 %collective-permute-done.50 = bf16[128,1408]{1,0:T(8,128)(2,1)} collective-permute-done((bf16[128,1408]{1,0:T(8,128)(2,1)}, bf16[128,1408]{1,0:T(8,128)(2,1)}, u32[]{:S(2)}, u32[]{:S(2)}) %collective-permute-start.50) | collective-permute-done | bytes 360480 | tf_op jit(solution)/shard_map/ppermute | solution.py:256
  514.0 5.7 collective-permute-start.56
  524.7 10.7 %collective-permute-done.47 = bf16[128,2048]{1,0:T(8,128)(2,1)S(1)} collective-permute-done((bf16[128,2048]{1,0:T(8,128)(2,1)}, bf16[128,2048]{1,0:T(8,128)(2,1)S(1)}, u32[]{:S(2)}, u32[]{:S(2)}) %collective-permute-start.47) | collective-permute-done | bytes 524320 | tf_op jit(solution)/shard_map/ppermute | solution.py:253
  542.9 12.4 %reduce-scatter.11.cloned.1.call-done = bf16[512,320]{0,1:T(8,128)(2,1)} async-done(((bf16[2048,320]{0,1:T(8,128)(2,1)}), bf16[512,320]{0,1:T(8,128)(2,1)}) %reduce-scatter.11.cloned.1.call-update) | async-done | bytes 327696 | tf_op jit(solution)/shard_map/reduce_scatter | solution.py:584
  557.0 4.1 all-to-all-start.1
  568.0 6.2 %convert_multiply_fusion = (f32[128,5632]{1,0:T(8,128)}, f32[128]{0:T(128)}, f32[128,5632]{1,0:T(8,128)}) fusion(f32[128]{0:T(128)S(1)} %copy-done.61, bf16[128,1408]{1,0:T(8,128)(2,1)} %get-tuple-element.184, bf16[128,1408]{1,0:T(8,128)(2,1)} %get-tuple-element.185, bf16[128,1408]{1,0:T(8,128)(2,1)} %get-tuple-element.186, ...), kind=kLoop, calls=%fused_computation.4 | loop fusion | flops 17301376 | bytes 11535360 | tf_op jit(solution)/shard_map/mul | solution.py:614
  (477 shorter events, 231.7 us)
Async XLA Ops:
  7.2 80.0 %all-gather.8.cloned.1.call-start = ((), (), s32[]{:S(2)}) async-start(), calls=%async_computation.11 | async-start | bytes 6488064 | tf_op jit(solution)/shard_map/all_gather | solution.py:365
  18.3 124.1 %all-gather.10.cloned.1.call-start = ((), (), s32[]{:S(2)}) async-start(), calls=%async_computation.12 | async-start | bytes 2359296 | tf_op jit(solution)/shard_map/all_gather | solution.py:370
  24.1 25.8 %collective-permute-start.5 = (bf16[512,320]{0,1:T(8,128)(2,1)S(1)}, bf16[512,320]{0,1:T(8,128)(2,1)S(1)}, u32[]{:S(2)}, u32[]{:S(2)}) collective-permute-start(bf16[512,320]{0,1:T(8,128)(2,1)S(1)} %copy_bitcast_fusion), channel_id=1, source_target_pairs={{0,4},{1,5},{2,6},{3,7},{4,8},{5,9},{6,10},{7,11},{8,12},{9,13},{1... | collective-permute-start | bytes 983048 | tf_op jit(solution)/shard_map/ppermute | solution.py:256
  25.5 24.3 %collective-permute-start.4 = (bf16[512,320]{0,1:T(8,128)(2,1)S(1)}, bf16[512,320]{0,1:T(8,128)(2,1)S(1)}, u32[]{:S(2)}, u32[]{:S(2)}) collective-permute-start(bf16[512,320]{0,1:T(8,128)(2,1)S(1)} %copy_bitcast_fusion), channel_id=1, source_target_pairs={{0,8},{1,9},{2,10},{3,11},{4,12},{5,13},{6,14},{7,15},{8,0},{9,1},... | collective-permute-start | bytes 983048 | tf_op jit(solution)/shard_map/ppermute | solution.py:256
  28.9 34.0 %collective-permute-start.10 = (bf16[128,2048]{1,0:T(8,128)(2,1)}, bf16[128,2048]{1,0:T(8,128)(2,1)S(1)}, u32[]{:S(2)}, u32[]{:S(2)}) collective-permute-start(bf16[128,2048]{1,0:T(8,128)(2,1)} %fusion.22), channel_id=1, source_target_pairs={{0,2},{1,3},{2,0},{3,1},{4,6},{5,7},{6,4},{7,5},{8,10},{9,11},{10,... | collective-permute-start | bytes 1572872 | tf_op jit(solution)/shard_map/ppermute | solution.py:253
  30.3 36.1 %collective-permute-start.9 = (bf16[128,2048]{1,0:T(8,128)(2,1)}, bf16[128,2048]{1,0:T(8,128)(2,1)S(1)}, u32[]{:S(2)}, u32[]{:S(2)}) collective-permute-start(bf16[128,2048]{1,0:T(8,128)(2,1)} %fusion.22), channel_id=1, source_target_pairs={{0,1},{1,0},{2,3},{3,2},{4,5},{5,4},{6,7},{7,6},{8,9},{9,8},{10,11... | collective-permute-start | bytes 1572872 | tf_op jit(solution)/shard_map/ppermute | solution.py:253
  50.2 31.7 %collective-permute-start.13 = (bf16[2048,320]{0,1:T(8,128)(2,1)S(1)}, bf16[2048,320]{0,1:T(8,128)(2,1)S(1)}, u32[]{:S(2)}, u32[]{:S(2)}) collective-permute-start(bf16[2048,320]{0,1:T(8,128)(2,1)S(1)} %constant_dynamic-slice_fusion.11), channel_id=1, source_target_pairs={{0,16},{16,0},{1,17},{17,1},{2,18},{18,2},{3,19},{19,3},{4,20},{20... | collective-permute-start | bytes 3932168 | tf_op jit(solution)/shard_map/ppermute | solution.py:259
  51.7 35.6 %collective-permute-start.17 = (bf16[128,1024]{1,0:T(8,128)(2,1)S(1)}, bf16[128,1024]{1,0:T(8,128)(2,1)}, u32[]{:S(2)}, u32[]{:S(2)}) collective-permute-start(bf16[128,1024]{1,0:T(8,128)(2,1)S(1)} %constant_dynamic-slice_fusion.12), channel_id=1, source_target_pairs={{0,0},{1,4},{2,8},{3,12},{4,1},{5,5},{6,9},{7,13},{8,2},{9,6},{10,... | collective-permute-start | bytes 786440 | tf_op jit(solution)/shard_map/ppermute | solution.py:357
  54.1 54.4 %collective-permute-start.8 = (bf16[128,1408]{1,0:T(8,128)(2,1)}, bf16[128,1408]{1,0:T(8,128)(2,1)}, u32[]{:S(2)}, u32[]{:S(2)}) collective-permute-start(bf16[128,1408]{1,0:T(8,128)(2,1)} %get-tuple-element.191), channel_id=1, source_target_pairs={{0,12},{1,13},{2,14},{3,15},{4,0},{5,1},{6,2},{7,3},{8,4},{9,5},{1... | collective-permute-start | bytes 1081352 | tf_op jit(solution)/shard_map/ppermute | solution.py:256
  75.2 33.3 %collective-permute-start.7 = (bf16[128,1408]{1,0:T(8,128)(2,1)}, bf16[128,1408]{1,0:T(8,128)(2,1)}, u32[]{:S(2)}, u32[]{:S(2)}) collective-permute-start(bf16[128,1408]{1,0:T(8,128)(2,1)} %get-tuple-element.192), channel_id=1, source_target_pairs={{0,8},{1,9},{2,10},{3,11},{4,12},{5,13},{6,14},{7,15},{8,0},{9,1},... | collective-permute-start | bytes 1081352 | tf_op jit(solution)/shard_map/ppermute | solution.py:256
  78.7 29.8 %collective-permute-start.6 = (bf16[128,1408]{1,0:T(8,128)(2,1)}, bf16[128,1408]{1,0:T(8,128)(2,1)}, u32[]{:S(2)}, u32[]{:S(2)}) collective-permute-start(bf16[128,1408]{1,0:T(8,128)(2,1)} %get-tuple-element.193), channel_id=1, source_target_pairs={{0,4},{1,5},{2,6},{3,7},{4,8},{5,9},{6,10},{7,11},{8,12},{9,13},{1... | collective-permute-start | bytes 1081352 | tf_op jit(solution)/shard_map/ppermute | solution.py:256
  87.3 171.2 %all-gather.6.cloned.1.call-start = ((), (), s32[]{:S(2)}) async-start(), calls=%async_computation.6 | async-start | bytes 12976128 | tf_op jit(solution)/shard_map/all_gather | solution.py:409
  113.0 306.4 %reduce-scatter.5.cloned.1.call-start = ((), (), s32[]{:S(2)}) async-start(), calls=%async_computation.7 | async-start | bytes 7208960 | tf_op jit(solution)/shard_map/reduce_scatter | solution.py:507
  131.4 44.9 %collective-permute-start.22 = (bf16[128,2048]{1,0:T(8,128)(2,1)S(1)}, bf16[128,2048]{1,0:T(8,128)(2,1)}, u32[]{:S(2)}, u32[]{:S(2)}) collective-permute-start(bf16[128,2048]{1,0:T(8,128)(2,1)S(1)} %bitcast_convert_fusion), channel_id=1, source_target_pairs={{0,8},{1,9},{2,10},{3,11},{4,12},{5,13},{6,14},{7,15},{8,0},{9,1},... | collective-permute-start | bytes 1572872 | tf_op jit(solution)/shard_map/ppermute | solution.py:256
  131.5 44.8 %collective-permute-start.21 = (bf16[128,2048]{1,0:T(8,128)(2,1)S(1)}, bf16[128,2048]{1,0:T(8,128)(2,1)}, u32[]{:S(2)}, u32[]{:S(2)}) collective-permute-start(bf16[128,2048]{1,0:T(8,128)(2,1)S(1)} %bitcast_convert_fusion), channel_id=1, source_target_pairs={{0,4},{1,5},{2,6},{3,7},{4,8},{5,9},{6,10},{7,11},{8,12},{9,13},{1... | collective-permute-start | bytes 1572872 | tf_op jit(solution)/shard_map/ppermute | solution.py:256
  145.6 34.7 %collective-permute-start.18 = (bf16[128,2048]{1,0:T(8,128)(2,1)S(1)}, bf16[128,2048]{1,0:T(8,128)(2,1)S(1)}, u32[]{:S(2)}, u32[]{:S(2)}) collective-permute-start(bf16[128,2048]{1,0:T(8,128)(2,1)S(1)} %get-tuple-element.171), channel_id=1, source_target_pairs={{0,1},{1,0},{2,3},{3,2},{4,5},{5,4},{6,7},{7,6},{8,9},{9,8},{10,11... | collective-permute-start | bytes 1572872 | tf_op jit(solution)/shard_map/ppermute | solution.py:253
  153.3 26.9 %collective-permute-start.20 = (bf16[128,2048]{1,0:T(8,128)(2,1)S(1)}, bf16[128,2048]{1,0:T(8,128)(2,1)S(1)}, u32[]{:S(2)}, u32[]{:S(2)}) collective-permute-start(bf16[128,2048]{1,0:T(8,128)(2,1)S(1)} %get-tuple-element.172), channel_id=1, source_target_pairs={{0,3},{1,2},{2,1},{3,0},{4,7},{5,6},{6,5},{7,4},{8,11},{9,10},{10,... | collective-permute-start | bytes 1572872 | tf_op jit(solution)/shard_map/ppermute | solution.py:253
  153.4 26.9 %collective-permute-start.19 = (bf16[128,2048]{1,0:T(8,128)(2,1)S(1)}, bf16[128,2048]{1,0:T(8,128)(2,1)S(1)}, u32[]{:S(2)}, u32[]{:S(2)}) collective-permute-start(bf16[128,2048]{1,0:T(8,128)(2,1)S(1)} %get-tuple-element.173), channel_id=1, source_target_pairs={{0,2},{1,3},{2,0},{3,1},{4,6},{5,7},{6,4},{7,5},{8,10},{9,11},{10,... | collective-permute-start | bytes 1572872 | tf_op jit(solution)/shard_map/ppermute | solution.py:253
  181.4 54.7 %collective-permute-start.26 = (bf16[128,2048]{1,0:T(8,128)(2,1)S(1)}, bf16[128,2048]{1,0:T(8,128)(2,1)S(1)}, u32[]{:S(2)}, u32[]{:S(2)}) collective-permute-start(bf16[128,2048]{1,0:T(8,128)(2,1)S(1)} %constant_dynamic-update-slice_fusion.12), channel_id=1, source_target_pairs={{0,12},{1,13},{2,14},{3,15},{4,0},{5,1},{6,2},{7,3},{8,4},{9,5},{1... | collective-permute-start | bytes 1572872 | tf_op jit(solution)/shard_map/ppermute | solution.py:256
  238.9 56.1 %collective-permute-start.28 = (bf16[512,2048]{1,0:T(8,128)(2,1)}, bf16[512,2048]{1,0:T(8,128)(2,1)}, u32[]{:S(2)}, u32[]{:S(2)}) collective-permute-start(bf16[512,2048]{1,0:T(8,128)(2,1)} %get-tuple-element.219), channel_id=1, source_target_pairs={{0,16},{16,0},{1,17},{17,1},{2,18},{18,2},{3,19},{19,3},{4,20},{20... | collective-permute-start | bytes 6291464 | tf_op jit(solution)/shard_map/ppermute | solution.py:259
  317.2 163.5 %reduce-scatter.7.cloned.1.call-start = ((), (), s32[]{:S(2)}) async-start(), calls=%async_computation.8 | async-start | bytes 1310720 | tf_op jit(solution)/shard_map/reduce_scatter | solution.py:526
  322.1 36.2 %collective-permute-start.30 = (bf16[128,2048]{1,0:T(8,128)(2,1)}, bf16[128,2048]{1,0:T(8,128)(2,1)}, u32[]{:S(2)}, u32[]{:S(2)}) collective-permute-start(bf16[128,2048]{1,0:T(8,128)(2,1)} %get-tuple-element.169), channel_id=1, source_target_pairs={{0,8},{1,9},{2,10},{3,11},{4,12},{5,13},{6,14},{7,15},{8,0},{9,1},... | collective-permute-start | bytes 1572872 | tf_op jit(solution)/shard_map/ppermute | solution.py:256
  366.4 31.8 %collective-permute-start.35 = (bf16[128,2048]{1,0:T(8,128)(2,1)S(1)}, bf16[128,2048]{1,0:T(8,128)(2,1)S(1)}, u32[]{:S(2)}, u32[]{:S(2)}) collective-permute-start(bf16[128,2048]{1,0:T(8,128)(2,1)S(1)} %get-tuple-element.163), channel_id=1, source_target_pairs={{0,8},{1,9},{2,10},{3,11},{4,12},{5,13},{6,14},{7,15},{8,0},{9,1},... | collective-permute-start | bytes 1572872 | tf_op jit(solution)/shard_map/ppermute | solution.py:256
  366.4 32.6 %collective-permute-start.34 = (bf16[128,2048]{1,0:T(8,128)(2,1)S(1)}, bf16[128,2048]{1,0:T(8,128)(2,1)}, u32[]{:S(2)}, u32[]{:S(2)}) collective-permute-start(bf16[128,2048]{1,0:T(8,128)(2,1)S(1)} %get-tuple-element.165), channel_id=1, source_target_pairs={{0,12},{1,13},{2,14},{3,15},{4,0},{5,1},{6,2},{7,3},{8,4},{9,5},{1... | collective-permute-start | bytes 1572872 | tf_op jit(solution)/shard_map/ppermute | solution.py:256
  419.4 100.2 %reduce-scatter.9.cloned.1.call-start = ((), (), s32[]{:S(2)}) async-start(), calls=%async_computation.9 | async-start | bytes 3604480 | tf_op jit(solution)/shard_map/reduce_scatter | solution.py:508
  422.8 132.5 %reduce-scatter.11.cloned.1.call-start = ((), (), s32[]{:S(2)}) async-start(), calls=%async_computation.10 | async-start | bytes 1638400 | tf_op jit(solution)/shard_map/reduce_scatter | solution.py:584
  438.5 33.1 %collective-permute-start.43 = (bf16[512,128]{1,0:T(8,128)(2,1)}, bf16[512,128]{1,0:T(8,128)(2,1)}, u32[]{:S(2)}, u32[]{:S(2)}) collective-permute-start(bf16[512,128]{1,0:T(8,128)(2,1)} %get-tuple-element.197), channel_id=1, source_target_pairs={{0,12},{1,13},{2,14},{3,15},{4,0},{5,1},{6,2},{7,3},{8,4},{9,5},{1... | collective-permute-start | bytes 393224 | tf_op jit(solution)/shard_map/ppermute | solution.py:256
  477.1 36.9 %collective-permute-start.50 = (bf16[128,1408]{1,0:T(8,128)(2,1)}, bf16[128,1408]{1,0:T(8,128)(2,1)}, u32[]{:S(2)}, u32[]{:S(2)}) collective-permute-start(bf16[128,1408]{1,0:T(8,128)(2,1)} %get-tuple-element.188), channel_id=1, source_target_pairs={{0,8},{1,9},{2,10},{3,11},{4,12},{5,13},{6,14},{7,15},{8,0},{9,1},... | collective-permute-start | bytes 1081352 | tf_op jit(solution)/shard_map/ppermute | solution.py:256
  478.5 41.1 %collective-permute-start.49 = (bf16[128,1408]{1,0:T(8,128)(2,1)}, bf16[128,1408]{1,0:T(8,128)(2,1)}, u32[]{:S(2)}, u32[]{:S(2)}) collective-permute-start(bf16[128,1408]{1,0:T(8,128)(2,1)} %get-tuple-element.189), channel_id=1, source_target_pairs={{0,4},{1,5},{2,6},{3,7},{4,8},{5,9},{6,10},{7,11},{8,12},{9,13},{1... | collective-permute-start | bytes 1081352 | tf_op jit(solution)/shard_map/ppermute | solution.py:256
  480.7 33.3 %collective-permute-start.55 = (bf16[128,1024]{1,0:T(8,128)(2,1)}, bf16[128,1024]{1,0:T(8,128)(2,1)}, u32[]{:S(2)}, u32[]{:S(2)}) collective-permute-start(bf16[128,1024]{1,0:T(8,128)(2,1)} %reduce-scatter.7.cloned.1.call-done), channel_id=1, source_target_pairs={{0,0},{4,1},{8,2},{12,3},{1,4},{5,5},{9,6},{13,7},{2,8},{6,9},{10,... | collective-permute-start | bytes 786440 | tf_op jit(solution)/shard_map/ppermute | solution.py:579
  494.2 30.5 %collective-permute-start.46 = (bf16[128,2048]{1,0:T(8,128)(2,1)}, bf16[128,2048]{1,0:T(8,128)(2,1)S(1)}, u32[]{:S(2)}, u32[]{:S(2)}) collective-permute-start(bf16[128,2048]{1,0:T(8,128)(2,1)} %get-tuple-element.158), channel_id=1, source_target_pairs={{0,1},{1,0},{2,3},{3,2},{4,5},{5,4},{6,7},{7,6},{8,9},{9,8},{10,11... | collective-permute-start | bytes 1572872 | tf_op jit(solution)/shard_map/ppermute | solution.py:253
  497.9 26.8 %collective-permute-start.48 = (bf16[128,2048]{1,0:T(8,128)(2,1)}, bf16[128,2048]{1,0:T(8,128)(2,1)S(1)}, u32[]{:S(2)}, u32[]{:S(2)}) collective-permute-start(bf16[128,2048]{1,0:T(8,128)(2,1)} %get-tuple-element.159), channel_id=1, source_target_pairs={{0,3},{1,2},{2,1},{3,0},{4,7},{5,6},{6,5},{7,4},{8,11},{9,10},{10,... | collective-permute-start | bytes 1572872 | tf_op jit(solution)/shard_map/ppermute | solution.py:253
  (110 other events, 1062.1 us)
Sparse Core Ops, SparseCore 0:
  10.5 51.6 all-gather.7
  87.4 35.0 all-gather.9
  125.0 87.1 all-gather.5
  317.3 82.5 reduce-scatter.4
  419.5 24.3 reduce-scatter.6
  447.4 40.4 reduce-scatter.8
  519.8 35.4 reduce-scatter.10

commit v8 on v7

--- a/solution.py
+++ b/solution.py
@@ -51,8 +51,113 @@
     return jnp.transpose(wide)[:8]
 
 
-def attend_kernel(seen_ref, q_ref, kk_ref, vv_ref, qpos_ref, kpos_ref, o_ref, lse_ref):
+def turn(values):
+    width = values.shape[1]
+    half_dim = HEAD_DIM // 2
+    lane = lax.broadcasted_iota(jnp.int32, values.shape, 1)
+    ahead = pltpu.roll(values, width - half_dim, 1)
+    behind = pltpu.roll(values, half_dim, 1)
+    return jnp.where(lane % HEAD_DIM < half_dim, -ahead, behind)
+
+
+def rotate(values, cosine, sine):
+    return values * cosine + turn(values) * sine
+
+
+def unrotate(grads, cosine, sine):
+    return grads * cosine - turn(grads * sine)
+
+
+def project_kernel(low_ref, w_ref, cos_ref, sin_ref, q_ref, kv_ref):
+    made = dot(low_ref[...], w_ref[...])
+    cosine, sine = cos_ref[...], sin_ref[...]
+    for i in range(q_ref.shape[1] // PAIR):
+        q = rotate(made[:, i * PAIR : (i + 1) * PAIR], cosine, sine).astype(bf16)
+        q_ref[:, i * PAIR : (i + 1) * PAIR] = (q.astype(f32) * HEAD_DIM ** (-0.5)).astype(bf16)
+    kv = made[:, q_ref.shape[1] :]
+    lane = lax.broadcasted_iota(jnp.int32, kv.shape, 1)
+    kv_ref[...] = jnp.where(lane < HEAD_DIM, rotate(kv, cosine, sine), kv).astype(bf16)
+
+
+def project(low, weights, cosine, sine):
+    tokens, width = low.shape
+    q_width = weights.shape[1] - PAIR
+    rows = block_rows(tokens)
+    return pl.pallas_call(
+        project_kernel,
+        out_shape=(
+            jax.ShapeDtypeStruct((tokens, q_width), bf16),
+            jax.ShapeDtypeStruct((tokens, PAIR), bf16),
+        ),
+        grid=(tokens // rows,),
+        in_specs=[
+            pl.BlockSpec((rows, width), lambda i: (i, 0)),
+            pl.BlockSpec(weights.shape, lambda i: (0, 0)),
+            pl.BlockSpec((rows, PAIR), lambda i: (i, 0)),
+            pl.BlockSpec((rows, PAIR), lambda i: (i, 0)),
+        ],
+        out_specs=[
+            pl.BlockSpec((rows, q_width), lambda i: (i, 0)),
+            pl.BlockSpec((rows, PAIR), lambda i: (i, 0)),
+        ],
+        name="project",
+    )(low, weights, cosine, sine)
+
+
+def feed_kernel(low_ref, w_ref, grad_hidden_ref, hidden_ref, grad_gate_ref, grad_up_ref, back_ref):
+    low = low_ref[...]
+    gate = dot(low, w_ref[0])
+    up = dot(low, w_ref[1])
+    grad_hidden = grad_hidden_ref[...]
+    sigmoid_gate = 1.0 / (1.0 + jnp.exp(-gate))
+    silu = gate * sigmoid_gate
+    hidden_ref[...] = (silu * up).astype(bf16)
+    grad_gate = (
+        grad_hidden * up * sigmoid_gate * (1.0 + gate * (1.0 - sigmoid_gate))
+    ).astype(bf16)
+    grad_up = (grad_hidden * silu).astype(bf16)
+    grad_gate_ref[...] = grad_gate
+    grad_up_ref[...] = grad_up
+    back_ref[...] = (
+        dot(grad_gate, w_ref[0], ((1,), (1,))) + dot(grad_up, w_ref[1], ((1,), (1,)))
+    ).astype(bf16)
+
+
+def feed(low, weights, grad_hidden):
+    tokens, width = low.shape
+    block = weights.shape[2]
+    rows = block_rows(tokens)
+    narrow = pl.BlockSpec((rows, block), lambda i: (i, 0))
+    wide = pl.BlockSpec((rows, width), lambda i: (i, 0))
+    return pl.pallas_call(
+        feed_kernel,
+        out_shape=(
+            jax.ShapeDtypeStruct((tokens, block), bf16),
+            jax.ShapeDtypeStruct((tokens, block), bf16),
+            jax.ShapeDtypeStruct((tokens, block), bf16),
+            jax.ShapeDtypeStruct((tokens, width), bf16),
+        ),
+        grid=(tokens // rows,),
+        in_specs=[wide, pl.BlockSpec(weights.shape, lambda i: (0, 0, 0)), narrow],
+        out_specs=[narrow, narrow, narrow, wide],
+        name="feed",
+    )(low, weights, grad_hidden)
+
+
+def both_lanes(kv_ref, kk_ref, vv_ref):
+    @pl.when(pl.program_id(0) == 0)
+    def _():
+        for index in range(kv_ref.shape[0]):
+            kv = kv_ref[index].astype(f32)
+            swapped = pltpu.roll(kv, HEAD_DIM, 1)
+            lane = lax.broadcasted_iota(jnp.int32, kv.shape, 1)
+            kk_ref[index] = jnp.where(lane < HEAD_DIM, kv, swapped).astype(bf16)
+            vv_ref[index] = jnp.where(lane < HEAD_DIM, swapped, kv).astype(bf16)
+
+
+def attend_kernel(seen_ref, q_ref, kv_ref, qpos_ref, kpos_ref, o_ref, lse_ref, kk_ref, vv_ref):
     rows = q_ref.shape[0]
+    both_lanes(kv_ref, kk_ref, vv_ref)
     stacked = stack_heads(q_ref[...], rows)
     qpos = jnp.concatenate([qpos_ref[...]] * GROUP_HEADS, axis=0)
 
@@ -81,10 +186,11 @@
 
 
 def attend_back_kernel(
-    seen_ref, q_ref, do_ref, o_ref, kk_ref, vv_ref, lse_ref, qpos_ref, kpos_ref,
-    dq_ref, dkk_ref, dvv_ref, qs_ref, dos_ref, delta_ref, dqs_ref,
+    seen_ref, q_ref, do_ref, o_ref, kv_ref, lse_ref, qpos_ref, kpos_ref, cos_ref, sin_ref,
+    dq_ref, dkv_ref, qs_ref, dos_ref, delta_ref, dqs_ref, kk_ref, vv_ref, dkk_ref, dvv_ref,
 ):
     rows = q_ref.shape[0]
+    both_lanes(kv_ref, kk_ref, vv_ref)
 
     @pl.when(pl.program_id(0) == 0)
     def _():
@@ -116,7 +222,20 @@
     def _(index):
         dqs_ref[...] += unit(index, False)
 
-    dq_ref[...] = unstack_heads(dqs_ref[...], rows)
+    grads = unstack_heads(dqs_ref[...], rows) * HEAD_DIM ** (-0.5)
+    cosine, sine = cos_ref[...], sin_ref[...]
+    for i in range(dq_ref.shape[1] // PAIR):
+        part = unrotate(grads[:, i * PAIR : (i + 1) * PAIR], cosine, sine)
+        dq_ref[:, i * PAIR : (i + 1) * PAIR] = part.astype(bf16)
+
+    @pl.when(pl.program_id(0) == pl.num_programs(0) - 1)
+    def _():
+        for index in range(kv_ref.shape[0]):
+            keys, values = dkk_ref[index], dvv_ref[index]
+            keys = keys + pltpu.roll(keys, HEAD_DIM, 1)
+            values = values + pltpu.roll(values, HEAD_DIM, 1)
+            lane = lax.broadcasted_iota(jnp.int32, keys.shape, 1)
+            dkv_ref[index] = jnp.where(lane < HEAD_DIM, keys, values).astype(bf16)
 
 
 def block_rows(length):
@@ -128,7 +247,7 @@
     return pl.BlockSpec(shape, lambda i, seen: zeros)
 
 
-def attend(seen, q, kk, vv, order):
+def attend(seen, q, kv, order):
     length, width = q.shape
     rows = block_rows(length)
     stacked = GROUP_HEADS * rows
@@ -144,8 +263,7 @@
             grid=(steps,),
             in_specs=[
                 pl.BlockSpec((rows, width), lambda i, seen: (i, 0)),
-                whole(kk.shape),
-                whole(vv.shape),
+                whole(kv.shape),
                 pl.BlockSpec((rows, 1), lambda i, seen: (i, 0)),
                 whole((1, length)),
             ],
@@ -153,12 +271,13 @@
                 pl.BlockSpec((rows, width), lambda i, seen: (i, 0)),
                 pl.BlockSpec((pl.Squeezed(), 8, stacked), lambda i, seen: (i, 0, 0)),
             ],
+            scratch_shapes=[pltpu.VMEM(kv.shape, bf16), pltpu.VMEM(kv.shape, bf16)],
         ),
         name="attend",
-    )(seen, q, kk, vv, order[:, None], order[None, :])
-
-
-def attend_back(seen, q, do, o, kk, vv, lse, order):
+    )(seen, q, kv, order[:, None], order[None, :])
+
+
+def attend_back(seen, q, do, o, kv, lse, order, cosine, sine):
     length, width = q.shape
     rows = block_rows(length)
     stacked = GROUP_HEADS * rows
@@ -166,9 +285,8 @@
     return pl.pallas_call(
         attend_back_kernel,
         out_shape=(
-            jax.ShapeDtypeStruct((length, width), f32),
-            jax.ShapeDtypeStruct(kk.shape, f32),
-            jax.ShapeDtypeStruct(vv.shape, f32),
+            jax.ShapeDtypeStruct((length, width), bf16),
+            jax.ShapeDtypeStruct(kv.shape, bf16),
         ),
         grid_spec=pltpu.PrefetchScalarGridSpec(
             num_scalar_prefetch=1,
@@ -177,26 +295,33 @@
                 pl.BlockSpec((rows, width), lambda i, seen: (i, 0)),
                 pl.BlockSpec((rows, width), lambda i, seen: (i, 0)),
                 pl.BlockSpec((rows, width), lambda i, seen: (i, 0)),
-                whole(kk.shape),
-                whole(vv.shape),
+                whole(kv.shape),
                 pl.BlockSpec((pl.Squeezed(), 8, stacked), lambda i, seen: (i, 0, 0)),
                 pl.BlockSpec((8, rows), lambda i, seen: (0, i)),
                 whole((length, 1)),
+                pl.BlockSpec((rows, PAIR), lambda i, seen: (i, 0)),
+                pl.BlockSpec((rows, PAIR), lambda i, seen: (i, 0)),
             ],
             out_specs=[
                 pl.BlockSpec((rows, width), lambda i, seen: (i, 0)),
-                whole(kk.shape),
-                whole(vv.shape),
+                whole(kv.shape),
             ],
             scratch_shapes=[
                 pltpu.VMEM((stacked, PAIR), bf16),
                 pltpu.VMEM((stacked, PAIR), bf16),
                 pltpu.VMEM((8, stacked), f32),
                 pltpu.VMEM((stacked, PAIR), f32),
+                pltpu.VMEM(kv.shape, bf16),
+                pltpu.VMEM(kv.shape, bf16),
+                pltpu.VMEM(kv.shape, f32),
+                pltpu.VMEM(kv.shape, f32),
             ],
         ),
         name="attend_back",
-    )(seen, q, do, o, kk, vv, lse, jnp.broadcast_to(order[None, :], (8, length)), order[:, None])
+    )(
+        seen, q, do, o, kv, lse, jnp.broadcast_to(order[None, :], (8, length)), order[:, None],
+        cosine, sine,
+    )
 
 
 def normalize(values):
@@ -212,21 +337,15 @@
     half_dim = HEAD_DIM // 2
     frequency = rope_base ** (-(jnp.arange(half_dim).astype(f32) * 2.0 / HEAD_DIM))
     angles = positions.astype(f32)[:, None] * frequency
-    angles = jnp.concatenate([angles, angles], axis=-1)
-    return jnp.cos(angles)[:, None, :], jnp.sin(angles)[:, None, :]
-
-
-def turn(values):
+    times = PAIR // half_dim
+    return jnp.tile(jnp.cos(angles), (1, times)), jnp.tile(jnp.sin(angles), (1, times))
+
+
+def unrotate_keys(grads, cosine, sine):
     half_dim = HEAD_DIM // 2
-    return jnp.concatenate([-values[..., half_dim:], values[..., :half_dim]], axis=-1)
-
-
-def rotate(values, cosine, sine):
-    return values * cosine + turn(values) * sine
-
-
-def unrotate(grads, cosine, sine):
-    return grads * cosine - turn(grads * sine)
+    sines = grads * sine
+    turned = jnp.concatenate([-sines[:, half_dim:], sines[:, :half_dim]], axis=1)
+    return grads * cosine - turned
 
 
 def tie(*values):
@@ -389,15 +508,12 @@
         grad_y = (
             cotangent.astype(f32) * select.astype(f32)[..., None]
         ).reshape(tokens, width)
-        projected = [dot(low_one, qkv_full[i]) for i in range(n_dp)]
         cut = q_width // n_dp
-        q = jnp.concatenate([one[:, :cut] for one in projected], axis=1)
-        kv = jnp.concatenate([one[:, cut:] for one in projected], axis=1)
         plane_tokens = GROUP * tokens
-        q = rotate(q.reshape(plane_tokens, GROUP_HEADS, HEAD_DIM), cosine, sine)
-        q = (q.astype(bf16).astype(f32) * HEAD_DIM ** (-0.5)).astype(bf16).reshape(plane_tokens, q_width)
-        k = rotate(kv[:, None, :HEAD_DIM], cosine, sine)[:, 0]
-        kv_low = jnp.concatenate([k, kv[:, HEAD_DIM:]], axis=1).astype(bf16)
+        qkv_weights = jnp.concatenate(
+            [one[:, :cut] for one in qkv_full] + [one[:, cut:] for one in qkv_full], axis=1
+        )
+        q, kv_low = project(low_one, qkv_weights, cosine, sine)
         kv_all = jnp.stack(gather_z(kv_low))
         grad_y_low, kv_all = tie(grad_y.astype(bf16), kv_all)
         *gate_up_sent, q = tie(*gate_up_sent, q)
@@ -410,11 +526,7 @@
             gate_up_part, both, axis_index_groups=in_plane_dp, tiled=False
         )
         gate_up_full = gate_up_full.reshape(2, width, ff_block)
-        gate_full = gate_up_full[0]
-        up_full = gate_up_full[1]
         grad_y_all = jnp.concatenate(gather_z(grad_y_low), axis=0)
-        kk = jnp.concatenate([kv_all[..., :HEAD_DIM]] * 2, axis=-1)
-        vv = jnp.concatenate([kv_all[..., HEAD_DIM:]] * 2, axis=-1)
 
         def by_seq(value, axis):
             shape = value.shape
@@ -432,9 +544,10 @@
         order = order.astype(jnp.int32)
         seen = (p + 1).astype(jnp.int32).reshape(1)
         q_seq = by_seq(q, 0)
-        kk_seq = by_seq(kk, 1)
-        vv_seq = by_seq(vv, 1)
-        pieces = [attend(seen, q_seq[i], kk_seq[i], vv_seq[i], order) for i in range(seqs)]
+        kv_seq = by_seq(kv_all, 1)
+        cos_seq = by_seq(cosine, 0)
+        sin_seq = by_seq(sine, 0)
+        pieces = [attend(seen, q_seq[i], kv_seq[i], order) for i in range(seqs)]
         o_seq = [one[0] for one in pieces]
         lse_seq = [one[1] for one in pieces]
         o = from_seq(jnp.stack(o_seq), 0)
@@ -446,12 +559,7 @@
         normed_two, inverse_two = normalize(x_mid)
         low_two = reorder(normed_two.astype(bf16))
         low_two, grad_y_all = tie(low_two, grad_y_all)
-        low_two = jnp.concatenate(gather_z(low_two), axis=0)
-        gate = dot(low_two, gate_full)
-        up_part = dot(low_two, up_full)
-        sigmoid_gate = 1.0 / (1.0 + jnp.exp(-gate))
-        hidden = (gate * sigmoid_gate * up_part).astype(bf16)
-
+        low_two_own, *low_two_sent = gather_z(low_two)
         grad_hidden = functools.reduce(
             jnp.add,
             [
@@ -459,14 +567,9 @@
                 for i in range(n_dp)
             ],
         )
-        grad_gate = (
-            grad_hidden * up_part * sigmoid_gate * (1.0 + gate * (1.0 - sigmoid_gate))
-        ).astype(bf16)
-        grad_up = (grad_hidden * gate * sigmoid_gate).astype(bf16)
-        grad_low_two = dot(grad_gate, gate_full, ((1,), (1,))) + dot(
-            grad_up, up_full, ((1,), (1,))
-        )
-        grad_low_two = grad_low_two.astype(bf16)
+        *low_two_sent, grad_hidden = tie(*low_two_sent, grad_hidden)
+        low_two = jnp.concatenate([low_two_own] + low_two_sent, axis=0)
+        hidden, grad_gate, grad_up, grad_low_two = feed(low_two, gate_up_full, grad_hidden)
         hidden_later, grad_gate_later, grad_up_later, grad_low_two = tie(
             hidden, grad_gate, grad_up, grad_low_two
         )
@@ -526,7 +629,8 @@
         out_sum = lax.psum_scatter(out_part_sum, "seq", axis_index_groups=across, tiled=True)
         pieces = [
             attend_back(
-                seen, q_seq[i], grad_o_seq[i], o_seq[i], kk_seq[i], vv_seq[i], lse_seq[i], order
+                seen, q_seq[i], grad_o_seq[i], o_seq[i], kv_seq[i], lse_seq[i], order,
+                cos_seq[i], sin_seq[i],
             )
             for i in range(seqs)
         ]
@@ -534,26 +638,18 @@
         mixed = functools.reduce(
             jnp.add, [g.astype(f32) for g in mixed_sent], mixed[:tokens].astype(f32)
         )
-        grad_q = from_seq(grad_q, 0) * HEAD_DIM ** (-0.5)
-        grad_kk = from_seq(jnp.stack([one[1] for one in pieces]), 1)
-        grad_vv = from_seq(jnp.stack([one[2] for one in pieces]), 1)
-        grad_kv = jnp.concatenate(
-            [
-                grad_kk[..., :HEAD_DIM] + grad_kk[..., HEAD_DIM:],
-                grad_vv[..., :HEAD_DIM] + grad_vv[..., HEAD_DIM:],
-            ],
-            axis=-1,
-        ).astype(bf16)
+        query_pre = from_seq(grad_q, 0)
+        grad_kv = from_seq(jnp.stack([one[1] for one in pieces]), 1)
         grad_kv = scatter_z([grad_kv[t] for t in range(planes)])
         grad_kv, gate_up_late = tie(grad_kv, gate_up_sum)
         gate_up_sent = []
         for t in range(planes):
             block = lax.dynamic_index_in_dim(gate_up_late, (p + t) % planes, 0, keepdims=False)
             gate_up_sent.append(shift_z(block, t) if t else block)
-        query_pre = unrotate(grad_q.reshape(plane_tokens, GROUP_HEADS, HEAD_DIM), cosine, sine)
-        query_pre = query_pre.reshape(plane_tokens, q_width).astype(bf16)
         query_pre, out_sum = tie(query_pre, out_sum)
-        key_pre = unrotate(grad_kv[:, None, :HEAD_DIM], cosine, sine)[:, 0]
+        key_pre = unrotate_keys(
+            grad_kv[:, :HEAD_DIM], cosine[:, :HEAD_DIM], sine[:, :HEAD_DIM]
+        )
         kv_pre = jnp.concatenate([key_pre, grad_kv[:, HEAD_DIM:]], axis=1).astype(bf16)
         pre = [
             jnp.concatenate(
@@ -563,8 +659,8 @@
         ]
         outputs = (x_mid + mixed).astype(bf16).reshape(seqs, rows, width)
 
-        grad_low_one = functools.reduce(
-            jnp.add, [dot(pre[i], qkv_full[i], ((1,), (1,))) for i in range(n_dp)]
+        grad_low_one = dot(
+            jnp.concatenate([query_pre, kv_pre], axis=1), qkv_weights, ((1,), (1,))
         ).astype(bf16)
         inner_one = scatter_w([grad_low_one[j * tokens : (j + 1) * tokens] for j in range(GROUP)])
         grad_inputs = grad_x_mid + norm_back(inner_one, normed_one, inverse_one)

time: 602 us -> 579 us (0.962)
  waiting for transfers between devices: 185 us -> 220 us
  Pallas kernels: 17.9 us -> 52.7 us
  matrix products: 69.8 us -> 36.9 us
  local copies, waits for them, and re-layouts: 89 us -> 66.9 us
  starting transfers between devices: 159 us -> 137 us
  other arithmetic: 55.8 us -> 41 us
    ppermute x27, starting transfers between devices: 84 us -> 48.8 us  [shift_z(): lax.ppermute(value, 'seq', [(s, (s + GROUP * t) % n_seq) for s in range(n...]
    pallas_call x0 -> x2, Pallas kernels: none -> 33.8 us  [the longest x1 27.8 us: feed(): pl.pallas_call(feed_kernel, out_shape=(jax.ShapeDtypeStruct((tokens, bloc...]
    dot_general x20 -> x13, matrix products: 69.8 us -> 36.9 us  [dot(): lax.dot_general(left, right, (contract, ((), ())), preferred_element_type...]
    ppermute x27, waiting for transfers between devices: 121 us -> 154 us  [shift_z(): lax.ppermute(value, 'seq', [(s, (s + GROUP * t) % n_seq) for s in range(n...]
    ppermute x17, waiting for transfers between devices: 48.5 us -> 37.1 us  [xor_w(): return lax.ppermute(value, 'seq', [(s, s ^ j) for s in range(n_seq)])]
    slice x5 -> x4, local copies, waits for them, and re-layouts: 11.3 us -> 0.21 us  [the longest x2 0.14 us: body(): one[:, :cut]]
    ppermute x13, starting transfers between devices: 34.1 us -> 44.9 us  [shift_dp(): return lax.ppermute(value, 'dp', [(c, (c + t) % n_dp) for c in range(n_dp)])]
    reduce_scatter x1, waiting for transfers between devices: 12.4 us -> 22 us  [body(): lax.psum_scatter(qkv_sum, 'seq', axis_index_groups=across, tiled=True)]
  transfers between devices with their start and end apart: 68 -> 68, of which waited for: 19 -> 25; matrix products, arithmetic and copies ran while one was open for 32% -> 22% of each run, Pallas kernels for 3% -> 9%
where the time goes in v8:
time: 579 us; the launch traced here: 571 us
  waiting for transfers between devices  220 us (38%)
  starting transfers between devices  137 us (24%)
  local copies, waits for them, and re-layouts  66.9 us (12%)
  Pallas kernels  52.7 us (9%)
  other arithmetic  41 us (7%)
  matrix products  36.9 us (6%)
  between operations  15.9 us (3%)
    ppermute x27, waiting for transfers between devices, shift_z(): lax.ppermute(value, 'seq', [(s, (s + GROUP * t) % n_seq) for s in range(n...  154 us
    ppermute x27, starting transfers between devices, shift_z(): lax.ppermute(value, 'seq', [(s, (s + GROUP * t) % n_seq) for s in range(n...  48.8 us
    ppermute x13, starting transfers between devices, shift_dp(): return lax.ppermute(value, 'dp', [(c, (c + t) % n_dp) for c in range(n_dp)])  44.9 us
    ppermute x17, waiting for transfers between devices, xor_w(): return lax.ppermute(value, 'seq', [(s, s ^ j) for s in range(n_seq)])  37.1 us
    dot_general x13, matrix products, dot(): lax.dot_general(left, right, (contract, ((), ())), preferred_element_type...  36.9 us
    ppermute x17, starting transfers between devices, xor_w(): return lax.ppermute(value, 'seq', [(s, s ^ j) for s in range(n_seq)])  29.1 us
    pallas_call x1, Pallas kernels, feed(): pl.pallas_call(feed_kernel, out_shape=(jax.ShapeDtypeStruct((tokens, bloc...  27.8 us
    unnamed x181, local copies, waits for them, and re-layouts  23.8 us
  transfers between devices with their start and end apart: 68, of which 25 were waited for; matrix products, arithmetic and copies ran while one was open for 22% of the time, Pallas kernels for 9%

profile of v8, /device:TPU:1, one launch (start us, length us, event | category | flops | bytes accessed | tf_op | source)
XLA Modules:
  0.0 570.6 jit_solution(15168756656510883219)
XLA Ops:
  15.0 4.1 all-to-all-start
  26.8 4.1 collective-permute-start.3
  35.8 24.0 %collective-permute-done.4 = bf16[512,320]{1,0:T(8,128)(2,1)S(1)} collective-permute-done((bf16[512,320]{1,0:T(8,128)(2,1)S(1)}, bf16[512,320]{1,0:T(8,128)(2,1)S(1)}, u32[]{:S(2)}, u32[]{:S(2)}) %collective-permute-start.4) | collective-permute-done | bytes 327712 | tf_op jit(solution)/shard_map/ppermute | solution.py:375
  61.9 5.2 collective-permute-start.13
  69.2 3.6 collective-permute-start.17
  82.2 14.3 %collective-permute-start.12 = (bf16[64,2048]{1,0:T(8,128)(2,1)S(1)}, bf16[64,2048]{1,0:T(8,128)(2,1)S(1)}, u32[]{:S(2)}, u32[]{:S(2)}) collective-permute-start(bf16[64,2048]{1,0:T(8,128)(2,1)S(1)} %slice.444), channel_id=1, source_target_pairs={{0,1},{1,0},{2,3},{3,2},{4,5},{5,4},{6,7},{7,6},{8,9},{9,8},{10,11... | collective-permute-start | bytes 786440 | tf_op jit(solution)/shard_map/ppermute | solution.py:372
  110.1 6.0 %project.1 = (bf16[512,512]{1,0:T(8,128)(2,1)}, bf16[512,128]{1,0:T(8,128)(2,1)}) custom-call(bf16[512,2048]{1,0:T(8,128)(2,1)} %get-tuple-element.238.low_ref, bf16[2048,640]{1,0:T(8,128)(2,1)} %pad_maximum_fusion.w_ref, f32[512,128]{1,0:T(8,128)} %copy.51.cos_ref, f32[512,128]{1,0:T(8,128)} %copy.52.sin_ref), custom_call_target="tpu_custom_call" | custom-call | tf_op jit(solution)/shard_map/project/pallas_call | solution.py:86
  116.1 11.2 %collective-permute-done.8 = bf16[128,1408]{1,0:T(8,128)(2,1)} collective-permute-done((bf16[128,1408]{1,0:T(8,128)(2,1)}, bf16[128,1408]{1,0:T(8,128)(2,1)}, u32[]{:S(2)}, u32[]{:S(2)}) %collective-permute-start.8) | collective-permute-done | bytes 360480 | tf_op jit(solution)/shard_map/ppermute | solution.py:375
  137.8 5.8 %collective-permute-done.15 = bf16[512,128]{1,0:T(8,128)(2,1)S(1)} collective-permute-done((bf16[512,128]{1,0:T(8,128)(2,1)S(1)}, bf16[512,128]{1,0:T(8,128)(2,1)S(1)}, u32[]{:S(2)}, u32[]{:S(2)}) %collective-permute-start.15) | collective-permute-done | bytes 131104 | tf_op jit(solution)/shard_map/ppermute | solution.py:375
  149.5 7.6 %attend.1 = (bf16[512,512]{1,0:T(8,128)(2,1)}, f32[4,8,1024]{2,1,0:T(8,128)}) custom-call(s32[1]{0:T(128)} %bitcast.1.seen_ref, bf16[512,512]{1,0:T(8,128)(2,1)} %get-tuple-element.77.q_ref, bf16[4,512,128]{2,1,0:T(8,128)(2,1)} %pad_maximum_fusion.9.kv_ref, s32[512,1]{1,0:T(8,128)} %copy.53.qpos_ref.kpos_ref, s32[1,512]{1,0:T(1,128)} %bitcast.159), custom_call_target="tpu_custom_call" | custom-call | tf_op jit(solution)/shard_map/attend/pallas_call | solution.py:255
  163.1 30.4 %collective-permute-done.22 = bf16[128,2048]{1,0:T(8,128)(2,1)} collective-permute-done((bf16[128,2048]{1,0:T(8,128)(2,1)S(1)}, bf16[128,2048]{1,0:T(8,128)(2,1)}, u32[]{:S(2)}, u32[]{:S(2)}) %collective-permute-start.22) | collective-permute-done | bytes 524320 | tf_op jit(solution)/shard_map/ppermute | solution.py:375
  207.5 10.2 %collective-permute-done.25 = bf16[128,2048]{1,0:T(8,128)(2,1)S(1)} collective-permute-done((bf16[128,2048]{1,0:T(8,128)(2,1)S(1)}, bf16[128,2048]{1,0:T(8,128)(2,1)S(1)}, u32[]{:S(2)}, u32[]{:S(2)}) %collective-permute-start.25) | collective-permute-done | bytes 524320 | tf_op jit(solution)/shard_map/ppermute | solution.py:375
  225.2 31.1 %collective-permute-start.28 = (bf16[512,2048]{1,0:T(8,128)(2,1)}, bf16[512,2048]{1,0:T(8,128)(2,1)}, u32[]{:S(2)}, u32[]{:S(2)}) collective-permute-start(bf16[512,2048]{1,0:T(8,128)(2,1)} %get-tuple-element.222.low_ref), channel_id=1, source_target_pairs={{0,16},{16,0},{1,17},{17,1},{2,18},{18,2},{3,19},{19,3},{4,20},{20... | collective-permute-start | bytes 6291464 | tf_op jit(solution)/shard_map/ppermute | solution.py:378
  256.3 27.8 %feed.1 = (bf16[512,1408]{1,0:T(8,128)(2,1)}, bf16[512,1408]{1,0:T(8,128)(2,1)}, bf16[512,1408]{1,0:T(8,128)(2,1)}, bf16[512,2048]{1,0:T(8,128)(2,1)}) custom-call(bf16[512,2048]{1,0:T(8,128)(2,1)} %get-tuple-element.222.low_ref, bf16[2,2048,1408]{2,1,0:T(8,128)(2,1)} %bitcast.133, f32[512,1408]{1,0:T(8,128)} %convolution_add_fusion.grad_hidden_ref), custom_call_target="tpu_custom_call" | custom-call | tf_op jit(solution)/shard_map/feed/pallas_call | solution.py:132
  293.2 8.6 %convolution_convert_fusion = bf16[2048,1408]{1,0:T(8,128)(2,1)} fusion(bf16[1024,2048]{1,0:T(8,128)(2,1)S(1)} %constant_dynamic-update-slice_fusion.32, bf16[512,1408]{1,0:T(8,128)(2,1)S(1)} %collective-permute-done.29, bf16[512,1408]{1,0:T(8,128)(2,1)S(1)} %get-tuple-element.163), kind=kOutput, calls=%fused_computation | convolution fusion | flops 5914230784 | bytes 12845056 | tf_op jit(solution)/shard_map/dot_general | solution.py:26
  301.8 7.1 %collective-permute-done.27 = bf16[128,2048]{1,0:T(8,128)(2,1)S(1)} collective-permute-done((bf16[128,2048]{1,0:T(8,128)(2,1)}, bf16[128,2048]{1,0:T(8,128)(2,1)S(1)}, u32[]{:S(2)}, u32[]{:S(2)}) %collective-permute-start.27) | collective-permute-done | bytes 524320 | tf_op jit(solution)/shard_map/ppermute | solution.py:375
  320.1 5.9 %convolution_convert_fusion.1 = bf16[1408,1024]{1,0:T(8,128)(2,1)} fusion(bf16[512,1408]{1,0:T(8,128)(2,1)} %collective-permute-done.32, bf16[512,1408]{1,0:T(8,128)(2,1)S(1)} %copy-done.50, bf16[512,1024]{1,0:T(8,128)(2,1)S(1)} %collective-permute-done.33, bf16[512,1024]{1,0:T(8,128)(2,1)S(1)} %get-tuple-element.173), kind=kOutput, calls=%fused_computation.1 | convolution fusion | flops 2964193280 | bytes 7864320 | tf_op jit(solution)/shard_map/dot_general | solution.py:26
  325.9 22.5 %collective-permute-done.30 = bf16[128,2048]{1,0:T(8,128)(2,1)} collective-permute-done((bf16[128,2048]{1,0:T(8,128)(2,1)}, bf16[128,2048]{1,0:T(8,128)(2,1)}, u32[]{:S(2)}, u32[]{:S(2)}) %collective-permute-start.30) | collective-permute-done | bytes 524320 | tf_op jit(solution)/shard_map/ppermute | solution.py:375
  356.1 9.5 %collective-permute-done.36 = bf16[128,2048]{1,0:T(8,128)(2,1)S(1)} collective-permute-done((bf16[128,2048]{1,0:T(8,128)(2,1)S(1)}, bf16[128,2048]{1,0:T(8,128)(2,1)S(1)}, u32[]{:S(2)}, u32[]{:S(2)}) %collective-permute-start.36) | collective-permute-done | bytes 524320 | tf_op jit(solution)/shard_map/ppermute | solution.py:372
  368.3 11.5 %collective-permute-done.38 = bf16[64,2048]{1,0:T(8,128)(2,1)S(1)} collective-permute-done((bf16[64,2048]{1,0:T(8,128)(2,1)S(1)}, bf16[64,2048]{1,0:T(8,128)(2,1)S(1)}, u32[]{:S(2)}, u32[]{:S(2)}) %collective-permute-start.38) | collective-permute-done | bytes 262176 | tf_op jit(solution)/shard_map/ppermute | solution.py:372
  380.7 9.3 %collective-permute-done.35 = bf16[128,2048]{1,0:T(8,128)(2,1)} collective-permute-done((bf16[128,2048]{1,0:T(8,128)(2,1)S(1)}, bf16[128,2048]{1,0:T(8,128)(2,1)}, u32[]{:S(2)}, u32[]{:S(2)}) %collective-permute-start.35) | collective-permute-done | bytes 524320 | tf_op jit(solution)/shard_map/ppermute | solution.py:375
  397.1 9.9 %collective-permute-done.40 = bf16[128,2048]{1,0:T(8,128)(2,1)S(1)} collective-permute-done((bf16[128,2048]{1,0:T(8,128)(2,1)}, bf16[128,2048]{1,0:T(8,128)(2,1)S(1)}, u32[]{:S(2)}, u32[]{:S(2)}) %collective-permute-start.40) | collective-permute-done | bytes 524320 | tf_op jit(solution)/shard_map/ppermute | solution.py:375
  408.7 3.8 collective-permute-done.52
  416.4 11.3 %attend_back.1 = (bf16[512,512]{1,0:T(8,128)(2,1)}, bf16[4,512,128]{2,1,0:T(8,128)(2,1)}) custom-call(s32[1]{0:T(128)} %bitcast.1.seen_ref, bf16[512,512]{1,0:T(8,128)(2,1)} %get-tuple-element.77.q_ref, bf16[512,512]{1,0:T(8,128)(2,1)} %bitcast.151, bf16[512,512]{1,0:T(8,128)(2,1)} %get-tuple-element.80.o_ref, ...), custom_call_target="tpu_custom_call" | custom-call | tf_op jit(solution)/shard_map/attend_back/pallas_call | solution.py:285
  428.7 4.4 collective-permute-start.45
  433.2 15.1 %collective-permute-start.44 = (bf16[512,128]{1,0:T(8,128)(2,1)S(1)}, bf16[512,128]{1,0:T(8,128)(2,1)S(1)}, u32[]{:S(2)}, u32[]{:S(2)}) collective-permute-start(bf16[512,128]{1,0:T(8,128)(2,1)S(1)} %get-tuple-element.220), channel_id=1, source_target_pairs={{0,8},{1,9},{2,10},{3,11},{4,12},{5,13},{6,14},{7,15},{8,0},{9,1},... | collective-permute-start | bytes 393224 | tf_op jit(solution)/shard_map/ppermute | solution.py:375
  451.6 6.0 %collective-permute-done.44 = bf16[512,128]{1,0:T(8,128)(2,1)S(1)} collective-permute-done((bf16[512,128]{1,0:T(8,128)(2,1)S(1)}, bf16[512,128]{1,0:T(8,128)(2,1)S(1)}, u32[]{:S(2)}, u32[]{:S(2)}) %collective-permute-start.44) | collective-permute-done | bytes 131104 | tf_op jit(solution)/shard_map/ppermute | solution.py:375
  478.9 9.7 %collective-permute-done.50 = bf16[128,1408]{1,0:T(8,128)(2,1)} collective-permute-done((bf16[128,1408]{1,0:T(8,128)(2,1)}, bf16[128,1408]{1,0:T(8,128)(2,1)}, u32[]{:S(2)}, u32[]{:S(2)}) %collective-permute-start.50) | collective-permute-done | bytes 360480 | tf_op jit(solution)/shard_map/ppermute | solution.py:375
  498.8 10.3 %collective-permute-done.46 = bf16[128,2048]{1,0:T(8,128)(2,1)S(1)} collective-permute-done((bf16[128,2048]{1,0:T(8,128)(2,1)}, bf16[128,2048]{1,0:T(8,128)(2,1)S(1)}, u32[]{:S(2)}, u32[]{:S(2)}) %collective-permute-start.46) | collective-permute-done | bytes 524320 | tf_op jit(solution)/shard_map/ppermute | solution.py:372
  516.6 22.0 %reduce-scatter.11.cloned.1.call-done = bf16[512,320]{0,1:T(8,128)(2,1)} async-done(((bf16[2048,320]{0,1:T(8,128)(2,1)}), bf16[512,320]{0,1:T(8,128)(2,1)}) %reduce-scatter.11.cloned.1.call-update) | async-done | bytes 327696 | tf_op jit(solution)/shard_map/reduce_scatter | solution.py:680
  540.4 4.1 all-to-all-start.1
  551.4 6.3 %convert_multiply_fusion = (f32[128,5632]{1,0:T(8,128)}, f32[128]{0:T(128)}, f32[128,5632]{1,0:T(8,128)}) fusion(f32[128]{0:T(128)S(1)} %convert_element_type.204, bf16[128,1408]{1,0:T(8,128)(2,1)} %get-tuple-element.191, bf16[128,1408]{1,0:T(8,128)(2,1)} %get-tuple-element.192, bf16[128,1408]{1,0:T(8,128)(2,1)} %get-tuple-element.193, ...), kind=kLoop, calls=%fused_computation.2 | loop fusion | flops 17301376 | bytes 11535360 | tf_op jit(solution)/shard_map/mul | solution.py:710
  (417 shorter events, 191.9 us)
Async XLA Ops:
  7.2 89.2 %all-gather.8.cloned.1.call-start = ((), (), s32[]{:S(2)}) async-start(), calls=%async_computation.11 | async-start | bytes 6488064 | tf_op jit(solution)/shard_map/all_gather | solution.py:484
  19.1 138.1 %all-gather.10.cloned.1.call-start = ((), (), s32[]{:S(2)}) async-start(), calls=%async_computation.12 | async-start | bytes 2359296 | tf_op jit(solution)/shard_map/all_gather | solution.py:489
  30.9 28.9 %collective-permute-start.4 = (bf16[512,320]{1,0:T(8,128)(2,1)S(1)}, bf16[512,320]{1,0:T(8,128)(2,1)S(1)}, u32[]{:S(2)}, u32[]{:S(2)}) collective-permute-start(bf16[512,320]{1,0:T(8,128)(2,1)S(1)} %bitcast.138), channel_id=1, source_target_pairs={{0,8},{1,9},{2,10},{3,11},{4,12},{5,13},{6,14},{7,15},{8,0},{9,1},... | collective-permute-start | bytes 983048 | tf_op jit(solution)/shard_map/ppermute | solution.py:375
  30.9 28.9 %collective-permute-start.5 = (bf16[512,320]{1,0:T(8,128)(2,1)S(1)}, bf16[512,320]{1,0:T(8,128)(2,1)S(1)}, u32[]{:S(2)}, u32[]{:S(2)}) collective-permute-start(bf16[512,320]{1,0:T(8,128)(2,1)S(1)} %bitcast.139), channel_id=1, source_target_pairs={{0,4},{1,5},{2,6},{3,7},{4,8},{5,9},{6,10},{7,11},{8,12},{9,13},{1... | collective-permute-start | bytes 983048 | tf_op jit(solution)/shard_map/ppermute | solution.py:375
  32.4 43.5 %collective-permute-start.9 = (bf16[128,2048]{1,0:T(8,128)(2,1)S(1)}, bf16[128,2048]{1,0:T(8,128)(2,1)}, u32[]{:S(2)}, u32[]{:S(2)}) collective-permute-start(bf16[128,2048]{1,0:T(8,128)(2,1)S(1)} %fusion.22), channel_id=1, source_target_pairs={{0,1},{1,0},{2,3},{3,2},{4,5},{5,4},{6,7},{7,6},{8,9},{9,8},{10,11... | collective-permute-start | bytes 1572872 | tf_op jit(solution)/shard_map/ppermute | solution.py:372
  33.3 47.2 %collective-permute-start.10 = (bf16[128,2048]{1,0:T(8,128)(2,1)S(1)}, bf16[128,2048]{1,0:T(8,128)(2,1)}, u32[]{:S(2)}, u32[]{:S(2)}) collective-permute-start(bf16[128,2048]{1,0:T(8,128)(2,1)S(1)} %fusion.22), channel_id=1, source_target_pairs={{0,2},{1,3},{2,0},{3,1},{4,6},{5,7},{6,4},{7,5},{8,10},{9,11},{10,... | collective-permute-start | bytes 1572872 | tf_op jit(solution)/shard_map/ppermute | solution.py:372
  61.9 41.3 %collective-permute-start.13 = (bf16[2048,320]{0,1:T(8,128)(2,1)}, bf16[2048,320]{0,1:T(8,128)(2,1)}, u32[]{:S(2)}, u32[]{:S(2)}) collective-permute-start(bf16[2048,320]{0,1:T(8,128)(2,1)} %copy.48), channel_id=1, source_target_pairs={{0,16},{16,0},{1,17},{17,1},{2,18},{18,2},{3,19},{19,3},{4,20},{20... | collective-permute-start | bytes 3932168 | tf_op jit(solution)/shard_map/ppermute | solution.py:378
  75.2 40.9 %collective-permute-start.6 = (bf16[128,1408]{1,0:T(8,128)(2,1)}, bf16[128,1408]{1,0:T(8,128)(2,1)}, u32[]{:S(2)}, u32[]{:S(2)}) collective-permute-start(bf16[128,1408]{1,0:T(8,128)(2,1)} %get-tuple-element.200), channel_id=1, source_target_pairs={{0,4},{1,5},{2,6},{3,7},{4,8},{5,9},{6,10},{7,11},{8,12},{9,13},{1... | collective-permute-start | bytes 1081352 | tf_op jit(solution)/shard_map/ppermute | solution.py:375
  75.9 40.2 %collective-permute-start.7 = (bf16[128,1408]{1,0:T(8,128)(2,1)}, bf16[128,1408]{1,0:T(8,128)(2,1)}, u32[]{:S(2)}, u32[]{:S(2)}) collective-permute-start(bf16[128,1408]{1,0:T(8,128)(2,1)} %get-tuple-element.199), channel_id=1, source_target_pairs={{0,8},{1,9},{2,10},{3,11},{4,12},{5,13},{6,14},{7,15},{8,0},{9,1},... | collective-permute-start | bytes 1081352 | tf_op jit(solution)/shard_map/ppermute | solution.py:375
  96.5 159.8 %all-gather.6.cloned.1.call-start = ((), (), s32[]{:S(2)}) async-start(), calls=%async_computation.6 | async-start | bytes 12976128 | tf_op jit(solution)/shard_map/all_gather | solution.py:525
  100.8 26.5 %collective-permute-start.8 = (bf16[128,1408]{1,0:T(8,128)(2,1)}, bf16[128,1408]{1,0:T(8,128)(2,1)}, u32[]{:S(2)}, u32[]{:S(2)}) collective-permute-start(bf16[128,1408]{1,0:T(8,128)(2,1)} %get-tuple-element.198), channel_id=1, source_target_pairs={{0,12},{1,13},{2,14},{3,15},{4,0},{5,1},{6,2},{7,3},{8,4},{9,5},{1... | collective-permute-start | bytes 1081352 | tf_op jit(solution)/shard_map/ppermute | solution.py:375
  131.8 275.1 %reduce-scatter.5.cloned.1.call-start = ((), (), s32[]{:S(2)}) async-start(), calls=%async_computation.7 | async-start | bytes 7208960 | tf_op jit(solution)/shard_map/reduce_scatter | solution.py:610
  145.9 47.5 %collective-permute-start.22 = (bf16[128,2048]{1,0:T(8,128)(2,1)S(1)}, bf16[128,2048]{1,0:T(8,128)(2,1)}, u32[]{:S(2)}, u32[]{:S(2)}) collective-permute-start(bf16[128,2048]{1,0:T(8,128)(2,1)S(1)} %bitcast_convert_fusion), channel_id=1, source_target_pairs={{0,8},{1,9},{2,10},{3,11},{4,12},{5,13},{6,14},{7,15},{8,0},{9,1},... | collective-permute-start | bytes 1572872 | tf_op jit(solution)/shard_map/ppermute | solution.py:375
  147.8 45.6 %collective-permute-start.21 = (bf16[128,2048]{1,0:T(8,128)(2,1)S(1)}, bf16[128,2048]{1,0:T(8,128)(2,1)}, u32[]{:S(2)}, u32[]{:S(2)}) collective-permute-start(bf16[128,2048]{1,0:T(8,128)(2,1)S(1)} %bitcast_convert_fusion), channel_id=1, source_target_pairs={{0,4},{1,5},{2,6},{3,7},{4,8},{5,9},{6,10},{7,11},{8,12},{9,13},{1... | collective-permute-start | bytes 1572872 | tf_op jit(solution)/shard_map/ppermute | solution.py:375
  160.3 35.9 %collective-permute-start.20 = (bf16[128,2048]{1,0:T(8,128)(2,1)S(1)}, bf16[128,2048]{1,0:T(8,128)(2,1)S(1)}, u32[]{:S(2)}, u32[]{:S(2)}) collective-permute-start(bf16[128,2048]{1,0:T(8,128)(2,1)S(1)} %get-tuple-element.179), channel_id=1, source_target_pairs={{0,3},{1,2},{2,1},{3,0},{4,7},{5,6},{6,5},{7,4},{8,11},{9,10},{10,... | collective-permute-start | bytes 1572872 | tf_op jit(solution)/shard_map/ppermute | solution.py:372
  160.5 35.7 %collective-permute-start.19 = (bf16[128,2048]{1,0:T(8,128)(2,1)S(1)}, bf16[128,2048]{1,0:T(8,128)(2,1)S(1)}, u32[]{:S(2)}, u32[]{:S(2)}) collective-permute-start(bf16[128,2048]{1,0:T(8,128)(2,1)S(1)} %get-tuple-element.180), channel_id=1, source_target_pairs={{0,2},{1,3},{2,0},{3,1},{4,6},{5,7},{6,4},{7,5},{8,10},{9,11},{10,... | collective-permute-start | bytes 1572872 | tf_op jit(solution)/shard_map/ppermute | solution.py:372
  161.4 34.9 %collective-permute-start.18 = (bf16[128,2048]{1,0:T(8,128)(2,1)S(1)}, bf16[128,2048]{1,0:T(8,128)(2,1)S(1)}, u32[]{:S(2)}, u32[]{:S(2)}) collective-permute-start(bf16[128,2048]{1,0:T(8,128)(2,1)S(1)} %get-tuple-element.178), channel_id=1, source_target_pairs={{0,1},{1,0},{2,3},{3,2},{4,5},{5,4},{6,7},{7,6},{8,9},{9,8},{10,11... | collective-permute-start | bytes 1572872 | tf_op jit(solution)/shard_map/ppermute | solution.py:372
  198.5 21.9 %collective-permute-start.26 = (bf16[128,2048]{1,0:T(8,128)(2,1)S(1)}, bf16[128,2048]{1,0:T(8,128)(2,1)S(1)}, u32[]{:S(2)}, u32[]{:S(2)}) collective-permute-start(bf16[128,2048]{1,0:T(8,128)(2,1)S(1)} %constant_dynamic-update-slice_fusion.12), channel_id=1, source_target_pairs={{0,12},{1,13},{2,14},{3,15},{4,0},{5,1},{6,2},{7,3},{8,4},{9,5},{1... | collective-permute-start | bytes 1572872 | tf_op jit(solution)/shard_map/ppermute | solution.py:375
  225.2 61.2 %collective-permute-start.28 = (bf16[512,2048]{1,0:T(8,128)(2,1)}, bf16[512,2048]{1,0:T(8,128)(2,1)}, u32[]{:S(2)}, u32[]{:S(2)}) collective-permute-start(bf16[512,2048]{1,0:T(8,128)(2,1)} %get-tuple-element.222.low_ref), channel_id=1, source_target_pairs={{0,16},{16,0},{1,17},{17,1},{2,18},{18,2},{3,19},{19,3},{4,20},{20... | collective-permute-start | bytes 6291464 | tf_op jit(solution)/shard_map/ppermute | solution.py:378
  309.0 156.3 %reduce-scatter.7.cloned.1.call-start = ((), (), s32[]{:S(2)}) async-start(), calls=%async_computation.8 | async-start | bytes 1310720 | tf_op jit(solution)/shard_map/reduce_scatter | solution.py:629
  311.6 36.8 %collective-permute-start.30 = (bf16[128,2048]{1,0:T(8,128)(2,1)}, bf16[128,2048]{1,0:T(8,128)(2,1)}, u32[]{:S(2)}, u32[]{:S(2)}) collective-permute-start(bf16[128,2048]{1,0:T(8,128)(2,1)} %get-tuple-element.176), channel_id=1, source_target_pairs={{0,8},{1,9},{2,10},{3,11},{4,12},{5,13},{6,14},{7,15},{8,0},{9,1},... | collective-permute-start | bytes 1572872 | tf_op jit(solution)/shard_map/ppermute | solution.py:375
  312.2 36.2 %collective-permute-start.31 = (bf16[128,2048]{1,0:T(8,128)(2,1)}, bf16[128,2048]{1,0:T(8,128)(2,1)}, u32[]{:S(2)}, u32[]{:S(2)}) collective-permute-start(bf16[128,2048]{1,0:T(8,128)(2,1)} %get-tuple-element.175), channel_id=1, source_target_pairs={{0,4},{1,5},{2,6},{3,7},{4,8},{5,9},{6,10},{7,11},{8,12},{9,13},{1... | collective-permute-start | bytes 1572872 | tf_op jit(solution)/shard_map/ppermute | solution.py:375
  355.2 24.6 %collective-permute-start.34 = (bf16[128,2048]{1,0:T(8,128)(2,1)S(1)}, bf16[128,2048]{1,0:T(8,128)(2,1)S(1)}, u32[]{:S(2)}, u32[]{:S(2)}) collective-permute-start(bf16[128,2048]{1,0:T(8,128)(2,1)S(1)} %get-tuple-element.172), channel_id=1, source_target_pairs={{0,12},{1,13},{2,14},{3,15},{4,0},{5,1},{6,2},{7,3},{8,4},{9,5},{1... | collective-permute-start | bytes 1572872 | tf_op jit(solution)/shard_map/ppermute | solution.py:375
  355.2 34.8 %collective-permute-start.35 = (bf16[128,2048]{1,0:T(8,128)(2,1)S(1)}, bf16[128,2048]{1,0:T(8,128)(2,1)}, u32[]{:S(2)}, u32[]{:S(2)}) collective-permute-start(bf16[128,2048]{1,0:T(8,128)(2,1)S(1)} %get-tuple-element.170), channel_id=1, source_target_pairs={{0,8},{1,9},{2,10},{3,11},{4,12},{5,13},{6,14},{7,15},{8,0},{9,1},... | collective-permute-start | bytes 1572872 | tf_op jit(solution)/shard_map/ppermute | solution.py:375
  407.0 83.1 %reduce-scatter.9.cloned.1.call-start = ((), (), s32[]{:S(2)}) async-start(), calls=%async_computation.9 | async-start | bytes 3604480 | tf_op jit(solution)/shard_map/reduce_scatter | solution.py:611
  408.4 130.2 %reduce-scatter.11.cloned.1.call-start = ((), (), s32[]{:S(2)}) async-start(), calls=%async_computation.10 | async-start | bytes 1638400 | tf_op jit(solution)/shard_map/reduce_scatter | solution.py:680
  428.7 22.8 %collective-permute-start.45 = (bf16[512,128]{1,0:T(8,128)(2,1)S(1)}, bf16[512,128]{1,0:T(8,128)(2,1)S(1)}, u32[]{:S(2)}, u32[]{:S(2)}) collective-permute-start(bf16[512,128]{1,0:T(8,128)(2,1)S(1)} %get-tuple-element.219), channel_id=1, source_target_pairs={{0,4},{1,5},{2,6},{3,7},{4,8},{5,9},{6,10},{7,11},{8,12},{9,13},{1... | collective-permute-start | bytes 393224 | tf_op jit(solution)/shard_map/ppermute | solution.py:375
  433.2 24.4 %collective-permute-start.44 = (bf16[512,128]{1,0:T(8,128)(2,1)S(1)}, bf16[512,128]{1,0:T(8,128)(2,1)S(1)}, u32[]{:S(2)}, u32[]{:S(2)}) collective-permute-start(bf16[512,128]{1,0:T(8,128)(2,1)S(1)} %get-tuple-element.220), channel_id=1, source_target_pairs={{0,8},{1,9},{2,10},{3,11},{4,12},{5,13},{6,14},{7,15},{8,0},{9,1},... | collective-permute-start | bytes 393224 | tf_op jit(solution)/shard_map/ppermute | solution.py:375
  462.8 25.8 %collective-permute-start.50 = (bf16[128,1408]{1,0:T(8,128)(2,1)}, bf16[128,1408]{1,0:T(8,128)(2,1)}, u32[]{:S(2)}, u32[]{:S(2)}) collective-permute-start(bf16[128,1408]{1,0:T(8,128)(2,1)} %get-tuple-element.195), channel_id=1, source_target_pairs={{0,8},{1,9},{2,10},{3,11},{4,12},{5,13},{6,14},{7,15},{8,0},{9,1},... | collective-permute-start | bytes 1081352 | tf_op jit(solution)/shard_map/ppermute | solution.py:375
  462.8 27.3 %collective-permute-start.51 = (bf16[128,1408]{1,0:T(8,128)(2,1)}, bf16[128,1408]{1,0:T(8,128)(2,1)}, u32[]{:S(2)}, u32[]{:S(2)}) collective-permute-start(bf16[128,1408]{1,0:T(8,128)(2,1)} %get-tuple-element.194), channel_id=1, source_target_pairs={{0,12},{1,13},{2,14},{3,15},{4,0},{5,1},{6,2},{7,3},{8,4},{9,5},{1... | collective-permute-start | bytes 1081352 | tf_op jit(solution)/shard_map/ppermute | solution.py:375
  471.7 23.5 %collective-permute-start.48 = (bf16[128,2048]{1,0:T(8,128)(2,1)}, bf16[128,2048]{1,0:T(8,128)(2,1)S(1)}, u32[]{:S(2)}, u32[]{:S(2)}) collective-permute-start(bf16[128,2048]{1,0:T(8,128)(2,1)} %get-tuple-element.166), channel_id=1, source_target_pairs={{0,3},{1,2},{2,1},{3,0},{4,7},{5,6},{6,5},{7,4},{8,11},{9,10},{10,... | collective-permute-start | bytes 1572872 | tf_op jit(solution)/shard_map/ppermute | solution.py:372
  477.1 21.7 %collective-permute-start.47 = (bf16[128,2048]{1,0:T(8,128)(2,1)}, bf16[128,2048]{1,0:T(8,128)(2,1)S(1)}, u32[]{:S(2)}, u32[]{:S(2)}) collective-permute-start(bf16[128,2048]{1,0:T(8,128)(2,1)} %get-tuple-element.167), channel_id=1, source_target_pairs={{0,2},{1,3},{2,0},{3,1},{4,6},{5,7},{6,4},{7,5},{8,10},{9,11},{10,... | collective-permute-start | bytes 1572872 | tf_op jit(solution)/shard_map/ppermute | solution.py:372
  (92 other events, 894.1 us)
Sparse Core Ops, SparseCore 0:
  10.5 54.0 all-gather.7
  96.6 40.2 all-gather.9
  138.8 89.2 all-gather.5
  309.1 81.7 reduce-scatter.4
  407.1 25.2 reduce-scatter.6
  435.9 40.4 reduce-scatter.8
  490.3 48.2 reduce-scatter.10

commit v9 on v8

--- a/solution.py
+++ b/solution.py
@@ -82,7 +82,7 @@
 def project(low, weights, cosine, sine):
     tokens, width = low.shape
     q_width = weights.shape[1] - PAIR
-    rows = block_rows(tokens)
+    rows = min(256, tokens)
     return pl.pallas_call(
         project_kernel,
         out_shape=(
@@ -126,7 +126,7 @@
 def feed(low, weights, grad_hidden):
     tokens, width = low.shape
     block = weights.shape[2]
-    rows = block_rows(tokens)
+    rows = min(256, tokens)
     narrow = pl.BlockSpec((rows, block), lambda i: (i, 0))
     wide = pl.BlockSpec((rows, width), lambda i: (i, 0))
     return pl.pallas_call(
@@ -461,72 +461,63 @@
         low_one, qkv_part, plane_pos = tie(normed_one.astype(bf16), qkv_part, plane_pos)
 
         ring = [qkv_part] + [shift_z(qkv_part, -t) for t in range(1, planes)]
+        low_one, *ring = tie(gather_w(low_one), *ring)
         qkv_ring = jnp.concatenate(ring + ring[: planes - 1], axis=0)
         qkv_mine = lax.dynamic_slice_in_dim(
             qkv_ring, ((planes - p) % planes) * GROUP * shard, width, 0
         )
-        low_one = gather_w(low_one)
-
         piece = shard // halves
         gate_up = jnp.where(c // halves == 0, scaled(w_gate, gain_two), scaled(w_up, gain_two))
-        out_part, gate_up, qkv_mine = tie(
-            pick(w_out, c, n_dp, 1), pick(gate_up, c % halves, halves, 0), qkv_mine
-        )
+        gate_up = pick(gate_up, c % halves, halves, 0)
+        grad_y = (
+            cotangent.astype(f32) * select.astype(f32)[..., None]
+        ).reshape(tokens, width)
+        out_part, grad_y_low, qkv_mine = tie(
+            pick(w_out, c, n_dp, 1), grad_y.astype(bf16), qkv_mine
+        )
+        grad_y_sent = gather_z(grad_y_low)
         qkv_full = collect_dp(qkv_mine, c)
         out_part = lax.ppermute(
             out_part, "seq", [(i, GROUP * (i % planes) + i // planes) for i in range(n_seq)]
         )
+        down_full = lax.all_gather(
+            pick(w_down, c, n_dp, 1), both, axis_index_groups=in_plane_dp, tiled=False
+        )
+        down_full = down_full.reshape(n_dp, ff_block, width // n_dp)
+        out_full = lax.all_gather(out_part, both, axis_index_groups=across_dp, tiled=False)
+        out_full = out_full.reshape(n_dp, planes * shard, width // n_dp)
+
+        blocks = [
+            (i * GROUP + j) * halves + h
+            for h in range(halves) for j in range(GROUP) for i in range(planes)
+        ]
+
+        def column_blocks(value, which):
+            return jnp.concatenate([value[:, i * piece : (i + 1) * piece] for i in which], axis=1)
+
+        def reorder(value):
+            return column_blocks(value, blocks)
+
+        def order_back(value):
+            return column_blocks(value, [blocks.index(i) for i in range(len(blocks))])
+
+        cosine, sine = rope_tables(plane_pos.reshape(GROUP * tokens))
+
+        cut = q_width // n_dp
+        plane_tokens = GROUP * tokens
+        qkv_weights = jnp.concatenate(
+            [one[:, :cut] for one in qkv_full] + [one[:, cut:] for one in qkv_full], axis=1
+        )
+        q, kv_low = project(low_one, qkv_weights, cosine, sine)
+        kv_all = jnp.stack(gather_z(kv_low))
+        *grad_y_sent, q = tie(*grad_y_sent, q)
+        grad_y_all = jnp.concatenate(grad_y_sent, axis=0)
+        gate_up, kv_all = tie(gate_up, kv_all)
         gate_up_sent = [
             shift_z(pick(gate_up, (p + t) % planes, planes, 1), t) if t
             else pick(gate_up, p, planes, 1)
             for t in range(planes)
         ]
-        down_full = lax.all_gather(
-            pick(w_down, c, n_dp, 1), both, axis_index_groups=in_plane_dp, tiled=False
-        )
-        out_part, down_full = tie(out_part, down_full)
-        down_full = down_full.reshape(n_dp, ff_block, width // n_dp)
-        out_full = lax.all_gather(out_part, both, axis_index_groups=across_dp, tiled=False)
-        out_full = out_full.reshape(n_dp, planes * shard, width // n_dp)
-
-        blocks = [
-            (i * GROUP + j) * halves + h
-            for h in range(halves) for j in range(GROUP) for i in range(planes)
-        ]
-
-        def column_blocks(value, which):
-            return jnp.concatenate([value[:, i * piece : (i + 1) * piece] for i in which], axis=1)
-
-        def reorder(value):
-            return column_blocks(value, blocks)
-
-        def order_back(value):
-            return column_blocks(value, [blocks.index(i) for i in range(len(blocks))])
-
-        cosine, sine = rope_tables(plane_pos.reshape(GROUP * tokens))
-
-        grad_y = (
-            cotangent.astype(f32) * select.astype(f32)[..., None]
-        ).reshape(tokens, width)
-        cut = q_width // n_dp
-        plane_tokens = GROUP * tokens
-        qkv_weights = jnp.concatenate(
-            [one[:, :cut] for one in qkv_full] + [one[:, cut:] for one in qkv_full], axis=1
-        )
-        q, kv_low = project(low_one, qkv_weights, cosine, sine)
-        kv_all = jnp.stack(gather_z(kv_low))
-        grad_y_low, kv_all = tie(grad_y.astype(bf16), kv_all)
-        *gate_up_sent, q = tie(*gate_up_sent, q)
-        gate_up_part = jnp.zeros((planes, piece, ff_block), bf16)
-        for t in range(planes):
-            gate_up_part = lax.dynamic_update_index_in_dim(
-                gate_up_part, gate_up_sent[t], (p - t) % planes, 0
-            )
-        gate_up_full = lax.all_gather(
-            gate_up_part, both, axis_index_groups=in_plane_dp, tiled=False
-        )
-        gate_up_full = gate_up_full.reshape(2, width, ff_block)
-        grad_y_all = jnp.concatenate(gather_z(grad_y_low), axis=0)
 
         def by_seq(value, axis):
             shape = value.shape
@@ -553,6 +544,16 @@
         o = from_seq(jnp.stack(o_seq), 0)
 
         branch = jnp.concatenate([dot(o, out_full[i]).astype(bf16) for i in range(n_dp)], axis=1)
+        *gate_up_sent, branch = tie(*gate_up_sent, branch)
+        gate_up_part = jnp.zeros((planes, piece, ff_block), bf16)
+        for t in range(planes):
+            gate_up_part = lax.dynamic_update_index_in_dim(
+                gate_up_part, gate_up_sent[t], (p - t) % planes, 0
+            )
+        gate_up_full = lax.all_gather(
+            gate_up_part, both, axis_index_groups=in_plane_dp, tiled=False
+        )
+        gate_up_full = gate_up_full.reshape(2, width, ff_block)
         branch = scatter_w([branch[j * tokens : (j + 1) * tokens] for j in range(GROUP)])
         x_mid = x_in + branch
 

time: 579 us -> 614 us (1.060)
  starting transfers between devices: 137 us -> 161 us
  Pallas kernels: 52.7 us -> 43.7 us
  waiting for transfers between devices: 220 us -> 229 us
  other arithmetic: 41 us -> 49.7 us
  matrix products: 36.9 us -> 44.7 us
    ppermute x27, starting transfers between devices: 48.8 us -> 115 us  [shift_z(): lax.ppermute(value, 'seq', [(s, (s + GROUP * t) % n_seq) for s in range(n...]
    ppermute x13, starting transfers between devices: 44.9 us -> 14.6 us  [shift_dp(): return lax.ppermute(value, 'dp', [(c, (c + t) % n_dp) for c in range(n_dp)])]
    ppermute x17, waiting for transfers between devices: 37.1 us -> 67.2 us  [xor_w(): return lax.ppermute(value, 'seq', [(s, s ^ j) for s in range(n_seq)])]
    ppermute x27, waiting for transfers between devices: 154 us -> 128 us  [shift_z(): lax.ppermute(value, 'seq', [(s, (s + GROUP * t) % n_seq) for s in range(n...]
    reduce_scatter x1, waiting for transfers between devices: 0.01 us -> 10.1 us  [body(): lax.psum_scatter(down_sum, 'seq', axis_index_groups=in_plane, tiled=True)]
    ppermute x17, starting transfers between devices: 29.1 us -> 19.6 us  [xor_w(): return lax.ppermute(value, 'seq', [(s, s ^ j) for s in range(n_seq)])]
    pallas_call x1, Pallas kernels: 27.8 us -> 19.7 us  [feed(): pl.pallas_call(feed_kernel, out_shape=(jax.ShapeDtypeStruct((tokens, bloc...]
    dot_general x13, matrix products: 36.9 us -> 44.7 us  [dot(): lax.dot_general(left, right, (contract, ((), ())), preferred_element_type...]
  transfers between devices with their start and end apart: 68 -> 68, of which waited for: 25 -> 30; matrix products, arithmetic and copies ran while one was open for 22% -> 23% of each run, Pallas kernels for 9% -> 7%
where the time goes in v9:
time: 614 us; the launch traced here: 606 us
  waiting for transfers between devices  229 us (37%)
  starting transfers between devices  161 us (26%)
  local copies, waits for them, and re-layouts  61.9 us (10%)
  other arithmetic  49.7 us (8%)
  matrix products  44.7 us (7%)
  Pallas kernels  43.7 us (7%)
  between operations  15.9 us (3%)
    ppermute x27, waiting for transfers between devices, shift_z(): lax.ppermute(value, 'seq', [(s, (s + GROUP * t) % n_seq) for s in range(n...  128 us
    ppermute x27, starting transfers between devices, shift_z(): lax.ppermute(value, 'seq', [(s, (s + GROUP * t) % n_seq) for s in range(n...  115 us
    ppermute x17, waiting for transfers between devices, xor_w(): return lax.ppermute(value, 'seq', [(s, s ^ j) for s in range(n_seq)])  67.2 us
    dot_general x13, matrix products, dot(): lax.dot_general(left, right, (contract, ((), ())), preferred_element_type...  44.7 us
    unnamed x166, local copies, waits for them, and re-layouts  20.4 us
    pallas_call x1, Pallas kernels, feed(): pl.pallas_call(feed_kernel, out_shape=(jax.ShapeDtypeStruct((tokens, bloc...  19.7 us
    ppermute x17, starting transfers between devices, xor_w(): return lax.ppermute(value, 'seq', [(s, s ^ j) for s in range(n_seq)])  19.6 us
    reduce_scatter x1, waiting for transfers between devices, body(): lax.psum_scatter(qkv_sum, 'seq', axis_index_groups=across, tiled=True)  17.5 us
  transfers between devices with their start and end apart: 68, of which 30 were waited for; matrix products, arithmetic and copies ran while one was open for 23% of the time, Pallas kernels for 7%

profile of v9, /device:TPU:1, one launch (start us, length us, event | category | flops | bytes accessed | tf_op | source)
XLA Modules:
  0.0 606.1 jit_solution(727659006821509954)
XLA Ops:
  48.3 16.9 %collective-permute-done.8 = bf16[512,320]{1,0:T(8,128)(2,1)S(1)} collective-permute-done((bf16[512,320]{1,0:T(8,128)(2,1)S(1)}, bf16[512,320]{1,0:T(8,128)(2,1)S(1)}, u32[]{:S(2)}, u32[]{:S(2)}) %collective-permute-start.8) | collective-permute-done | bytes 327712 | tf_op jit(solution)/shard_map/ppermute | solution.py:375
  80.7 17.7 %collective-permute-start.17 = (bf16[128,2048]{1,0:T(8,128)(2,1)}, bf16[128,2048]{1,0:T(8,128)(2,1)}, u32[]{:S(2)}, u32[]{:S(2)}) collective-permute-start(bf16[128,2048]{1,0:T(8,128)(2,1)} %bitcast_convert_fusion), channel_id=1, source_target_pairs={{0,4},{1,5},{2,6},{3,7},{4,8},{5,9},{6,10},{7,11},{8,12},{9,13},{1... | collective-permute-start | bytes 1572872 | tf_op jit(solution)/shard_map/ppermute | solution.py:375
  107.3 5.1 project.1
  116.5 21.4 %collective-permute-start.11 = (bf16[512,128]{1,0:T(8,128)(2,1)}, bf16[512,128]{1,0:T(8,128)(2,1)S(1)}, u32[]{:S(2)}, u32[]{:S(2)}) collective-permute-start(bf16[512,128]{1,0:T(8,128)(2,1)} %get-tuple-element.88), channel_id=1, source_target_pairs={{0,4},{1,5},{2,6},{3,7},{4,8},{5,9},{6,10},{7,11},{8,12},{9,13},{1... | collective-permute-start | bytes 393224 | tf_op jit(solution)/shard_map/ppermute | solution.py:375
  148.1 16.7 %collective-permute-done.12 = bf16[512,128]{1,0:T(8,128)(2,1)S(1)} collective-permute-done((bf16[512,128]{1,0:T(8,128)(2,1)}, bf16[512,128]{1,0:T(8,128)(2,1)S(1)}, u32[]{:S(2)}, u32[]{:S(2)}) %collective-permute-start.12) | collective-permute-done | bytes 131104 | tf_op jit(solution)/shard_map/ppermute | solution.py:375
  176.5 7.6 %attend.1 = (bf16[512,512]{1,0:T(8,128)(2,1)}, f32[4,8,1024]{2,1,0:T(8,128)}) custom-call(s32[1]{0:T(128)} %bitcast.17.seen_ref, bf16[512,512]{1,0:T(8,128)(2,1)} %get-tuple-element.92.q_ref, bf16[4,512,128]{2,1,0:T(8,128)(2,1)} %pad_maximum_fusion.9.kv_ref, s32[512,1]{1,0:T(8,128)} %copy.53.qpos_ref.kpos_ref, s32[1,512]{1,0:T(1,128)} %bitcast.144), custom_call_target="tpu_custom_call" | custom-call | tf_op jit(solution)/shard_map/attend/pallas_call | solution.py:255
  187.4 9.1 %collective-permute-done.15 = bf16[128,1408]{1,0:T(8,128)(2,1)} collective-permute-done((bf16[128,1408]{1,0:T(8,128)(2,1)}, bf16[128,1408]{1,0:T(8,128)(2,1)}, u32[]{:S(2)}, u32[]{:S(2)}) %collective-permute-start.15) | collective-permute-done | bytes 360480 | tf_op jit(solution)/shard_map/ppermute | solution.py:375
  203.9 5.3 collective-permute-start.23
  212.9 8.1 %collective-permute-done.23 = bf16[128,2048]{1,0:T(8,128)(2,1)S(1)} collective-permute-done((bf16[128,2048]{1,0:T(8,128)(2,1)S(1)}, bf16[128,2048]{1,0:T(8,128)(2,1)S(1)}, u32[]{:S(2)}, u32[]{:S(2)}) %collective-permute-start.23) | collective-permute-done | bytes 524320 | tf_op jit(solution)/shard_map/ppermute | solution.py:372
  221.0 20.4 %collective-permute-done.22 = bf16[128,2048]{1,0:T(8,128)(2,1)S(1)} collective-permute-done((bf16[128,2048]{1,0:T(8,128)(2,1)S(1)}, bf16[128,2048]{1,0:T(8,128)(2,1)S(1)}, u32[]{:S(2)}, u32[]{:S(2)}) %collective-permute-start.22) | collective-permute-done | bytes 524320 | tf_op jit(solution)/shard_map/ppermute | solution.py:372
  243.5 12.8 %collective-permute-start.24 = (bf16[128,2048]{1,0:T(8,128)(2,1)S(1)}, bf16[128,2048]{1,0:T(8,128)(2,1)}, u32[]{:S(2)}, u32[]{:S(2)}) collective-permute-start(bf16[128,2048]{1,0:T(8,128)(2,1)S(1)} %constant_dynamic-update-slice_fusion.12), channel_id=1, source_target_pairs={{0,4},{1,5},{2,6},{3,7},{4,8},{5,9},{6,10},{7,11},{8,12},{9,13},{1... | collective-permute-start | bytes 1572872 | tf_op jit(solution)/shard_map/ppermute | solution.py:375
  260.1 5.2 fusion.20
  269.2 20.3 %collective-permute-done.25 = bf16[128,2048]{1,0:T(8,128)(2,1)S(1)} collective-permute-done((bf16[128,2048]{1,0:T(8,128)(2,1)S(1)}, bf16[128,2048]{1,0:T(8,128)(2,1)S(1)}, u32[]{:S(2)}, u32[]{:S(2)}) %collective-permute-start.25) | collective-permute-done | bytes 524320 | tf_op jit(solution)/shard_map/ppermute | solution.py:375
  295.5 19.7 %feed.1 = (bf16[512,1408]{1,0:T(8,128)(2,1)}, bf16[512,1408]{1,0:T(8,128)(2,1)}, bf16[512,1408]{1,0:T(8,128)(2,1)}, bf16[512,2048]{1,0:T(8,128)(2,1)}) custom-call(bf16[512,2048]{1,0:T(8,128)(2,1)} %get-tuple-element.230.low_ref, bf16[2,2048,1408]{2,1,0:T(8,128)(2,1)} %bitcast.125, f32[512,1408]{1,0:T(8,128)} %convolution_add_fusion.grad_hidden_ref), custom_call_target="tpu_custom_call" | custom-call | tf_op jit(solution)/shard_map/feed/pallas_call | solution.py:132
  321.6 14.2 %collective-permute-start.27 = (bf16[128,2048]{1,0:T(8,128)(2,1)}, bf16[128,2048]{1,0:T(8,128)(2,1)S(1)}, u32[]{:S(2)}, u32[]{:S(2)}) collective-permute-start(bf16[128,2048]{1,0:T(8,128)(2,1)} %get-tuple-element.191), channel_id=1, source_target_pairs={{0,12},{1,13},{2,14},{3,15},{4,0},{5,1},{6,2},{7,3},{8,4},{9,5},{1... | collective-permute-start | bytes 1572872 | tf_op jit(solution)/shard_map/ppermute | solution.py:375
  335.8 8.6 %convolution_convert_fusion = bf16[2048,1408]{1,0:T(8,128)(2,1)} fusion(bf16[1024,2048]{1,0:T(8,128)(2,1)S(1)} %constant_dynamic-update-slice_fusion.32, bf16[512,1408]{1,0:T(8,128)(2,1)S(1)} %collective-permute-done.29, bf16[512,1408]{1,0:T(8,128)(2,1)S(1)} %get-tuple-element.177), kind=kOutput, calls=%fused_computation | convolution fusion | flops 5914230784 | bytes 12845056 | tf_op jit(solution)/shard_map/dot_general | solution.py:26
  363.6 6.4 %convolution_convert_fusion.1 = bf16[1408,1024]{1,0:T(8,128)(2,1)} fusion(bf16[512,1408]{1,0:T(8,128)(2,1)} %collective-permute-done.32, bf16[512,1408]{1,0:T(8,128)(2,1)} %get-tuple-element.115, bf16[512,1024]{1,0:T(8,128)(2,1)S(1)} %collective-permute-done.33, bf16[512,1024]{1,0:T(8,128)(2,1)S(1)} %get-tuple-element.187), kind=kOutput, calls=%fused_computation.5 | convolution fusion | flops 2964193280 | bytes 7864320 | tf_op jit(solution)/shard_map/dot_general | solution.py:26
  369.9 17.2 %collective-permute-done.30 = bf16[128,2048]{1,0:T(8,128)(2,1)} collective-permute-done((bf16[128,2048]{1,0:T(8,128)(2,1)}, bf16[128,2048]{1,0:T(8,128)(2,1)}, u32[]{:S(2)}, u32[]{:S(2)}) %collective-permute-start.30) | collective-permute-done | bytes 524320 | tf_op jit(solution)/shard_map/ppermute | solution.py:375
  396.2 8.3 %collective-permute-done.36 = bf16[128,2048]{1,0:T(8,128)(2,1)S(1)} collective-permute-done((bf16[128,2048]{1,0:T(8,128)(2,1)S(1)}, bf16[128,2048]{1,0:T(8,128)(2,1)S(1)}, u32[]{:S(2)}, u32[]{:S(2)}) %collective-permute-start.36) | collective-permute-done | bytes 524320 | tf_op jit(solution)/shard_map/ppermute | solution.py:372
  406.0 12.3 %collective-permute-done.38 = bf16[64,2048]{1,0:T(8,128)(2,1)S(1)} collective-permute-done((bf16[64,2048]{1,0:T(8,128)(2,1)S(1)}, bf16[64,2048]{1,0:T(8,128)(2,1)S(1)}, u32[]{:S(2)}, u32[]{:S(2)}) %collective-permute-start.38) | collective-permute-done | bytes 262176 | tf_op jit(solution)/shard_map/ppermute | solution.py:372
  419.3 11.1 %collective-permute-done.35 = bf16[128,2048]{1,0:T(8,128)(2,1)} collective-permute-done((bf16[128,2048]{1,0:T(8,128)(2,1)S(1)}, bf16[128,2048]{1,0:T(8,128)(2,1)}, u32[]{:S(2)}, u32[]{:S(2)}) %collective-permute-start.35) | collective-permute-done | bytes 524320 | tf_op jit(solution)/shard_map/ppermute | solution.py:375
  437.2 10.2 %collective-permute-done.40 = bf16[128,2048]{1,0:T(8,128)(2,1)} collective-permute-done((bf16[128,2048]{1,0:T(8,128)(2,1)}, bf16[128,2048]{1,0:T(8,128)(2,1)}, u32[]{:S(2)}, u32[]{:S(2)}) %collective-permute-start.40) | collective-permute-done | bytes 524320 | tf_op jit(solution)/shard_map/ppermute | solution.py:375
  450.0 11.3 %attend_back.1 = (bf16[512,512]{1,0:T(8,128)(2,1)}, bf16[4,512,128]{2,1,0:T(8,128)(2,1)}) custom-call(s32[1]{0:T(128)} %bitcast.17.seen_ref, bf16[512,512]{1,0:T(8,128)(2,1)} %get-tuple-element.92.q_ref, bf16[512,512]{1,0:T(8,128)(2,1)} %bitcast.136, bf16[512,512]{1,0:T(8,128)(2,1)} %get-tuple-element.94.o_ref, ...), custom_call_target="tpu_custom_call" | custom-call | tf_op jit(solution)/shard_map/attend_back/pallas_call | solution.py:285
  462.4 4.5 collective-permute-start.45
  466.9 14.2 %collective-permute-start.44 = (bf16[512,128]{1,0:T(8,128)(2,1)S(1)}, bf16[512,128]{1,0:T(8,128)(2,1)S(1)}, u32[]{:S(2)}, u32[]{:S(2)}) collective-permute-start(bf16[512,128]{1,0:T(8,128)(2,1)S(1)} %get-tuple-element.228), channel_id=1, source_target_pairs={{0,8},{1,9},{2,10},{3,11},{4,12},{5,13},{6,14},{7,15},{8,0},{9,1},... | collective-permute-start | bytes 393224 | tf_op jit(solution)/shard_map/ppermute | solution.py:375
  484.7 5.7 collective-permute-done.44
  516.7 5.3 collective-permute-done.50
  523.5 10.1 %reduce-scatter.9.cloned.1.call-done = bf16[352,1024]{1,0:T(8,128)(2,1)} async-done(((bf16[1408,1024]{1,0:T(8,128)(2,1)}), bf16[352,1024]{1,0:T(8,128)(2,1)}) %reduce-scatter.9.cloned.1.call-update) | async-done | bytes 720912 | tf_op jit(solution)/shard_map/reduce_scatter | solution.py:612
  539.5 4.7 collective-permute-done.47
  544.1 5.6 collective-permute-done.46
  557.2 17.5 %reduce-scatter.11.cloned.1.call-done = bf16[512,320]{0,1:T(8,128)(2,1)} async-done(((bf16[2048,320]{0,1:T(8,128)(2,1)}), bf16[512,320]{0,1:T(8,128)(2,1)}) %reduce-scatter.11.cloned.1.call-update) | async-done | bytes 327696 | tf_op jit(solution)/shard_map/reduce_scatter | solution.py:681
  587.5 6.2 %convert_multiply_fusion = (f32[128,5632]{1,0:T(8,128)}, f32[128]{0:T(128)}, f32[128,5632]{1,0:T(8,128)}) fusion(f32[128]{0:T(128)S(1)} %convert_element_type.204, bf16[128,1408]{1,0:T(8,128)(2,1)} %get-tuple-element.205, bf16[128,1408]{1,0:T(8,128)(2,1)} %get-tuple-element.206, bf16[128,1408]{1,0:T(8,128)(2,1)} %get-tuple-element.207, ...), kind=kLoop, calls=%fused_computation.6 | loop fusion | flops 17301376 | bytes 11535360 | tf_op jit(solution)/shard_map/mul | solution.py:711
  (402 shorter events, 230.5 us)
Async XLA Ops:
  22.0 162.1 %all-gather.8.cloned.1.call-start = ((), (), s32[]{:S(2)}) async-start(), calls=%async_computation.11 | async-start | bytes 2359296 | tf_op jit(solution)/shard_map/all_gather | solution.py:487
  34.6 30.5 %collective-permute-start.8 = (bf16[512,320]{1,0:T(8,128)(2,1)S(1)}, bf16[512,320]{1,0:T(8,128)(2,1)S(1)}, u32[]{:S(2)}, u32[]{:S(2)}) collective-permute-start(bf16[512,320]{1,0:T(8,128)(2,1)S(1)} %bitcast.127), channel_id=1, source_target_pairs={{0,8},{1,9},{2,10},{3,11},{4,12},{5,13},{6,14},{7,15},{8,0},{9,1},... | collective-permute-start | bytes 983048 | tf_op jit(solution)/shard_map/ppermute | solution.py:375
  34.6 30.5 %collective-permute-start.9 = (bf16[512,320]{1,0:T(8,128)(2,1)S(1)}, bf16[512,320]{1,0:T(8,128)(2,1)S(1)}, u32[]{:S(2)}, u32[]{:S(2)}) collective-permute-start(bf16[512,320]{1,0:T(8,128)(2,1)S(1)} %bitcast.128), channel_id=1, source_target_pairs={{0,4},{1,5},{2,6},{3,7},{4,8},{5,9},{6,10},{7,11},{8,12},{9,13},{1... | collective-permute-start | bytes 983048 | tf_op jit(solution)/shard_map/ppermute | solution.py:375
  67.2 192.9 %all-gather.10.cloned.1.call-start = ((), (), s32[]{:S(2)}) async-start(), calls=%async_computation.12 | async-start | bytes 6488064 | tf_op jit(solution)/shard_map/all_gather | solution.py:483
  68.2 227.3 %all-gather.6.cloned.1.call-start = ((), (), s32[]{:S(2)}) async-start(), calls=%async_computation.6 | async-start | bytes 12976128 | tf_op jit(solution)/shard_map/all_gather | solution.py:553
  71.6 28.9 %collective-permute-start.10 = (bf16[2048,320]{0,1:T(8,128)(2,1)}, bf16[2048,320]{0,1:T(8,128)(2,1)}, u32[]{:S(2)}, u32[]{:S(2)}) collective-permute-start(bf16[2048,320]{0,1:T(8,128)(2,1)} %copy.48), channel_id=1, source_target_pairs={{0,16},{16,0},{1,17},{17,1},{2,18},{18,2},{3,19},{19,3},{4,20},{20... | collective-permute-start | bytes 3932168 | tf_op jit(solution)/shard_map/ppermute | solution.py:378
  80.7 35.8 %collective-permute-start.17 = (bf16[128,2048]{1,0:T(8,128)(2,1)}, bf16[128,2048]{1,0:T(8,128)(2,1)}, u32[]{:S(2)}, u32[]{:S(2)}) collective-permute-start(bf16[128,2048]{1,0:T(8,128)(2,1)} %bitcast_convert_fusion), channel_id=1, source_target_pairs={{0,4},{1,5},{2,6},{3,7},{4,8},{5,9},{6,10},{7,11},{8,12},{9,13},{1... | collective-permute-start | bytes 1572872 | tf_op jit(solution)/shard_map/ppermute | solution.py:375
  98.4 44.0 %collective-permute-start.18 = (bf16[128,2048]{1,0:T(8,128)(2,1)}, bf16[128,2048]{1,0:T(8,128)(2,1)}, u32[]{:S(2)}, u32[]{:S(2)}) collective-permute-start(bf16[128,2048]{1,0:T(8,128)(2,1)} %bitcast_convert_fusion), channel_id=1, source_target_pairs={{0,8},{1,9},{2,10},{3,11},{4,12},{5,13},{6,14},{7,15},{8,0},{9,1},... | collective-permute-start | bytes 1572872 | tf_op jit(solution)/shard_map/ppermute | solution.py:375
  98.4 46.9 %collective-permute-start.19 = (bf16[128,2048]{1,0:T(8,128)(2,1)}, bf16[128,2048]{1,0:T(8,128)(2,1)}, u32[]{:S(2)}, u32[]{:S(2)}) collective-permute-start(bf16[128,2048]{1,0:T(8,128)(2,1)} %bitcast_convert_fusion), channel_id=1, source_target_pairs={{0,12},{1,13},{2,14},{3,15},{4,0},{5,1},{6,2},{7,3},{8,4},{9,5},{1... | collective-permute-start | bytes 1572872 | tf_op jit(solution)/shard_map/ppermute | solution.py:375
  112.4 35.7 %collective-permute-start.13 = (bf16[512,128]{1,0:T(8,128)(2,1)}, bf16[512,128]{1,0:T(8,128)(2,1)S(1)}, u32[]{:S(2)}, u32[]{:S(2)}) collective-permute-start(bf16[512,128]{1,0:T(8,128)(2,1)} %get-tuple-element.88), channel_id=1, source_target_pairs={{0,12},{1,13},{2,14},{3,15},{4,0},{5,1},{6,2},{7,3},{8,4},{9,5},{1... | collective-permute-start | bytes 393224 | tf_op jit(solution)/shard_map/ppermute | solution.py:375
  113.9 50.9 %collective-permute-start.12 = (bf16[512,128]{1,0:T(8,128)(2,1)}, bf16[512,128]{1,0:T(8,128)(2,1)S(1)}, u32[]{:S(2)}, u32[]{:S(2)}) collective-permute-start(bf16[512,128]{1,0:T(8,128)(2,1)} %get-tuple-element.88), channel_id=1, source_target_pairs={{0,8},{1,9},{2,10},{3,11},{4,12},{5,13},{6,14},{7,15},{8,0},{9,1},... | collective-permute-start | bytes 393224 | tf_op jit(solution)/shard_map/ppermute | solution.py:375
  116.5 48.3 %collective-permute-start.11 = (bf16[512,128]{1,0:T(8,128)(2,1)}, bf16[512,128]{1,0:T(8,128)(2,1)S(1)}, u32[]{:S(2)}, u32[]{:S(2)}) collective-permute-start(bf16[512,128]{1,0:T(8,128)(2,1)} %get-tuple-element.88), channel_id=1, source_target_pairs={{0,4},{1,5},{2,6},{3,7},{4,8},{5,9},{6,10},{7,11},{8,12},{9,13},{1... | collective-permute-start | bytes 393224 | tf_op jit(solution)/shard_map/ppermute | solution.py:375
  171.9 24.6 %collective-permute-start.15 = (bf16[128,1408]{1,0:T(8,128)(2,1)}, bf16[128,1408]{1,0:T(8,128)(2,1)}, u32[]{:S(2)}, u32[]{:S(2)}) collective-permute-start(bf16[128,1408]{1,0:T(8,128)(2,1)} %get-tuple-element.213), channel_id=1, source_target_pairs={{0,8},{1,9},{2,10},{3,11},{4,12},{5,13},{6,14},{7,15},{8,0},{9,1},... | collective-permute-start | bytes 1081352 | tf_op jit(solution)/shard_map/ppermute | solution.py:375
  203.8 243.6 %reduce-scatter.5.cloned.1.call-start = ((), (), s32[]{:S(2)}) async-start(), calls=%async_computation.7 | async-start | bytes 7208960 | tf_op jit(solution)/shard_map/reduce_scatter | solution.py:611
  209.2 32.2 %collective-permute-start.22 = (bf16[128,2048]{1,0:T(8,128)(2,1)S(1)}, bf16[128,2048]{1,0:T(8,128)(2,1)S(1)}, u32[]{:S(2)}, u32[]{:S(2)}) collective-permute-start(bf16[128,2048]{1,0:T(8,128)(2,1)S(1)} %get-tuple-element.194), channel_id=1, source_target_pairs={{0,2},{1,3},{2,0},{3,1},{4,6},{5,7},{6,4},{7,5},{8,10},{9,11},{10,... | collective-permute-start | bytes 1572872 | tf_op jit(solution)/shard_map/ppermute | solution.py:372
  209.9 31.5 %collective-permute-start.21 = (bf16[128,2048]{1,0:T(8,128)(2,1)S(1)}, bf16[128,2048]{1,0:T(8,128)(2,1)S(1)}, u32[]{:S(2)}, u32[]{:S(2)}) collective-permute-start(bf16[128,2048]{1,0:T(8,128)(2,1)S(1)} %get-tuple-element.192), channel_id=1, source_target_pairs={{0,1},{1,0},{2,3},{3,2},{4,5},{5,4},{6,7},{7,6},{8,9},{9,8},{10,11... | collective-permute-start | bytes 1572872 | tf_op jit(solution)/shard_map/ppermute | solution.py:372
  243.5 25.7 %collective-permute-start.24 = (bf16[128,2048]{1,0:T(8,128)(2,1)S(1)}, bf16[128,2048]{1,0:T(8,128)(2,1)}, u32[]{:S(2)}, u32[]{:S(2)}) collective-permute-start(bf16[128,2048]{1,0:T(8,128)(2,1)S(1)} %constant_dynamic-update-slice_fusion.12), channel_id=1, source_target_pairs={{0,4},{1,5},{2,6},{3,7},{4,8},{5,9},{6,10},{7,11},{8,12},{9,13},{1... | collective-permute-start | bytes 1572872 | tf_op jit(solution)/shard_map/ppermute | solution.py:375
  256.3 33.2 %collective-permute-start.25 = (bf16[128,2048]{1,0:T(8,128)(2,1)S(1)}, bf16[128,2048]{1,0:T(8,128)(2,1)S(1)}, u32[]{:S(2)}, u32[]{:S(2)}) collective-permute-start(bf16[128,2048]{1,0:T(8,128)(2,1)S(1)} %constant_dynamic-update-slice_fusion.12), channel_id=1, source_target_pairs={{0,8},{1,9},{2,10},{3,11},{4,12},{5,13},{6,14},{7,15},{8,0},{9,1},... | collective-permute-start | bytes 1572872 | tf_op jit(solution)/shard_map/ppermute | solution.py:375
  256.4 33.2 %collective-permute-start.26 = (bf16[128,2048]{1,0:T(8,128)(2,1)S(1)}, bf16[128,2048]{1,0:T(8,128)(2,1)S(1)}, u32[]{:S(2)}, u32[]{:S(2)}) collective-permute-start(bf16[128,2048]{1,0:T(8,128)(2,1)S(1)} %constant_dynamic-update-slice_fusion.12), channel_id=1, source_target_pairs={{0,12},{1,13},{2,14},{3,15},{4,0},{5,1},{6,2},{7,3},{8,4},{9,5},{1... | collective-permute-start | bytes 1572872 | tf_op jit(solution)/shard_map/ppermute | solution.py:375
  321.6 25.8 %collective-permute-start.27 = (bf16[128,2048]{1,0:T(8,128)(2,1)}, bf16[128,2048]{1,0:T(8,128)(2,1)S(1)}, u32[]{:S(2)}, u32[]{:S(2)}) collective-permute-start(bf16[128,2048]{1,0:T(8,128)(2,1)} %get-tuple-element.191), channel_id=1, source_target_pairs={{0,12},{1,13},{2,14},{3,15},{4,0},{5,1},{6,2},{7,3},{8,4},{9,5},{1... | collective-permute-start | bytes 1572872 | tf_op jit(solution)/shard_map/ppermute | solution.py:375
  347.4 152.1 %reduce-scatter.7.cloned.1.call-start = ((), (), s32[]{:S(2)}) async-start(), calls=%async_computation.8 | async-start | bytes 1310720 | tf_op jit(solution)/shard_map/reduce_scatter | solution.py:630
  350.4 36.8 %collective-permute-start.30 = (bf16[128,2048]{1,0:T(8,128)(2,1)}, bf16[128,2048]{1,0:T(8,128)(2,1)}, u32[]{:S(2)}, u32[]{:S(2)}) collective-permute-start(bf16[128,2048]{1,0:T(8,128)(2,1)} %get-tuple-element.190), channel_id=1, source_target_pairs={{0,8},{1,9},{2,10},{3,11},{4,12},{5,13},{6,14},{7,15},{8,0},{9,1},... | collective-permute-start | bytes 1572872 | tf_op jit(solution)/shard_map/ppermute | solution.py:375
  351.3 35.8 %collective-permute-start.31 = (bf16[128,2048]{1,0:T(8,128)(2,1)}, bf16[128,2048]{1,0:T(8,128)(2,1)}, u32[]{:S(2)}, u32[]{:S(2)}) collective-permute-start(bf16[128,2048]{1,0:T(8,128)(2,1)} %get-tuple-element.189), channel_id=1, source_target_pairs={{0,4},{1,5},{2,6},{3,7},{4,8},{5,9},{6,10},{7,11},{8,12},{9,13},{1... | collective-permute-start | bytes 1572872 | tf_op jit(solution)/shard_map/ppermute | solution.py:375
  394.4 35.9 %collective-permute-start.35 = (bf16[128,2048]{1,0:T(8,128)(2,1)S(1)}, bf16[128,2048]{1,0:T(8,128)(2,1)}, u32[]{:S(2)}, u32[]{:S(2)}) collective-permute-start(bf16[128,2048]{1,0:T(8,128)(2,1)S(1)} %get-tuple-element.184), channel_id=1, source_target_pairs={{0,8},{1,9},{2,10},{3,11},{4,12},{5,13},{6,14},{7,15},{8,0},{9,1},... | collective-permute-start | bytes 1572872 | tf_op jit(solution)/shard_map/ppermute | solution.py:375
  447.4 86.3 %reduce-scatter.9.cloned.1.call-start = ((), (), s32[]{:S(2)}) async-start(), calls=%async_computation.9 | async-start | bytes 3604480 | tf_op jit(solution)/shard_map/reduce_scatter | solution.py:612
  447.9 126.8 %reduce-scatter.11.cloned.1.call-start = ((), (), s32[]{:S(2)}) async-start(), calls=%async_computation.10 | async-start | bytes 1638400 | tf_op jit(solution)/shard_map/reduce_scatter | solution.py:681
  448.0 59.6 %collective-permute-start.52 = (bf16[512,2048]{1,0:T(8,128)(2,1)}, bf16[512,2048]{1,0:T(8,128)(2,1)}, u32[]{:S(2)}, u32[]{:S(2)}) collective-permute-start(bf16[512,2048]{1,0:T(8,128)(2,1)} %copy-done.18), channel_id=1, source_target_pairs={{0,16},{16,0},{1,17},{17,1},{2,18},{18,2},{3,19},{19,3},{4,20},{20... | collective-permute-start | bytes 6291464 | tf_op jit(solution)/shard_map/ppermute | solution.py:378
  496.4 25.6 %collective-permute-start.50 = (bf16[128,1408]{1,0:T(8,128)(2,1)}, bf16[128,1408]{1,0:T(8,128)(2,1)}, u32[]{:S(2)}, u32[]{:S(2)}) collective-permute-start(bf16[128,1408]{1,0:T(8,128)(2,1)} %get-tuple-element.209), channel_id=1, source_target_pairs={{0,8},{1,9},{2,10},{3,11},{4,12},{5,13},{6,14},{7,15},{8,0},{9,1},... | collective-permute-start | bytes 1081352 | tf_op jit(solution)/shard_map/ppermute | solution.py:375
  496.4 37.2 %collective-permute-start.51 = (bf16[128,1408]{1,0:T(8,128)(2,1)}, bf16[128,1408]{1,0:T(8,128)(2,1)}, u32[]{:S(2)}, u32[]{:S(2)}) collective-permute-start(bf16[128,1408]{1,0:T(8,128)(2,1)} %get-tuple-element.208), channel_id=1, source_target_pairs={{0,12},{1,13},{2,14},{3,15},{4,0},{5,1},{6,2},{7,3},{8,4},{9,5},{1... | collective-permute-start | bytes 1081352 | tf_op jit(solution)/shard_map/ppermute | solution.py:375
  507.6 31.9 %collective-permute-start.48 = (bf16[128,2048]{1,0:T(8,128)(2,1)}, bf16[128,2048]{1,0:T(8,128)(2,1)S(1)}, u32[]{:S(2)}, u32[]{:S(2)}) collective-permute-start(bf16[128,2048]{1,0:T(8,128)(2,1)} %get-tuple-element.180), channel_id=1, source_target_pairs={{0,3},{1,2},{2,1},{3,0},{4,7},{5,6},{6,5},{7,4},{8,11},{9,10},{10,... | collective-permute-start | bytes 1572872 | tf_op jit(solution)/shard_map/ppermute | solution.py:372
  514.6 29.5 %collective-permute-start.47 = (bf16[128,2048]{1,0:T(8,128)(2,1)}, bf16[128,2048]{1,0:T(8,128)(2,1)S(1)}, u32[]{:S(2)}, u32[]{:S(2)}) collective-permute-start(bf16[128,2048]{1,0:T(8,128)(2,1)} %get-tuple-element.181), channel_id=1, source_target_pairs={{0,2},{1,3},{2,0},{3,1},{4,6},{5,7},{6,4},{7,5},{8,10},{9,11},{10,... | collective-permute-start | bytes 1572872 | tf_op jit(solution)/shard_map/ppermute | solution.py:372
  522.0 27.7 %collective-permute-start.46 = (bf16[128,2048]{1,0:T(8,128)(2,1)}, bf16[128,2048]{1,0:T(8,128)(2,1)S(1)}, u32[]{:S(2)}, u32[]{:S(2)}) collective-permute-start(bf16[128,2048]{1,0:T(8,128)(2,1)} %get-tuple-element.179), channel_id=1, source_target_pairs={{0,1},{1,0},{2,3},{3,2},{4,5},{5,4},{6,7},{7,6},{8,9},{9,8},{10,11... | collective-permute-start | bytes 1572872 | tf_op jit(solution)/shard_map/ppermute | solution.py:372
  (85 other events, 1083.7 us)
Sparse Core Ops, SparseCore 0:
  67.3 72.9 all-gather.7
  142.7 55.2 all-gather.9
  203.9 91.0 all-gather.5
  347.5 82.5 reduce-scatter.4
  447.5 25.0 reduce-scatter.6
  476.0 57.5 reduce-scatter.8
  536.5 38.1 reduce-scatter.10

commit v10 on v8

--- a/solution.py
+++ b/solution.py
@@ -82,7 +82,7 @@
 def project(low, weights, cosine, sine):
     tokens, width = low.shape
     q_width = weights.shape[1] - PAIR
-    rows = block_rows(tokens)
+    rows = min(256, tokens)
     return pl.pallas_call(
         project_kernel,
         out_shape=(
@@ -126,7 +126,7 @@
 def feed(low, weights, grad_hidden):
     tokens, width = low.shape
     block = weights.shape[2]
-    rows = block_rows(tokens)
+    rows = min(256, tokens)
     narrow = pl.BlockSpec((rows, block), lambda i: (i, 0))
     wide = pl.BlockSpec((rows, width), lambda i: (i, 0))
     return pl.pallas_call(
@@ -461,12 +461,11 @@
         low_one, qkv_part, plane_pos = tie(normed_one.astype(bf16), qkv_part, plane_pos)
 
         ring = [qkv_part] + [shift_z(qkv_part, -t) for t in range(1, planes)]
+        low_one, *ring = tie(gather_w(low_one), *ring)
         qkv_ring = jnp.concatenate(ring + ring[: planes - 1], axis=0)
         qkv_mine = lax.dynamic_slice_in_dim(
             qkv_ring, ((planes - p) % planes) * GROUP * shard, width, 0
         )
-        low_one = gather_w(low_one)
-
         piece = shard // halves
         gate_up = jnp.where(c // halves == 0, scaled(w_gate, gain_two), scaled(w_up, gain_two))
         out_part, gate_up, qkv_mine = tie(
@@ -680,6 +679,28 @@
         qkv_sum = lax.psum_scatter(
             qkv_sum, "seq", axis_index_groups=across, tiled=True
         )
+        grad_w_down = jnp.concatenate(collect_dp(down_sum, c), axis=1).astype(f32)
+        gate_up_rows = jnp.zeros((planes, piece, ff_block), bf16)
+        for t in range(planes):
+            gate_up_rows = lax.dynamic_update_index_in_dim(
+                gate_up_rows, gate_up_sent[t], (p - t) % planes, 0
+            )
+        gate_up_rows = collect_dp(gate_up_rows, c)
+
+        def rows_of(members):
+            wide = [jnp.concatenate([one[i] for i in range(planes)], axis=1) for one in members]
+            return jnp.concatenate(wide, axis=0).astype(f32)
+
+        gate_rows = rows_of(gate_up_rows[:halves])
+        up_rows = rows_of(gate_up_rows[halves:])
+        grad_w_gate = gate_rows * gain_two
+        grad_w_up = up_rows * gain_two
+        grad_gain_mlp = jnp.sum(
+            gate_rows * w_gate.astype(f32) + up_rows * w_up.astype(f32), axis=1
+        )
+        qkv_sum, grad_w_gate, grad_w_up, grad_w_down, grad_gain_mlp = tie(
+            qkv_sum, grad_w_gate, grad_w_up, grad_w_down, grad_gain_mlp
+        )
         qkv_sum = qkv_sum.reshape(GROUP, shard, part_width)
         qkv_sum = lax.all_to_all(qkv_sum, "seq", 0, 0, axis_index_groups=in_plane, tiled=True)
         qkv_sum = collect_dp(qkv_sum, c)
@@ -692,25 +713,6 @@
         k_sum = kv_sum[..., :HEAD_DIM].reshape(shard, GROUP * HEAD_DIM)
         v_sum = kv_sum[..., HEAD_DIM:].reshape(shard, GROUP * HEAD_DIM)
 
-        grad_w_down = jnp.concatenate(collect_dp(down_sum, c), axis=1).astype(f32)
-        gate_up_rows = jnp.zeros((planes, piece, ff_block), bf16)
-        for t in range(planes):
-            gate_up_rows = lax.dynamic_update_index_in_dim(
-                gate_up_rows, gate_up_sent[t], (p - t) % planes, 0
-            )
-        gate_up_rows = collect_dp(gate_up_rows, c)
-
-        def rows_of(members):
-            wide = [jnp.concatenate([one[i] for i in range(planes)], axis=1) for one in members]
-            return jnp.concatenate(wide, axis=0).astype(f32)
-
-        gate_rows = rows_of(gate_up_rows[:halves])
-        up_rows = rows_of(gate_up_rows[halves:])
-        grad_w_gate = gate_rows * gain_two
-        grad_w_up = up_rows * gain_two
-        grad_gain_mlp = jnp.sum(
-            gate_rows * w_gate.astype(f32) + up_rows * w_up.astype(f32), axis=1
-        )
         grad_gain_attn = (
             jnp.sum(q_sum * w_query.astype(f32), axis=1)
             + jnp.sum(k_sum * w_key.astype(f32), axis=1)

time: 579 us -> 614 us (1.060)
  waiting for transfers between devices: 220 us -> 242 us
  starting transfers between devices: 137 us -> 157 us
  Pallas kernels: 52.7 us -> 43.6 us
    ppermute x27, starting transfers between devices: 48.8 us -> 114 us  [shift_z(): lax.ppermute(value, 'seq', [(s, (s + GROUP * t) % n_seq) for s in range(n...]
    ppermute x13, starting transfers between devices: 44.9 us -> 15.7 us  [shift_dp(): return lax.ppermute(value, 'dp', [(c, (c + t) % n_dp) for c in range(n_dp)])]
    ppermute x17, starting transfers between devices: 29.1 us -> 15.1 us  [xor_w(): return lax.ppermute(value, 'seq', [(s, s ^ j) for s in range(n_seq)])]
    reduce_scatter x1, waiting for transfers between devices: 0.01 us -> 11.4 us  [body(): lax.psum_scatter(down_sum, 'seq', axis_index_groups=in_plane, tiled=True)]
    pallas_call x1, Pallas kernels: 27.8 us -> 19.7 us  [feed(): pl.pallas_call(feed_kernel, out_shape=(jax.ShapeDtypeStruct((tokens, bloc...]
    mul x1 -> x0, other arithmetic: 6.29 us -> none  [body(): grad_w_up = up_rows * gain_two]
    unnamed x181 -> x186, local copies, waits for them, and re-layouts: 23.8 us -> 20.9 us
  transfers between devices with their start and end apart: 68 -> 68, of which waited for: 25 -> 28; matrix products, arithmetic and copies ran while one was open for 22% -> 22% of each run, Pallas kernels for 9% -> 7%
where the time goes in v10:
time: 614 us; the launch traced here: 605 us
  waiting for transfers between devices  242 us (39%)
  starting transfers between devices  157 us (26%)
  local copies, waits for them, and re-layouts  63.8 us (10%)
  other arithmetic  44.5 us (7%)
  Pallas kernels  43.6 us (7%)
  matrix products  38.3 us (6%)
  between operations  16.3 us (3%)
    ppermute x27, waiting for transfers between devices, shift_z(): lax.ppermute(value, 'seq', [(s, (s + GROUP * t) % n_seq) for s in range(n...  159 us
    ppermute x27, starting transfers between devices, shift_z(): lax.ppermute(value, 'seq', [(s, (s + GROUP * t) % n_seq) for s in range(n...  114 us
    ppermute x17, waiting for transfers between devices, xor_w(): return lax.ppermute(value, 'seq', [(s, s ^ j) for s in range(n_seq)])  43.2 us
    dot_general x13, matrix products, dot(): lax.dot_general(left, right, (contract, ((), ())), preferred_element_type...  38.3 us
    unnamed x186, local copies, waits for them, and re-layouts  20.9 us
    reduce_scatter x1, waiting for transfers between devices, body(): lax.psum_scatter(qkv_sum, 'seq', axis_index_groups=across, tiled=True)  20.5 us
    pallas_call x1, Pallas kernels, feed(): pl.pallas_call(feed_kernel, out_shape=(jax.ShapeDtypeStruct((tokens, bloc...  19.7 us
    ppermute x13, starting transfers between devices, shift_dp(): return lax.ppermute(value, 'dp', [(c, (c + t) % n_dp) for c in range(n_dp)])  15.7 us
  transfers between devices with their start and end apart: 68, of which 28 were waited for; matrix products, arithmetic and copies ran while one was open for 22% of the time, Pallas kernels for 7%

profile of v10, /device:TPU:1, one launch (start us, length us, event | category | flops | bytes accessed | tf_op | source)
XLA Modules:
  0.0 605.3 jit_solution(13848807955698225831)
XLA Ops:
  37.2 5.8 collective-permute-done.3
  48.7 7.9 %collective-permute-done.5 = bf16[64,2048]{1,0:T(8,128)(2,1)S(1)} collective-permute-done((bf16[64,2048]{1,0:T(8,128)(2,1)S(1)}, bf16[64,2048]{1,0:T(8,128)(2,1)S(1)}, u32[]{:S(2)}, u32[]{:S(2)}) %collective-permute-start.5) | collective-permute-done | bytes 262176 | tf_op jit(solution)/shard_map/ppermute | solution.py:372
  58.8 6.5 %collective-permute-done.8 = bf16[512,320]{1,0:T(8,128)(2,1)S(1)} collective-permute-done((bf16[512,320]{1,0:T(8,128)(2,1)S(1)}, bf16[512,320]{1,0:T(8,128)(2,1)S(1)}, u32[]{:S(2)}, u32[]{:S(2)}) %collective-permute-start.8) | collective-permute-done | bytes 327712 | tf_op jit(solution)/shard_map/ppermute | solution.py:375
  67.6 5.6 collective-permute-start.13
  79.2 28.4 %collective-permute-start.10 = (bf16[128,1408]{1,0:T(8,128)(2,1)}, bf16[128,1408]{1,0:T(8,128)(2,1)}, u32[]{:S(2)}, u32[]{:S(2)}) collective-permute-start(bf16[128,1408]{1,0:T(8,128)(2,1)} %get-tuple-element.220), channel_id=1, source_target_pairs={{0,4},{1,5},{2,6},{3,7},{4,8},{5,9},{6,10},{7,11},{8,12},{9,13},{1... | collective-permute-start | bytes 1081352 | tf_op jit(solution)/shard_map/ppermute | solution.py:375
  116.5 5.0 project.1
  121.5 20.3 %collective-permute-done.11 = bf16[128,1408]{1,0:T(8,128)(2,1)} collective-permute-done((bf16[128,1408]{1,0:T(8,128)(2,1)}, bf16[128,1408]{1,0:T(8,128)(2,1)}, u32[]{:S(2)}, u32[]{:S(2)}) %collective-permute-start.11) | collective-permute-done | bytes 360480 | tf_op jit(solution)/shard_map/ppermute | solution.py:375
  141.9 5.3 collective-permute-done.12
  152.0 10.8 %collective-permute-start.16 = (bf16[512,128]{1,0:T(8,128)(2,1)S(1)}, bf16[512,128]{1,0:T(8,128)(2,1)S(1)}, u32[]{:S(2)}, u32[]{:S(2)}) collective-permute-start(bf16[512,128]{1,0:T(8,128)(2,1)S(1)} %copy-done.43), channel_id=1, source_target_pairs={{0,12},{1,13},{2,14},{3,15},{4,0},{5,1},{6,2},{7,3},{8,4},{9,5},{1... | collective-permute-start | bytes 393224 | tf_op jit(solution)/shard_map/ppermute | solution.py:375
  164.8 8.5 %collective-permute-done.15 = bf16[512,128]{1,0:T(8,128)(2,1)S(1)} collective-permute-done((bf16[512,128]{1,0:T(8,128)(2,1)S(1)}, bf16[512,128]{1,0:T(8,128)(2,1)S(1)}, u32[]{:S(2)}, u32[]{:S(2)}) %collective-permute-start.15) | collective-permute-done | bytes 131104 | tf_op jit(solution)/shard_map/ppermute | solution.py:375
  178.7 7.6 %attend.1 = (bf16[512,512]{1,0:T(8,128)(2,1)}, f32[4,8,1024]{2,1,0:T(8,128)}) custom-call(s32[1]{0:T(128)} %bitcast.1.seen_ref, bf16[512,512]{1,0:T(8,128)(2,1)} %get-tuple-element.92.q_ref, bf16[4,512,128]{2,1,0:T(8,128)(2,1)} %pad_maximum_fusion.9.kv_ref, s32[512,1]{1,0:T(8,128)} %copy.53.qpos_ref.kpos_ref, s32[1,512]{1,0:T(1,128)} %bitcast.158), custom_call_target="tpu_custom_call" | custom-call | tf_op jit(solution)/shard_map/attend/pallas_call | solution.py:255
  192.7 29.1 %collective-permute-done.22 = bf16[128,2048]{1,0:T(8,128)(2,1)} collective-permute-done((bf16[128,2048]{1,0:T(8,128)(2,1)S(1)}, bf16[128,2048]{1,0:T(8,128)(2,1)}, u32[]{:S(2)}, u32[]{:S(2)}) %collective-permute-start.22) | collective-permute-done | bytes 524320 | tf_op jit(solution)/shard_map/ppermute | solution.py:375
  230.4 14.1 %collective-permute-start.24 = (bf16[128,2048]{1,0:T(8,128)(2,1)S(1)}, bf16[128,2048]{1,0:T(8,128)(2,1)S(1)}, u32[]{:S(2)}, u32[]{:S(2)}) collective-permute-start(bf16[128,2048]{1,0:T(8,128)(2,1)S(1)} %constant_dynamic-update-slice_fusion.12), channel_id=1, source_target_pairs={{0,4},{1,5},{2,6},{3,7},{4,8},{5,9},{6,10},{7,11},{8,12},{9,13},{1... | collective-permute-start | bytes 1572872 | tf_op jit(solution)/shard_map/ppermute | solution.py:375
  244.4 9.2 %collective-permute-start.25 = (bf16[128,2048]{1,0:T(8,128)(2,1)S(1)}, bf16[128,2048]{1,0:T(8,128)(2,1)S(1)}, u32[]{:S(2)}, u32[]{:S(2)}) collective-permute-start(bf16[128,2048]{1,0:T(8,128)(2,1)S(1)} %constant_dynamic-update-slice_fusion.12), channel_id=1, source_target_pairs={{0,8},{1,9},{2,10},{3,11},{4,12},{5,13},{6,14},{7,15},{8,0},{9,1},... | collective-permute-start | bytes 1572872 | tf_op jit(solution)/shard_map/ppermute | solution.py:375
  264.7 23.6 %collective-permute-done.25 = bf16[128,2048]{1,0:T(8,128)(2,1)S(1)} collective-permute-done((bf16[128,2048]{1,0:T(8,128)(2,1)S(1)}, bf16[128,2048]{1,0:T(8,128)(2,1)S(1)}, u32[]{:S(2)}, u32[]{:S(2)}) %collective-permute-start.25) | collective-permute-done | bytes 524320 | tf_op jit(solution)/shard_map/ppermute | solution.py:375
  293.6 19.7 %feed.1 = (bf16[512,1408]{1,0:T(8,128)(2,1)}, bf16[512,1408]{1,0:T(8,128)(2,1)}, bf16[512,1408]{1,0:T(8,128)(2,1)}, bf16[512,2048]{1,0:T(8,128)(2,1)}) custom-call(bf16[512,2048]{1,0:T(8,128)(2,1)} %get-tuple-element.236.low_ref, bf16[2,2048,1408]{2,1,0:T(8,128)(2,1)} %bitcast.132, f32[512,1408]{1,0:T(8,128)} %convolution_add_fusion.grad_hidden_ref), custom_call_target="tpu_custom_call" | custom-call | tf_op jit(solution)/shard_map/feed/pallas_call | solution.py:132
  319.8 10.8 %collective-permute-start.27 = (bf16[128,2048]{1,0:T(8,128)(2,1)}, bf16[128,2048]{1,0:T(8,128)(2,1)S(1)}, u32[]{:S(2)}, u32[]{:S(2)}) collective-permute-start(bf16[128,2048]{1,0:T(8,128)(2,1)} %get-tuple-element.197), channel_id=1, source_target_pairs={{0,12},{1,13},{2,14},{3,15},{4,0},{5,1},{6,2},{7,3},{8,4},{9,5},{1... | collective-permute-start | bytes 1572872 | tf_op jit(solution)/shard_map/ppermute | solution.py:375
  330.6 8.6 %convolution_convert_fusion = bf16[2048,1408]{1,0:T(8,128)(2,1)} fusion(bf16[1024,2048]{1,0:T(8,128)(2,1)S(1)} %constant_dynamic-update-slice_fusion.32, bf16[512,1408]{1,0:T(8,128)(2,1)S(1)} %collective-permute-done.29, bf16[512,1408]{1,0:T(8,128)(2,1)S(1)} %get-tuple-element.183), kind=kOutput, calls=%fused_computation | convolution fusion | flops 5914230784 | bytes 12845056 | tf_op jit(solution)/shard_map/dot_general | solution.py:26
  355.9 5.9 convolution_convert_fusion.1
  361.8 21.5 %collective-permute-done.30 = bf16[128,2048]{1,0:T(8,128)(2,1)} collective-permute-done((bf16[128,2048]{1,0:T(8,128)(2,1)}, bf16[128,2048]{1,0:T(8,128)(2,1)}, u32[]{:S(2)}, u32[]{:S(2)}) %collective-permute-start.30) | collective-permute-done | bytes 524320 | tf_op jit(solution)/shard_map/ppermute | solution.py:375
  390.9 8.3 %collective-permute-done.36 = bf16[128,2048]{1,0:T(8,128)(2,1)S(1)} collective-permute-done((bf16[128,2048]{1,0:T(8,128)(2,1)S(1)}, bf16[128,2048]{1,0:T(8,128)(2,1)S(1)}, u32[]{:S(2)}, u32[]{:S(2)}) %collective-permute-start.36) | collective-permute-done | bytes 524320 | tf_op jit(solution)/shard_map/ppermute | solution.py:372
  400.9 12.0 %collective-permute-done.38 = bf16[64,2048]{1,0:T(8,128)(2,1)S(1)} collective-permute-done((bf16[64,2048]{1,0:T(8,128)(2,1)S(1)}, bf16[64,2048]{1,0:T(8,128)(2,1)S(1)}, u32[]{:S(2)}, u32[]{:S(2)}) %collective-permute-start.38) | collective-permute-done | bytes 262176 | tf_op jit(solution)/shard_map/ppermute | solution.py:372
  413.7 10.9 %collective-permute-done.35 = bf16[128,2048]{1,0:T(8,128)(2,1)} collective-permute-done((bf16[128,2048]{1,0:T(8,128)(2,1)S(1)}, bf16[128,2048]{1,0:T(8,128)(2,1)}, u32[]{:S(2)}, u32[]{:S(2)}) %collective-permute-start.35) | collective-permute-done | bytes 524320 | tf_op jit(solution)/shard_map/ppermute | solution.py:375
  431.9 10.1 %collective-permute-done.40 = bf16[128,2048]{1,0:T(8,128)(2,1)S(1)} collective-permute-done((bf16[128,2048]{1,0:T(8,128)(2,1)}, bf16[128,2048]{1,0:T(8,128)(2,1)S(1)}, u32[]{:S(2)}, u32[]{:S(2)}) %collective-permute-start.40) | collective-permute-done | bytes 524320 | tf_op jit(solution)/shard_map/ppermute | solution.py:375
  443.2 11.3 %attend_back.1 = (bf16[512,512]{1,0:T(8,128)(2,1)}, bf16[4,512,128]{2,1,0:T(8,128)(2,1)}) custom-call(s32[1]{0:T(128)} %bitcast.1.seen_ref, bf16[512,512]{1,0:T(8,128)(2,1)} %get-tuple-element.92.q_ref, bf16[512,512]{1,0:T(8,128)(2,1)} %bitcast.150, bf16[512,512]{1,0:T(8,128)(2,1)} %get-tuple-element.95.o_ref, ...), custom_call_target="tpu_custom_call" | custom-call | tf_op jit(solution)/shard_map/attend_back/pallas_call | solution.py:285
  455.6 4.7 collective-permute-start.45
  460.3 14.2 %collective-permute-start.44 = (bf16[512,128]{1,0:T(8,128)(2,1)S(1)}, bf16[512,128]{1,0:T(8,128)(2,1)S(1)}, u32[]{:S(2)}, u32[]{:S(2)}) collective-permute-start(bf16[512,128]{1,0:T(8,128)(2,1)S(1)} %get-tuple-element.234), channel_id=1, source_target_pairs={{0,8},{1,9},{2,10},{3,11},{4,12},{5,13},{6,14},{7,15},{8,0},{9,1},... | collective-permute-start | bytes 393224 | tf_op jit(solution)/shard_map/ppermute | solution.py:375
  476.7 7.1 %collective-permute-done.44 = bf16[512,128]{1,0:T(8,128)(2,1)S(1)} collective-permute-done((bf16[512,128]{1,0:T(8,128)(2,1)S(1)}, bf16[512,128]{1,0:T(8,128)(2,1)S(1)}, u32[]{:S(2)}, u32[]{:S(2)}) %collective-permute-start.44) | collective-permute-done | bytes 131104 | tf_op jit(solution)/shard_map/ppermute | solution.py:375
  509.6 6.3 %collective-permute-done.50 = bf16[128,1408]{1,0:T(8,128)(2,1)} collective-permute-done((bf16[128,1408]{1,0:T(8,128)(2,1)}, bf16[128,1408]{1,0:T(8,128)(2,1)}, u32[]{:S(2)}, u32[]{:S(2)}) %collective-permute-start.50) | collective-permute-done | bytes 360480 | tf_op jit(solution)/shard_map/ppermute | solution.py:375
  519.8 11.4 %reduce-scatter.9.cloned.1.call-done = bf16[352,1024]{1,0:T(8,128)(2,1)} async-done(((bf16[1408,1024]{1,0:T(8,128)(2,1)}), bf16[352,1024]{1,0:T(8,128)(2,1)}) %reduce-scatter.9.cloned.1.call-update) | async-done | bytes 720912 | tf_op jit(solution)/shard_map/reduce_scatter | solution.py:610
  553.2 5.4 fusion.7
  558.6 20.5 %reduce-scatter.11.cloned.1.call-done = bf16[512,320]{0,1:T(8,128)(2,1)} async-done(((bf16[2048,320]{0,1:T(8,128)(2,1)}), bf16[512,320]{0,1:T(8,128)(2,1)}) %reduce-scatter.11.cloned.1.call-update) | async-done | bytes 327696 | tf_op jit(solution)/shard_map/reduce_scatter | solution.py:679
  (422 shorter events, 212.6 us)
Async XLA Ops:
  7.2 66.6 %all-gather.8.cloned.1.call-start = ((), (), s32[]{:S(2)}) async-start(), calls=%async_computation.11 | async-start | bytes 6488064 | tf_op jit(solution)/shard_map/all_gather | solution.py:483
  19.1 167.2 %all-gather.10.cloned.1.call-start = ((), (), s32[]{:S(2)}) async-start(), calls=%async_computation.12 | async-start | bytes 2359296 | tf_op jit(solution)/shard_map/all_gather | solution.py:488
  32.5 26.3 %collective-permute-start.7 = (bf16[512,320]{1,0:T(8,128)(2,1)S(1)}, bf16[512,320]{1,0:T(8,128)(2,1)S(1)}, u32[]{:S(2)}, u32[]{:S(2)}) collective-permute-start(bf16[512,320]{1,0:T(8,128)(2,1)S(1)} %bitcast.136), channel_id=1, source_target_pairs={{0,12},{1,13},{2,14},{3,15},{4,0},{5,1},{6,2},{7,3},{8,4},{9,5},{1... | collective-permute-start | bytes 983048 | tf_op jit(solution)/shard_map/ppermute | solution.py:375
  36.8 28.5 %collective-permute-start.8 = (bf16[512,320]{1,0:T(8,128)(2,1)S(1)}, bf16[512,320]{1,0:T(8,128)(2,1)S(1)}, u32[]{:S(2)}, u32[]{:S(2)}) collective-permute-start(bf16[512,320]{1,0:T(8,128)(2,1)S(1)} %bitcast.137), channel_id=1, source_target_pairs={{0,8},{1,9},{2,10},{3,11},{4,12},{5,13},{6,14},{7,15},{8,0},{9,1},... | collective-permute-start | bytes 983048 | tf_op jit(solution)/shard_map/ppermute | solution.py:375
  36.8 28.5 %collective-permute-start.9 = (bf16[512,320]{1,0:T(8,128)(2,1)S(1)}, bf16[512,320]{1,0:T(8,128)(2,1)S(1)}, u32[]{:S(2)}, u32[]{:S(2)}) collective-permute-start(bf16[512,320]{1,0:T(8,128)(2,1)S(1)} %bitcast.138), channel_id=1, source_target_pairs={{0,4},{1,5},{2,6},{3,7},{4,8},{5,9},{6,10},{7,11},{8,12},{9,13},{1... | collective-permute-start | bytes 983048 | tf_op jit(solution)/shard_map/ppermute | solution.py:375
  67.6 42.1 %collective-permute-start.13 = (bf16[2048,320]{0,1:T(8,128)(2,1)}, bf16[2048,320]{0,1:T(8,128)(2,1)}, u32[]{:S(2)}, u32[]{:S(2)}) collective-permute-start(bf16[2048,320]{0,1:T(8,128)(2,1)} %copy.48), channel_id=1, source_target_pairs={{0,16},{16,0},{1,17},{17,1},{2,18},{18,2},{3,19},{19,3},{4,20},{20... | collective-permute-start | bytes 3932168 | tf_op jit(solution)/shard_map/ppermute | solution.py:378
  74.6 219.1 %all-gather.6.cloned.1.call-start = ((), (), s32[]{:S(2)}) async-start(), calls=%async_computation.6 | async-start | bytes 12976128 | tf_op jit(solution)/shard_map/all_gather | solution.py:524
  79.2 42.4 %collective-permute-start.10 = (bf16[128,1408]{1,0:T(8,128)(2,1)}, bf16[128,1408]{1,0:T(8,128)(2,1)}, u32[]{:S(2)}, u32[]{:S(2)}) collective-permute-start(bf16[128,1408]{1,0:T(8,128)(2,1)} %get-tuple-element.220), channel_id=1, source_target_pairs={{0,4},{1,5},{2,6},{3,7},{4,8},{5,9},{6,10},{7,11},{8,12},{9,13},{1... | collective-permute-start | bytes 1081352 | tf_op jit(solution)/shard_map/ppermute | solution.py:375
  107.6 34.2 %collective-permute-start.11 = (bf16[128,1408]{1,0:T(8,128)(2,1)}, bf16[128,1408]{1,0:T(8,128)(2,1)}, u32[]{:S(2)}, u32[]{:S(2)}) collective-permute-start(bf16[128,1408]{1,0:T(8,128)(2,1)} %get-tuple-element.219), channel_id=1, source_target_pairs={{0,8},{1,9},{2,10},{3,11},{4,12},{5,13},{6,14},{7,15},{8,0},{9,1},... | collective-permute-start | bytes 1081352 | tf_op jit(solution)/shard_map/ppermute | solution.py:375
  107.6 39.6 %collective-permute-start.12 = (bf16[128,1408]{1,0:T(8,128)(2,1)}, bf16[128,1408]{1,0:T(8,128)(2,1)}, u32[]{:S(2)}, u32[]{:S(2)}) collective-permute-start(bf16[128,1408]{1,0:T(8,128)(2,1)} %get-tuple-element.218), channel_id=1, source_target_pairs={{0,12},{1,13},{2,14},{3,15},{4,0},{5,1},{6,2},{7,3},{8,4},{9,5},{1... | collective-permute-start | bytes 1081352 | tf_op jit(solution)/shard_map/ppermute | solution.py:375
  151.7 290.2 %reduce-scatter.5.cloned.1.call-start = ((), (), s32[]{:S(2)}) async-start(), calls=%async_computation.7 | async-start | bytes 7208960 | tf_op jit(solution)/shard_map/reduce_scatter | solution.py:609
  174.3 47.6 %collective-permute-start.22 = (bf16[128,2048]{1,0:T(8,128)(2,1)S(1)}, bf16[128,2048]{1,0:T(8,128)(2,1)}, u32[]{:S(2)}, u32[]{:S(2)}) collective-permute-start(bf16[128,2048]{1,0:T(8,128)(2,1)S(1)} %bitcast_convert_fusion), channel_id=1, source_target_pairs={{0,8},{1,9},{2,10},{3,11},{4,12},{5,13},{6,14},{7,15},{8,0},{9,1},... | collective-permute-start | bytes 1572872 | tf_op jit(solution)/shard_map/ppermute | solution.py:375
  177.0 44.9 %collective-permute-start.21 = (bf16[128,2048]{1,0:T(8,128)(2,1)S(1)}, bf16[128,2048]{1,0:T(8,128)(2,1)}, u32[]{:S(2)}, u32[]{:S(2)}) collective-permute-start(bf16[128,2048]{1,0:T(8,128)(2,1)S(1)} %bitcast_convert_fusion), channel_id=1, source_target_pairs={{0,4},{1,5},{2,6},{3,7},{4,8},{5,9},{6,10},{7,11},{8,12},{9,13},{1... | collective-permute-start | bytes 1572872 | tf_op jit(solution)/shard_map/ppermute | solution.py:375
  189.5 34.7 %collective-permute-start.20 = (bf16[128,2048]{1,0:T(8,128)(2,1)S(1)}, bf16[128,2048]{1,0:T(8,128)(2,1)S(1)}, u32[]{:S(2)}, u32[]{:S(2)}) collective-permute-start(bf16[128,2048]{1,0:T(8,128)(2,1)S(1)} %get-tuple-element.199), channel_id=1, source_target_pairs={{0,3},{1,2},{2,1},{3,0},{4,7},{5,6},{6,5},{7,4},{8,11},{9,10},{10,... | collective-permute-start | bytes 1572872 | tf_op jit(solution)/shard_map/ppermute | solution.py:372
  189.6 37.1 %collective-permute-start.19 = (bf16[128,2048]{1,0:T(8,128)(2,1)S(1)}, bf16[128,2048]{1,0:T(8,128)(2,1)S(1)}, u32[]{:S(2)}, u32[]{:S(2)}) collective-permute-start(bf16[128,2048]{1,0:T(8,128)(2,1)S(1)} %get-tuple-element.200), channel_id=1, source_target_pairs={{0,2},{1,3},{2,0},{3,1},{4,6},{5,7},{6,4},{7,5},{8,10},{9,11},{10,... | collective-permute-start | bytes 1572872 | tf_op jit(solution)/shard_map/ppermute | solution.py:372
  192.7 36.6 %collective-permute-start.18 = (bf16[128,2048]{1,0:T(8,128)(2,1)S(1)}, bf16[128,2048]{1,0:T(8,128)(2,1)S(1)}, u32[]{:S(2)}, u32[]{:S(2)}) collective-permute-start(bf16[128,2048]{1,0:T(8,128)(2,1)S(1)} %get-tuple-element.198), channel_id=1, source_target_pairs={{0,1},{1,0},{2,3},{3,2},{4,5},{5,4},{6,7},{7,6},{8,9},{9,8},{10,11... | collective-permute-start | bytes 1572872 | tf_op jit(solution)/shard_map/ppermute | solution.py:372
  230.4 34.4 %collective-permute-start.24 = (bf16[128,2048]{1,0:T(8,128)(2,1)S(1)}, bf16[128,2048]{1,0:T(8,128)(2,1)S(1)}, u32[]{:S(2)}, u32[]{:S(2)}) collective-permute-start(bf16[128,2048]{1,0:T(8,128)(2,1)S(1)} %constant_dynamic-update-slice_fusion.12), channel_id=1, source_target_pairs={{0,4},{1,5},{2,6},{3,7},{4,8},{5,9},{6,10},{7,11},{8,12},{9,13},{1... | collective-permute-start | bytes 1572872 | tf_op jit(solution)/shard_map/ppermute | solution.py:375
  244.4 43.9 %collective-permute-start.25 = (bf16[128,2048]{1,0:T(8,128)(2,1)S(1)}, bf16[128,2048]{1,0:T(8,128)(2,1)S(1)}, u32[]{:S(2)}, u32[]{:S(2)}) collective-permute-start(bf16[128,2048]{1,0:T(8,128)(2,1)S(1)} %constant_dynamic-update-slice_fusion.12), channel_id=1, source_target_pairs={{0,8},{1,9},{2,10},{3,11},{4,12},{5,13},{6,14},{7,15},{8,0},{9,1},... | collective-permute-start | bytes 1572872 | tf_op jit(solution)/shard_map/ppermute | solution.py:375
  253.7 34.6 %collective-permute-start.26 = (bf16[128,2048]{1,0:T(8,128)(2,1)S(1)}, bf16[128,2048]{1,0:T(8,128)(2,1)S(1)}, u32[]{:S(2)}, u32[]{:S(2)}) collective-permute-start(bf16[128,2048]{1,0:T(8,128)(2,1)S(1)} %constant_dynamic-update-slice_fusion.12), channel_id=1, source_target_pairs={{0,12},{1,13},{2,14},{3,15},{4,0},{5,1},{6,2},{7,3},{8,4},{9,5},{1... | collective-permute-start | bytes 1572872 | tf_op jit(solution)/shard_map/ppermute | solution.py:375
  343.9 150.4 %reduce-scatter.7.cloned.1.call-start = ((), (), s32[]{:S(2)}) async-start(), calls=%async_computation.8 | async-start | bytes 1310720 | tf_op jit(solution)/shard_map/reduce_scatter | solution.py:628
  346.6 36.8 %collective-permute-start.30 = (bf16[128,2048]{1,0:T(8,128)(2,1)}, bf16[128,2048]{1,0:T(8,128)(2,1)}, u32[]{:S(2)}, u32[]{:S(2)}) collective-permute-start(bf16[128,2048]{1,0:T(8,128)(2,1)} %get-tuple-element.196), channel_id=1, source_target_pairs={{0,8},{1,9},{2,10},{3,11},{4,12},{5,13},{6,14},{7,15},{8,0},{9,1},... | collective-permute-start | bytes 1572872 | tf_op jit(solution)/shard_map/ppermute | solution.py:375
  347.1 36.2 %collective-permute-start.31 = (bf16[128,2048]{1,0:T(8,128)(2,1)}, bf16[128,2048]{1,0:T(8,128)(2,1)}, u32[]{:S(2)}, u32[]{:S(2)}) collective-permute-start(bf16[128,2048]{1,0:T(8,128)(2,1)} %get-tuple-element.195), channel_id=1, source_target_pairs={{0,4},{1,5},{2,6},{3,7},{4,8},{5,9},{6,10},{7,11},{8,12},{9,13},{1... | collective-permute-start | bytes 1572872 | tf_op jit(solution)/shard_map/ppermute | solution.py:375
  389.3 35.4 %collective-permute-start.35 = (bf16[128,2048]{1,0:T(8,128)(2,1)S(1)}, bf16[128,2048]{1,0:T(8,128)(2,1)}, u32[]{:S(2)}, u32[]{:S(2)}) collective-permute-start(bf16[128,2048]{1,0:T(8,128)(2,1)S(1)} %get-tuple-element.190), channel_id=1, source_target_pairs={{0,8},{1,9},{2,10},{3,11},{4,12},{5,13},{6,14},{7,15},{8,0},{9,1},... | collective-permute-start | bytes 1572872 | tf_op jit(solution)/shard_map/ppermute | solution.py:375
  441.9 89.2 %reduce-scatter.9.cloned.1.call-start = ((), (), s32[]{:S(2)}) async-start(), calls=%async_computation.9 | async-start | bytes 3604480 | tf_op jit(solution)/shard_map/reduce_scatter | solution.py:610
  442.5 136.5 %reduce-scatter.11.cloned.1.call-start = ((), (), s32[]{:S(2)}) async-start(), calls=%async_computation.10 | async-start | bytes 1638400 | tf_op jit(solution)/shard_map/reduce_scatter | solution.py:679
  474.5 28.2 %collective-permute-start.52 = (bf16[512,2048]{1,0:T(8,128)(2,1)}, bf16[512,2048]{1,0:T(8,128)(2,1)}, u32[]{:S(2)}, u32[]{:S(2)}) collective-permute-start(bf16[512,2048]{1,0:T(8,128)(2,1)} %copy-done.14), channel_id=1, source_target_pairs={{0,16},{16,0},{1,17},{17,1},{2,18},{18,2},{3,19},{19,3},{4,20},{20... | collective-permute-start | bytes 6291464 | tf_op jit(solution)/shard_map/ppermute | solution.py:378
  491.2 24.7 %collective-permute-start.50 = (bf16[128,1408]{1,0:T(8,128)(2,1)}, bf16[128,1408]{1,0:T(8,128)(2,1)}, u32[]{:S(2)}, u32[]{:S(2)}) collective-permute-start(bf16[128,1408]{1,0:T(8,128)(2,1)} %get-tuple-element.215), channel_id=1, source_target_pairs={{0,8},{1,9},{2,10},{3,11},{4,12},{5,13},{6,14},{7,15},{8,0},{9,1},... | collective-permute-start | bytes 1081352 | tf_op jit(solution)/shard_map/ppermute | solution.py:375
  491.2 39.9 %collective-permute-start.51 = (bf16[128,1408]{1,0:T(8,128)(2,1)}, bf16[128,1408]{1,0:T(8,128)(2,1)}, u32[]{:S(2)}, u32[]{:S(2)}) collective-permute-start(bf16[128,1408]{1,0:T(8,128)(2,1)} %get-tuple-element.214), channel_id=1, source_target_pairs={{0,12},{1,13},{2,14},{3,15},{4,0},{5,1},{6,2},{7,3},{8,4},{9,5},{1... | collective-permute-start | bytes 1081352 | tf_op jit(solution)/shard_map/ppermute | solution.py:375
  502.7 39.0 %collective-permute-start.48 = (bf16[128,2048]{1,0:T(8,128)(2,1)}, bf16[128,2048]{1,0:T(8,128)(2,1)S(1)}, u32[]{:S(2)}, u32[]{:S(2)}) collective-permute-start(bf16[128,2048]{1,0:T(8,128)(2,1)} %get-tuple-element.186), channel_id=1, source_target_pairs={{0,3},{1,2},{2,1},{3,0},{4,7},{5,6},{6,5},{7,4},{8,11},{9,10},{10,... | collective-permute-start | bytes 1572872 | tf_op jit(solution)/shard_map/ppermute | solution.py:372
  504.0 38.3 %collective-permute-start.47 = (bf16[128,2048]{1,0:T(8,128)(2,1)}, bf16[128,2048]{1,0:T(8,128)(2,1)S(1)}, u32[]{:S(2)}, u32[]{:S(2)}) collective-permute-start(bf16[128,2048]{1,0:T(8,128)(2,1)} %get-tuple-element.187), channel_id=1, source_target_pairs={{0,2},{1,3},{2,0},{3,1},{4,6},{5,7},{6,4},{7,5},{8,10},{9,11},{10,... | collective-permute-start | bytes 1572872 | tf_op jit(solution)/shard_map/ppermute | solution.py:372
  509.4 34.7 %collective-permute-start.46 = (bf16[128,2048]{1,0:T(8,128)(2,1)}, bf16[128,2048]{1,0:T(8,128)(2,1)}, u32[]{:S(2)}, u32[]{:S(2)}) collective-permute-start(bf16[128,2048]{1,0:T(8,128)(2,1)} %get-tuple-element.185), channel_id=1, source_target_pairs={{0,1},{1,0},{2,3},{3,2},{4,5},{5,4},{6,7},{7,6},{8,9},{9,8},{10,11... | collective-permute-start | bytes 1572872 | tf_op jit(solution)/shard_map/ppermute | solution.py:372
  541.7 49.4 %collective-permute-start.58 = (bf16[128,1024]{1,0:T(8,128)(2,1)}, bf16[128,1024]{1,0:T(8,128)(2,1)}, u32[]{:S(2)}, u32[]{:S(2)}) collective-permute-start(bf16[128,1024]{1,0:T(8,128)(2,1)} %collective-permute-done.57), channel_id=1, source_target_pairs={{0,16},{16,0},{1,17},{17,1},{2,18},{18,2},{3,19},{19,3},{4,20},{20... | collective-permute-start | bytes 786440 | tf_op jit(solution)/shard_map/ppermute | solution.py:378
  (95 other events, 1003.0 us)
Sparse Core Ops, SparseCore 0:
  10.5 56.9 all-gather.7
  74.7 71.1 all-gather.9
  151.9 96.9 all-gather.5
  344.0 79.9 reduce-scatter.4
  442.1 24.6 reduce-scatter.6
  470.2 60.8 reduce-scatter.8
  541.8 37.2 reduce-scatter.10

commit v11 on v8

--- a/solution.py
+++ b/solution.py
@@ -82,7 +82,7 @@
 def project(low, weights, cosine, sine):
     tokens, width = low.shape
     q_width = weights.shape[1] - PAIR
-    rows = block_rows(tokens)
+    rows = min(256, tokens)
     return pl.pallas_call(
         project_kernel,
         out_shape=(
@@ -126,7 +126,7 @@
 def feed(low, weights, grad_hidden):
     tokens, width = low.shape
     block = weights.shape[2]
-    rows = block_rows(tokens)
+    rows = min(256, tokens)
     narrow = pl.BlockSpec((rows, block), lambda i: (i, 0))
     wide = pl.BlockSpec((rows, width), lambda i: (i, 0))
     return pl.pallas_call(

time: 579 us -> 571 us (0.986)
  Pallas kernels: 52.7 us -> 43.8 us
    pallas_call x1, Pallas kernels: 27.8 us -> 19.7 us  [feed(): pl.pallas_call(feed_kernel, out_shape=(jax.ShapeDtypeStruct((tokens, bloc...]
  transfers between devices with their start and end apart: 68 -> 68, of which waited for: 25 -> 25; matrix products, arithmetic and copies ran while one was open for 22% -> 23% of each run, Pallas kernels for 9% -> 8%
where the time goes in v11:
time: 571 us; the launch traced here: 563 us
  waiting for transfers between devices  221 us (39%)
  starting transfers between devices  137 us (24%)
  local copies, waits for them, and re-layouts  66.9 us (12%)
  Pallas kernels  43.8 us (8%)
  other arithmetic  41 us (7%)
  matrix products  37 us (6%)
  between operations  16.1 us (3%)
    ppermute x27, waiting for transfers between devices, shift_z(): lax.ppermute(value, 'seq', [(s, (s + GROUP * t) % n_seq) for s in range(n...  155 us
    ppermute x27, starting transfers between devices, shift_z(): lax.ppermute(value, 'seq', [(s, (s + GROUP * t) % n_seq) for s in range(n...  48.9 us
    ppermute x13, starting transfers between devices, shift_dp(): return lax.ppermute(value, 'dp', [(c, (c + t) % n_dp) for c in range(n_dp)])  44.9 us
    ppermute x17, waiting for transfers between devices, xor_w(): return lax.ppermute(value, 'seq', [(s, s ^ j) for s in range(n_seq)])  37.1 us
    dot_general x13, matrix products, dot(): lax.dot_general(left, right, (contract, ((), ())), preferred_element_type...  37 us
    ppermute x17, starting transfers between devices, xor_w(): return lax.ppermute(value, 'seq', [(s, s ^ j) for s in range(n_seq)])  29.2 us
    unnamed x181, local copies, waits for them, and re-layouts  23.8 us
    reduce_scatter x1, waiting for transfers between devices, body(): lax.psum_scatter(qkv_sum, 'seq', axis_index_groups=across, tiled=True)  22 us
  transfers between devices with their start and end apart: 68, of which 25 were waited for; matrix products, arithmetic and copies ran while one was open for 23% of the time, Pallas kernels for 8%

profile of v11, /device:TPU:1, one launch (start us, length us, event | category | flops | bytes accessed | tf_op | source)
XLA Modules:
  0.0 563.0 jit_solution(3795249370768453772)
XLA Ops:
  15.0 4.1 all-to-all-start
  26.8 4.1 collective-permute-start.3
  35.8 24.0 %collective-permute-done.4 = bf16[512,320]{1,0:T(8,128)(2,1)S(1)} collective-permute-done((bf16[512,320]{1,0:T(8,128)(2,1)S(1)}, bf16[512,320]{1,0:T(8,128)(2,1)S(1)}, u32[]{:S(2)}, u32[]{:S(2)}) %collective-permute-start.4) | collective-permute-done | bytes 327712 | tf_op jit(solution)/shard_map/ppermute | solution.py:375
  61.9 5.2 collective-permute-start.13
  69.2 3.6 collective-permute-start.17
  82.2 14.3 %collective-permute-start.12 = (bf16[64,2048]{1,0:T(8,128)(2,1)S(1)}, bf16[64,2048]{1,0:T(8,128)(2,1)S(1)}, u32[]{:S(2)}, u32[]{:S(2)}) collective-permute-start(bf16[64,2048]{1,0:T(8,128)(2,1)S(1)} %slice.444), channel_id=1, source_target_pairs={{0,1},{1,0},{2,3},{3,2},{4,5},{5,4},{6,7},{7,6},{8,9},{9,8},{10,11... | collective-permute-start | bytes 786440 | tf_op jit(solution)/shard_map/ppermute | solution.py:372
  110.1 5.2 project.1
  115.3 12.0 %collective-permute-done.8 = bf16[128,1408]{1,0:T(8,128)(2,1)} collective-permute-done((bf16[128,1408]{1,0:T(8,128)(2,1)}, bf16[128,1408]{1,0:T(8,128)(2,1)}, u32[]{:S(2)}, u32[]{:S(2)}) %collective-permute-start.8) | collective-permute-done | bytes 360480 | tf_op jit(solution)/shard_map/ppermute | solution.py:375
  137.8 5.8 %collective-permute-done.15 = bf16[512,128]{1,0:T(8,128)(2,1)S(1)} collective-permute-done((bf16[512,128]{1,0:T(8,128)(2,1)S(1)}, bf16[512,128]{1,0:T(8,128)(2,1)S(1)}, u32[]{:S(2)}, u32[]{:S(2)}) %collective-permute-start.15) | collective-permute-done | bytes 131104 | tf_op jit(solution)/shard_map/ppermute | solution.py:375
  149.5 7.6 %attend.1 = (bf16[512,512]{1,0:T(8,128)(2,1)}, f32[4,8,1024]{2,1,0:T(8,128)}) custom-call(s32[1]{0:T(128)} %bitcast.1.seen_ref, bf16[512,512]{1,0:T(8,128)(2,1)} %get-tuple-element.77.q_ref, bf16[4,512,128]{2,1,0:T(8,128)(2,1)} %pad_maximum_fusion.9.kv_ref, s32[512,1]{1,0:T(8,128)} %copy.53.qpos_ref.kpos_ref, s32[1,512]{1,0:T(1,128)} %bitcast.159), custom_call_target="tpu_custom_call" | custom-call | tf_op jit(solution)/shard_map/attend/pallas_call | solution.py:255
  163.1 30.4 %collective-permute-done.22 = bf16[128,2048]{1,0:T(8,128)(2,1)} collective-permute-done((bf16[128,2048]{1,0:T(8,128)(2,1)S(1)}, bf16[128,2048]{1,0:T(8,128)(2,1)}, u32[]{:S(2)}, u32[]{:S(2)}) %collective-permute-start.22) | collective-permute-done | bytes 524320 | tf_op jit(solution)/shard_map/ppermute | solution.py:375
  207.5 10.2 %collective-permute-done.25 = bf16[128,2048]{1,0:T(8,128)(2,1)S(1)} collective-permute-done((bf16[128,2048]{1,0:T(8,128)(2,1)S(1)}, bf16[128,2048]{1,0:T(8,128)(2,1)S(1)}, u32[]{:S(2)}, u32[]{:S(2)}) %collective-permute-start.25) | collective-permute-done | bytes 524320 | tf_op jit(solution)/shard_map/ppermute | solution.py:375
  225.2 31.1 %collective-permute-start.28 = (bf16[512,2048]{1,0:T(8,128)(2,1)}, bf16[512,2048]{1,0:T(8,128)(2,1)}, u32[]{:S(2)}, u32[]{:S(2)}) collective-permute-start(bf16[512,2048]{1,0:T(8,128)(2,1)} %get-tuple-element.222.low_ref), channel_id=1, source_target_pairs={{0,16},{16,0},{1,17},{17,1},{2,18},{18,2},{3,19},{19,3},{4,20},{20... | collective-permute-start | bytes 6291464 | tf_op jit(solution)/shard_map/ppermute | solution.py:378
  256.3 19.7 %feed.1 = (bf16[512,1408]{1,0:T(8,128)(2,1)}, bf16[512,1408]{1,0:T(8,128)(2,1)}, bf16[512,1408]{1,0:T(8,128)(2,1)}, bf16[512,2048]{1,0:T(8,128)(2,1)}) custom-call(bf16[512,2048]{1,0:T(8,128)(2,1)} %get-tuple-element.222.low_ref, bf16[2,2048,1408]{2,1,0:T(8,128)(2,1)} %bitcast.133, f32[512,1408]{1,0:T(8,128)} %convolution_add_fusion.grad_hidden_ref), custom_call_target="tpu_custom_call" | custom-call | tf_op jit(solution)/shard_map/feed/pallas_call | solution.py:132
  285.3 8.6 %convolution_convert_fusion = bf16[2048,1408]{1,0:T(8,128)(2,1)} fusion(bf16[1024,2048]{1,0:T(8,128)(2,1)S(1)} %constant_dynamic-update-slice_fusion.32, bf16[512,1408]{1,0:T(8,128)(2,1)S(1)} %collective-permute-done.29, bf16[512,1408]{1,0:T(8,128)(2,1)S(1)} %get-tuple-element.163), kind=kOutput, calls=%fused_computation | convolution fusion | flops 5914230784 | bytes 12845056 | tf_op jit(solution)/shard_map/dot_general | solution.py:26
  293.9 7.1 %collective-permute-done.27 = bf16[128,2048]{1,0:T(8,128)(2,1)S(1)} collective-permute-done((bf16[128,2048]{1,0:T(8,128)(2,1)}, bf16[128,2048]{1,0:T(8,128)(2,1)S(1)}, u32[]{:S(2)}, u32[]{:S(2)}) %collective-permute-start.27) | collective-permute-done | bytes 524320 | tf_op jit(solution)/shard_map/ppermute | solution.py:375
  312.1 5.9 %convolution_convert_fusion.1 = bf16[1408,1024]{1,0:T(8,128)(2,1)} fusion(bf16[512,1408]{1,0:T(8,128)(2,1)} %collective-permute-done.32, bf16[512,1408]{1,0:T(8,128)(2,1)S(1)} %copy-done.50, bf16[512,1024]{1,0:T(8,128)(2,1)S(1)} %collective-permute-done.33, bf16[512,1024]{1,0:T(8,128)(2,1)S(1)} %get-tuple-element.173), kind=kOutput, calls=%fused_computation.1 | convolution fusion | flops 2964193280 | bytes 7864320 | tf_op jit(solution)/shard_map/dot_general | solution.py:26
  317.9 22.5 %collective-permute-done.30 = bf16[128,2048]{1,0:T(8,128)(2,1)} collective-permute-done((bf16[128,2048]{1,0:T(8,128)(2,1)}, bf16[128,2048]{1,0:T(8,128)(2,1)}, u32[]{:S(2)}, u32[]{:S(2)}) %collective-permute-start.30) | collective-permute-done | bytes 524320 | tf_op jit(solution)/shard_map/ppermute | solution.py:375
  348.2 9.5 %collective-permute-done.36 = bf16[128,2048]{1,0:T(8,128)(2,1)S(1)} collective-permute-done((bf16[128,2048]{1,0:T(8,128)(2,1)S(1)}, bf16[128,2048]{1,0:T(8,128)(2,1)S(1)}, u32[]{:S(2)}, u32[]{:S(2)}) %collective-permute-start.36) | collective-permute-done | bytes 524320 | tf_op jit(solution)/shard_map/ppermute | solution.py:372
  360.3 11.5 %collective-permute-done.38 = bf16[64,2048]{1,0:T(8,128)(2,1)S(1)} collective-permute-done((bf16[64,2048]{1,0:T(8,128)(2,1)S(1)}, bf16[64,2048]{1,0:T(8,128)(2,1)S(1)}, u32[]{:S(2)}, u32[]{:S(2)}) %collective-permute-start.38) | collective-permute-done | bytes 262176 | tf_op jit(solution)/shard_map/ppermute | solution.py:372
  372.6 9.3 %collective-permute-done.35 = bf16[128,2048]{1,0:T(8,128)(2,1)} collective-permute-done((bf16[128,2048]{1,0:T(8,128)(2,1)S(1)}, bf16[128,2048]{1,0:T(8,128)(2,1)}, u32[]{:S(2)}, u32[]{:S(2)}) %collective-permute-start.35) | collective-permute-done | bytes 524320 | tf_op jit(solution)/shard_map/ppermute | solution.py:375
  389.1 10.1 %collective-permute-done.40 = bf16[128,2048]{1,0:T(8,128)(2,1)S(1)} collective-permute-done((bf16[128,2048]{1,0:T(8,128)(2,1)}, bf16[128,2048]{1,0:T(8,128)(2,1)S(1)}, u32[]{:S(2)}, u32[]{:S(2)}) %collective-permute-start.40) | collective-permute-done | bytes 524320 | tf_op jit(solution)/shard_map/ppermute | solution.py:375
  400.7 4.0 collective-permute-done.52
  408.6 11.3 %attend_back.1 = (bf16[512,512]{1,0:T(8,128)(2,1)}, bf16[4,512,128]{2,1,0:T(8,128)(2,1)}) custom-call(s32[1]{0:T(128)} %bitcast.1.seen_ref, bf16[512,512]{1,0:T(8,128)(2,1)} %get-tuple-element.77.q_ref, bf16[512,512]{1,0:T(8,128)(2,1)} %bitcast.151, bf16[512,512]{1,0:T(8,128)(2,1)} %get-tuple-element.80.o_ref, ...), custom_call_target="tpu_custom_call" | custom-call | tf_op jit(solution)/shard_map/attend_back/pallas_call | solution.py:285
  421.0 4.4 collective-permute-start.45
  425.4 15.1 %collective-permute-start.44 = (bf16[512,128]{1,0:T(8,128)(2,1)S(1)}, bf16[512,128]{1,0:T(8,128)(2,1)S(1)}, u32[]{:S(2)}, u32[]{:S(2)}) collective-permute-start(bf16[512,128]{1,0:T(8,128)(2,1)S(1)} %get-tuple-element.220), channel_id=1, source_target_pairs={{0,8},{1,9},{2,10},{3,11},{4,12},{5,13},{6,14},{7,15},{8,0},{9,1},... | collective-permute-start | bytes 393224 | tf_op jit(solution)/shard_map/ppermute | solution.py:375
  443.8 6.0 %collective-permute-done.44 = bf16[512,128]{1,0:T(8,128)(2,1)S(1)} collective-permute-done((bf16[512,128]{1,0:T(8,128)(2,1)S(1)}, bf16[512,128]{1,0:T(8,128)(2,1)S(1)}, u32[]{:S(2)}, u32[]{:S(2)}) %collective-permute-start.44) | collective-permute-done | bytes 131104 | tf_op jit(solution)/shard_map/ppermute | solution.py:375
  471.1 9.7 %collective-permute-done.50 = bf16[128,1408]{1,0:T(8,128)(2,1)} collective-permute-done((bf16[128,1408]{1,0:T(8,128)(2,1)}, bf16[128,1408]{1,0:T(8,128)(2,1)}, u32[]{:S(2)}, u32[]{:S(2)}) %collective-permute-start.50) | collective-permute-done | bytes 360480 | tf_op jit(solution)/shard_map/ppermute | solution.py:375
  491.0 10.3 %collective-permute-done.46 = bf16[128,2048]{1,0:T(8,128)(2,1)S(1)} collective-permute-done((bf16[128,2048]{1,0:T(8,128)(2,1)}, bf16[128,2048]{1,0:T(8,128)(2,1)S(1)}, u32[]{:S(2)}, u32[]{:S(2)}) %collective-permute-start.46) | collective-permute-done | bytes 524320 | tf_op jit(solution)/shard_map/ppermute | solution.py:372
  508.9 22.0 %reduce-scatter.11.cloned.1.call-done = bf16[512,320]{0,1:T(8,128)(2,1)} async-done(((bf16[2048,320]{0,1:T(8,128)(2,1)}), bf16[512,320]{0,1:T(8,128)(2,1)}) %reduce-scatter.11.cloned.1.call-update) | async-done | bytes 327696 | tf_op jit(solution)/shard_map/reduce_scatter | solution.py:680
  532.6 4.1 all-to-all-start.1
  543.6 6.3 %convert_multiply_fusion = (f32[128,5632]{1,0:T(8,128)}, f32[128]{0:T(128)}, f32[128,5632]{1,0:T(8,128)}) fusion(f32[128]{0:T(128)S(1)} %convert_element_type.204, bf16[128,1408]{1,0:T(8,128)(2,1)} %get-tuple-element.191, bf16[128,1408]{1,0:T(8,128)(2,1)} %get-tuple-element.192, bf16[128,1408]{1,0:T(8,128)(2,1)} %get-tuple-element.193, ...), kind=kLoop, calls=%fused_computation.2 | loop fusion | flops 17301376 | bytes 11535360 | tf_op jit(solution)/shard_map/mul | solution.py:710
  (417 shorter events, 191.9 us)
Async XLA Ops:
  7.2 89.2 %all-gather.8.cloned.1.call-start = ((), (), s32[]{:S(2)}) async-start(), calls=%async_computation.11 | async-start | bytes 6488064 | tf_op jit(solution)/shard_map/all_gather | solution.py:484
  19.1 138.1 %all-gather.10.cloned.1.call-start = ((), (), s32[]{:S(2)}) async-start(), calls=%async_computation.12 | async-start | bytes 2359296 | tf_op jit(solution)/shard_map/all_gather | solution.py:489
  30.9 28.9 %collective-permute-start.4 = (bf16[512,320]{1,0:T(8,128)(2,1)S(1)}, bf16[512,320]{1,0:T(8,128)(2,1)S(1)}, u32[]{:S(2)}, u32[]{:S(2)}) collective-permute-start(bf16[512,320]{1,0:T(8,128)(2,1)S(1)} %bitcast.138), channel_id=1, source_target_pairs={{0,8},{1,9},{2,10},{3,11},{4,12},{5,13},{6,14},{7,15},{8,0},{9,1},... | collective-permute-start | bytes 983048 | tf_op jit(solution)/shard_map/ppermute | solution.py:375
  30.9 28.9 %collective-permute-start.5 = (bf16[512,320]{1,0:T(8,128)(2,1)S(1)}, bf16[512,320]{1,0:T(8,128)(2,1)S(1)}, u32[]{:S(2)}, u32[]{:S(2)}) collective-permute-start(bf16[512,320]{1,0:T(8,128)(2,1)S(1)} %bitcast.139), channel_id=1, source_target_pairs={{0,4},{1,5},{2,6},{3,7},{4,8},{5,9},{6,10},{7,11},{8,12},{9,13},{1... | collective-permute-start | bytes 983048 | tf_op jit(solution)/shard_map/ppermute | solution.py:375
  32.4 43.5 %collective-permute-start.9 = (bf16[128,2048]{1,0:T(8,128)(2,1)S(1)}, bf16[128,2048]{1,0:T(8,128)(2,1)}, u32[]{:S(2)}, u32[]{:S(2)}) collective-permute-start(bf16[128,2048]{1,0:T(8,128)(2,1)S(1)} %fusion.22), channel_id=1, source_target_pairs={{0,1},{1,0},{2,3},{3,2},{4,5},{5,4},{6,7},{7,6},{8,9},{9,8},{10,11... | collective-permute-start | bytes 1572872 | tf_op jit(solution)/shard_map/ppermute | solution.py:372
  33.3 47.2 %collective-permute-start.10 = (bf16[128,2048]{1,0:T(8,128)(2,1)S(1)}, bf16[128,2048]{1,0:T(8,128)(2,1)}, u32[]{:S(2)}, u32[]{:S(2)}) collective-permute-start(bf16[128,2048]{1,0:T(8,128)(2,1)S(1)} %fusion.22), channel_id=1, source_target_pairs={{0,2},{1,3},{2,0},{3,1},{4,6},{5,7},{6,4},{7,5},{8,10},{9,11},{10,... | collective-permute-start | bytes 1572872 | tf_op jit(solution)/shard_map/ppermute | solution.py:372
  61.9 41.3 %collective-permute-start.13 = (bf16[2048,320]{0,1:T(8,128)(2,1)}, bf16[2048,320]{0,1:T(8,128)(2,1)}, u32[]{:S(2)}, u32[]{:S(2)}) collective-permute-start(bf16[2048,320]{0,1:T(8,128)(2,1)} %copy.48), channel_id=1, source_target_pairs={{0,16},{16,0},{1,17},{17,1},{2,18},{18,2},{3,19},{19,3},{4,20},{20... | collective-permute-start | bytes 3932168 | tf_op jit(solution)/shard_map/ppermute | solution.py:378
  75.2 40.1 %collective-permute-start.6 = (bf16[128,1408]{1,0:T(8,128)(2,1)}, bf16[128,1408]{1,0:T(8,128)(2,1)}, u32[]{:S(2)}, u32[]{:S(2)}) collective-permute-start(bf16[128,1408]{1,0:T(8,128)(2,1)} %get-tuple-element.200), channel_id=1, source_target_pairs={{0,4},{1,5},{2,6},{3,7},{4,8},{5,9},{6,10},{7,11},{8,12},{9,13},{1... | collective-permute-start | bytes 1081352 | tf_op jit(solution)/shard_map/ppermute | solution.py:375
  75.9 39.4 %collective-permute-start.7 = (bf16[128,1408]{1,0:T(8,128)(2,1)}, bf16[128,1408]{1,0:T(8,128)(2,1)}, u32[]{:S(2)}, u32[]{:S(2)}) collective-permute-start(bf16[128,1408]{1,0:T(8,128)(2,1)} %get-tuple-element.199), channel_id=1, source_target_pairs={{0,8},{1,9},{2,10},{3,11},{4,12},{5,13},{6,14},{7,15},{8,0},{9,1},... | collective-permute-start | bytes 1081352 | tf_op jit(solution)/shard_map/ppermute | solution.py:375
  96.5 159.8 %all-gather.6.cloned.1.call-start = ((), (), s32[]{:S(2)}) async-start(), calls=%async_computation.6 | async-start | bytes 12976128 | tf_op jit(solution)/shard_map/all_gather | solution.py:525
  100.8 26.5 %collective-permute-start.8 = (bf16[128,1408]{1,0:T(8,128)(2,1)}, bf16[128,1408]{1,0:T(8,128)(2,1)}, u32[]{:S(2)}, u32[]{:S(2)}) collective-permute-start(bf16[128,1408]{1,0:T(8,128)(2,1)} %get-tuple-element.198), channel_id=1, source_target_pairs={{0,12},{1,13},{2,14},{3,15},{4,0},{5,1},{6,2},{7,3},{8,4},{9,5},{1... | collective-permute-start | bytes 1081352 | tf_op jit(solution)/shard_map/ppermute | solution.py:375
  131.8 267.3 %reduce-scatter.5.cloned.1.call-start = ((), (), s32[]{:S(2)}) async-start(), calls=%async_computation.7 | async-start | bytes 7208960 | tf_op jit(solution)/shard_map/reduce_scatter | solution.py:610
  145.9 47.5 %collective-permute-start.22 = (bf16[128,2048]{1,0:T(8,128)(2,1)S(1)}, bf16[128,2048]{1,0:T(8,128)(2,1)}, u32[]{:S(2)}, u32[]{:S(2)}) collective-permute-start(bf16[128,2048]{1,0:T(8,128)(2,1)S(1)} %bitcast_convert_fusion), channel_id=1, source_target_pairs={{0,8},{1,9},{2,10},{3,11},{4,12},{5,13},{6,14},{7,15},{8,0},{9,1},... | collective-permute-start | bytes 1572872 | tf_op jit(solution)/shard_map/ppermute | solution.py:375
  147.8 45.6 %collective-permute-start.21 = (bf16[128,2048]{1,0:T(8,128)(2,1)S(1)}, bf16[128,2048]{1,0:T(8,128)(2,1)}, u32[]{:S(2)}, u32[]{:S(2)}) collective-permute-start(bf16[128,2048]{1,0:T(8,128)(2,1)S(1)} %bitcast_convert_fusion), channel_id=1, source_target_pairs={{0,4},{1,5},{2,6},{3,7},{4,8},{5,9},{6,10},{7,11},{8,12},{9,13},{1... | collective-permute-start | bytes 1572872 | tf_op jit(solution)/shard_map/ppermute | solution.py:375
  160.3 35.9 %collective-permute-start.20 = (bf16[128,2048]{1,0:T(8,128)(2,1)S(1)}, bf16[128,2048]{1,0:T(8,128)(2,1)S(1)}, u32[]{:S(2)}, u32[]{:S(2)}) collective-permute-start(bf16[128,2048]{1,0:T(8,128)(2,1)S(1)} %get-tuple-element.179), channel_id=1, source_target_pairs={{0,3},{1,2},{2,1},{3,0},{4,7},{5,6},{6,5},{7,4},{8,11},{9,10},{10,... | collective-permute-start | bytes 1572872 | tf_op jit(solution)/shard_map/ppermute | solution.py:372
  160.6 35.7 %collective-permute-start.19 = (bf16[128,2048]{1,0:T(8,128)(2,1)S(1)}, bf16[128,2048]{1,0:T(8,128)(2,1)S(1)}, u32[]{:S(2)}, u32[]{:S(2)}) collective-permute-start(bf16[128,2048]{1,0:T(8,128)(2,1)S(1)} %get-tuple-element.180), channel_id=1, source_target_pairs={{0,2},{1,3},{2,0},{3,1},{4,6},{5,7},{6,4},{7,5},{8,10},{9,11},{10,... | collective-permute-start | bytes 1572872 | tf_op jit(solution)/shard_map/ppermute | solution.py:372
  161.4 34.9 %collective-permute-start.18 = (bf16[128,2048]{1,0:T(8,128)(2,1)S(1)}, bf16[128,2048]{1,0:T(8,128)(2,1)S(1)}, u32[]{:S(2)}, u32[]{:S(2)}) collective-permute-start(bf16[128,2048]{1,0:T(8,128)(2,1)S(1)} %get-tuple-element.178), channel_id=1, source_target_pairs={{0,1},{1,0},{2,3},{3,2},{4,5},{5,4},{6,7},{7,6},{8,9},{9,8},{10,11... | collective-permute-start | bytes 1572872 | tf_op jit(solution)/shard_map/ppermute | solution.py:372
  198.5 21.9 %collective-permute-start.26 = (bf16[128,2048]{1,0:T(8,128)(2,1)S(1)}, bf16[128,2048]{1,0:T(8,128)(2,1)S(1)}, u32[]{:S(2)}, u32[]{:S(2)}) collective-permute-start(bf16[128,2048]{1,0:T(8,128)(2,1)S(1)} %constant_dynamic-update-slice_fusion.12), channel_id=1, source_target_pairs={{0,12},{1,13},{2,14},{3,15},{4,0},{5,1},{6,2},{7,3},{8,4},{9,5},{1... | collective-permute-start | bytes 1572872 | tf_op jit(solution)/shard_map/ppermute | solution.py:375
  225.2 53.1 %collective-permute-start.28 = (bf16[512,2048]{1,0:T(8,128)(2,1)}, bf16[512,2048]{1,0:T(8,128)(2,1)}, u32[]{:S(2)}, u32[]{:S(2)}) collective-permute-start(bf16[512,2048]{1,0:T(8,128)(2,1)} %get-tuple-element.222.low_ref), channel_id=1, source_target_pairs={{0,16},{16,0},{1,17},{17,1},{2,18},{18,2},{3,19},{19,3},{4,20},{20... | collective-permute-start | bytes 6291464 | tf_op jit(solution)/shard_map/ppermute | solution.py:378
  301.0 156.5 %reduce-scatter.7.cloned.1.call-start = ((), (), s32[]{:S(2)}) async-start(), calls=%async_computation.8 | async-start | bytes 1310720 | tf_op jit(solution)/shard_map/reduce_scatter | solution.py:629
  303.6 36.8 %collective-permute-start.30 = (bf16[128,2048]{1,0:T(8,128)(2,1)}, bf16[128,2048]{1,0:T(8,128)(2,1)}, u32[]{:S(2)}, u32[]{:S(2)}) collective-permute-start(bf16[128,2048]{1,0:T(8,128)(2,1)} %get-tuple-element.176), channel_id=1, source_target_pairs={{0,8},{1,9},{2,10},{3,11},{4,12},{5,13},{6,14},{7,15},{8,0},{9,1},... | collective-permute-start | bytes 1572872 | tf_op jit(solution)/shard_map/ppermute | solution.py:375
  304.2 36.2 %collective-permute-start.31 = (bf16[128,2048]{1,0:T(8,128)(2,1)}, bf16[128,2048]{1,0:T(8,128)(2,1)}, u32[]{:S(2)}, u32[]{:S(2)}) collective-permute-start(bf16[128,2048]{1,0:T(8,128)(2,1)} %get-tuple-element.175), channel_id=1, source_target_pairs={{0,4},{1,5},{2,6},{3,7},{4,8},{5,9},{6,10},{7,11},{8,12},{9,13},{1... | collective-permute-start | bytes 1572872 | tf_op jit(solution)/shard_map/ppermute | solution.py:375
  347.2 24.6 %collective-permute-start.34 = (bf16[128,2048]{1,0:T(8,128)(2,1)S(1)}, bf16[128,2048]{1,0:T(8,128)(2,1)S(1)}, u32[]{:S(2)}, u32[]{:S(2)}) collective-permute-start(bf16[128,2048]{1,0:T(8,128)(2,1)S(1)} %get-tuple-element.172), channel_id=1, source_target_pairs={{0,12},{1,13},{2,14},{3,15},{4,0},{5,1},{6,2},{7,3},{8,4},{9,5},{1... | collective-permute-start | bytes 1572872 | tf_op jit(solution)/shard_map/ppermute | solution.py:375
  347.2 34.8 %collective-permute-start.35 = (bf16[128,2048]{1,0:T(8,128)(2,1)S(1)}, bf16[128,2048]{1,0:T(8,128)(2,1)}, u32[]{:S(2)}, u32[]{:S(2)}) collective-permute-start(bf16[128,2048]{1,0:T(8,128)(2,1)S(1)} %get-tuple-element.170), channel_id=1, source_target_pairs={{0,8},{1,9},{2,10},{3,11},{4,12},{5,13},{6,14},{7,15},{8,0},{9,1},... | collective-permute-start | bytes 1572872 | tf_op jit(solution)/shard_map/ppermute | solution.py:375
  399.2 83.1 %reduce-scatter.9.cloned.1.call-start = ((), (), s32[]{:S(2)}) async-start(), calls=%async_computation.9 | async-start | bytes 3604480 | tf_op jit(solution)/shard_map/reduce_scatter | solution.py:611
  400.6 130.2 %reduce-scatter.11.cloned.1.call-start = ((), (), s32[]{:S(2)}) async-start(), calls=%async_computation.10 | async-start | bytes 1638400 | tf_op jit(solution)/shard_map/reduce_scatter | solution.py:680
  421.0 22.8 %collective-permute-start.45 = (bf16[512,128]{1,0:T(8,128)(2,1)S(1)}, bf16[512,128]{1,0:T(8,128)(2,1)S(1)}, u32[]{:S(2)}, u32[]{:S(2)}) collective-permute-start(bf16[512,128]{1,0:T(8,128)(2,1)S(1)} %get-tuple-element.219), channel_id=1, source_target_pairs={{0,4},{1,5},{2,6},{3,7},{4,8},{5,9},{6,10},{7,11},{8,12},{9,13},{1... | collective-permute-start | bytes 393224 | tf_op jit(solution)/shard_map/ppermute | solution.py:375
  425.4 24.4 %collective-permute-start.44 = (bf16[512,128]{1,0:T(8,128)(2,1)S(1)}, bf16[512,128]{1,0:T(8,128)(2,1)S(1)}, u32[]{:S(2)}, u32[]{:S(2)}) collective-permute-start(bf16[512,128]{1,0:T(8,128)(2,1)S(1)} %get-tuple-element.220), channel_id=1, source_target_pairs={{0,8},{1,9},{2,10},{3,11},{4,12},{5,13},{6,14},{7,15},{8,0},{9,1},... | collective-permute-start | bytes 393224 | tf_op jit(solution)/shard_map/ppermute | solution.py:375
  455.0 25.8 %collective-permute-start.50 = (bf16[128,1408]{1,0:T(8,128)(2,1)}, bf16[128,1408]{1,0:T(8,128)(2,1)}, u32[]{:S(2)}, u32[]{:S(2)}) collective-permute-start(bf16[128,1408]{1,0:T(8,128)(2,1)} %get-tuple-element.195), channel_id=1, source_target_pairs={{0,8},{1,9},{2,10},{3,11},{4,12},{5,13},{6,14},{7,15},{8,0},{9,1},... | collective-permute-start | bytes 1081352 | tf_op jit(solution)/shard_map/ppermute | solution.py:375
  455.0 27.3 %collective-permute-start.51 = (bf16[128,1408]{1,0:T(8,128)(2,1)}, bf16[128,1408]{1,0:T(8,128)(2,1)}, u32[]{:S(2)}, u32[]{:S(2)}) collective-permute-start(bf16[128,1408]{1,0:T(8,128)(2,1)} %get-tuple-element.194), channel_id=1, source_target_pairs={{0,12},{1,13},{2,14},{3,15},{4,0},{5,1},{6,2},{7,3},{8,4},{9,5},{1... | collective-permute-start | bytes 1081352 | tf_op jit(solution)/shard_map/ppermute | solution.py:375
  464.0 23.5 %collective-permute-start.48 = (bf16[128,2048]{1,0:T(8,128)(2,1)}, bf16[128,2048]{1,0:T(8,128)(2,1)S(1)}, u32[]{:S(2)}, u32[]{:S(2)}) collective-permute-start(bf16[128,2048]{1,0:T(8,128)(2,1)} %get-tuple-element.166), channel_id=1, source_target_pairs={{0,3},{1,2},{2,1},{3,0},{4,7},{5,6},{6,5},{7,4},{8,11},{9,10},{10,... | collective-permute-start | bytes 1572872 | tf_op jit(solution)/shard_map/ppermute | solution.py:372
  469.3 21.7 %collective-permute-start.47 = (bf16[128,2048]{1,0:T(8,128)(2,1)}, bf16[128,2048]{1,0:T(8,128)(2,1)S(1)}, u32[]{:S(2)}, u32[]{:S(2)}) collective-permute-start(bf16[128,2048]{1,0:T(8,128)(2,1)} %get-tuple-element.167), channel_id=1, source_target_pairs={{0,2},{1,3},{2,0},{3,1},{4,6},{5,7},{6,4},{7,5},{8,10},{9,11},{10,... | collective-permute-start | bytes 1572872 | tf_op jit(solution)/shard_map/ppermute | solution.py:372
  (92 other events, 894.5 us)
Sparse Core Ops, SparseCore 0:
  10.5 54.0 all-gather.7
  96.6 40.2 all-gather.9
  138.8 89.2 all-gather.5
  301.1 81.7 reduce-scatter.4
  399.3 25.2 reduce-scatter.6
  428.1 40.4 reduce-scatter.8
  482.5 48.2 reduce-scatter.10

commit v12 on v10

--- a/solution.py
+++ b/solution.py
@@ -461,11 +461,12 @@
         low_one, qkv_part, plane_pos = tie(normed_one.astype(bf16), qkv_part, plane_pos)
 
         ring = [qkv_part] + [shift_z(qkv_part, -t) for t in range(1, planes)]
-        low_one, *ring = tie(gather_w(low_one), *ring)
         qkv_ring = jnp.concatenate(ring + ring[: planes - 1], axis=0)
         qkv_mine = lax.dynamic_slice_in_dim(
             qkv_ring, ((planes - p) % planes) * GROUP * shard, width, 0
         )
+        low_one = gather_w(low_one)
+
         piece = shard // halves
         gate_up = jnp.where(c // halves == 0, scaled(w_gate, gain_two), scaled(w_up, gain_two))
         out_part, gate_up, qkv_mine = tie(
@@ -626,6 +627,11 @@
         mixed_sent = mixed_sent[:early] + list(late)
         gate_up_sum, out_part_sum = tie(gate_up_sum, out_part_sum)
         out_sum = lax.psum_scatter(out_part_sum, "seq", axis_index_groups=across, tiled=True)
+        grad_o_seq, gate_up_late = tie(grad_o_seq, gate_up_sum)
+        gate_up_sent = []
+        for t in range(planes):
+            block = lax.dynamic_index_in_dim(gate_up_late, (p + t) % planes, 0, keepdims=False)
+            gate_up_sent.append(shift_z(block, t) if t else block)
         pieces = [
             attend_back(
                 seen, q_seq[i], grad_o_seq[i], o_seq[i], kv_seq[i], lse_seq[i], order,
@@ -639,12 +645,8 @@
         )
         query_pre = from_seq(grad_q, 0)
         grad_kv = from_seq(jnp.stack([one[1] for one in pieces]), 1)
+        *gate_up_sent, grad_kv = tie(*gate_up_sent, grad_kv)
         grad_kv = scatter_z([grad_kv[t] for t in range(planes)])
-        grad_kv, gate_up_late = tie(grad_kv, gate_up_sum)
-        gate_up_sent = []
-        for t in range(planes):
-            block = lax.dynamic_index_in_dim(gate_up_late, (p + t) % planes, 0, keepdims=False)
-            gate_up_sent.append(shift_z(block, t) if t else block)
         query_pre, out_sum = tie(query_pre, out_sum)
         key_pre = unrotate_keys(
             grad_kv[:, :HEAD_DIM], cosine[:, :HEAD_DIM], sine[:, :HEAD_DIM]
@@ -670,7 +672,7 @@
             exchange_dp(jnp.concatenate(pre, axis=1), c, 1),
             ((0,), (0,)),
         ).astype(bf16)
-        *gate_up_sent, down_sum, qkv_sum = tie(*gate_up_sent, down_sum, qkv_sum)
+        down_sum, qkv_sum = tie(down_sum, qkv_sum)
         out_sum = lax.ppermute(
             out_sum, "seq", [(GROUP * (i % planes) + i // planes, i) for i in range(n_seq)]
         )

time: 614 us -> 579 us (0.943)
  starting transfers between devices: 157 us -> 128 us
    ppermute x27, starting transfers between devices: 114 us -> 38.4 us  [shift_z(): lax.ppermute(value, 'seq', [(s, (s + GROUP * t) % n_seq) for s in range(n...]
    ppermute x13, starting transfers between devices: 15.7 us -> 48.2 us  [shift_dp(): return lax.ppermute(value, 'dp', [(c, (c + t) % n_dp) for c in range(n_dp)])]
    ppermute x17, starting transfers between devices: 15.1 us -> 28.8 us  [xor_w(): return lax.ppermute(value, 'seq', [(s, s ^ j) for s in range(n_seq)])]
    reduce_scatter x1, waiting for transfers between devices: 20.5 us -> 11.1 us  [body(): lax.psum_scatter(qkv_sum, 'seq', axis_index_groups=across, tiled=True)]
    unnamed x186 -> x197, local copies, waits for them, and re-layouts: 20.9 us -> 25 us
  transfers between devices with their start and end apart: 68 -> 68, of which waited for: 28 -> 27; matrix products, arithmetic and copies ran while one was open for 22% -> 23% of each run, Pallas kernels for 7% -> 8%
where the time goes in v12:
time: 579 us; the launch traced here: 571 us
  waiting for transfers between devices  236 us (41%)
  starting transfers between devices  128 us (22%)
  local copies, waits for them, and re-layouts  66.3 us (11%)
  Pallas kernels  43.7 us (8%)
  other arithmetic  42.1 us (7%)
  matrix products  38.9 us (7%)
  between operations  15.9 us (3%)
    ppermute x27, waiting for transfers between devices, shift_z(): lax.ppermute(value, 'seq', [(s, (s + GROUP * t) % n_seq) for s in range(n...  159 us
    ppermute x13, starting transfers between devices, shift_dp(): return lax.ppermute(value, 'dp', [(c, (c + t) % n_dp) for c in range(n_dp)])  48.2 us
    ppermute x17, waiting for transfers between devices, xor_w(): return lax.ppermute(value, 'seq', [(s, s ^ j) for s in range(n_seq)])  43.3 us
    dot_general x13, matrix products, dot(): lax.dot_general(left, right, (contract, ((), ())), preferred_element_type...  38.9 us
    ppermute x27, starting transfers between devices, shift_z(): lax.ppermute(value, 'seq', [(s, (s + GROUP * t) % n_seq) for s in range(n...  38.4 us
    ppermute x17, starting transfers between devices, xor_w(): return lax.ppermute(value, 'seq', [(s, s ^ j) for s in range(n_seq)])  28.8 us
    unnamed x197, local copies, waits for them, and re-layouts  25 us
    pallas_call x1, Pallas kernels, feed(): pl.pallas_call(feed_kernel, out_shape=(jax.ShapeDtypeStruct((tokens, bloc...  19.6 us
  transfers between devices with their start and end apart: 68, of which 27 were waited for; matrix products, arithmetic and copies ran while one was open for 23% of the time, Pallas kernels for 8%

profile of v12, /device:TPU:1, one launch (start us, length us, event | category | flops | bytes accessed | tf_op | source)
XLA Modules:
  0.0 571.0 jit_solution(9107593541717471848)
XLA Ops:
  15.0 4.1 all-to-all-start
  26.9 4.0 collective-permute-start.3
  35.8 24.0 %collective-permute-done.4 = bf16[512,320]{1,0:T(8,128)(2,1)S(1)} collective-permute-done((bf16[512,320]{1,0:T(8,128)(2,1)S(1)}, bf16[512,320]{1,0:T(8,128)(2,1)S(1)}, u32[]{:S(2)}, u32[]{:S(2)}) %collective-permute-start.4) | collective-permute-done | bytes 327712 | tf_op jit(solution)/shard_map/ppermute | solution.py:375
  61.8 5.3 collective-permute-start.13
  69.2 3.6 collective-permute-start.17
  82.2 14.3 %collective-permute-start.12 = (bf16[64,2048]{1,0:T(8,128)(2,1)S(1)}, bf16[64,2048]{1,0:T(8,128)(2,1)S(1)}, u32[]{:S(2)}, u32[]{:S(2)}) collective-permute-start(bf16[64,2048]{1,0:T(8,128)(2,1)S(1)} %slice.444), channel_id=1, source_target_pairs={{0,1},{1,0},{2,3},{3,2},{4,5},{5,4},{6,7},{7,6},{8,9},{9,8},{10,11... | collective-permute-start | bytes 786440 | tf_op jit(solution)/shard_map/ppermute | solution.py:372
  110.1 5.2 project.1
  115.3 12.1 %collective-permute-done.8 = bf16[128,1408]{1,0:T(8,128)(2,1)} collective-permute-done((bf16[128,1408]{1,0:T(8,128)(2,1)}, bf16[128,1408]{1,0:T(8,128)(2,1)}, u32[]{:S(2)}, u32[]{:S(2)}) %collective-permute-start.8) | collective-permute-done | bytes 360480 | tf_op jit(solution)/shard_map/ppermute | solution.py:375
  137.8 5.9 %collective-permute-done.15 = bf16[512,128]{1,0:T(8,128)(2,1)S(1)} collective-permute-done((bf16[512,128]{1,0:T(8,128)(2,1)S(1)}, bf16[512,128]{1,0:T(8,128)(2,1)S(1)}, u32[]{:S(2)}, u32[]{:S(2)}) %collective-permute-start.15) | collective-permute-done | bytes 131104 | tf_op jit(solution)/shard_map/ppermute | solution.py:375
  149.8 7.6 %attend.1 = (bf16[512,512]{1,0:T(8,128)(2,1)}, f32[4,8,1024]{2,1,0:T(8,128)}) custom-call(s32[1]{0:T(128)} %bitcast.1.seen_ref, bf16[512,512]{1,0:T(8,128)(2,1)} %get-tuple-element.83.q_ref, bf16[4,512,128]{2,1,0:T(8,128)(2,1)} %pad_maximum_fusion.9.kv_ref, s32[512,1]{1,0:T(8,128)} %copy.53.qpos_ref.kpos_ref, s32[1,512]{1,0:T(1,128)} %bitcast.159), custom_call_target="tpu_custom_call" | custom-call | tf_op jit(solution)/shard_map/attend/pallas_call | solution.py:255
  163.3 30.2 %collective-permute-done.22 = bf16[128,2048]{1,0:T(8,128)(2,1)} collective-permute-done((bf16[128,2048]{1,0:T(8,128)(2,1)S(1)}, bf16[128,2048]{1,0:T(8,128)(2,1)}, u32[]{:S(2)}, u32[]{:S(2)}) %collective-permute-start.22) | collective-permute-done | bytes 524320 | tf_op jit(solution)/shard_map/ppermute | solution.py:375
  207.4 10.3 %collective-permute-done.25 = bf16[128,2048]{1,0:T(8,128)(2,1)S(1)} collective-permute-done((bf16[128,2048]{1,0:T(8,128)(2,1)S(1)}, bf16[128,2048]{1,0:T(8,128)(2,1)S(1)}, u32[]{:S(2)}, u32[]{:S(2)}) %collective-permute-start.25) | collective-permute-done | bytes 524320 | tf_op jit(solution)/shard_map/ppermute | solution.py:375
  225.1 31.5 %collective-permute-start.28 = (bf16[512,2048]{1,0:T(8,128)(2,1)}, bf16[512,2048]{1,0:T(8,128)(2,1)}, u32[]{:S(2)}, u32[]{:S(2)}) collective-permute-start(bf16[512,2048]{1,0:T(8,128)(2,1)} %get-tuple-element.234.low_ref), channel_id=1, source_target_pairs={{0,16},{16,0},{1,17},{17,1},{2,18},{18,2},{3,19},{19,3},{4,20},{20... | collective-permute-start | bytes 6291464 | tf_op jit(solution)/shard_map/ppermute | solution.py:378
  256.6 19.6 %feed.1 = (bf16[512,1408]{1,0:T(8,128)(2,1)}, bf16[512,1408]{1,0:T(8,128)(2,1)}, bf16[512,1408]{1,0:T(8,128)(2,1)}, bf16[512,2048]{1,0:T(8,128)(2,1)}) custom-call(bf16[512,2048]{1,0:T(8,128)(2,1)} %get-tuple-element.234.low_ref, bf16[2,2048,1408]{2,1,0:T(8,128)(2,1)} %bitcast.133, f32[512,1408]{1,0:T(8,128)} %convolution_add_fusion.grad_hidden_ref), custom_call_target="tpu_custom_call" | custom-call | tf_op jit(solution)/shard_map/feed/pallas_call | solution.py:132
  285.6 8.6 %convolution_convert_fusion = bf16[2048,1408]{1,0:T(8,128)(2,1)} fusion(bf16[1024,2048]{1,0:T(8,128)(2,1)S(1)} %constant_dynamic-update-slice_fusion.32, bf16[512,1408]{1,0:T(8,128)(2,1)S(1)} %collective-permute-done.29, bf16[512,1408]{1,0:T(8,128)(2,1)S(1)} %get-tuple-element.175), kind=kOutput, calls=%fused_computation | convolution fusion | flops 5914230784 | bytes 12845056 | tf_op jit(solution)/shard_map/dot_general | solution.py:26
  294.2 7.1 %collective-permute-done.27 = bf16[128,2048]{1,0:T(8,128)(2,1)S(1)} collective-permute-done((bf16[128,2048]{1,0:T(8,128)(2,1)}, bf16[128,2048]{1,0:T(8,128)(2,1)S(1)}, u32[]{:S(2)}, u32[]{:S(2)}) %collective-permute-start.27) | collective-permute-done | bytes 524320 | tf_op jit(solution)/shard_map/ppermute | solution.py:375
  305.6 3.5 convolution_convert_fusion.4
  312.4 5.9 %convolution_convert_fusion.1 = bf16[1408,1024]{1,0:T(8,128)(2,1)} fusion(bf16[512,1408]{1,0:T(8,128)(2,1)} %collective-permute-done.32, bf16[512,1408]{1,0:T(8,128)(2,1)S(1)} %copy-done.57, bf16[512,1024]{1,0:T(8,128)(2,1)S(1)} %collective-permute-done.33, bf16[512,1024]{1,0:T(8,128)(2,1)S(1)} %get-tuple-element.185), kind=kOutput, calls=%fused_computation.1 | convolution fusion | flops 2964193280 | bytes 7864320 | tf_op jit(solution)/shard_map/dot_general | solution.py:26
  318.3 22.5 %collective-permute-done.30 = bf16[128,2048]{1,0:T(8,128)(2,1)} collective-permute-done((bf16[128,2048]{1,0:T(8,128)(2,1)}, bf16[128,2048]{1,0:T(8,128)(2,1)}, u32[]{:S(2)}, u32[]{:S(2)}) %collective-permute-start.30) | collective-permute-done | bytes 524320 | tf_op jit(solution)/shard_map/ppermute | solution.py:375
  348.5 10.4 %collective-permute-done.36 = bf16[128,2048]{1,0:T(8,128)(2,1)S(1)} collective-permute-done((bf16[128,2048]{1,0:T(8,128)(2,1)S(1)}, bf16[128,2048]{1,0:T(8,128)(2,1)S(1)}, u32[]{:S(2)}, u32[]{:S(2)}) %collective-permute-start.36) | collective-permute-done | bytes 524320 | tf_op jit(solution)/shard_map/ppermute | solution.py:372
  361.5 11.5 %collective-permute-done.38 = bf16[64,2048]{1,0:T(8,128)(2,1)S(1)} collective-permute-done((bf16[64,2048]{1,0:T(8,128)(2,1)S(1)}, bf16[64,2048]{1,0:T(8,128)(2,1)S(1)}, u32[]{:S(2)}, u32[]{:S(2)}) %collective-permute-start.38) | collective-permute-done | bytes 262176 | tf_op jit(solution)/shard_map/ppermute | solution.py:372
  373.8 8.5 %collective-permute-done.35 = bf16[128,2048]{1,0:T(8,128)(2,1)} collective-permute-done((bf16[128,2048]{1,0:T(8,128)(2,1)S(1)}, bf16[128,2048]{1,0:T(8,128)(2,1)}, u32[]{:S(2)}, u32[]{:S(2)}) %collective-permute-start.35) | collective-permute-done | bytes 524320 | tf_op jit(solution)/shard_map/ppermute | solution.py:375
  392.5 8.0 %collective-permute-done.40 = bf16[128,2048]{1,0:T(8,128)(2,1)S(1)} collective-permute-done((bf16[128,2048]{1,0:T(8,128)(2,1)}, bf16[128,2048]{1,0:T(8,128)(2,1)S(1)}, u32[]{:S(2)}, u32[]{:S(2)}) %collective-permute-start.40) | collective-permute-done | bytes 524320 | tf_op jit(solution)/shard_map/ppermute | solution.py:375
  411.3 11.3 %attend_back.1 = (bf16[512,512]{1,0:T(8,128)(2,1)}, bf16[4,512,128]{2,1,0:T(8,128)(2,1)}) custom-call(s32[1]{0:T(128)} %bitcast.1.seen_ref, bf16[512,512]{1,0:T(8,128)(2,1)} %get-tuple-element.83.q_ref, bf16[512,512]{1,0:T(8,128)(2,1)} %bitcast.151, bf16[512,512]{1,0:T(8,128)(2,1)} %get-tuple-element.86.o_ref, ...), custom_call_target="tpu_custom_call" | custom-call | tf_op jit(solution)/shard_map/attend_back/pallas_call | solution.py:285
  422.6 21.4 %collective-permute-done.44 = bf16[128,1408]{1,0:T(8,128)(2,1)} collective-permute-done((bf16[128,1408]{1,0:T(8,128)(2,1)S(1)}, bf16[128,1408]{1,0:T(8,128)(2,1)}, u32[]{:S(2)}, u32[]{:S(2)}) %collective-permute-start.44) | collective-permute-done | bytes 360480 | tf_op jit(solution)/shard_map/ppermute | solution.py:375
  447.0 8.5 %collective-permute-start.48 = (bf16[512,128]{1,0:T(8,128)(2,1)S(1)}, bf16[512,128]{1,0:T(8,128)(2,1)S(1)}, u32[]{:S(2)}, u32[]{:S(2)}) collective-permute-start(bf16[512,128]{1,0:T(8,128)(2,1)S(1)} %get-tuple-element.231), channel_id=1, source_target_pairs={{0,4},{1,5},{2,6},{3,7},{4,8},{5,9},{6,10},{7,11},{8,12},{9,13},{1... | collective-permute-start | bytes 393224 | tf_op jit(solution)/shard_map/ppermute | solution.py:375
  477.6 17.1 %reduce-scatter.9.cloned.1.call-done = bf16[352,1024]{1,0:T(8,128)(2,1)} async-done(((bf16[1408,1024]{1,0:T(8,128)(2,1)}), bf16[352,1024]{1,0:T(8,128)(2,1)}) %reduce-scatter.9.cloned.1.call-update) | async-done | bytes 720912 | tf_op jit(solution)/shard_map/reduce_scatter | solution.py:611
  495.6 3.7 convolution_convert_fusion.2
  505.3 5.5 fusion.3
  513.9 13.9 %collective-permute-done.50 = bf16[128,2048]{1,0:T(8,128)(2,1)S(1)} collective-permute-done((bf16[128,2048]{1,0:T(8,128)(2,1)S(1)}, bf16[128,2048]{1,0:T(8,128)(2,1)S(1)}, u32[]{:S(2)}, u32[]{:S(2)}) %collective-permute-start.50) | collective-permute-done | bytes 524320 | tf_op jit(solution)/shard_map/ppermute | solution.py:372
  532.9 11.1 %reduce-scatter.11.cloned.1.call-done = bf16[512,320]{0,1:T(8,128)(2,1)} async-done(((bf16[2048,320]{0,1:T(8,128)(2,1)}), bf16[512,320]{0,1:T(8,128)(2,1)}) %reduce-scatter.11.cloned.1.call-update) | async-done | bytes 327696 | tf_op jit(solution)/shard_map/reduce_scatter | solution.py:681
  545.8 3.5 all-to-all-start.1
  (433 shorter events, 195.5 us)
Async XLA Ops:
  7.2 89.3 %all-gather.8.cloned.1.call-start = ((), (), s32[]{:S(2)}) async-start(), calls=%async_computation.11 | async-start | bytes 6488064 | tf_op jit(solution)/shard_map/all_gather | solution.py:484
  19.1 138.3 %all-gather.10.cloned.1.call-start = ((), (), s32[]{:S(2)}) async-start(), calls=%async_computation.12 | async-start | bytes 2359296 | tf_op jit(solution)/shard_map/all_gather | solution.py:489
  30.9 28.9 %collective-permute-start.4 = (bf16[512,320]{1,0:T(8,128)(2,1)S(1)}, bf16[512,320]{1,0:T(8,128)(2,1)S(1)}, u32[]{:S(2)}, u32[]{:S(2)}) collective-permute-start(bf16[512,320]{1,0:T(8,128)(2,1)S(1)} %bitcast.138), channel_id=1, source_target_pairs={{0,8},{1,9},{2,10},{3,11},{4,12},{5,13},{6,14},{7,15},{8,0},{9,1},... | collective-permute-start | bytes 983048 | tf_op jit(solution)/shard_map/ppermute | solution.py:375
  30.9 28.9 %collective-permute-start.5 = (bf16[512,320]{1,0:T(8,128)(2,1)S(1)}, bf16[512,320]{1,0:T(8,128)(2,1)S(1)}, u32[]{:S(2)}, u32[]{:S(2)}) collective-permute-start(bf16[512,320]{1,0:T(8,128)(2,1)S(1)} %bitcast.139), channel_id=1, source_target_pairs={{0,4},{1,5},{2,6},{3,7},{4,8},{5,9},{6,10},{7,11},{8,12},{9,13},{1... | collective-permute-start | bytes 983048 | tf_op jit(solution)/shard_map/ppermute | solution.py:375
  32.3 43.6 %collective-permute-start.9 = (bf16[128,2048]{1,0:T(8,128)(2,1)S(1)}, bf16[128,2048]{1,0:T(8,128)(2,1)}, u32[]{:S(2)}, u32[]{:S(2)}) collective-permute-start(bf16[128,2048]{1,0:T(8,128)(2,1)S(1)} %fusion.22), channel_id=1, source_target_pairs={{0,1},{1,0},{2,3},{3,2},{4,5},{5,4},{6,7},{7,6},{8,9},{9,8},{10,11... | collective-permute-start | bytes 1572872 | tf_op jit(solution)/shard_map/ppermute | solution.py:372
  33.2 47.3 %collective-permute-start.10 = (bf16[128,2048]{1,0:T(8,128)(2,1)S(1)}, bf16[128,2048]{1,0:T(8,128)(2,1)}, u32[]{:S(2)}, u32[]{:S(2)}) collective-permute-start(bf16[128,2048]{1,0:T(8,128)(2,1)S(1)} %fusion.22), channel_id=1, source_target_pairs={{0,2},{1,3},{2,0},{3,1},{4,6},{5,7},{6,4},{7,5},{8,10},{9,11},{10,... | collective-permute-start | bytes 1572872 | tf_op jit(solution)/shard_map/ppermute | solution.py:372
  61.8 41.4 %collective-permute-start.13 = (bf16[2048,320]{0,1:T(8,128)(2,1)}, bf16[2048,320]{0,1:T(8,128)(2,1)}, u32[]{:S(2)}, u32[]{:S(2)}) collective-permute-start(bf16[2048,320]{0,1:T(8,128)(2,1)} %copy.48), channel_id=1, source_target_pairs={{0,16},{16,0},{1,17},{17,1},{2,18},{18,2},{3,19},{19,3},{4,20},{20... | collective-permute-start | bytes 3932168 | tf_op jit(solution)/shard_map/ppermute | solution.py:378
  75.2 40.1 %collective-permute-start.6 = (bf16[128,1408]{1,0:T(8,128)(2,1)}, bf16[128,1408]{1,0:T(8,128)(2,1)}, u32[]{:S(2)}, u32[]{:S(2)}) collective-permute-start(bf16[128,1408]{1,0:T(8,128)(2,1)} %get-tuple-element.212), channel_id=1, source_target_pairs={{0,4},{1,5},{2,6},{3,7},{4,8},{5,9},{6,10},{7,11},{8,12},{9,13},{1... | collective-permute-start | bytes 1081352 | tf_op jit(solution)/shard_map/ppermute | solution.py:375
  75.9 39.4 %collective-permute-start.7 = (bf16[128,1408]{1,0:T(8,128)(2,1)}, bf16[128,1408]{1,0:T(8,128)(2,1)}, u32[]{:S(2)}, u32[]{:S(2)}) collective-permute-start(bf16[128,1408]{1,0:T(8,128)(2,1)} %get-tuple-element.211), channel_id=1, source_target_pairs={{0,8},{1,9},{2,10},{3,11},{4,12},{5,13},{6,14},{7,15},{8,0},{9,1},... | collective-permute-start | bytes 1081352 | tf_op jit(solution)/shard_map/ppermute | solution.py:375
  96.5 160.1 %all-gather.6.cloned.1.call-start = ((), (), s32[]{:S(2)}) async-start(), calls=%async_computation.6 | async-start | bytes 12976128 | tf_op jit(solution)/shard_map/all_gather | solution.py:525
  101.0 26.4 %collective-permute-start.8 = (bf16[128,1408]{1,0:T(8,128)(2,1)}, bf16[128,1408]{1,0:T(8,128)(2,1)}, u32[]{:S(2)}, u32[]{:S(2)}) collective-permute-start(bf16[128,1408]{1,0:T(8,128)(2,1)} %get-tuple-element.210), channel_id=1, source_target_pairs={{0,12},{1,13},{2,14},{3,15},{4,0},{5,1},{6,2},{7,3},{8,4},{9,5},{1... | collective-permute-start | bytes 1081352 | tf_op jit(solution)/shard_map/ppermute | solution.py:375
  131.9 268.6 %reduce-scatter.5.cloned.1.call-start = ((), (), s32[]{:S(2)}) async-start(), calls=%async_computation.7 | async-start | bytes 7208960 | tf_op jit(solution)/shard_map/reduce_scatter | solution.py:610
  146.0 47.5 %collective-permute-start.22 = (bf16[128,2048]{1,0:T(8,128)(2,1)S(1)}, bf16[128,2048]{1,0:T(8,128)(2,1)}, u32[]{:S(2)}, u32[]{:S(2)}) collective-permute-start(bf16[128,2048]{1,0:T(8,128)(2,1)S(1)} %bitcast_convert_fusion), channel_id=1, source_target_pairs={{0,8},{1,9},{2,10},{3,11},{4,12},{5,13},{6,14},{7,15},{8,0},{9,1},... | collective-permute-start | bytes 1572872 | tf_op jit(solution)/shard_map/ppermute | solution.py:375
  147.9 45.6 %collective-permute-start.21 = (bf16[128,2048]{1,0:T(8,128)(2,1)S(1)}, bf16[128,2048]{1,0:T(8,128)(2,1)}, u32[]{:S(2)}, u32[]{:S(2)}) collective-permute-start(bf16[128,2048]{1,0:T(8,128)(2,1)S(1)} %bitcast_convert_fusion), channel_id=1, source_target_pairs={{0,4},{1,5},{2,6},{3,7},{4,8},{5,9},{6,10},{7,11},{8,12},{9,13},{1... | collective-permute-start | bytes 1572872 | tf_op jit(solution)/shard_map/ppermute | solution.py:375
  160.6 35.6 %collective-permute-start.20 = (bf16[128,2048]{1,0:T(8,128)(2,1)S(1)}, bf16[128,2048]{1,0:T(8,128)(2,1)S(1)}, u32[]{:S(2)}, u32[]{:S(2)}) collective-permute-start(bf16[128,2048]{1,0:T(8,128)(2,1)S(1)} %get-tuple-element.191), channel_id=1, source_target_pairs={{0,3},{1,2},{2,1},{3,0},{4,7},{5,6},{6,5},{7,4},{8,11},{9,10},{10,... | collective-permute-start | bytes 1572872 | tf_op jit(solution)/shard_map/ppermute | solution.py:372
  160.8 35.4 %collective-permute-start.19 = (bf16[128,2048]{1,0:T(8,128)(2,1)S(1)}, bf16[128,2048]{1,0:T(8,128)(2,1)S(1)}, u32[]{:S(2)}, u32[]{:S(2)}) collective-permute-start(bf16[128,2048]{1,0:T(8,128)(2,1)S(1)} %get-tuple-element.192), channel_id=1, source_target_pairs={{0,2},{1,3},{2,0},{3,1},{4,6},{5,7},{6,4},{7,5},{8,10},{9,11},{10,... | collective-permute-start | bytes 1572872 | tf_op jit(solution)/shard_map/ppermute | solution.py:372
  161.4 34.7 %collective-permute-start.18 = (bf16[128,2048]{1,0:T(8,128)(2,1)S(1)}, bf16[128,2048]{1,0:T(8,128)(2,1)S(1)}, u32[]{:S(2)}, u32[]{:S(2)}) collective-permute-start(bf16[128,2048]{1,0:T(8,128)(2,1)S(1)} %get-tuple-element.190), channel_id=1, source_target_pairs={{0,1},{1,0},{2,3},{3,2},{4,5},{5,4},{6,7},{7,6},{8,9},{9,8},{10,11... | collective-permute-start | bytes 1572872 | tf_op jit(solution)/shard_map/ppermute | solution.py:372
  225.1 53.4 %collective-permute-start.28 = (bf16[512,2048]{1,0:T(8,128)(2,1)}, bf16[512,2048]{1,0:T(8,128)(2,1)}, u32[]{:S(2)}, u32[]{:S(2)}) collective-permute-start(bf16[512,2048]{1,0:T(8,128)(2,1)} %get-tuple-element.234.low_ref), channel_id=1, source_target_pairs={{0,16},{16,0},{1,17},{17,1},{2,18},{18,2},{3,19},{19,3},{4,20},{20... | collective-permute-start | bytes 6291464 | tf_op jit(solution)/shard_map/ppermute | solution.py:378
  301.3 169.6 %reduce-scatter.7.cloned.1.call-start = ((), (), s32[]{:S(2)}) async-start(), calls=%async_computation.8 | async-start | bytes 1310720 | tf_op jit(solution)/shard_map/reduce_scatter | solution.py:629
  304.0 36.8 %collective-permute-start.30 = (bf16[128,2048]{1,0:T(8,128)(2,1)}, bf16[128,2048]{1,0:T(8,128)(2,1)}, u32[]{:S(2)}, u32[]{:S(2)}) collective-permute-start(bf16[128,2048]{1,0:T(8,128)(2,1)} %get-tuple-element.188), channel_id=1, source_target_pairs={{0,8},{1,9},{2,10},{3,11},{4,12},{5,13},{6,14},{7,15},{8,0},{9,1},... | collective-permute-start | bytes 1572872 | tf_op jit(solution)/shard_map/ppermute | solution.py:375
  304.6 36.2 %collective-permute-start.31 = (bf16[128,2048]{1,0:T(8,128)(2,1)}, bf16[128,2048]{1,0:T(8,128)(2,1)}, u32[]{:S(2)}, u32[]{:S(2)}) collective-permute-start(bf16[128,2048]{1,0:T(8,128)(2,1)} %get-tuple-element.187), channel_id=1, source_target_pairs={{0,4},{1,5},{2,6},{3,7},{4,8},{5,9},{6,10},{7,11},{8,12},{9,13},{1... | collective-permute-start | bytes 1572872 | tf_op jit(solution)/shard_map/ppermute | solution.py:375
  347.6 25.5 %collective-permute-start.34 = (bf16[128,2048]{1,0:T(8,128)(2,1)S(1)}, bf16[128,2048]{1,0:T(8,128)(2,1)S(1)}, u32[]{:S(2)}, u32[]{:S(2)}) collective-permute-start(bf16[128,2048]{1,0:T(8,128)(2,1)S(1)} %get-tuple-element.184), channel_id=1, source_target_pairs={{0,12},{1,13},{2,14},{3,15},{4,0},{5,1},{6,2},{7,3},{8,4},{9,5},{1... | collective-permute-start | bytes 1572872 | tf_op jit(solution)/shard_map/ppermute | solution.py:375
  347.6 34.8 %collective-permute-start.35 = (bf16[128,2048]{1,0:T(8,128)(2,1)S(1)}, bf16[128,2048]{1,0:T(8,128)(2,1)}, u32[]{:S(2)}, u32[]{:S(2)}) collective-permute-start(bf16[128,2048]{1,0:T(8,128)(2,1)S(1)} %get-tuple-element.182), channel_id=1, source_target_pairs={{0,8},{1,9},{2,10},{3,11},{4,12},{5,13},{6,14},{7,15},{8,0},{9,1},... | collective-permute-start | bytes 1572872 | tf_op jit(solution)/shard_map/ppermute | solution.py:375
  384.2 22.6 %collective-permute-start.52 = (bf16[512,2048]{1,0:T(8,128)(2,1)}, bf16[512,2048]{1,0:T(8,128)(2,1)}, u32[]{:S(2)}, u32[]{:S(2)}) collective-permute-start(bf16[512,2048]{1,0:T(8,128)(2,1)} %get-tuple-element.250.low_ref), channel_id=1, source_target_pairs={{0,16},{16,0},{1,17},{17,1},{2,18},{18,2},{3,19},{19,3},{4,20},{20... | collective-permute-start | bytes 6291464 | tf_op jit(solution)/shard_map/ppermute | solution.py:378
  400.5 94.2 %reduce-scatter.9.cloned.1.call-start = ((), (), s32[]{:S(2)}) async-start(), calls=%async_computation.9 | async-start | bytes 3604480 | tf_op jit(solution)/shard_map/reduce_scatter | solution.py:611
  403.5 40.4 %collective-permute-start.44 = (bf16[128,1408]{1,0:T(8,128)(2,1)S(1)}, bf16[128,1408]{1,0:T(8,128)(2,1)}, u32[]{:S(2)}, u32[]{:S(2)}) collective-permute-start(bf16[128,1408]{1,0:T(8,128)(2,1)S(1)} %get-tuple-element.207), channel_id=1, source_target_pairs={{0,8},{1,9},{2,10},{3,11},{4,12},{5,13},{6,14},{7,15},{8,0},{9,1},... | collective-permute-start | bytes 1081352 | tf_op jit(solution)/shard_map/ppermute | solution.py:375
  404.3 41.6 %collective-permute-start.45 = (bf16[128,1408]{1,0:T(8,128)(2,1)S(1)}, bf16[128,1408]{1,0:T(8,128)(2,1)}, u32[]{:S(2)}, u32[]{:S(2)}) collective-permute-start(bf16[128,1408]{1,0:T(8,128)(2,1)S(1)} %get-tuple-element.206), channel_id=1, source_target_pairs={{0,12},{1,13},{2,14},{3,15},{4,0},{5,1},{6,2},{7,3},{8,4},{9,5},{1... | collective-permute-start | bytes 1081352 | tf_op jit(solution)/shard_map/ppermute | solution.py:375
  410.0 134.0 %reduce-scatter.11.cloned.1.call-start = ((), (), s32[]{:S(2)}) async-start(), calls=%async_computation.10 | async-start | bytes 1638400 | tf_op jit(solution)/shard_map/reduce_scatter | solution.py:681
  500.8 27.1 %collective-permute-start.50 = (bf16[128,2048]{1,0:T(8,128)(2,1)S(1)}, bf16[128,2048]{1,0:T(8,128)(2,1)S(1)}, u32[]{:S(2)}, u32[]{:S(2)}) collective-permute-start(bf16[128,2048]{1,0:T(8,128)(2,1)S(1)} %get-tuple-element.179), channel_id=1, source_target_pairs={{0,2},{1,3},{2,0},{3,1},{4,6},{5,7},{6,4},{7,5},{8,10},{9,11},{10,... | collective-permute-start | bytes 1572872 | tf_op jit(solution)/shard_map/ppermute | solution.py:372
  502.0 28.2 %collective-permute-start.49 = (bf16[128,2048]{1,0:T(8,128)(2,1)S(1)}, bf16[128,2048]{1,0:T(8,128)(2,1)S(1)}, u32[]{:S(2)}, u32[]{:S(2)}) collective-permute-start(bf16[128,2048]{1,0:T(8,128)(2,1)S(1)} %get-tuple-element.177), channel_id=1, source_target_pairs={{0,1},{1,0},{2,3},{3,2},{4,5},{5,4},{6,7},{7,6},{8,9},{9,8},{10,11... | collective-permute-start | bytes 1572872 | tf_op jit(solution)/shard_map/ppermute | solution.py:372
  503.6 27.0 %collective-permute-start.55 = (bf16[352,1024]{1,0:T(8,128)(2,1)S(1)}, bf16[352,1024]{1,0:T(8,128)(2,1)S(1)}, u32[]{:S(2)}, u32[]{:S(2)}) collective-permute-start(bf16[352,1024]{1,0:T(8,128)(2,1)S(1)} %copy-done.26), channel_id=1, source_target_pairs={{0,16},{16,0},{1,17},{17,1},{2,18},{18,2},{3,19},{19,3},{4,20},{20... | collective-permute-start | bytes 2162696 | tf_op jit(solution)/shard_map/ppermute | solution.py:378
  510.8 46.2 %collective-permute-start.58 = (bf16[128,1024]{1,0:T(8,128)(2,1)}, bf16[128,1024]{1,0:T(8,128)(2,1)}, u32[]{:S(2)}, u32[]{:S(2)}) collective-permute-start(bf16[128,1024]{1,0:T(8,128)(2,1)} %collective-permute-done.57), channel_id=1, source_target_pairs={{0,16},{16,0},{1,17},{17,1},{2,18},{18,2},{3,19},{19,3},{4,20},{20... | collective-permute-start | bytes 786440 | tf_op jit(solution)/shard_map/ppermute | solution.py:378
  (100 other events, 860.8 us)
Sparse Core Ops, SparseCore 0:
  10.5 54.0 all-gather.7
  96.7 40.1 all-gather.9
  138.8 89.1 all-gather.5
  301.4 81.7 reduce-scatter.4
  400.7 46.9 reduce-scatter.6
  451.1 43.5 reduce-scatter.8
  497.0 46.9 reduce-scatter.10

commit v13 on v12

--- a/solution.py
+++ b/solution.py
@@ -625,7 +625,7 @@
         grad_o_seq = by_seq(grad_o, 0)
         *late, grad_o_seq, out_part_sum = tie(*mixed_sent[early:], grad_o_seq, out_part_sum)
         mixed_sent = mixed_sent[:early] + list(late)
-        gate_up_sum, out_part_sum = tie(gate_up_sum, out_part_sum)
+        gate_up_sum, down_sum, out_part_sum = tie(gate_up_sum, down_sum, out_part_sum)
         out_sum = lax.psum_scatter(out_part_sum, "seq", axis_index_groups=across, tiled=True)
         grad_o_seq, gate_up_late = tie(grad_o_seq, gate_up_sum)
         gate_up_sent = []

time: 579 us -> 596 us (1.029)
  waiting for transfers between devices: 236 us -> 244 us
    reduce_scatter x1, waiting for transfers between devices: 0.01 us -> 26.7 us  [body(): lax.psum_scatter(gate_up_sum, 'seq', axis_index_groups=in_plane, tiled=True)]
    reduce_scatter x1, waiting for transfers between devices: 17.1 us -> 0.01 us  [body(): lax.psum_scatter(down_sum, 'seq', axis_index_groups=in_plane, tiled=True)]
    ppermute x27, starting transfers between devices: 38.4 us -> 47.6 us  [shift_z(): lax.ppermute(value, 'seq', [(s, (s + GROUP * t) % n_seq) for s in range(n...]
    ppermute x13, starting transfers between devices: 48.2 us -> 41.8 us  [shift_dp(): return lax.ppermute(value, 'dp', [(c, (c + t) % n_dp) for c in range(n_dp)])]
    unnamed x197 -> x195, local copies, waits for them, and re-layouts: 25 us -> 21.5 us
  transfers between devices with their start and end apart: 68 -> 68, of which waited for: 27 -> 28; matrix products, arithmetic and copies ran while one was open for 23% -> 23% of each run, Pallas kernels for 8% -> 4%
where the time goes in v13:
time: 596 us; the launch traced here: 588 us
  waiting for transfers between devices  244 us (41%)
  starting transfers between devices  132 us (22%)
  local copies, waits for them, and re-layouts  65.4 us (11%)
  matrix products  44.3 us (7%)
  Pallas kernels  43.7 us (7%)
  other arithmetic  41.5 us (7%)
  between operations  16.1 us (3%)
    ppermute x27, waiting for transfers between devices, shift_z(): lax.ppermute(value, 'seq', [(s, (s + GROUP * t) % n_seq) for s in range(n...  159 us
    ppermute x27, starting transfers between devices, shift_z(): lax.ppermute(value, 'seq', [(s, (s + GROUP * t) % n_seq) for s in range(n...  47.6 us
    dot_general x13, matrix products, dot(): lax.dot_general(left, right, (contract, ((), ())), preferred_element_type...  44.3 us
    ppermute x13, starting transfers between devices, shift_dp(): return lax.ppermute(value, 'dp', [(c, (c + t) % n_dp) for c in range(n_dp)])  41.8 us
    ppermute x17, waiting for transfers between devices, xor_w(): return lax.ppermute(value, 'seq', [(s, s ^ j) for s in range(n_seq)])  39.3 us
    ppermute x17, starting transfers between devices, xor_w(): return lax.ppermute(value, 'seq', [(s, s ^ j) for s in range(n_seq)])  29.9 us
    reduce_scatter x1, waiting for transfers between devices, body(): lax.psum_scatter(gate_up_sum, 'seq', axis_index_groups=in_plane, tiled=True)  26.7 us
    unnamed x195, local copies, waits for them, and re-layouts  21.5 us
  transfers between devices with their start and end apart: 68, of which 28 were waited for; matrix products, arithmetic and copies ran while one was open for 23% of the time, Pallas kernels for 4%

profile of v13, /device:TPU:1, one launch (start us, length us, event | category | flops | bytes accessed | tf_op | source)
XLA Modules:
  0.0 588.0 jit_solution(5241148433264295419)
XLA Ops:
  15.0 4.1 all-to-all-start
  26.8 4.0 collective-permute-start.3
  35.8 23.9 %collective-permute-done.4 = bf16[512,320]{1,0:T(8,128)(2,1)S(1)} collective-permute-done((bf16[512,320]{1,0:T(8,128)(2,1)S(1)}, bf16[512,320]{1,0:T(8,128)(2,1)S(1)}, u32[]{:S(2)}, u32[]{:S(2)}) %collective-permute-start.4) | collective-permute-done | bytes 327712 | tf_op jit(solution)/shard_map/ppermute | solution.py:375
  61.8 5.3 collective-permute-start.13
  69.1 3.6 collective-permute-start.17
  82.1 14.3 %collective-permute-start.12 = (bf16[64,2048]{1,0:T(8,128)(2,1)S(1)}, bf16[64,2048]{1,0:T(8,128)(2,1)S(1)}, u32[]{:S(2)}, u32[]{:S(2)}) collective-permute-start(bf16[64,2048]{1,0:T(8,128)(2,1)S(1)} %slice.444), channel_id=1, source_target_pairs={{0,1},{1,0},{2,3},{3,2},{4,5},{5,4},{6,7},{7,6},{8,9},{9,8},{10,11... | collective-permute-start | bytes 786440 | tf_op jit(solution)/shard_map/ppermute | solution.py:372
  110.1 5.2 project.1
  115.3 12.1 %collective-permute-done.8 = bf16[128,1408]{1,0:T(8,128)(2,1)} collective-permute-done((bf16[128,1408]{1,0:T(8,128)(2,1)}, bf16[128,1408]{1,0:T(8,128)(2,1)}, u32[]{:S(2)}, u32[]{:S(2)}) %collective-permute-start.8) | collective-permute-done | bytes 360480 | tf_op jit(solution)/shard_map/ppermute | solution.py:375
  137.8 5.7 collective-permute-done.15
  149.5 7.6 %attend.1 = (bf16[512,512]{1,0:T(8,128)(2,1)}, f32[4,8,1024]{2,1,0:T(8,128)}) custom-call(s32[1]{0:T(128)} %bitcast.1.seen_ref, bf16[512,512]{1,0:T(8,128)(2,1)} %get-tuple-element.84.q_ref, bf16[4,512,128]{2,1,0:T(8,128)(2,1)} %pad_maximum_fusion.9.kv_ref, s32[512,1]{1,0:T(8,128)} %copy.53.qpos_ref.kpos_ref, s32[1,512]{1,0:T(1,128)} %bitcast.159), custom_call_target="tpu_custom_call" | custom-call | tf_op jit(solution)/shard_map/attend/pallas_call | solution.py:255
  163.0 30.4 %collective-permute-done.22 = bf16[128,2048]{1,0:T(8,128)(2,1)} collective-permute-done((bf16[128,2048]{1,0:T(8,128)(2,1)S(1)}, bf16[128,2048]{1,0:T(8,128)(2,1)}, u32[]{:S(2)}, u32[]{:S(2)}) %collective-permute-start.22) | collective-permute-done | bytes 524320 | tf_op jit(solution)/shard_map/ppermute | solution.py:375
  207.6 10.2 %collective-permute-done.25 = bf16[128,2048]{1,0:T(8,128)(2,1)S(1)} collective-permute-done((bf16[128,2048]{1,0:T(8,128)(2,1)S(1)}, bf16[128,2048]{1,0:T(8,128)(2,1)S(1)}, u32[]{:S(2)}, u32[]{:S(2)}) %collective-permute-start.25) | collective-permute-done | bytes 524320 | tf_op jit(solution)/shard_map/ppermute | solution.py:375
  223.9 4.1 all-gather.6.cloned.1.call-done
  228.0 19.6 %feed.1 = (bf16[512,1408]{1,0:T(8,128)(2,1)}, bf16[512,1408]{1,0:T(8,128)(2,1)}, bf16[512,1408]{1,0:T(8,128)(2,1)}, bf16[512,2048]{1,0:T(8,128)(2,1)}) custom-call(bf16[512,2048]{1,0:T(8,128)(2,1)} %get-tuple-element.236.low_ref, bf16[2,2048,1408]{2,1,0:T(8,128)(2,1)} %bitcast.133, f32[512,1408]{1,0:T(8,128)} %convolution_add_fusion.grad_hidden_ref), custom_call_target="tpu_custom_call" | custom-call | tf_op jit(solution)/shard_map/feed/pallas_call | solution.py:132
  247.6 27.0 %collective-permute-start.32 = (bf16[512,1408]{1,0:T(8,128)(2,1)}, bf16[512,1408]{1,0:T(8,128)(2,1)}, u32[]{:S(2)}, u32[]{:S(2)}) collective-permute-start(bf16[512,1408]{1,0:T(8,128)(2,1)} %get-tuple-element.106), channel_id=1, source_target_pairs={{0,16},{16,0},{1,17},{17,1},{2,18},{18,2},{3,19},{19,3},{4,20},{20... | collective-permute-start | bytes 4325384 | tf_op jit(solution)/shard_map/ppermute | solution.py:378
  278.1 4.9 collective-permute-start.30
  284.0 5.9 %convolution_convert_fusion.1 = bf16[1408,1024]{1,0:T(8,128)(2,1)} fusion(bf16[512,1408]{1,0:T(8,128)(2,1)} %collective-permute-done.32, bf16[512,1408]{1,0:T(8,128)(2,1)S(1)} %copy-done.55, bf16[512,1024]{1,0:T(8,128)(2,1)S(1)} %collective-permute-done.33, bf16[512,1024]{1,0:T(8,128)(2,1)S(1)} %get-tuple-element.187), kind=kOutput, calls=%fused_computation.1 | convolution fusion | flops 2964193280 | bytes 7864320 | tf_op jit(solution)/shard_map/dot_general | solution.py:26
  289.9 27.8 %collective-permute-done.30 = bf16[128,2048]{1,0:T(8,128)(2,1)S(1)} collective-permute-done((bf16[128,2048]{1,0:T(8,128)(2,1)}, bf16[128,2048]{1,0:T(8,128)(2,1)S(1)}, u32[]{:S(2)}, u32[]{:S(2)}) %collective-permute-start.30) | collective-permute-done | bytes 524320 | tf_op jit(solution)/shard_map/ppermute | solution.py:375
  326.1 11.0 %convolution_convert_fusion = bf16[2048,1408]{1,0:T(8,128)(2,1)} fusion(bf16[1024,2048]{1,0:T(8,128)(2,1)} %constant_dynamic-update-slice_fusion.32, bf16[512,1408]{1,0:T(8,128)(2,1)S(1)} %collective-permute-done.29, bf16[512,1408]{1,0:T(8,128)(2,1)S(1)} %get-tuple-element.177), kind=kOutput, calls=%fused_computation | convolution fusion | flops 5914230784 | bytes 12845056 | tf_op jit(solution)/shard_map/dot_general | solution.py:26
  340.9 4.1 convolution_convert_fusion.4
  357.5 12.7 %collective-permute-done.36 = bf16[128,2048]{1,0:T(8,128)(2,1)S(1)} collective-permute-done((bf16[128,2048]{1,0:T(8,128)(2,1)S(1)}, bf16[128,2048]{1,0:T(8,128)(2,1)S(1)}, u32[]{:S(2)}, u32[]{:S(2)}) %collective-permute-start.36) | collective-permute-done | bytes 524320 | tf_op jit(solution)/shard_map/ppermute | solution.py:372
  371.8 6.0 %collective-permute-done.38 = bf16[64,2048]{1,0:T(8,128)(2,1)S(1)} collective-permute-done((bf16[64,2048]{1,0:T(8,128)(2,1)S(1)}, bf16[64,2048]{1,0:T(8,128)(2,1)S(1)}, u32[]{:S(2)}, u32[]{:S(2)}) %collective-permute-start.38) | collective-permute-done | bytes 262176 | tf_op jit(solution)/shard_map/ppermute | solution.py:372
  378.4 13.5 %collective-permute-done.35 = bf16[128,2048]{1,0:T(8,128)(2,1)} collective-permute-done((bf16[128,2048]{1,0:T(8,128)(2,1)S(1)}, bf16[128,2048]{1,0:T(8,128)(2,1)}, u32[]{:S(2)}, u32[]{:S(2)}) %collective-permute-start.35) | collective-permute-done | bytes 524320 | tf_op jit(solution)/shard_map/ppermute | solution.py:375
  399.8 3.5 fusion.17
  403.3 6.2 %collective-permute-done.40 = bf16[128,2048]{1,0:T(8,128)(2,1)S(1)} collective-permute-done((bf16[128,2048]{1,0:T(8,128)(2,1)}, bf16[128,2048]{1,0:T(8,128)(2,1)S(1)}, u32[]{:S(2)}, u32[]{:S(2)}) %collective-permute-start.40) | collective-permute-done | bytes 524320 | tf_op jit(solution)/shard_map/ppermute | solution.py:375
  409.5 26.7 %reduce-scatter.5.cloned.1.call-done = bf16[512,1408]{1,0:T(8,128)(2,1)} async-done(((bf16[2048,1408]{1,0:T(8,128)(2,1)}), bf16[512,1408]{1,0:T(8,128)(2,1)}) %reduce-scatter.5.cloned.1.call-update) | async-done | bytes 1441808 | tf_op jit(solution)/shard_map/reduce_scatter | solution.py:610
  447.0 11.3 %attend_back.1 = (bf16[512,512]{1,0:T(8,128)(2,1)}, bf16[4,512,128]{2,1,0:T(8,128)(2,1)}) custom-call(s32[1]{0:T(128)} %bitcast.1.seen_ref, bf16[512,512]{1,0:T(8,128)(2,1)} %get-tuple-element.84.q_ref, bf16[512,512]{1,0:T(8,128)(2,1)} %bitcast.151, bf16[512,512]{1,0:T(8,128)(2,1)} %get-tuple-element.87.o_ref, ...), custom_call_target="tpu_custom_call" | custom-call | tf_op jit(solution)/shard_map/attend_back/pallas_call | solution.py:285
  458.4 18.6 %collective-permute-done.44 = bf16[128,1408]{1,0:T(8,128)(2,1)} collective-permute-done((bf16[128,1408]{1,0:T(8,128)(2,1)S(1)}, bf16[128,1408]{1,0:T(8,128)(2,1)}, u32[]{:S(2)}, u32[]{:S(2)}) %collective-permute-start.44) | collective-permute-done | bytes 360480 | tf_op jit(solution)/shard_map/ppermute | solution.py:375
  478.6 13.8 %collective-permute-start.48 = (bf16[512,128]{1,0:T(8,128)(2,1)S(1)}, bf16[512,128]{1,0:T(8,128)(2,1)S(1)}, u32[]{:S(2)}, u32[]{:S(2)}) collective-permute-start(bf16[512,128]{1,0:T(8,128)(2,1)S(1)} %get-tuple-element.233), channel_id=1, source_target_pairs={{0,4},{1,5},{2,6},{3,7},{4,8},{5,9},{6,10},{7,11},{8,12},{9,13},{1... | collective-permute-start | bytes 393224 | tf_op jit(solution)/shard_map/ppermute | solution.py:375
  522.7 5.5 fusion.3
  531.5 13.7 %collective-permute-done.50 = bf16[128,2048]{1,0:T(8,128)(2,1)S(1)} collective-permute-done((bf16[128,2048]{1,0:T(8,128)(2,1)S(1)}, bf16[128,2048]{1,0:T(8,128)(2,1)S(1)}, u32[]{:S(2)}, u32[]{:S(2)}) %collective-permute-start.50) | collective-permute-done | bytes 524320 | tf_op jit(solution)/shard_map/ppermute | solution.py:372
  550.4 10.9 %reduce-scatter.11.cloned.1.call-done = bf16[512,320]{0,1:T(8,128)(2,1)} async-done(((bf16[2048,320]{0,1:T(8,128)(2,1)}), bf16[512,320]{0,1:T(8,128)(2,1)}) %reduce-scatter.11.cloned.1.call-update) | async-done | bytes 327696 | tf_op jit(solution)/shard_map/reduce_scatter | solution.py:681
  (431 shorter events, 198.6 us)
Async XLA Ops:
  7.2 89.2 %all-gather.8.cloned.1.call-start = ((), (), s32[]{:S(2)}) async-start(), calls=%async_computation.11 | async-start | bytes 6488064 | tf_op jit(solution)/shard_map/all_gather | solution.py:484
  19.1 138.0 %all-gather.10.cloned.1.call-start = ((), (), s32[]{:S(2)}) async-start(), calls=%async_computation.12 | async-start | bytes 2359296 | tf_op jit(solution)/shard_map/all_gather | solution.py:489
  30.9 28.8 %collective-permute-start.4 = (bf16[512,320]{1,0:T(8,128)(2,1)S(1)}, bf16[512,320]{1,0:T(8,128)(2,1)S(1)}, u32[]{:S(2)}, u32[]{:S(2)}) collective-permute-start(bf16[512,320]{1,0:T(8,128)(2,1)S(1)} %bitcast.138), channel_id=1, source_target_pairs={{0,8},{1,9},{2,10},{3,11},{4,12},{5,13},{6,14},{7,15},{8,0},{9,1},... | collective-permute-start | bytes 983048 | tf_op jit(solution)/shard_map/ppermute | solution.py:375
  30.9 28.9 %collective-permute-start.5 = (bf16[512,320]{1,0:T(8,128)(2,1)S(1)}, bf16[512,320]{1,0:T(8,128)(2,1)S(1)}, u32[]{:S(2)}, u32[]{:S(2)}) collective-permute-start(bf16[512,320]{1,0:T(8,128)(2,1)S(1)} %bitcast.139), channel_id=1, source_target_pairs={{0,4},{1,5},{2,6},{3,7},{4,8},{5,9},{6,10},{7,11},{8,12},{9,13},{1... | collective-permute-start | bytes 983048 | tf_op jit(solution)/shard_map/ppermute | solution.py:375
  32.4 43.5 %collective-permute-start.9 = (bf16[128,2048]{1,0:T(8,128)(2,1)S(1)}, bf16[128,2048]{1,0:T(8,128)(2,1)}, u32[]{:S(2)}, u32[]{:S(2)}) collective-permute-start(bf16[128,2048]{1,0:T(8,128)(2,1)S(1)} %fusion.22), channel_id=1, source_target_pairs={{0,1},{1,0},{2,3},{3,2},{4,5},{5,4},{6,7},{7,6},{8,9},{9,8},{10,11... | collective-permute-start | bytes 1572872 | tf_op jit(solution)/shard_map/ppermute | solution.py:372
  33.3 47.3 %collective-permute-start.10 = (bf16[128,2048]{1,0:T(8,128)(2,1)S(1)}, bf16[128,2048]{1,0:T(8,128)(2,1)}, u32[]{:S(2)}, u32[]{:S(2)}) collective-permute-start(bf16[128,2048]{1,0:T(8,128)(2,1)S(1)} %fusion.22), channel_id=1, source_target_pairs={{0,2},{1,3},{2,0},{3,1},{4,6},{5,7},{6,4},{7,5},{8,10},{9,11},{10,... | collective-permute-start | bytes 1572872 | tf_op jit(solution)/shard_map/ppermute | solution.py:372
  61.8 41.4 %collective-permute-start.13 = (bf16[2048,320]{0,1:T(8,128)(2,1)}, bf16[2048,320]{0,1:T(8,128)(2,1)}, u32[]{:S(2)}, u32[]{:S(2)}) collective-permute-start(bf16[2048,320]{0,1:T(8,128)(2,1)} %copy.48), channel_id=1, source_target_pairs={{0,16},{16,0},{1,17},{17,1},{2,18},{18,2},{3,19},{19,3},{4,20},{20... | collective-permute-start | bytes 3932168 | tf_op jit(solution)/shard_map/ppermute | solution.py:378
  75.1 40.2 %collective-permute-start.6 = (bf16[128,1408]{1,0:T(8,128)(2,1)}, bf16[128,1408]{1,0:T(8,128)(2,1)}, u32[]{:S(2)}, u32[]{:S(2)}) collective-permute-start(bf16[128,1408]{1,0:T(8,128)(2,1)} %get-tuple-element.214), channel_id=1, source_target_pairs={{0,4},{1,5},{2,6},{3,7},{4,8},{5,9},{6,10},{7,11},{8,12},{9,13},{1... | collective-permute-start | bytes 1081352 | tf_op jit(solution)/shard_map/ppermute | solution.py:375
  75.9 39.4 %collective-permute-start.7 = (bf16[128,1408]{1,0:T(8,128)(2,1)}, bf16[128,1408]{1,0:T(8,128)(2,1)}, u32[]{:S(2)}, u32[]{:S(2)}) collective-permute-start(bf16[128,1408]{1,0:T(8,128)(2,1)} %get-tuple-element.213), channel_id=1, source_target_pairs={{0,8},{1,9},{2,10},{3,11},{4,12},{5,13},{6,14},{7,15},{8,0},{9,1},... | collective-permute-start | bytes 1081352 | tf_op jit(solution)/shard_map/ppermute | solution.py:375
  96.5 131.5 %all-gather.6.cloned.1.call-start = ((), (), s32[]{:S(2)}) async-start(), calls=%async_computation.6 | async-start | bytes 12976128 | tf_op jit(solution)/shard_map/all_gather | solution.py:525
  100.9 26.5 %collective-permute-start.8 = (bf16[128,1408]{1,0:T(8,128)(2,1)}, bf16[128,1408]{1,0:T(8,128)(2,1)}, u32[]{:S(2)}, u32[]{:S(2)}) collective-permute-start(bf16[128,1408]{1,0:T(8,128)(2,1)} %get-tuple-element.212), channel_id=1, source_target_pairs={{0,12},{1,13},{2,14},{3,15},{4,0},{5,1},{6,2},{7,3},{8,4},{9,5},{1... | collective-permute-start | bytes 1081352 | tf_op jit(solution)/shard_map/ppermute | solution.py:375
  131.8 277.7 %reduce-scatter.7.cloned.1.call-start = ((), (), s32[]{:S(2)}) async-start(), calls=%async_computation.8 | async-start | bytes 3604480 | tf_op jit(solution)/shard_map/reduce_scatter | solution.py:611
  145.9 47.5 %collective-permute-start.22 = (bf16[128,2048]{1,0:T(8,128)(2,1)S(1)}, bf16[128,2048]{1,0:T(8,128)(2,1)}, u32[]{:S(2)}, u32[]{:S(2)}) collective-permute-start(bf16[128,2048]{1,0:T(8,128)(2,1)S(1)} %bitcast_convert_fusion), channel_id=1, source_target_pairs={{0,8},{1,9},{2,10},{3,11},{4,12},{5,13},{6,14},{7,15},{8,0},{9,1},... | collective-permute-start | bytes 1572872 | tf_op jit(solution)/shard_map/ppermute | solution.py:375
  147.8 45.6 %collective-permute-start.21 = (bf16[128,2048]{1,0:T(8,128)(2,1)S(1)}, bf16[128,2048]{1,0:T(8,128)(2,1)}, u32[]{:S(2)}, u32[]{:S(2)}) collective-permute-start(bf16[128,2048]{1,0:T(8,128)(2,1)S(1)} %bitcast_convert_fusion), channel_id=1, source_target_pairs={{0,4},{1,5},{2,6},{3,7},{4,8},{5,9},{6,10},{7,11},{8,12},{9,13},{1... | collective-permute-start | bytes 1572872 | tf_op jit(solution)/shard_map/ppermute | solution.py:375
  160.3 36.0 %collective-permute-start.20 = (bf16[128,2048]{1,0:T(8,128)(2,1)S(1)}, bf16[128,2048]{1,0:T(8,128)(2,1)S(1)}, u32[]{:S(2)}, u32[]{:S(2)}) collective-permute-start(bf16[128,2048]{1,0:T(8,128)(2,1)S(1)} %get-tuple-element.193), channel_id=1, source_target_pairs={{0,3},{1,2},{2,1},{3,0},{4,7},{5,6},{6,5},{7,4},{8,11},{9,10},{10,... | collective-permute-start | bytes 1572872 | tf_op jit(solution)/shard_map/ppermute | solution.py:372
  160.5 35.7 %collective-permute-start.19 = (bf16[128,2048]{1,0:T(8,128)(2,1)S(1)}, bf16[128,2048]{1,0:T(8,128)(2,1)S(1)}, u32[]{:S(2)}, u32[]{:S(2)}) collective-permute-start(bf16[128,2048]{1,0:T(8,128)(2,1)S(1)} %get-tuple-element.194), channel_id=1, source_target_pairs={{0,2},{1,3},{2,0},{3,1},{4,6},{5,7},{6,4},{7,5},{8,10},{9,11},{10,... | collective-permute-start | bytes 1572872 | tf_op jit(solution)/shard_map/ppermute | solution.py:372
  161.2 35.0 %collective-permute-start.18 = (bf16[128,2048]{1,0:T(8,128)(2,1)S(1)}, bf16[128,2048]{1,0:T(8,128)(2,1)S(1)}, u32[]{:S(2)}, u32[]{:S(2)}) collective-permute-start(bf16[128,2048]{1,0:T(8,128)(2,1)S(1)} %get-tuple-element.192), channel_id=1, source_target_pairs={{0,1},{1,0},{2,3},{3,2},{4,5},{5,4},{6,7},{7,6},{8,9},{9,8},{10,11... | collective-permute-start | bytes 1572872 | tf_op jit(solution)/shard_map/ppermute | solution.py:372
  247.6 36.3 %collective-permute-start.32 = (bf16[512,1408]{1,0:T(8,128)(2,1)}, bf16[512,1408]{1,0:T(8,128)(2,1)}, u32[]{:S(2)}, u32[]{:S(2)}) collective-permute-start(bf16[512,1408]{1,0:T(8,128)(2,1)} %get-tuple-element.106), channel_id=1, source_target_pairs={{0,16},{16,0},{1,17},{17,1},{2,18},{18,2},{3,19},{19,3},{4,20},{20... | collective-permute-start | bytes 4325384 | tf_op jit(solution)/shard_map/ppermute | solution.py:378
  278.1 39.6 %collective-permute-start.30 = (bf16[128,2048]{1,0:T(8,128)(2,1)}, bf16[128,2048]{1,0:T(8,128)(2,1)S(1)}, u32[]{:S(2)}, u32[]{:S(2)}) collective-permute-start(bf16[128,2048]{1,0:T(8,128)(2,1)} %get-tuple-element.190), channel_id=1, source_target_pairs={{0,8},{1,9},{2,10},{3,11},{4,12},{5,13},{6,14},{7,15},{8,0},{9,1},... | collective-permute-start | bytes 1572872 | tf_op jit(solution)/shard_map/ppermute | solution.py:375
  282.9 34.7 %collective-permute-start.31 = (bf16[128,2048]{1,0:T(8,128)(2,1)}, bf16[128,2048]{1,0:T(8,128)(2,1)}, u32[]{:S(2)}, u32[]{:S(2)}) collective-permute-start(bf16[128,2048]{1,0:T(8,128)(2,1)} %get-tuple-element.189), channel_id=1, source_target_pairs={{0,4},{1,5},{2,6},{3,7},{4,8},{5,9},{6,10},{7,11},{8,12},{9,13},{1... | collective-permute-start | bytes 1572872 | tf_op jit(solution)/shard_map/ppermute | solution.py:375
  317.7 118.5 %reduce-scatter.5.cloned.1.call-start = ((), (), s32[]{:S(2)}) async-start(), calls=%async_computation.7 | async-start | bytes 7208960 | tf_op jit(solution)/shard_map/reduce_scatter | solution.py:610
  339.5 166.6 %reduce-scatter.9.cloned.1.call-start = ((), (), s32[]{:S(2)}) async-start(), calls=%async_computation.9 | async-start | bytes 1310720 | tf_op jit(solution)/shard_map/reduce_scatter | solution.py:629
  339.6 103.3 %collective-permute-start.52 = (bf16[512,2048]{1,0:T(8,128)(2,1)}, bf16[512,2048]{1,0:T(8,128)(2,1)}, u32[]{:S(2)}, u32[]{:S(2)}) collective-permute-start(bf16[512,2048]{1,0:T(8,128)(2,1)} %get-tuple-element.252.low_ref), channel_id=1, source_target_pairs={{0,16},{16,0},{1,17},{17,1},{2,18},{18,2},{3,19},{19,3},{4,20},{20... | collective-permute-start | bytes 6291464 | tf_op jit(solution)/shard_map/ppermute | solution.py:378
  354.9 23.6 %collective-permute-start.34 = (bf16[128,2048]{1,0:T(8,128)(2,1)S(1)}, bf16[128,2048]{1,0:T(8,128)(2,1)}, u32[]{:S(2)}, u32[]{:S(2)}) collective-permute-start(bf16[128,2048]{1,0:T(8,128)(2,1)S(1)} %get-tuple-element.186), channel_id=1, source_target_pairs={{0,12},{1,13},{2,14},{3,15},{4,0},{5,1},{6,2},{7,3},{8,4},{9,5},{1... | collective-permute-start | bytes 1572872 | tf_op jit(solution)/shard_map/ppermute | solution.py:375
  356.7 35.2 %collective-permute-start.35 = (bf16[128,2048]{1,0:T(8,128)(2,1)S(1)}, bf16[128,2048]{1,0:T(8,128)(2,1)}, u32[]{:S(2)}, u32[]{:S(2)}) collective-permute-start(bf16[128,2048]{1,0:T(8,128)(2,1)S(1)} %get-tuple-element.184), channel_id=1, source_target_pairs={{0,8},{1,9},{2,10},{3,11},{4,12},{5,13},{6,14},{7,15},{8,0},{9,1},... | collective-permute-start | bytes 1572872 | tf_op jit(solution)/shard_map/ppermute | solution.py:375
  439.6 37.3 %collective-permute-start.44 = (bf16[128,1408]{1,0:T(8,128)(2,1)S(1)}, bf16[128,1408]{1,0:T(8,128)(2,1)}, u32[]{:S(2)}, u32[]{:S(2)}) collective-permute-start(bf16[128,1408]{1,0:T(8,128)(2,1)S(1)} %get-tuple-element.209), channel_id=1, source_target_pairs={{0,8},{1,9},{2,10},{3,11},{4,12},{5,13},{6,14},{7,15},{8,0},{9,1},... | collective-permute-start | bytes 1081352 | tf_op jit(solution)/shard_map/ppermute | solution.py:375
  441.8 35.7 %collective-permute-start.45 = (bf16[128,1408]{1,0:T(8,128)(2,1)S(1)}, bf16[128,1408]{1,0:T(8,128)(2,1)}, u32[]{:S(2)}, u32[]{:S(2)}) collective-permute-start(bf16[128,1408]{1,0:T(8,128)(2,1)S(1)} %get-tuple-element.208), channel_id=1, source_target_pairs={{0,12},{1,13},{2,14},{3,15},{4,0},{5,1},{6,2},{7,3},{8,4},{9,5},{1... | collective-permute-start | bytes 1081352 | tf_op jit(solution)/shard_map/ppermute | solution.py:375
  446.2 115.2 %reduce-scatter.11.cloned.1.call-start = ((), (), s32[]{:S(2)}) async-start(), calls=%async_computation.10 | async-start | bytes 1638400 | tf_op jit(solution)/shard_map/reduce_scatter | solution.py:681
  518.1 27.1 %collective-permute-start.50 = (bf16[128,2048]{1,0:T(8,128)(2,1)S(1)}, bf16[128,2048]{1,0:T(8,128)(2,1)S(1)}, u32[]{:S(2)}, u32[]{:S(2)}) collective-permute-start(bf16[128,2048]{1,0:T(8,128)(2,1)S(1)} %get-tuple-element.181), channel_id=1, source_target_pairs={{0,2},{1,3},{2,0},{3,1},{4,6},{5,7},{6,4},{7,5},{8,10},{9,11},{10,... | collective-permute-start | bytes 1572872 | tf_op jit(solution)/shard_map/ppermute | solution.py:372
  519.3 28.4 %collective-permute-start.49 = (bf16[128,2048]{1,0:T(8,128)(2,1)S(1)}, bf16[128,2048]{1,0:T(8,128)(2,1)S(1)}, u32[]{:S(2)}, u32[]{:S(2)}) collective-permute-start(bf16[128,2048]{1,0:T(8,128)(2,1)S(1)} %get-tuple-element.179), channel_id=1, source_target_pairs={{0,1},{1,0},{2,3},{3,2},{4,5},{5,4},{6,7},{7,6},{8,9},{9,8},{10,11... | collective-permute-start | bytes 1572872 | tf_op jit(solution)/shard_map/ppermute | solution.py:372
  521.1 27.0 %collective-permute-start.55 = (bf16[352,1024]{1,0:T(8,128)(2,1)S(1)}, bf16[352,1024]{1,0:T(8,128)(2,1)S(1)}, u32[]{:S(2)}, u32[]{:S(2)}) collective-permute-start(bf16[352,1024]{1,0:T(8,128)(2,1)S(1)} %copy-done.29), channel_id=1, source_target_pairs={{0,16},{16,0},{1,17},{17,1},{2,18},{18,2},{3,19},{19,3},{4,20},{20... | collective-permute-start | bytes 2162696 | tf_op jit(solution)/shard_map/ppermute | solution.py:378
  528.1 45.6 %collective-permute-start.58 = (bf16[128,1024]{1,0:T(8,128)(2,1)}, bf16[128,1024]{1,0:T(8,128)(2,1)}, u32[]{:S(2)}, u32[]{:S(2)}) collective-permute-start(bf16[128,1024]{1,0:T(8,128)(2,1)} %collective-permute-done.57), channel_id=1, source_target_pairs={{0,16},{16,0},{1,17},{17,1},{2,18},{18,2},{3,19},{19,3},{4,20},{20... | collective-permute-start | bytes 786440 | tf_op jit(solution)/shard_map/ppermute | solution.py:378
  (99 other events, 854.0 us)
Sparse Core Ops, SparseCore 0:
  10.5 54.0 all-gather.7
  96.6 40.1 all-gather.9
  138.8 89.1 all-gather.5
  317.8 45.2 reduce-scatter.6
  366.0 70.2 reduce-scatter.4
  446.3 40.7 reduce-scatter.8
  512.9 48.3 reduce-scatter.10
